TPU v7x, 512 devices: a whole 4x8x8 slice. The times are simulated.
512 devices in a mesh: dp: 4 (over x), expert: 16 (over z, core), etp: 8 (over y).
Axes of the slice: x: 4, y: 8, z: 8, core: 2. Of those that a mesh axis runs over, the one named last changes fastest.
Arguments:
- tokens: bfloat16 [9728, 4096], P(('dp', 'expert'), 'etp'), may hold values from -6 to 6
- cotangent: bfloat16 [9728, 4096], P(('dp', 'expert'), 'etp'), may hold values from -6 to 6
- gates: bfloat16 [9728, 8], P(('dp', 'expert')), may hold values from 0.049804688 to 0.5
- experts_hit: int32 [9728, 8], P(('dp', 'expert')), may hold values from -1 to 15, as said below
- positions: int32 [9728, 8], P(('dp', 'expert')), may hold values from -1 to 18, as said below
- gate_w: bfloat16 [16, 4096, 1536], P('expert', 'dp', 'etp'), may hold values from -0.09375 to 0.09375
- up_w: bfloat16 [16, 4096, 1536], P('expert', 'dp', 'etp'), may hold values from -0.09375 to 0.09375
- down_w: bfloat16 [16, 1536, 4096], P('expert', 'etp', 'dp'), may hold values from -0.15625 to 0.15625
Outputs:
- input_grad: bfloat16 [9728, 4096], P(('dp', 'expert'), 'etp')
- down_grad: bfloat16 [16, 1536, 4096], P('expert', 'etp', 'dp')
Inputs may be any that keep to these rules, and one draw needn't show every extreme that they name: experts_hit and positions are -1 together, for routes to experts outside these 16. In the rows of one device, the routes to one expert hold positions 0 to n - 1 once each, with n between 1 and 19; no token names an expert twice. `positions`: see experts_hit.
All inputs are finite; a program needn't handle non-finite values.
Results may differ from a plain program's by a relative error of at most 0.018.
Values may be sent and summed in bfloat16 or wider, within the bound.
No kernel may reach another device: no remote copies, remote signals or barrier semaphores. Data moves between devices by JAX's collectives and lax.ppermute only.
A program may use at most 64 MiB of HBM per device.

v0:
```python
import jax
import jax.numpy as jnp
from jax import lax
from jax.sharding import PartitionSpec as P

CAP = 19


def expert_grads(feats, grads, gate_col, w_gate, w_up, w_down):
    gate_pre = jnp.dot(feats, w_gate, preferred_element_type=jnp.float32)
    up_pre = jnp.dot(feats, w_up, preferred_element_type=jnp.float32)
    sig = jax.nn.sigmoid(gate_pre)
    act = gate_pre * sig
    hidden_b = (act * up_pre).astype(jnp.bfloat16)
    back = lax.dot_general(
        grads, w_down, (((1,), (1,)), ((), ())), preferred_element_type=jnp.float32
    )
    gate_f = gate_col.astype(jnp.float32)[:, None]
    d_hidden = gate_f * back
    d_gate_b = (d_hidden * up_pre * sig * (1.0 + gate_pre * (1.0 - sig))).astype(jnp.bfloat16)
    d_up_b = (d_hidden * act).astype(jnp.bfloat16)
    d_part = lax.dot_general(
        d_gate_b, w_gate, (((1,), (1,)), ((), ())), preferred_element_type=jnp.float32
    )
    d_part = d_part + lax.dot_general(
        d_up_b, w_up, (((1,), (1,)), ((), ())), preferred_element_type=jnp.float32
    )
    scaled = (gate_f * grads).astype(jnp.bfloat16)
    term = lax.dot_general(
        hidden_b, scaled, (((0,), (0,)), ((), ())), preferred_element_type=jnp.float32
    )
    return (d_part.astype(jnp.bfloat16), term)


def local(tokens, cotangent, gates, experts_hit, positions, gate_w, up_w, down_w):
    width = lax.axis_size("expert")
    rows_dev = tokens.shape[0]
    routes = experts_hit.shape[1]
    slots = width * CAP
    valid = experts_hit >= 0
    flat = jnp.where(valid, experts_hit * CAP + positions, slots)
    flat_all = flat.reshape(-1)
    token_ids = jnp.repeat(jnp.arange(rows_dev, dtype=jnp.int32), routes)
    owner = jnp.zeros((slots + 1,), jnp.int32).at[flat_all].set(token_ids)[:slots]
    filled = jnp.zeros((slots + 1,), jnp.bool_).at[flat_all].set(True)[:slots]
    slot_gate = jnp.zeros((slots + 1,), jnp.bfloat16).at[flat_all].set(gates.reshape(-1))[:slots]
    slot_gate = slot_gate.reshape(width, CAP)

    def pack(source):
        rows = jnp.where(filled[:, None], source[owner], jnp.zeros((), source.dtype))
        return rows.reshape(width, CAP, source.shape[1])

    full_x, full_dy = (
        lax.all_gather(tokens, "etp", axis=1, tiled=True),
        lax.all_gather(cotangent, "etp", axis=1, tiled=True),
    )
    recv_x, recv_dy, recv_gate = (
        lax.all_to_all(pack(full_x), "expert", split_axis=0, concat_axis=0, tiled=True),
        lax.all_to_all(pack(full_dy), "expert", split_axis=0, concat_axis=0, tiled=True),
        lax.all_to_all(slot_gate, "expert", split_axis=0, concat_axis=0, tiled=True),
    )
    full_width = recv_x.shape[2]
    feats = recv_x.reshape(slots, full_width)
    grads = recv_dy.reshape(slots, full_width)
    w_gate, w_up, w_down = (
        lax.all_gather(gate_w[0], "dp", axis=0, tiled=True),
        lax.all_gather(up_w[0], "dp", axis=0, tiled=True),
        lax.all_gather(down_w[0], "dp", axis=1, tiled=True),
    )
    d_part_b, term = expert_grads(feats, grads, recv_gate.reshape(slots), w_gate, w_up, w_down)
    down_grad = lax.psum_scatter(term.astype(jnp.bfloat16), "dp", scatter_dimension=1, tiled=True)[
        None
    ]
    summed = lax.psum_scatter(
        d_part_b.astype(jnp.float32).astype(jnp.bfloat16), "etp", scatter_dimension=1, tiled=True
    ).astype(jnp.float32)
    returned = lax.all_to_all(
        summed.reshape(width, CAP, summed.shape[1]).astype(jnp.bfloat16),
        "expert",
        split_axis=0,
        concat_axis=0,
        tiled=True,
    ).astype(jnp.float32)
    narrow = returned.shape[2]
    table = jnp.concatenate(
        [returned.reshape(slots, narrow), jnp.zeros((1, narrow), jnp.float32)], axis=0
    )
    total = jnp.zeros((rows_dev, narrow), jnp.float32)
    for route in range(routes):
        total = total + table[flat[:, route]]
    input_grad = total.astype(jnp.bfloat16)
    return (input_grad, down_grad)


def solution(mesh):
    placed = (
        P(("dp", "expert"), "etp"),
        P(("dp", "expert"), "etp"),
        P(("dp", "expert"), None),
        P(("dp", "expert"), None),
        P(("dp", "expert"), None),
        P("expert", "dp", "etp"),
        P("expert", "dp", "etp"),
        P("expert", "etp", "dp"),
    )
    return jax.shard_map(
        local,
        mesh=mesh,
        in_specs=placed,
        out_specs=(P(("dp", "expert"), "etp"), P("expert", "etp", "dp")),
        check_vma=False,
    )
```

profile of v0, /device:TPU:1, one launch (start us, length us, event | category | flops | bytes accessed | tf_op | source)
XLA Modules:
  0.0 373.5 jit_solution(14487152539822425806)
XLA Ops:
  8.0 0.0 all-gather.9.cloned.1.call-start
  8.0 0.7 all-gather.9.cloned.1.call-update
  8.7 0.0 all-gather.11.cloned.1.call-start
  8.8 0.7 all-gather.11.cloned.1.call-update
  9.5 0.7 add_select_fusion
  10.2 0.1 copy.12
  10.3 0.1 reshape.80
  10.4 0.8 copy.13
  11.2 0.1 reshape.171
  11.4 12.6 %scatter_custom_fusion = bf16[305]{0:T(512)(128)(2,1)S(1)} fusion(s32[1216]{0:T(1024)S(1)} %fusion.18, bf16[1216]{0:T(1024)(128)(2,1)S(1)} %reshape.171, bf16[]{:T(256)} %constant.9.clone.1), kind=kCustom, calls=%fused_computation.64 | custom fusion | bytes 612 | tf_op jit(solution)/shard_map/scatter | solution.py:46
  24.0 0.7 all_to_all.20
  24.7 11.8 %all-to-all-start = ((bf16[16,1,19]{2,1,0:T(2,128)(2,1)}), bf16[16,1,19]{2,1,0:T(2,128)(2,1)S(1)}, u32[]{:S(2)}, u32[]{:S(2)}) async-start(bf16[16,1,19]{2,1,0:T(2,128)(2,1)} %all_to_all.20), calls=%async_computation | async-start | bytes 16384 | tf_op jit(solution)/shard_map/all_to_all | solution.py:60
  36.6 0.1 reshape.187
  36.7 11.4 %scatter_custom_fusion.1 = pred[305]{0:T(512)(128)(4,1)S(1)} fusion(s32[1216]{0:T(1024)S(1)} %fusion.18, pred[1216]{0:T(1024)(128)(4,1)S(1)} %broadcast.66, pred[]{:T(512)} %constant.14.clone.1), kind=kCustom, calls=%fused_computation.62 | custom fusion | bytes 306 | tf_op jit(solution)/shard_map/scatter | solution.py:45
  48.1 0.1 broadcast_in_dim.63
  48.2 6.4 %scatter_custom_fusion.2 = s32[305]{0:T(512)S(1)} fusion(s32[1216]{0:T(1024)S(1)} %fusion.18, s32[1216]{0:T(1024)S(1)} %reshape.187, s32[]{:T(128)} %constant.10.clone.1), kind=kCustom, calls=%fused_computation.60 | custom fusion | bytes 1224 | tf_op jit(solution)/shard_map/scatter | solution.py:44
  54.6 9.5 %gather_fusion = bf16[304,4096]{1,0:T(8,128)(2,1)} fusion(bf16[152,4096]{1,0:T(8,128)(2,1)} %all-gather.9.cloned.1.call-done, s32[1024]{0:T(1024)S(1)} %pad_clamp_fusion.8), kind=kCustom, calls=%fused_computation | custom fusion | bytes 4981952 | tf_op jit(solution)/shard_map/gather | solution.py:50
  64.1 2.2 gather.35
  66.3 30.1 %all-gather.11.cloned.1.call-done = bf16[152,4096]{1,0:T(8,128)(2,1)} async-done(((bf16[152,512]{1,0:T(8,128)(2,1)}), bf16[152,4096]{1,0:T(8,128)(2,1)}) %all-gather.11.cloned.1.call-update) | async-done | bytes 1245200 | tf_op jit(solution)/shard_map/all_gather | solution.py:54
  96.3 9.5 %gather_fusion.1 = bf16[304,4096]{1,0:T(8,128)(2,1)} fusion(bf16[152,4096]{1,0:T(8,128)(2,1)} %all-gather.11.cloned.1.call-done, s32[1024]{0:T(1024)S(1)} %pad_clamp_fusion.8), kind=kCustom, calls=%fused_computation.1 | custom fusion | bytes 4981952 | tf_op jit(solution)/shard_map/gather | solution.py:50
  105.8 3.4 gather.37
  109.2 5.0 %broadcast_select_fusion.1 = (bf16[16,19,4096]{2,1,0:T(8,128)(2,1)}, bf16[16,19,4096]{2,1,0:T(8,128)(2,1)}) fusion(bf16[16,19,4096]{2,1,0:T(8,128)(2,1)S(1)} %gather.35, pred[16,19]{1,0:T(8,128)(4,1)S(1)} %broadcast_in_dim.63, bf16[16,19,4096]{2,1,0:T(8,128)(2,1)} %gather.37), kind=kLoop, calls=%fused_computation.18 | loop fusion | flops 2490368 | bytes 9961776 | tf_op jit(solution)/shard_map/jit(_where)/select_n | solution.py:50
  114.2 12.3 %all-to-all-start.1 = ((bf16[16,19,4096]{2,1,0:T(8,128)(2,1)}), bf16[16,19,4096]{2,1,0:T(8,128)(2,1)S(1)}, u32[]{:S(2)}, u32[]{:S(2)}) async-start(bf16[16,19,4096]{2,1,0:T(8,128)(2,1)} %get-tuple-element.10), calls=%async_computation.1 | async-start | bytes 6291456 | tf_op jit(solution)/shard_map/all_to_all | solution.py:59
  126.4 0.0 all-gather.17.cloned.1.call-start
  126.5 0.5 all-gather.17.cloned.1.call-update
  127.0 70.4 %all-to-all-done.1 = bf16[16,19,4096]{2,1,0:T(8,128)(2,1)S(1)} async-done(((bf16[16,19,4096]{2,1,0:T(8,128)(2,1)}), bf16[16,19,4096]{2,1,0:T(8,128)(2,1)S(1)}, u32[]{:S(2)}, u32[]{:S(2)}) %all-to-all-start.1) | async-done | bytes 2490400 | tf_op jit(solution)/shard_map/all_to_all | solution.py:59
  197.4 5.4 %all-to-all-start.2 = ((bf16[16,19,4096]{2,1,0:T(8,128)(2,1)}), bf16[16,19,4096]{2,1,0:T(8,128)(2,1)}, u32[]{:S(2)}, u32[]{:S(2)}) async-start(bf16[16,19,4096]{2,1,0:T(8,128)(2,1)} %get-tuple-element.11), calls=%async_computation.2 | async-start | bytes 6291456 | tf_op jit(solution)/shard_map/all_to_all | solution.py:58
  202.9 0.0 all-gather.15.cloned.1.call-start
  202.9 0.5 all-gather.15.cloned.1.call-update
  203.4 0.0 all-gather.13.cloned.1.call-start
  203.5 0.5 all-gather.13.cloned.1.call-update
  204.0 0.3 reduce-scatter.3.cloned.1.call-start
  204.3 0.1 reshape.86
  204.4 2.1 reshape.83
  206.5 67.5 %all-to-all-done.2 = bf16[16,19,4096]{2,1,0:T(8,128)(2,1)} async-done(((bf16[16,19,4096]{2,1,0:T(8,128)(2,1)}), bf16[16,19,4096]{2,1,0:T(8,128)(2,1)}, u32[]{:S(2)}, u32[]{:S(2)}) %all-to-all-start.2) | async-done | bytes 2490400 | tf_op jit(solution)/shard_map/all_to_all | solution.py:58
  273.9 2.3 reshape.84
  276.3 0.0 all-gather.17.cloned.1.call-done
  276.3 1.4 copy-done.1
  277.8 2.6 fusion.4
  280.4 0.0 all-gather.15.cloned.1.call-done
  280.4 3.5 fusion.7
  283.9 0.0 all-gather.13.cloned.1.call-done
  283.9 2.7 fusion.11
  286.7 0.9 fusion.2
  287.6 0.5 copy-done.2
  288.1 2.3 fusion
  290.4 0.0 reduce-scatter.5.cloned.1.call-start
  290.5 2.2 convolution_convert_fusion
  292.8 36.3 %reduce-scatter.3.cloned.1.call-done = bf16[304,512]{1,0:T(8,128)(2,1)} async-done(((bf16[304,4096]{1,0:T(8,128)(2,1)}), bf16[304,512]{1,0:T(8,128)(2,1)}) %reduce-scatter.3.cloned.1.call-update) | async-done | bytes 311312 | tf_op jit(solution)/shard_map/reduce_scatter | solution.py:74
  329.1 1.8 convert_element_type.47
  330.9 11.6 %all-to-all-start.3 = ((bf16[16,19,512]{2,1,0:T(8,128)(2,1)}), bf16[16,19,512]{2,1,0:T(8,128)(2,1)S(1)}, u32[]{:S(2)}, u32[]{:S(2)}) async-start(bf16[16,19,512]{2,1,0:T(8,128)(2,1)} %convert_element_type.47), calls=%async_computation.4 | async-start | bytes 786432 | tf_op jit(solution)/shard_map/all_to_all | solution.py:77
  342.6 14.5 %all-to-all-done.3 = bf16[16,19,512]{2,1,0:T(8,128)(2,1)S(1)} async-done(((bf16[16,19,512]{2,1,0:T(8,128)(2,1)}), bf16[16,19,512]{2,1,0:T(8,128)(2,1)S(1)}, u32[]{:S(2)}, u32[]{:S(2)}) %all-to-all-start.3) | async-done | bytes 311328 | tf_op jit(solution)/shard_map/all_to_all | solution.py:77
  357.1 0.1 reshape.85
  357.2 0.1 pad_convert_fusion
  357.3 0.8 gather_fusion.2
  358.1 0.8 gather_fusion.3
  358.9 0.8 gather_fusion.4
  359.7 0.8 gather_fusion.5
  360.5 0.8 gather_fusion.6
  361.3 0.8 gather_fusion.7
  362.1 0.8 gather_fusion.8
  362.9 0.8 gather_fusion.9
  363.7 0.9 add_convert_fusion
  364.6 1.5 reduce-scatter.5.cloned.1.call-done
  (25 shorter events, 0.2 us)
Async XLA Ops:
  8.0 46.6 %all-gather.9.cloned.1.call-start = ((), (), s32[]{:S(2)}) async-start(), calls=%async_computation.6 | async-start | bytes 1400832 | tf_op jit(solution)/shard_map/all_gather | solution.py:55
  8.7 87.6 %all-gather.11.cloned.1.call-start = ((), (), s32[]{:S(2)}) async-start(), calls=%async_computation.7 | async-start | bytes 1400832 | tf_op jit(solution)/shard_map/all_gather | solution.py:54
  24.7 89.5 %all-to-all-start = ((bf16[16,1,19]{2,1,0:T(2,128)(2,1)}), bf16[16,1,19]{2,1,0:T(2,128)(2,1)S(1)}, u32[]{:S(2)}, u32[]{:S(2)}) async-start(bf16[16,1,19]{2,1,0:T(2,128)(2,1)} %all_to_all.20), calls=%async_computation | async-start | bytes 16384 | tf_op jit(solution)/shard_map/all_to_all | solution.py:60
  114.2 83.2 %all-to-all-start.1 = ((bf16[16,19,4096]{2,1,0:T(8,128)(2,1)}), bf16[16,19,4096]{2,1,0:T(8,128)(2,1)S(1)}, u32[]{:S(2)}, u32[]{:S(2)}) async-start(bf16[16,19,4096]{2,1,0:T(8,128)(2,1)} %get-tuple-element.10), calls=%async_computation.1 | async-start | bytes 6291456 | tf_op jit(solution)/shard_map/all_to_all | solution.py:59
  126.4 149.9 %all-gather.17.cloned.1.call-start = ((), (), s32[]{:S(2)}) async-start(), calls=%async_computation.12 | async-start | bytes 1966080 | tf_op jit(solution)/shard_map/all_gather | solution.py:66
  197.4 76.5 %all-to-all-start.2 = ((bf16[16,19,4096]{2,1,0:T(8,128)(2,1)}), bf16[16,19,4096]{2,1,0:T(8,128)(2,1)}, u32[]{:S(2)}, u32[]{:S(2)}) async-start(bf16[16,19,4096]{2,1,0:T(8,128)(2,1)} %get-tuple-element.11), calls=%async_computation.2 | async-start | bytes 6291456 | tf_op jit(solution)/shard_map/all_to_all | solution.py:58
  202.9 77.5 %all-gather.15.cloned.1.call-start = ((), (), s32[]{:S(2)}) async-start(), calls=%async_computation.11 | async-start | bytes 1966080 | tf_op jit(solution)/shard_map/all_gather | solution.py:67
  203.4 80.5 %all-gather.13.cloned.1.call-start = ((), (), s32[]{:S(2)}) async-start(), calls=%async_computation.10 | async-start | bytes 1966080 | tf_op jit(solution)/shard_map/all_gather | solution.py:68
  204.0 125.1 %reduce-scatter.3.cloned.1.call-start = ((), (), s32[]{:S(2)}) async-start(), calls=%async_computation.8 | async-start | bytes 2801664 | tf_op jit(solution)/shard_map/reduce_scatter | solution.py:74
  276.3 1.5 copy-start.1
  280.3 3.6 copy-start
  283.9 2.7 copy-start.3
  286.7 1.4 copy-start.2
  290.4 75.7 %reduce-scatter.5.cloned.1.call-start = ((), (), s32[]{:S(2)}) async-start(), calls=%async_computation.9 | async-start | bytes 1966080 | tf_op jit(solution)/shard_map/reduce_scatter | solution.py:71
  330.9 26.2 %all-to-all-start.3 = ((bf16[16,19,512]{2,1,0:T(8,128)(2,1)}), bf16[16,19,512]{2,1,0:T(8,128)(2,1)S(1)}, u32[]{:S(2)}, u32[]{:S(2)}) async-start(bf16[16,19,512]{2,1,0:T(8,128)(2,1)} %convert_element_type.47), calls=%async_computation.4 | async-start | bytes 786432 | tf_op jit(solution)/shard_map/all_to_all | solution.py:77
Sparse Core Ops, SparseCore 0:
  10.9 42.8 all-gather.8
  55.9 40.3 all-gather.10
  290.6 38.4 reduce-scatter.2
  332.6 33.4 reduce-scatter.4
Sparse Core Ops, SparseCore 1:
  129.0 29.6 all-gather.16
  205.4 29.6 all-gather.14
  237.0 31.8 all-gather.12
where the time goes:
time: 374 us; the launch traced here: 373 us
  waiting for transfers between devices  223 us (60%)
  local copies, waits for them, and re-layouts  71.7 us (19%)
  starting transfers between devices  41.6 us (11%)
  between operations  15.8 us (4%)
  matrix products  14.3 us (4%)
  other arithmetic  6.76 us (2%)
    all_to_all x1, waiting for transfers between devices, local(): lax.all_to_all(pack(full_dy), 'expert', split_axis=0, concat_axis=0, tile...  70.4 us
    all_to_all x1, waiting for transfers between devices, local(): lax.all_to_all(pack(full_x), 'expert', split_axis=0, concat_axis=0, tiled...  67.5 us
    reduce_scatter x1, waiting for transfers between devices, local(): lax.psum_scatter(d_part_b.astype(jnp.float32).astype(jnp.bfloat16), 'etp'...  36.3 us
    all_gather x1, waiting for transfers between devices, local(): lax.all_gather(tokens, 'etp', axis=1, tiled=True)  30.1 us
    gather x4, local copies, waits for them, and re-layouts, pack(): source[owner]  24.5 us
    all_to_all x1, waiting for transfers between devices, local(): lax.all_to_all(summed.reshape(width, CAP, summed.shape[1]).astype(jnp.bfl...  14.5 us
    scatter x1, local copies, waits for them, and re-layouts, local(): jnp.zeros((slots + 1,), jnp.bfloat16).at[flat_all].set(gates.reshape(-1))  12.6 us
    all_to_all x1, starting transfers between devices, local(): lax.all_to_all(pack(full_dy), 'expert', split_axis=0, concat_axis=0, tile...  12.3 us
  transfers between devices with their start and end apart: 11, of which 6 were waited for; matrix products, arithmetic and copies ran while one was open for 23% of the time, Pallas kernels for 0%

commit v1 on v0

v1 whole, which is shorter than its diff:
```python
import jax
import jax.numpy as jnp
from jax import lax
from jax.sharding import PartitionSpec as P

CAP = 19


def expert_grads(feats, grads, gate_col, w_gate, w_up, w_down):
    gate_pre = jnp.dot(feats, w_gate, preferred_element_type=jnp.float32)
    up_pre = jnp.dot(feats, w_up, preferred_element_type=jnp.float32)
    sig = jax.nn.sigmoid(gate_pre)
    act = gate_pre * sig
    hidden_b = (act * up_pre).astype(jnp.bfloat16)
    back = lax.dot_general(
        grads, w_down, (((1,), (1,)), ((), ())), preferred_element_type=jnp.float32
    )
    gate_f = gate_col.astype(jnp.float32)[:, None]
    d_hidden = gate_f * back
    d_gate_b = (d_hidden * up_pre * sig * (1.0 + gate_pre * (1.0 - sig))).astype(jnp.bfloat16)
    d_up_b = (d_hidden * act).astype(jnp.bfloat16)
    d_part = lax.dot_general(
        d_gate_b, w_gate, (((1,), (1,)), ((), ())), preferred_element_type=jnp.float32
    )
    d_part = d_part + lax.dot_general(
        d_up_b, w_up, (((1,), (1,)), ((), ())), preferred_element_type=jnp.float32
    )
    scaled = (gate_f * grads).astype(jnp.bfloat16)
    term = lax.dot_general(
        hidden_b, scaled, (((0,), (0,)), ((), ())), preferred_element_type=jnp.float32
    )
    return (d_part.astype(jnp.bfloat16), term)


def local(tokens, cotangent, gates, experts_hit, positions, gate_w, up_w, down_w):
    width = lax.axis_size("expert")
    rows_dev, routes = experts_hit.shape
    slots = width * CAP
    narrow = tokens.shape[1]
    valid = experts_hit >= 0
    flat = jnp.where(valid, experts_hit * CAP + positions, slots)
    slot_ids = jnp.arange(slots, dtype=jnp.int32)
    hit = flat[None, :, :] == slot_ids[:, None, None]
    onehot = jnp.any(hit, axis=2).astype(jnp.bfloat16)
    slot_gate = jnp.sum(
        jnp.where(hit, gates.astype(jnp.float32)[None, :, :], 0.0), axis=(1, 2)
    ).astype(jnp.bfloat16)
    both = jnp.concatenate([tokens, cotangent], axis=1)
    packed = jnp.dot(onehot, both, preferred_element_type=jnp.float32).astype(jnp.bfloat16)
    recv = lax.all_to_all(
        packed.reshape(width, CAP, 2 * narrow), "expert", split_axis=0, concat_axis=0, tiled=True
    )
    recv_gate = lax.all_to_all(
        slot_gate.reshape(width, CAP), "expert", split_axis=0, concat_axis=0, tiled=True
    )
    pair = recv.reshape(slots, 2, narrow).transpose(1, 0, 2)
    full = lax.all_gather(pair, "etp", axis=2, tiled=True)
    feats = full[0]
    grads = full[1]
    w_gate, w_up, w_down = (
        lax.all_gather(gate_w[0], "dp", axis=0, tiled=True),
        lax.all_gather(up_w[0], "dp", axis=0, tiled=True),
        lax.all_gather(down_w[0], "dp", axis=1, tiled=True),
    )
    d_part_b, term = expert_grads(feats, grads, recv_gate.reshape(slots), w_gate, w_up, w_down)
    down_grad = lax.psum_scatter(term.astype(jnp.bfloat16), "dp", scatter_dimension=1, tiled=True)[
        None
    ]
    summed = lax.psum_scatter(d_part_b, "etp", scatter_dimension=1, tiled=True)
    returned = lax.all_to_all(
        summed.reshape(width, CAP, narrow), "expert", split_axis=0, concat_axis=0, tiled=True
    ).reshape(slots, narrow)
    total = lax.dot_general(
        onehot, returned, (((0,), (0,)), ((), ())), preferred_element_type=jnp.float32
    )
    input_grad = total.astype(jnp.bfloat16)
    return (input_grad, down_grad)


def solution(mesh):
    placed = (
        P(("dp", "expert"), "etp"),
        P(("dp", "expert"), "etp"),
        P(("dp", "expert"), None),
        P(("dp", "expert"), None),
        P(("dp", "expert"), None),
        P("expert", "dp", "etp"),
        P("expert", "dp", "etp"),
        P("expert", "etp", "dp"),
    )
    return jax.shard_map(
        local,
        mesh=mesh,
        in_specs=placed,
        out_specs=(P(("dp", "expert"), "etp"), P("expert", "etp", "dp")),
        check_vma=False,
    )
```

time: 374 us -> 312 us (0.83)
  blocking collectives: 0 us -> 70.6 us
  local copies, waits for them, and re-layouts: 71.7 us -> 16.3 us
  waiting for transfers between devices: 223 us -> 178 us
  starting transfers between devices: 41.6 us -> 0.46 us
  matrix products: 14.3 us -> 30.4 us
  other arithmetic: 6.76 us -> 1.81 us
    all_to_all x4 -> x0, waiting for transfers between devices: 152 us -> none  [the longest x1 70.4 us: local(): lax.all_to_all(pack(full_dy), 'expert', split_axis=0, concat_axis=0, tile...]
    all_to_all x0 -> x3, blocking collectives: none -> 70.6 us  [the longest x1 34.6 us: local(): lax.all_to_all(packed.reshape(width, CAP, 2 * narrow), 'expert', split_ax...]
    all_to_all x4 -> x0, starting transfers between devices: 41.1 us -> none  [the longest x1 12.3 us: local(): lax.all_to_all(pack(full_dy), 'expert', split_axis=0, concat_axis=0, tile...]
    gather x12 -> x0, local copies, waits for them, and re-layouts: 30.9 us -> none  [the longest x4 24.5 us: pack(): source[owner]]
    scatter x3 -> x0, local copies, waits for them, and re-layouts: 30.4 us -> none  [the longest x1 12.6 us: local(): jnp.zeros((slots + 1,), jnp.bfloat16).at[flat_all].set(gates.reshape(-1))]
    all_gather x1, waiting for transfers between devices: 0.03 us -> 28.2 us  [local(): lax.all_gather(up_w[0], 'dp', axis=0, tiled=True)]
    all_gather x1, waiting for transfers between devices: 0.03 us -> 28 us  [local(): lax.all_gather(down_w[0], 'dp', axis=1, tiled=True)]
    all_gather x2 -> x1, waiting for transfers between devices: 30.1 us -> 53.1 us  [local(): full = lax.all_gather(pair, 'etp', axis=2, tiled=True)]
  transfers between devices with their start and end apart: 11 -> 6, of which waited for: 6 -> 6; matrix products, arithmetic and copies ran while one was open for 23% -> 11% of each run, Pallas kernels for 0% -> 0%
where the time goes in v1:
time: 312 us
  waiting for transfers between devices  178 us (57%)
  blocking collectives  70.6 us (23%)
  matrix products  30.4 us (10%)
  local copies, waits for them, and re-layouts  16.3 us (5%)
  between operations  14.2 us (5%)
    all_gather x1, waiting for transfers between devices, local(): full = lax.all_gather(pair, 'etp', axis=2, tiled=True)  53.1 us
    reduce_scatter x1, waiting for transfers between devices, local(): summed = lax.psum_scatter(d_part_b, 'etp', scatter_dimension=1, tiled=True)  35.1 us
    all_to_all x1, blocking collectives, local(): lax.all_to_all(packed.reshape(width, CAP, 2 * narrow), 'expert', split_ax...  34.6 us
    all_gather x1, waiting for transfers between devices, local(): lax.all_gather(up_w[0], 'dp', axis=0, tiled=True)  28.2 us
    all_gather x1, waiting for transfers between devices, local(): lax.all_gather(down_w[0], 'dp', axis=1, tiled=True)  28 us
    all_to_all x1, blocking collectives, local(): lax.all_to_all(summed.reshape(width, CAP, narrow), 'expert', split_axis=0...  26.4 us
    all_gather x1, waiting for transfers between devices, local(): lax.all_gather(gate_w[0], 'dp', axis=0, tiled=True)  22.7 us
    slice x1, local copies, waits for them, and re-layouts, local(): grads = full[1]  12.9 us
  transfers between devices with their start and end apart: 6, of which 6 were waited for; matrix products, arithmetic and copies ran while one was open for 11% of the time, Pallas kernels for 0%

profile of v1, /device:TPU:1, one launch (start us, length us, event | category | flops | bytes accessed | tf_op | source)
XLA Modules:
  0.0 311.6 jit_solution(13129486732746623393)
XLA Ops:
  7.2 0.0 all-gather.8.cloned.1.call-start
  7.2 0.7 add_select_fusion
  7.9 0.1 copy.17
  8.0 0.7 fusion.9
  8.7 1.4 convolution_convert_fusion.1
  10.1 0.2 reshape.42
  10.3 0.0 copy-start.2
  10.3 34.6 %all_to_all.16 = bf16[16,19,1024]{2,1,0:T(8,128)(2,1)S(1)} all-to-all(bf16[16,19,1024]{2,1,0:T(8,128)(2,1)S(1)} %reshape.42), channel_id=1, replica_groups=mesh['dp'=4,'expert'=16,'etp'=8] {'expert'}, dimensions={0} | all-to-all | bytes 1245184 | tf_op jit(solution)/shard_map/all_to_all | solution.py:50
  44.9 1.2 reshape.43
  46.0 0.0 all-gather.8.cloned.1.call-update
  46.1 0.0 all-gather.14.cloned.1.call-start
  46.1 0.7 all-gather.14.cloned.1.call-update
  46.8 0.0 all-gather.12.cloned.1.call-start
  46.9 0.7 all-gather.12.cloned.1.call-update
  47.6 0.0 all-gather.10.cloned.1.call-start
  47.6 0.5 all-gather.10.cloned.1.call-update
  48.1 0.0 reduce-scatter.3.cloned.1.call-start
  48.2 0.0 copy-done.2
  48.2 0.1 copy.18
  48.3 0.4 select_reduce_fusion
  48.7 0.1 convert_element_type.70
  48.8 9.7 %all_to_all.17 = bf16[16,1,19]{2,1,0:T(2,128)(2,1)S(1)} all-to-all(bf16[16,1,19]{2,1,0:T(2,128)(2,1)S(1)} %convert_element_type.70), channel_id=1, replica_groups=mesh['dp'=4,'expert'=16,'etp'=8] {'expert'}, dimensions={0} | all-to-all | bytes 1216 | tf_op jit(solution)/shard_map/all_to_all | solution.py:53
  58.5 0.1 reshape.46
  58.6 53.1 %all-gather.8.cloned.1.call-done = bf16[2,304,4096]{2,0,1:T(2,128)(2,1)} async-done(((bf16[2,304,512]{2,0,1:T(2,128)(2,1)}), bf16[2,304,4096]{2,0,1:T(2,128)(2,1)}) %all-gather.8.cloned.1.call-update) | async-done | bytes 4980752 | tf_op jit(solution)/shard_map/all_gather | solution.py:57
  111.7 12.9 %fusion.36 = (bf16[1,304,4096]{2,0,1:T(2,128)(2,1)}, bf16[1,304,4096]{2,0,1:T(2,128)(2,1)}) fusion(bf16[2,304,4096]{2,0,1:T(2,128)(2,1)} %all-gather.8.cloned.1.call-done), kind=kLoop, calls=%fused_computation.43 | loop fusion | bytes 9961472 | tf_op jit(solution)/shard_map/slice | solution.py:59
  124.5 22.7 %all-gather.14.cloned.1.call-done = bf16[1,4096,192]{1,2,0:T(8,128)(2,1)} async-done(((bf16[1,1024,192]{1,2,0:T(8,128)(2,1)}), bf16[1,4096,192]{1,2,0:T(8,128)(2,1)}) %all-gather.14.cloned.1.call-update) | async-done | bytes 1572880 | tf_op jit(solution)/shard_map/all_gather | solution.py:61
  147.2 6.0 %fusion.1 = f32[304,192]{0,1:T(8,128)S(1)} fusion(bf16[1,4096,192]{1,2,0:T(8,128)(2,1)} %all-gather.14.cloned.1.call-done, bf16[1,304,4096]{2,0,1:T(2,128)(2,1)} %get-tuple-element.3), kind=kOutput, calls=%fused_computation.4 | convolution fusion | flops 478150656 | bytes 4296704 | tf_op jit(solution)/shard_map/dot_general | solution.py:10
  153.2 28.2 %all-gather.12.cloned.1.call-done = bf16[1,4096,192]{1,2,0:T(8,128)(2,1)} async-done(((bf16[1,1024,192]{1,2,0:T(8,128)(2,1)}), bf16[1,4096,192]{1,2,0:T(8,128)(2,1)}) %all-gather.12.cloned.1.call-update) | async-done | bytes 1572880 | tf_op jit(solution)/shard_map/all_gather | solution.py:62
  181.3 6.0 %fusion.3 = f32[304,192]{0,1:T(8,128)S(1)} fusion(bf16[1,4096,192]{1,2,0:T(8,128)(2,1)} %all-gather.12.cloned.1.call-done, bf16[1,304,4096]{2,0,1:T(2,128)(2,1)} %get-tuple-element.3), kind=kOutput, calls=%fused_computation.6 | convolution fusion | flops 478150656 | bytes 4296704 | tf_op jit(solution)/shard_map/dot_general | solution.py:11
  187.3 28.0 %all-gather.10.cloned.1.call-done = bf16[1,192,4096]{2,1,0:T(8,128)(2,1)} async-done(((bf16[1,192,1024]{2,1,0:T(8,128)(2,1)}), bf16[1,192,4096]{2,1,0:T(8,128)(2,1)}) %all-gather.10.cloned.1.call-update) | async-done | bytes 1572880 | tf_op jit(solution)/shard_map/all_gather | solution.py:63
  215.3 0.0 copy-start.1
  215.3 6.1 %fusion.16 = f32[304,192]{0,1:T(8,128)S(1)} fusion(bf16[1,192,4096]{2,1,0:T(8,128)(2,1)} %all-gather.10.cloned.1.call-done, bf16[1,304,4096]{2,0,1:T(2,128)(2,1)} %get-tuple-element.2, f32[304]{0:T(512)S(1)} %reshape.46), kind=kOutput, calls=%fused_computation.22 | convolution fusion | flops 478209024 | bytes 4297920 | tf_op jit(solution)/shard_map/dot_general | solution.py:15
  221.4 0.0 copy-done.1
  221.4 0.0 copy-start
  221.4 0.9 fusion.10
  222.3 0.5 copy-done
  222.8 2.4 fusion
  225.2 0.0 reduce-scatter.3.cloned.1.call-update
  225.2 0.3 reduce-scatter.5.cloned.1.call-start
  225.5 6.8 %convolution_convert_fusion = bf16[192,4096]{1,0:T(8,128)(2,1)} fusion(f32[304]{0:T(512)S(1)} %reshape.46, bf16[1,304,4096]{2,0,1:T(2,128)(2,1)} %get-tuple-element.2, f32[304,192]{0,1:T(8,128)S(1)} %fusion.3, f32[304,192]{0,1:T(8,128)S(1)} %fusion.1), kind=kOutput, calls=%fused_computation.2 | convolution fusion | flops 483022848 | bytes 4531392 | tf_op jit(solution)/shard_map/dot_general | solution.py:29
  232.3 0.0 reduce-scatter.5.cloned.1.call-update
  232.3 35.1 %reduce-scatter.3.cloned.1.call-done = bf16[304,512]{1,0:T(8,128)(2,1)} async-done(((bf16[304,4096]{1,0:T(8,128)(2,1)}), bf16[304,512]{1,0:T(8,128)(2,1)}) %reduce-scatter.3.cloned.1.call-update) | async-done | bytes 311312 | tf_op jit(solution)/shard_map/reduce_scatter | solution.py:69
  267.4 1.1 reshape.44
  268.5 26.4 %all_to_all.18 = bf16[16,19,512]{2,1,0:T(8,128)(2,1)S(1)} all-to-all(bf16[16,19,512]{2,1,0:T(8,128)(2,1)S(1)} %reshape.44), channel_id=1, replica_groups=mesh['dp'=4,'expert'=16,'etp'=8] {'expert'}, dimensions={0} | all-to-all | bytes 622592 | tf_op jit(solution)/shard_map/all_to_all | solution.py:70
  294.8 0.1 reshape.45
  295.0 0.9 convolution_convert_fusion.2
  295.9 8.8 %reduce-scatter.5.cloned.1.call-done = bf16[192,1024]{1,0:T(8,128)(2,1)} async-done(((bf16[192,4096]{1,0:T(8,128)(2,1)}), bf16[192,1024]{1,0:T(8,128)(2,1)}) %reduce-scatter.5.cloned.1.call-update) | async-done | bytes 393232 | tf_op jit(solution)/shard_map/reduce_scatter | solution.py:66
  (1 shorter events, 0.0 us)
Async XLA Ops:
  7.2 104.5 %all-gather.8.cloned.1.call-start = ((), (), s32[]{:S(2)}) async-start(), calls=%async_computation.5 | async-start | bytes 5603328 | tf_op jit(solution)/shard_map/all_gather | solution.py:57
  10.3 37.9 %copy-start.2 = (bf16[152,8]{0,1:T(8,128)(2,1)S(1)}, bf16[152,8]{0,1:T(8,128)(2,1)}, u32[]{:S(2)}) copy-start(bf16[152,8]{0,1:T(8,128)(2,1)} %param.10) | copy-start | bytes 7300
  46.1 101.2 %all-gather.14.cloned.1.call-start = ((), (), s32[]{:S(2)}) async-start(), calls=%async_computation.10 | async-start | bytes 1966080 | tf_op jit(solution)/shard_map/all_gather | solution.py:61
  46.8 134.5 %all-gather.12.cloned.1.call-start = ((), (), s32[]{:S(2)}) async-start(), calls=%async_computation.9 | async-start | bytes 1966080 | tf_op jit(solution)/shard_map/all_gather | solution.py:62
  47.6 167.7 %all-gather.10.cloned.1.call-start = ((), (), s32[]{:S(2)}) async-start(), calls=%async_computation.8 | async-start | bytes 1966080 | tf_op jit(solution)/shard_map/all_gather | solution.py:63
  48.1 219.3 %reduce-scatter.3.cloned.1.call-start = ((), (), s32[]{:S(2)}) async-start(), calls=%async_computation.6 | async-start | bytes 2801664 | tf_op jit(solution)/shard_map/reduce_scatter | solution.py:69
  215.3 6.1 %copy-start.1 = (bf16[1,4096,192]{1,2,0:T(8,128)(2,1)S(1)}, bf16[1,4096,192]{1,2,0:T(8,128)(2,1)}, u32[]{:S(2)}) copy-start(bf16[1,4096,192]{1,2,0:T(8,128)(2,1)} %all-gather.14.cloned.1.call-done) | copy-start | bytes 4718596
  221.4 1.4 copy-start
  225.2 79.5 %reduce-scatter.5.cloned.1.call-start = ((), (), s32[]{:S(2)}) async-start(), calls=%async_computation.7 | async-start | bytes 1966080 | tf_op jit(solution)/shard_map/reduce_scatter | solution.py:66
Sparse Core Ops, SparseCore 0:
  46.2 65.4 all-gather.7
  113.8 33.3 all-gather.13
  149.3 31.9 all-gather.11
  183.3 31.9 all-gather.9
  225.3 42.0 reduce-scatter.2
  270.9 33.7 reduce-scatter.4

commit v2 on v1

--- a/solution.py
+++ b/solution.py
@@ -6,15 +6,13 @@
 CAP = 19
 
 
-def expert_grads(feats, grads, gate_col, w_gate, w_up, w_down):
+def expert_grads(feats, grads, gate_col, w_gate, w_up, w_down_t):
     gate_pre = jnp.dot(feats, w_gate, preferred_element_type=jnp.float32)
     up_pre = jnp.dot(feats, w_up, preferred_element_type=jnp.float32)
     sig = jax.nn.sigmoid(gate_pre)
     act = gate_pre * sig
     hidden_b = (act * up_pre).astype(jnp.bfloat16)
-    back = lax.dot_general(
-        grads, w_down, (((1,), (1,)), ((), ())), preferred_element_type=jnp.float32
-    )
+    back = jnp.dot(grads, w_down_t, preferred_element_type=jnp.float32)
     gate_f = gate_col.astype(jnp.float32)[:, None]
     d_hidden = gate_f * back
     d_gate_b = (d_hidden * up_pre * sig * (1.0 + gate_pre * (1.0 - sig))).astype(jnp.bfloat16)
@@ -34,6 +32,7 @@
 
 def local(tokens, cotangent, gates, experts_hit, positions, gate_w, up_w, down_w):
     width = lax.axis_size("expert")
+    split = lax.axis_size("etp")
     rows_dev, routes = experts_hit.shape
     slots = width * CAP
     narrow = tokens.shape[1]
@@ -47,22 +46,24 @@
     ).astype(jnp.bfloat16)
     both = jnp.concatenate([tokens, cotangent], axis=1)
     packed = jnp.dot(onehot, both, preferred_element_type=jnp.float32).astype(jnp.bfloat16)
+    gate_row = jnp.pad(slot_gate.reshape(width, 1, CAP), ((0, 0), (0, 0), (0, 2 * narrow - CAP)))
+    block = jnp.concatenate([packed.reshape(width, CAP, 2 * narrow), gate_row], axis=1)
+    send = jnp.broadcast_to(block[:, None], (width, split, CAP + 1, 2 * narrow))
     recv = lax.all_to_all(
-        packed.reshape(width, CAP, 2 * narrow), "expert", split_axis=0, concat_axis=0, tiled=True
-    )
-    recv_gate = lax.all_to_all(
-        slot_gate.reshape(width, CAP), "expert", split_axis=0, concat_axis=0, tiled=True
-    )
-    pair = recv.reshape(slots, 2, narrow).transpose(1, 0, 2)
-    full = lax.all_gather(pair, "etp", axis=2, tiled=True)
-    feats = full[0]
-    grads = full[1]
-    w_gate, w_up, w_down = (
-        lax.all_gather(gate_w[0], "dp", axis=0, tiled=True),
-        lax.all_gather(up_w[0], "dp", axis=0, tiled=True),
-        lax.all_gather(down_w[0], "dp", axis=1, tiled=True),
-    )
-    d_part_b, term = expert_grads(feats, grads, recv_gate.reshape(slots), w_gate, w_up, w_down)
+        send.reshape(width * split, CAP + 1, 2 * narrow),
+        ("expert", "etp"),
+        split_axis=0,
+        concat_axis=0,
+        tiled=True,
+    ).reshape(width, split, CAP + 1, 2 * narrow)
+    rows = recv[:, :, :CAP, :].transpose(0, 2, 1, 3)
+    feats = rows[:, :, :, :narrow].reshape(slots, split * narrow)
+    grads = rows[:, :, :, narrow:].reshape(slots, split * narrow)
+    recv_gate = recv[:, 0, CAP, :CAP].reshape(slots)
+    stack = jnp.stack([gate_w[0], up_w[0], down_w[0].T], axis=0)
+    w_all = lax.all_gather(stack, "dp", axis=1, tiled=True)
+    w_gate, w_up, w_down_t = w_all[0], w_all[1], w_all[2]
+    d_part_b, term = expert_grads(feats, grads, recv_gate, w_gate, w_up, w_down_t)
     down_grad = lax.psum_scatter(term.astype(jnp.bfloat16), "dp", scatter_dimension=1, tiled=True)[
         None
     ]

time: 312 us -> 342 us (1.096)
  waiting for transfers between devices: 178 us -> 247 us
  blocking collectives: 70.6 us -> 26.3 us
  starting transfers between devices: 0.46 us -> 19.3 us
  matrix products: 30.4 us -> 14.7 us
    all_to_all x0 -> x1, waiting for transfers between devices: none -> 157 us  [local(): lax.all_to_all(send.reshape(width * split, CAP + 1, 2 * narrow), ('expert...]
    all_gather x4 -> x1, waiting for transfers between devices: 132 us -> 0.02 us  [local(): w_all = lax.all_gather(stack, 'dp', axis=1, tiled=True)]
    reduce_scatter x1, waiting for transfers between devices: 35.1 us -> 80.1 us  [local(): summed = lax.psum_scatter(d_part_b, 'etp', scatter_dimension=1, tiled=True)]
    all_to_all x2 -> x0, blocking collectives: 44.3 us -> none  [the longest x1 34.6 us: local(): lax.all_to_all(packed.reshape(width, CAP, 2 * narrow), 'expert', split_ax...]
    all_to_all x0 -> x1, starting transfers between devices: none -> 19 us  [local(): lax.all_to_all(send.reshape(width * split, CAP + 1, 2 * narrow), ('expert...]
    slice x1 -> x3, local copies, waits for them, and re-layouts: 12.9 us -> 0.65 us  [the longest x2 0.49 us: local(): grads = rows[:, :, :, narrow:].reshape(slots, split * narrow)]
    all_to_all x0 -> x1, local copies, waits for them, and re-layouts: none -> 5.69 us  [local(): lax.all_to_all(send.reshape(width * split, CAP + 1, 2 * narrow), ('expert...]
    dot_general x1, matrix products: 6.07 us -> 1.18 us  [expert_grads(): back = jnp.dot(grads, w_down_t, preferred_element_type=jnp.float32)]
  transfers between devices with their start and end apart: 6 -> 4, of which waited for: 6 -> 3; matrix products, arithmetic and copies ran while one was open for 11% -> 5% of each run, Pallas kernels for 0% -> 0%
where the time goes in v2:
time: 342 us; the launch traced here: 341 us
  waiting for transfers between devices  247 us (72%)
  blocking collectives  26.3 us (8%)
  starting transfers between devices  19.3 us (6%)
  local copies, waits for them, and re-layouts  17.5 us (5%)
  matrix products  14.7 us (4%)
  between operations  13.9 us (4%)
    all_to_all x1, waiting for transfers between devices, local(): lax.all_to_all(send.reshape(width * split, CAP + 1, 2 * narrow), ('expert...  157 us
    reduce_scatter x1, waiting for transfers between devices, local(): summed = lax.psum_scatter(d_part_b, 'etp', scatter_dimension=1, tiled=True)  80.1 us
    all_to_all x1, blocking collectives, local(): lax.all_to_all(summed.reshape(width, CAP, narrow), 'expert', split_axis=0...  26.3 us
    all_to_all x1, starting transfers between devices, local(): lax.all_to_all(send.reshape(width * split, CAP + 1, 2 * narrow), ('expert...  19 us
    reduce_scatter x1, waiting for transfers between devices, local(): lax.psum_scatter(term.astype(jnp.bfloat16), 'dp', scatter_dimension=1, ti...  9.1 us
  transfers between devices with their start and end apart: 4, of which 3 were waited for; matrix products, arithmetic and copies ran while one was open for 5% of the time, Pallas kernels for 0%

profile of v2, /device:TPU:1, one launch (start us, length us, event | category | flops | bytes accessed | tf_op | source)
XLA Modules:
  0.0 341.4 jit_solution(11927686268550531165)
XLA Ops:
  7.2 0.0 copy-start.6
  7.2 0.7 add_select_fusion
  7.9 0.1 copy.27
  8.0 0.7 fusion.2
  8.7 1.4 convolution_convert_fusion.1
  10.0 0.2 reshape.47
  10.2 0.0 copy-done.6
  10.3 0.1 copy.28
  10.4 0.4 select_reduce_fusion
  10.8 0.1 convert_element_type.71
  10.9 0.1 fusion.9
  11.0 3.5 %broadcast_in_dim.32 = bf16[16,8,20,1024]{3,2,1,0:T(8,128)(2,1)} broadcast(bf16[16,20,1024]{2,1,0:T(8,128)(2,1)S(1)} %fusion.9), dimensions={0,2,3} | broadcast | bytes 5898240 | tf_op jit(solution)/shard_map/broadcast_in_dim | solution.py:51
  14.4 0.0 copy-start.3
  14.4 0.0 copy-start.4
  14.4 0.0 copy-start.5
  14.4 19.0 %all-to-all-start = ((bf16[128,20,1024]{2,1,0:T(8,128)(2,1)}), bf16[128,20,1024]{2,1,0:T(8,128)(2,1)}, u32[]{:S(2)}, u32[]{:S(2)}) async-start(bf16[128,20,1024]{2,1,0:T(8,128)(2,1)} %bitcast.37), calls=%async_computation | async-start | bytes 12582912 | tf_op jit(solution)/shard_map/all_to_all | solution.py:52
  33.4 0.0 all-gather.2.cloned.1.call-start
  33.5 0.0 copy-done.3
  33.5 0.0 copy-done.4
  33.5 0.0 copy-done.5
  33.5 1.2 pad_maximum_fusion
  34.6 0.0 all-gather.2.cloned.1.call-update
  34.7 0.2 reduce-scatter.3.cloned.1.call-start
  34.9 157.4 %all-to-all-done = bf16[128,20,1024]{2,1,0:T(8,128)(2,1)} async-done(((bf16[128,20,1024]{2,1,0:T(8,128)(2,1)}), bf16[128,20,1024]{2,1,0:T(8,128)(2,1)}, u32[]{:S(2)}, u32[]{:S(2)}) %all-to-all-start) | async-done | bytes 5242912 | tf_op jit(solution)/shard_map/all_to_all | solution.py:52
  192.3 5.7 %copy.36 = bf16[128,20,1024]{2,0,1:T(8,128)(2,1)S(1)} copy(bf16[128,20,1024]{2,1,0:T(8,128)(2,1)} %all-to-all-done) | data formatting | bytes 10485760 | tf_op jit(solution)/shard_map/all_to_all | solution.py:52
  198.0 0.8 slice_bitcast_fusion
  198.8 0.3 fusion.22
  199.1 0.2 copy.31
  199.3 2.6 copy.33
  201.9 0.1 reshape.54
  202.0 0.2 copy.32
  202.1 1.1 copy.34
  203.3 0.0 copy-start.1
  203.3 0.0 all-gather.2.cloned.1.call-done
  203.3 1.4 copy-done.1
  204.7 0.0 copy-start.2
  204.7 2.7 fusion.7
  207.5 0.1 copy-done.2
  207.5 0.0 copy-start
  207.5 3.0 fusion.5
  210.6 0.0 copy-done
  210.6 1.2 fusion.8
  211.8 0.9 fusion.6
  212.6 2.3 fusion
  215.0 0.0 reduce-scatter.3.cloned.1.call-update
  215.0 0.0 reduce-scatter.5.cloned.1.call-start
  215.1 2.2 convolution_convert_fusion
  217.3 0.0 reduce-scatter.5.cloned.1.call-update
  217.3 80.1 %reduce-scatter.3.cloned.1.call-done = bf16[304,512]{1,0:T(8,128)(2,1)} async-done(((bf16[304,4096]{1,0:T(8,128)(2,1)}), bf16[304,512]{1,0:T(8,128)(2,1)}) %reduce-scatter.3.cloned.1.call-update) | async-done | bytes 311312 | tf_op jit(solution)/shard_map/reduce_scatter | solution.py:70
  297.4 1.1 reshape.52
  298.5 26.3 %all_to_all.10 = bf16[16,19,512]{2,1,0:T(8,128)(2,1)S(1)} all-to-all(bf16[16,19,512]{2,1,0:T(8,128)(2,1)S(1)} %reshape.52), channel_id=1, replica_groups=mesh['dp'=4,'expert'=16,'etp'=8] {'expert'}, dimensions={0} | all-to-all | bytes 622592 | tf_op jit(solution)/shard_map/all_to_all | solution.py:71
  324.7 0.1 reshape.53
  324.8 0.9 convolution_convert_fusion.2
  325.8 9.1 %reduce-scatter.5.cloned.1.call-done = bf16[192,1024]{1,0:T(8,128)(2,1)} async-done(((bf16[192,4096]{1,0:T(8,128)(2,1)}), bf16[192,1024]{1,0:T(8,128)(2,1)}) %reduce-scatter.5.cloned.1.call-update) | async-done | bytes 393232 | tf_op jit(solution)/shard_map/reduce_scatter | solution.py:67
  (1 shorter events, 0.0 us)
Async XLA Ops:
  7.2 3.1 copy-start.6
  14.4 19.0 %copy-start.3 = (bf16[1,192,1024]{2,1,0:T(8,128)(2,1)S(1)}, bf16[1,192,1024]{2,1,0:T(8,128)(2,1)}, u32[]{:S(2)}) copy-start(bf16[1,192,1024]{2,1,0:T(8,128)(2,1)} %param.15) | copy-start | bytes 1179652
  14.4 19.0 %copy-start.4 = (bf16[1,1024,192]{1,2,0:T(8,128)(2,1)S(1)}, bf16[1,1024,192]{1,2,0:T(8,128)(2,1)}, u32[]{:S(2)}) copy-start(bf16[1,1024,192]{1,2,0:T(8,128)(2,1)} %param.14) | copy-start | bytes 1179652
  14.4 19.0 %copy-start.5 = (bf16[1,1024,192]{1,2,0:T(8,128)(2,1)S(1)}, bf16[1,1024,192]{1,2,0:T(8,128)(2,1)}, u32[]{:S(2)}) copy-start(bf16[1,1024,192]{1,2,0:T(8,128)(2,1)} %param.13) | copy-start | bytes 1179652
  14.4 177.9 %all-to-all-start = ((bf16[128,20,1024]{2,1,0:T(8,128)(2,1)}), bf16[128,20,1024]{2,1,0:T(8,128)(2,1)}, u32[]{:S(2)}, u32[]{:S(2)}) async-start(bf16[128,20,1024]{2,1,0:T(8,128)(2,1)} %bitcast.37), calls=%async_computation | async-start | bytes 12582912 | tf_op jit(solution)/shard_map/all_to_all | solution.py:52
  33.4 169.9 %all-gather.2.cloned.1.call-start = ((), (), s32[]{:S(2)}) async-start(), calls=%async_computation.4 | async-start | bytes 5898240 | tf_op jit(solution)/shard_map/all_gather | solution.py:64
  34.7 262.7 %reduce-scatter.3.cloned.1.call-start = ((), (), s32[]{:S(2)}) async-start(), calls=%async_computation.5 | async-start | bytes 2801664 | tf_op jit(solution)/shard_map/reduce_scatter | solution.py:70
  203.3 1.5 copy-start.1
  204.7 2.8 copy-start.2
  207.5 3.0 copy-start
  215.0 119.9 %reduce-scatter.5.cloned.1.call-start = ((), (), s32[]{:S(2)}) async-start(), calls=%async_computation.6 | async-start | bytes 1966080 | tf_op jit(solution)/shard_map/reduce_scatter | solution.py:67
Sparse Core Ops, SparseCore 0:
  36.4 58.6 all-gather.1
  215.1 82.2 reduce-scatter.2
  301.1 33.7 reduce-scatter.4

commit v3 on v2

--- a/solution.py
+++ b/solution.py
@@ -30,9 +30,33 @@
     return (d_part.astype(jnp.bfloat16), term)
 
 
+def gather_dp(piece, axis):
+    size = lax.axis_size("dp")
+    me = lax.axis_index("dp")
+    got = [piece]
+    for shift in range(1, size):
+        got.append(lax.ppermute(piece, "dp", [(i, (i + shift) % size) for i in range(size)]))
+    order = (me - jnp.arange(size, dtype=jnp.int32)) % size
+    ranked = jnp.take(jnp.stack(got, axis=0), order, axis=0)
+    return jnp.concatenate([ranked[i] for i in range(size)], axis=axis)
+
+
+def scatter_sum_dp(term_b):
+    size = lax.axis_size("dp")
+    me = lax.axis_index("dp")
+    quarter = term_b.shape[1] // size
+    parts = term_b.reshape(term_b.shape[0], size, quarter)
+    total = jnp.take(parts, me, axis=1).astype(jnp.float32)
+    for shift in range(1, size):
+        outgoing = jnp.take(parts, (me + shift) % size, axis=1)
+        total = total + lax.ppermute(
+            outgoing, "dp", [(i, (i + shift) % size) for i in range(size)]
+        ).astype(jnp.float32)
+    return total.astype(jnp.bfloat16)
+
+
 def local(tokens, cotangent, gates, experts_hit, positions, gate_w, up_w, down_w):
     width = lax.axis_size("expert")
-    split = lax.axis_size("etp")
     rows_dev, routes = experts_hit.shape
     slots = width * CAP
     narrow = tokens.shape[1]
@@ -48,25 +72,17 @@
     packed = jnp.dot(onehot, both, preferred_element_type=jnp.float32).astype(jnp.bfloat16)
     gate_row = jnp.pad(slot_gate.reshape(width, 1, CAP), ((0, 0), (0, 0), (0, 2 * narrow - CAP)))
     block = jnp.concatenate([packed.reshape(width, CAP, 2 * narrow), gate_row], axis=1)
-    send = jnp.broadcast_to(block[:, None], (width, split, CAP + 1, 2 * narrow))
-    recv = lax.all_to_all(
-        send.reshape(width * split, CAP + 1, 2 * narrow),
-        ("expert", "etp"),
-        split_axis=0,
-        concat_axis=0,
-        tiled=True,
-    ).reshape(width, split, CAP + 1, 2 * narrow)
-    rows = recv[:, :, :CAP, :].transpose(0, 2, 1, 3)
-    feats = rows[:, :, :, :narrow].reshape(slots, split * narrow)
-    grads = rows[:, :, :, narrow:].reshape(slots, split * narrow)
-    recv_gate = recv[:, 0, CAP, :CAP].reshape(slots)
+    recv = lax.all_to_all(block, "expert", split_axis=0, concat_axis=0, tiled=True)
+    recv_gate = recv[:, CAP, :CAP].reshape(slots)
+    pair = recv[:, :CAP, :].reshape(slots, 2, narrow).transpose(1, 0, 2)
+    full = lax.all_gather(pair, "etp", axis=2, tiled=True)
+    feats = full[0]
+    grads = full[1]
     stack = jnp.stack([gate_w[0], up_w[0], down_w[0].T], axis=0)
-    w_all = lax.all_gather(stack, "dp", axis=1, tiled=True)
+    w_all = gather_dp(stack, 1)
     w_gate, w_up, w_down_t = w_all[0], w_all[1], w_all[2]
     d_part_b, term = expert_grads(feats, grads, recv_gate, w_gate, w_up, w_down_t)
-    down_grad = lax.psum_scatter(term.astype(jnp.bfloat16), "dp", scatter_dimension=1, tiled=True)[
-        None
-    ]
+    down_grad = scatter_sum_dp(term.astype(jnp.bfloat16))[None]
     summed = lax.psum_scatter(d_part_b, "etp", scatter_dimension=1, tiled=True)
     returned = lax.all_to_all(
         summed.reshape(width, CAP, narrow), "expert", split_axis=0, concat_axis=0, tiled=True

time: 342 us -> 224 us (0.65)
  waiting for transfers between devices: 247 us -> 76.9 us
  starting transfers between devices: 19.3 us -> 33 us
  local copies, waits for them, and re-layouts: 17.5 us -> 29.6 us
  other arithmetic: 3.08 us -> 13.8 us
  blocking collectives: 26.3 us -> 34.7 us
  matrix products: 14.7 us -> 20.5 us
    all_to_all x1, waiting for transfers between devices: 157 us -> 13.4 us  [local(): lax.all_to_all(summed.reshape(width, CAP, narrow), 'expert', split_axis=0...]
    reduce_scatter x1, waiting for transfers between devices: 80.1 us -> 17.6 us  [local(): summed = lax.psum_scatter(d_part_b, 'etp', scatter_dimension=1, tiled=True)]
    ppermute x0 -> x6, waiting for transfers between devices: none -> 45.9 us  [the longest x3 45.9 us: gather_dp(): lax.ppermute(piece, 'dp', [(i, (i + shift) % size) for i in range(size)])]
    ppermute x0 -> x6, starting transfers between devices: none -> 21 us  [the longest x3 11.1 us: gather_dp(): lax.ppermute(piece, 'dp', [(i, (i + shift) % size) for i in range(size)])]
    slice x3 -> x1, local copies, waits for them, and re-layouts: 0.65 us -> 14.7 us  [local(): grads = full[1]]
    reduce_scatter x1 -> x0, waiting for transfers between devices: 9.1 us -> none  [local(): lax.psum_scatter(term.astype(jnp.bfloat16), 'dp', scatter_dimension=1, ti...]
    all_to_all x1, blocking collectives: 26.3 us -> 34.7 us  [local(): lax.all_to_all(block, 'expert', split_axis=0, concat_axis=0, tiled=True)]
    all_to_all x1, starting transfers between devices: 19 us -> 12 us  [local(): lax.all_to_all(summed.reshape(width, CAP, narrow), 'expert', split_axis=0...]
  transfers between devices with their start and end apart: 4 -> 9, of which waited for: 3 -> 5; matrix products, arithmetic and copies ran while one was open for 5% -> 13% of each run, Pallas kernels for 0% -> 0%
where the time goes in v3:
time: 224 us; the launch traced here: 223 us
  waiting for transfers between devices  76.9 us (34%)
  blocking collectives  34.7 us (15%)
  starting transfers between devices  33 us (15%)
  local copies, waits for them, and re-layouts  29.6 us (13%)
  matrix products  20.5 us (9%)
  between operations  14.5 us (6%)
  other arithmetic  13.8 us (6%)
    ppermute x3, waiting for transfers between devices, gather_dp(): lax.ppermute(piece, 'dp', [(i, (i + shift) % size) for i in range(size)])  45.9 us
    all_to_all x1, blocking collectives, local(): lax.all_to_all(block, 'expert', split_axis=0, concat_axis=0, tiled=True)  34.7 us
    reduce_scatter x1, waiting for transfers between devices, local(): summed = lax.psum_scatter(d_part_b, 'etp', scatter_dimension=1, tiled=True)  17.6 us
    slice x1, local copies, waits for them, and re-layouts, local(): grads = full[1]  14.7 us
    all_to_all x1, waiting for transfers between devices, local(): lax.all_to_all(summed.reshape(width, CAP, narrow), 'expert', split_axis=0...  13.4 us
    all_to_all x1, starting transfers between devices, local(): lax.all_to_all(summed.reshape(width, CAP, narrow), 'expert', split_axis=0...  12 us
    ppermute x3, starting transfers between devices, gather_dp(): lax.ppermute(piece, 'dp', [(i, (i + shift) % size) for i in range(size)])  11.1 us
    ppermute x3, starting transfers between devices, scatter_sum_dp(): lax.ppermute(outgoing, 'dp', [(i, (i + shift) % size) for i in range(size)])  9.84 us
  transfers between devices with their start and end apart: 9, of which 5 were waited for; matrix products, arithmetic and copies ran while one was open for 13% of the time, Pallas kernels for 0%

profile of v3, /device:TPU:1, one launch (start us, length us, event | category | flops | bytes accessed | tf_op | source)
XLA Modules:
  0.0 223.0 jit_solution(5487376526246325992)
XLA Ops:
  7.2 0.0 all-gather.2.cloned.1.call-start
  7.2 0.7 add_select_fusion
  7.9 0.1 copy.23
  8.0 0.7 fusion.9
  8.7 0.0 copy-start.5
  8.7 0.8 copy.24
  9.5 0.4 select_reduce_fusion
  9.9 0.1 convert_element_type.91
  10.0 0.0 copy-done.5
  10.0 1.4 convolution_convert_fusion.1
  11.4 0.2 reshape.95
  11.6 0.0 copy-start.2
  11.6 0.0 copy-start.3
  11.6 0.0 copy-start.4
  11.7 0.1 fusion.19
  11.8 34.7 %all_to_all.10 = bf16[16,20,1024]{2,1,0:T(8,128)(2,1)S(1)} all-to-all(bf16[16,20,1024]{2,1,0:T(8,128)(2,1)S(1)} %fusion.19), channel_id=1, replica_groups=mesh['dp'=4,'expert'=16,'etp'=8] {'expert'}, dimensions={0} | all-to-all | bytes 1310720 | tf_op jit(solution)/shard_map/all_to_all | solution.py:75
  46.5 1.2 reshape.96
  47.7 0.0 all-gather.2.cloned.1.call-update
  47.7 0.0 reduce-scatter.2.cloned.1.call-start
  47.8 0.0 copy-done.2
  47.8 0.0 copy-done.3
  47.8 0.0 copy-done.4
  47.8 1.2 fusion.40
  49.0 4.6 %collective-permute-start.1 = (bf16[3,1024,192]{1,2,0:T(8,128)(2,1)}, bf16[3,1024,192]{1,2,0:T(8,128)(2,1)S(1)}, u32[]{:S(2)}, u32[]{:S(2)}) collective-permute-start(bf16[3,1024,192]{1,2,0:T(8,128)(2,1)} %get-tuple-element.25), channel_id=1, source_target_pairs={{0,256},{128,384},{256,0},{384,128},{1,257},{129,385},{257,1},{385... | collective-permute-start | bytes 3538952 | tf_op jit(solution)/shard_map/ppermute | solution.py:38
  53.7 2.2 collective-permute-start
  55.9 4.3 %collective-permute-start.2 = (bf16[3,1024,192]{1,2,0:T(8,128)(2,1)}, bf16[3,1024,192]{1,2,0:T(8,128)(2,1)}, u32[]{:S(2)}, u32[]{:S(2)}) collective-permute-start(bf16[3,1024,192]{1,2,0:T(8,128)(2,1)} %get-tuple-element.25), channel_id=1, source_target_pairs={{0,384},{128,0},{256,128},{384,256},{1,385},{129,1},{257,129},{385... | collective-permute-start | bytes 3538952 | tf_op jit(solution)/shard_map/ppermute | solution.py:38
  60.2 20.4 %collective-permute-done.1 = bf16[3,1024,192]{1,2,0:T(8,128)(2,1)S(1)} collective-permute-done((bf16[3,1024,192]{1,2,0:T(8,128)(2,1)}, bf16[3,1024,192]{1,2,0:T(8,128)(2,1)S(1)}, u32[]{:S(2)}, u32[]{:S(2)}) %collective-permute-start.1) | collective-permute-done | bytes 1179680 | tf_op jit(solution)/shard_map/ppermute | solution.py:38
  80.6 25.3 %collective-permute-done = bf16[3,1024,192]{1,2,0:T(8,128)(2,1)} collective-permute-done((bf16[3,1024,192]{1,2,0:T(8,128)(2,1)}, bf16[3,1024,192]{1,2,0:T(8,128)(2,1)}, u32[]{:S(2)}, u32[]{:S(2)}) %collective-permute-start) | collective-permute-done | bytes 1179680 | tf_op jit(solution)/shard_map/ppermute | solution.py:38
  105.9 0.1 collective-permute-done.2
  106.1 3.8 %pad_maximum_fusion = bf16[4,3,1024,192]{2,3,1,0:T(8,128)(2,1)} fusion(bf16[1,3,1024,192]{2,3,1,0:T(8,128)(2,1)} %bitcast.7, bf16[1,3,1024,192]{2,3,1,0:T(8,128)(2,1)S(1)} %bitcast.66, bf16[1,3,1024,192]{2,3,1,0:T(8,128)(2,1)} %bitcast.5, bf16[1,3,1024,192]{2,3,1,0:T(8,128)(2,1)S(1)} %get-tuple-element.24), kind=kLoop, calls=%fused_computation.5 | loop fusion | flops 7077888 | bytes 9437184 | tf_op jit(solution)/shard_map/stack | solution.py:40
  109.8 5.4 %gather_fusion = bf16[4,3,1024,192]{2,3,1,0:T(8,128)(2,1)} fusion(bf16[4,3,1024,192]{2,3,1,0:T(8,128)(2,1)} %pad_maximum_fusion, s32[1024]{0:T(1024)S(1)} %pad_clamp_fusion), kind=kCustom, calls=%fused_computation | custom fusion | bytes 9437200 | tf_op jit(solution)/shard_map/jit(_take)/gather | solution.py:40
  115.3 2.9 %broadcast_select_fusion = bf16[4,3,1024,192]{2,3,1,0:T(8,128)(2,1)S(1)} fusion(bf16[4,3,1024,192]{2,3,1,0:T(8,128)(2,1)} %gather_fusion, pred[4]{0:T(512)(128)(4,1)S(1)} %compare_and_fusion), kind=kLoop, calls=%fused_computation.7 | loop fusion | flops 2359296 | bytes 9437188 | tf_op jit(solution)/shard_map/jit(_take)/select_n | solution.py:40
  118.1 0.5 slice_bitcast_fusion.11
  118.6 2.4 %pad_maximum_fusion.1 = bf16[3,4096,192]{1,2,0:T(8,128)(2,1)} fusion(bf16[3,1024,192]{1,2,0:T(8,128)(2,1)S(1)} %get-tuple-element.17, bf16[3,1024,192]{1,2,0:T(8,128)(2,1)S(1)} %get-tuple-element.18, bf16[3,1024,192]{1,2,0:T(8,128)(2,1)S(1)} %get-tuple-element.19, bf16[3,1024,192]{1,2,0:T(8,128)(2,1)S(1)} %get-tuple-element.16), kind=kLoop, calls=%fused_computation.6 | loop fusion | flops 18874368 | bytes 9437184 | tf_op jit(solution)/shard_map/concatenate | solution.py:41
  121.0 0.1 reshape.163
  121.1 0.0 all-gather.2.cloned.1.call-done
  121.2 0.0 copy-start
  121.2 14.7 %fusion.41 = (bf16[1,304,4096]{2,0,1:T(2,128)(2,1)S(1)}, bf16[1,304,4096]{2,0,1:T(2,128)(2,1)S(1)}) fusion(bf16[2,304,4096]{2,0,1:T(2,128)(2,1)} %all-gather.2.cloned.1.call-done), kind=kLoop, calls=%fused_computation.82 | loop fusion | bytes 9961472 | tf_op jit(solution)/shard_map/slice | solution.py:80
  135.9 3.1 %fusion.1 = f32[304,192]{0,1:T(8,128)S(1)} fusion(bf16[3,4096,192]{1,2,0:T(8,128)(2,1)S(1)} %copy-done, bf16[1,304,4096]{2,0,1:T(2,128)(2,1)S(1)} %get-tuple-element.15), kind=kOutput, calls=%fused_computation.8 | convolution fusion | flops 478150656 | bytes 6787072 | tf_op jit(solution)/shard_map/dot_general | solution.py:10
  138.9 3.0 %fusion.3 = f32[304,192]{0,1:T(8,128)S(1)} fusion(bf16[3,4096,192]{1,2,0:T(8,128)(2,1)S(1)} %copy-done, bf16[1,304,4096]{2,0,1:T(2,128)(2,1)S(1)} %get-tuple-element.15), kind=kOutput, calls=%fused_computation.10 | convolution fusion | flops 478150656 | bytes 6787072 | tf_op jit(solution)/shard_map/dot_general | solution.py:11
  142.0 3.1 %fusion.12 = f32[304,192]{0,1:T(8,128)S(1)} fusion(bf16[3,4096,192]{1,2,0:T(8,128)(2,1)S(1)} %copy-done, bf16[1,304,4096]{2,0,1:T(2,128)(2,1)S(1)} %get-tuple-element.14, f32[304]{0:T(512)S(1)} %reshape.163), kind=kOutput, calls=%fused_computation.31 | convolution fusion | flops 478209024 | bytes 6789120 | tf_op jit(solution)/shard_map/dot_general | solution.py:15
  145.0 0.9 fusion.11
  145.9 2.4 %fusion = bf16[304,4096]{1,0:T(8,128)(2,1)} fusion(f32[304,4096]{1,0:T(8,128)S(1)} %fusion.11, bf16[3,4096,192]{1,2,0:T(8,128)(2,1)S(1)} %copy-done, f32[304,192]{0,1:T(8,128)S(1)} %fusion.12, f32[304,192]{0,1:T(8,128)S(1)} %fusion.1), kind=kOutput, calls=%fused_computation.2 | convolution fusion | flops 480991232 | bytes 9633792 | tf_op jit(solution)/shard_map/dot_general | solution.py:23
  148.3 0.0 reduce-scatter.2.cloned.1.call-update
  148.4 5.8 %convolution_convert_fusion = bf16[192,4096]{1,0:T(8,128)(2,1)S(1)} fusion(f32[304]{0:T(512)S(1)} %reshape.163, bf16[1,304,4096]{2,0,1:T(2,128)(2,1)} %copy-done.1, f32[304,192]{0,1:T(8,128)S(1)} %fusion.3, f32[304,192]{0,1:T(8,128)S(1)} %fusion.1), kind=kOutput, calls=%fused_computation.3 | convolution fusion | flops 483022848 | bytes 4531392 | tf_op jit(solution)/shard_map/dot_general | solution.py:27
  154.2 1.2 reshape.99
  155.4 3.3 %constant_dynamic-slice_fusion.3 = (bf16[192,1,1024]{2,1,0:T(2,128)(2,1)S(1)}, bf16[192,1,1024]{2,1,0:T(2,128)(2,1)S(1)}, bf16[192,1,1024]{2,1,0:T(2,128)(2,1)S(1)}, bf16[192,1,1024]{2,1,0:T(2,128)(2,1)S(1)}) fusion(bf16[192,4,1024]{2,1,0:T(4,128)(2,1)S(1)} %reshape.99, s32[]{:T(128)S(6)} %select_n.90, s32[]{:T(128)S(6)} %select_n.94, s32[]{:T(128)S(6)} %select_n.92, ...), kind=kLoop, calls=%fused_computation.73 | loop fusion | bytes 3145744 | tf_op jit(solution)/shard_map/jit(_take) | solution.py:49
  158.7 0.2 fusion.21
  158.9 4.2 %collective-permute-start.5 = (bf16[192,1024]{1,0:T(8,128)(2,1)S(1)}, bf16[192,1024]{1,0:T(8,128)(2,1)S(1)}, u32[]{:S(2)}, u32[]{:S(2)}) collective-permute-start(bf16[192,1024]{1,0:T(8,128)(2,1)S(1)} %fusion.21), channel_id=1, source_target_pairs={{0,384},{128,0},{256,128},{384,256},{1,385},{129,1},{257,129},{385... | collective-permute-start | bytes 1179656 | tf_op jit(solution)/shard_map/ppermute | solution.py:52
  163.1 0.2 fusion.23
  163.3 1.9 collective-permute-start.3
  165.2 0.2 fusion.22
  165.4 3.7 %collective-permute-start.4 = (bf16[192,1024]{1,0:T(8,128)(2,1)S(1)}, bf16[192,1024]{1,0:T(8,128)(2,1)S(1)}, u32[]{:S(2)}, u32[]{:S(2)}) collective-permute-start(bf16[192,1024]{1,0:T(8,128)(2,1)S(1)} %fusion.22), channel_id=1, source_target_pairs={{0,256},{128,384},{256,0},{384,128},{1,257},{129,385},{257,1},{385... | collective-permute-start | bytes 1179656 | tf_op jit(solution)/shard_map/ppermute | solution.py:52
  169.1 17.6 %reduce-scatter.2.cloned.1.call-done = bf16[304,512]{1,0:T(8,128)(2,1)} async-done(((bf16[304,4096]{1,0:T(8,128)(2,1)}), bf16[304,512]{1,0:T(8,128)(2,1)}) %reduce-scatter.2.cloned.1.call-update) | async-done | bytes 311312 | tf_op jit(solution)/shard_map/reduce_scatter | solution.py:86
  186.7 1.8 reshape.97
  188.5 12.0 %all-to-all-start.1 = ((bf16[16,19,512]{2,1,0:T(8,128)(2,1)}), bf16[16,19,512]{2,1,0:T(8,128)(2,1)S(1)}, u32[]{:S(2)}, u32[]{:S(2)}) async-start(bf16[16,19,512]{2,1,0:T(8,128)(2,1)} %reshape.97), calls=%async_computation.2 | async-start | bytes 786432 | tf_op jit(solution)/shard_map/all_to_all | solution.py:87
  200.5 0.0 collective-permute-done.5
  200.5 0.0 copy-start.6
  200.6 0.0 collective-permute-done.3
  200.6 0.0 collective-permute-done.4
  200.6 1.1 fusion.20
  201.7 13.4 %all-to-all-done.1 = bf16[16,19,512]{2,1,0:T(8,128)(2,1)S(1)} async-done(((bf16[16,19,512]{2,1,0:T(8,128)(2,1)}), bf16[16,19,512]{2,1,0:T(8,128)(2,1)S(1)}, u32[]{:S(2)}, u32[]{:S(2)}) %all-to-all-start.1) | async-done | bytes 311328 | tf_op jit(solution)/shard_map/all_to_all | solution.py:87
  215.1 0.1 reshape.98
  215.2 0.9 convolution_convert_fusion.2
  (8 shorter events, 0.1 us)
Async XLA Ops:
  7.2 114.0 %all-gather.2.cloned.1.call-start = ((), (), s32[]{:S(2)}) async-start(), calls=%async_computation.3 | async-start | bytes 5603328 | tf_op jit(solution)/shard_map/all_gather | solution.py:78
  8.7 1.3 copy-start.5
  11.6 36.1 %copy-start.2 = (bf16[1,192,1024]{2,1,0:T(8,128)(2,1)S(1)}, bf16[1,192,1024]{2,1,0:T(8,128)(2,1)}, u32[]{:S(2)}) copy-start(bf16[1,192,1024]{2,1,0:T(8,128)(2,1)} %param.17) | copy-start | bytes 1179652
  11.6 36.1 %copy-start.3 = (bf16[1,1024,192]{1,2,0:T(8,128)(2,1)S(1)}, bf16[1,1024,192]{1,2,0:T(8,128)(2,1)}, u32[]{:S(2)}) copy-start(bf16[1,1024,192]{1,2,0:T(8,128)(2,1)} %param.16) | copy-start | bytes 1179652
  11.6 36.1 %copy-start.4 = (bf16[1,1024,192]{1,2,0:T(8,128)(2,1)S(1)}, bf16[1,1024,192]{1,2,0:T(8,128)(2,1)}, u32[]{:S(2)}) copy-start(bf16[1,1024,192]{1,2,0:T(8,128)(2,1)} %param.15) | copy-start | bytes 1179652
  47.7 139.0 %reduce-scatter.2.cloned.1.call-start = ((), (), s32[]{:S(2)}) async-start(), calls=%async_computation.4 | async-start | bytes 2801664 | tf_op jit(solution)/shard_map/reduce_scatter | solution.py:86
  49.0 31.6 %collective-permute-start.1 = (bf16[3,1024,192]{1,2,0:T(8,128)(2,1)}, bf16[3,1024,192]{1,2,0:T(8,128)(2,1)S(1)}, u32[]{:S(2)}, u32[]{:S(2)}) collective-permute-start(bf16[3,1024,192]{1,2,0:T(8,128)(2,1)} %get-tuple-element.25), channel_id=1, source_target_pairs={{0,256},{128,384},{256,0},{384,128},{1,257},{129,385},{257,1},{385... | collective-permute-start | bytes 3538952 | tf_op jit(solution)/shard_map/ppermute | solution.py:38
  53.7 52.3 %collective-permute-start = (bf16[3,1024,192]{1,2,0:T(8,128)(2,1)}, bf16[3,1024,192]{1,2,0:T(8,128)(2,1)}, u32[]{:S(2)}, u32[]{:S(2)}) collective-permute-start(bf16[3,1024,192]{1,2,0:T(8,128)(2,1)} %get-tuple-element.25), channel_id=1, source_target_pairs={{0,128},{128,256},{256,384},{384,0},{1,129},{129,257},{257,385},{3... | collective-permute-start | bytes 3538952 | tf_op jit(solution)/shard_map/ppermute | solution.py:38
  55.9 50.2 %collective-permute-start.2 = (bf16[3,1024,192]{1,2,0:T(8,128)(2,1)}, bf16[3,1024,192]{1,2,0:T(8,128)(2,1)}, u32[]{:S(2)}, u32[]{:S(2)}) collective-permute-start(bf16[3,1024,192]{1,2,0:T(8,128)(2,1)} %get-tuple-element.25), channel_id=1, source_target_pairs={{0,384},{128,0},{256,128},{384,256},{1,385},{129,1},{257,129},{385... | collective-permute-start | bytes 3538952 | tf_op jit(solution)/shard_map/ppermute | solution.py:38
  121.2 14.7 %copy-start = (bf16[3,4096,192]{1,2,0:T(8,128)(2,1)S(1)}, bf16[3,4096,192]{1,2,0:T(8,128)(2,1)}, u32[]{:S(2)}) copy-start(bf16[3,4096,192]{1,2,0:T(8,128)(2,1)} %pad_maximum_fusion.1) | copy-start | bytes 14155780
  135.8 6.1 %copy-start.1 = (bf16[1,304,4096]{2,0,1:T(2,128)(2,1)}, bf16[1,304,4096]{2,0,1:T(2,128)(2,1)S(1)}, u32[]{:S(2)}) copy-start(bf16[1,304,4096]{2,0,1:T(2,128)(2,1)S(1)} %get-tuple-element.14) | copy-start | bytes 7471108
  158.9 41.6 %collective-permute-start.5 = (bf16[192,1024]{1,0:T(8,128)(2,1)S(1)}, bf16[192,1024]{1,0:T(8,128)(2,1)S(1)}, u32[]{:S(2)}, u32[]{:S(2)}) collective-permute-start(bf16[192,1024]{1,0:T(8,128)(2,1)S(1)} %fusion.21), channel_id=1, source_target_pairs={{0,384},{128,0},{256,128},{384,256},{1,385},{129,1},{257,129},{385... | collective-permute-start | bytes 1179656 | tf_op jit(solution)/shard_map/ppermute | solution.py:52
  163.3 37.3 %collective-permute-start.3 = (bf16[192,1024]{1,0:T(8,128)(2,1)S(1)}, bf16[192,1024]{1,0:T(8,128)(2,1)S(1)}, u32[]{:S(2)}, u32[]{:S(2)}) collective-permute-start(bf16[192,1024]{1,0:T(8,128)(2,1)S(1)} %fusion.23), channel_id=1, source_target_pairs={{0,128},{128,256},{256,384},{384,0},{1,129},{129,257},{257,385},{3... | collective-permute-start | bytes 1179656 | tf_op jit(solution)/shard_map/ppermute | solution.py:52
  165.4 35.2 %collective-permute-start.4 = (bf16[192,1024]{1,0:T(8,128)(2,1)S(1)}, bf16[192,1024]{1,0:T(8,128)(2,1)S(1)}, u32[]{:S(2)}, u32[]{:S(2)}) collective-permute-start(bf16[192,1024]{1,0:T(8,128)(2,1)S(1)} %fusion.22), channel_id=1, source_target_pairs={{0,256},{128,384},{256,0},{384,128},{1,257},{129,385},{257,1},{385... | collective-permute-start | bytes 1179656 | tf_op jit(solution)/shard_map/ppermute | solution.py:52
  188.5 26.5 %all-to-all-start.1 = ((bf16[16,19,512]{2,1,0:T(8,128)(2,1)}), bf16[16,19,512]{2,1,0:T(8,128)(2,1)S(1)}, u32[]{:S(2)}, u32[]{:S(2)}) async-start(bf16[16,19,512]{2,1,0:T(8,128)(2,1)} %reshape.97), calls=%async_computation.2 | async-start | bytes 786432 | tf_op jit(solution)/shard_map/all_to_all | solution.py:87
  200.5 14.7 %copy-start.6 = (pred[304,152]{0,1:T(8,128)(4,1)S(1)}, pred[304,152]{0,1:T(8,128)(4,1)}, u32[]{:S(2)}) copy-start(pred[304,152]{0,1:T(8,128)(4,1)} %copy-done.5) | copy-start | bytes 138628
Sparse Core Ops, SparseCore 0:
  47.8 65.1 all-gather.1
  148.4 38.2 reduce-scatter.1

commit v4 on v3

--- a/solution.py
+++ b/solution.py
@@ -7,12 +7,20 @@
 
 
 def expert_grads(feats, grads, gate_col, w_gate, w_up, w_down_t):
-    gate_pre = jnp.dot(feats, w_gate, preferred_element_type=jnp.float32)
-    up_pre = jnp.dot(feats, w_up, preferred_element_type=jnp.float32)
+    split, _, narrow = feats.shape
+    by_block = (((0, 2), (0, 1)), ((), ()))
+    gate_pre = lax.dot_general(
+        feats, w_gate.reshape(split, narrow, -1), by_block, preferred_element_type=jnp.float32
+    )
+    up_pre = lax.dot_general(
+        feats, w_up.reshape(split, narrow, -1), by_block, preferred_element_type=jnp.float32
+    )
     sig = jax.nn.sigmoid(gate_pre)
     act = gate_pre * sig
     hidden_b = (act * up_pre).astype(jnp.bfloat16)
-    back = jnp.dot(grads, w_down_t, preferred_element_type=jnp.float32)
+    back = lax.dot_general(
+        grads, w_down_t.reshape(split, narrow, -1), by_block, preferred_element_type=jnp.float32
+    )
     gate_f = gate_col.astype(jnp.float32)[:, None]
     d_hidden = gate_f * back
     d_gate_b = (d_hidden * up_pre * sig * (1.0 + gate_pre * (1.0 - sig))).astype(jnp.bfloat16)
@@ -23,11 +31,11 @@
     d_part = d_part + lax.dot_general(
         d_up_b, w_up, (((1,), (1,)), ((), ())), preferred_element_type=jnp.float32
     )
-    scaled = (gate_f * grads).astype(jnp.bfloat16)
+    scaled = (gate_f[None] * grads).astype(jnp.bfloat16)
     term = lax.dot_general(
-        hidden_b, scaled, (((0,), (0,)), ((), ())), preferred_element_type=jnp.float32
+        hidden_b, scaled, (((0,), (1,)), ((), ())), preferred_element_type=jnp.float32
     )
-    return (d_part.astype(jnp.bfloat16), term)
+    return (d_part.astype(jnp.bfloat16), term.reshape(term.shape[0], split * narrow))
 
 
 def gather_dp(piece, axis):
@@ -68,14 +76,28 @@
     slot_gate = jnp.sum(
         jnp.where(hit, gates.astype(jnp.float32)[None, :, :], 0.0), axis=(1, 2)
     ).astype(jnp.bfloat16)
-    both = jnp.concatenate([tokens, cotangent], axis=1)
-    packed = jnp.dot(onehot, both, preferred_element_type=jnp.float32).astype(jnp.bfloat16)
-    gate_row = jnp.pad(slot_gate.reshape(width, 1, CAP), ((0, 0), (0, 0), (0, 2 * narrow - CAP)))
-    block = jnp.concatenate([packed.reshape(width, CAP, 2 * narrow), gate_row], axis=1)
+    packed_x = jnp.dot(onehot, tokens, preferred_element_type=jnp.float32).astype(jnp.bfloat16)
+    packed_dy = jnp.dot(onehot, cotangent, preferred_element_type=jnp.float32).astype(jnp.bfloat16)
+    gate_row = jnp.pad(slot_gate.reshape(width, 1, CAP), ((0, 0), (0, 0), (0, narrow - CAP)))
+    block = jnp.concatenate(
+        [
+            packed_x.reshape(width, CAP, narrow),
+            gate_row,
+            packed_dy.reshape(width, CAP, narrow),
+            jnp.zeros_like(gate_row),
+        ],
+        axis=1,
+    )
     recv = lax.all_to_all(block, "expert", split_axis=0, concat_axis=0, tiled=True)
     recv_gate = recv[:, CAP, :CAP].reshape(slots)
-    pair = recv[:, :CAP, :].reshape(slots, 2, narrow).transpose(1, 0, 2)
-    full = lax.all_gather(pair, "etp", axis=2, tiled=True)
+    pair = jnp.stack(
+        [
+            recv[:, :CAP, :].reshape(slots, narrow),
+            recv[:, CAP + 1 : 2 * CAP + 1, :].reshape(slots, narrow),
+        ],
+        axis=0,
+    )
+    full = lax.all_gather(pair, "etp", axis=1, tiled=False)
     feats = full[0]
     grads = full[1]
     stack = jnp.stack([gate_w[0], up_w[0], down_w[0].T], axis=0)

time: 224 us -> 212 us (0.946)
  matrix products: 20.5 us -> 10.3 us
  waiting for transfers between devices: 76.9 us -> 85.4 us
  starting transfers between devices: 33 us -> 28.7 us
  local copies, waits for them, and re-layouts: 29.6 us -> 26.5 us
  blocking collectives: 34.7 us -> 31.9 us
    slice x1, local copies, waits for them, and re-layouts: 14.7 us -> 2.89 us  [local(): grads = full[1]]
    dot_general x5 -> x6, matrix products: 16.4 us -> 6.18 us  [the longest x1 1.3 us: expert_grads(): lax.dot_general(feats, w_up.reshape(split, narrow, -1), by_block, preferr...]
    unnamed x14 -> x33, local copies, waits for them, and re-layouts: 0.04 us -> 8.43 us
    ppermute x3, waiting for transfers between devices: 45.9 us -> 51.7 us  [gather_dp(): lax.ppermute(piece, 'dp', [(i, (i + shift) % size) for i in range(size)])]
    all_to_all x1, blocking collectives: 34.7 us -> 31.9 us  [local(): lax.all_to_all(block, 'expert', split_axis=0, concat_axis=0, tiled=True)]
    ppermute x3, starting transfers between devices: 9.84 us -> 7.19 us  [scatter_sum_dp(): lax.ppermute(outgoing, 'dp', [(i, (i + shift) % size) for i in range(size)])]
    reduce_scatter x1, waiting for transfers between devices: 17.6 us -> 20.3 us  [local(): summed = lax.psum_scatter(d_part_b, 'etp', scatter_dimension=1, tiled=True)]
  transfers between devices with their start and end apart: 9 -> 9, of which waited for: 5 -> 4; matrix products, arithmetic and copies ran while one was open for 13% -> 15% of each run, Pallas kernels for 0% -> 0%
where the time goes in v4:
time: 212 us
  waiting for transfers between devices  85.4 us (40%)
  blocking collectives  31.9 us (15%)
  starting transfers between devices  28.7 us (14%)
  local copies, waits for them, and re-layouts  26.5 us (12%)
  between operations  14.6 us (7%)
  other arithmetic  14.5 us (7%)
  matrix products  10.3 us (5%)
    ppermute x3, waiting for transfers between devices, gather_dp(): lax.ppermute(piece, 'dp', [(i, (i + shift) % size) for i in range(size)])  51.7 us
    all_to_all x1, blocking collectives, local(): lax.all_to_all(block, 'expert', split_axis=0, concat_axis=0, tiled=True)  31.9 us
    reduce_scatter x1, waiting for transfers between devices, local(): summed = lax.psum_scatter(d_part_b, 'etp', scatter_dimension=1, tiled=True)  20.3 us
    all_to_all x1, waiting for transfers between devices, local(): lax.all_to_all(summed.reshape(width, CAP, narrow), 'expert', split_axis=0...  13.4 us
    all_to_all x1, starting transfers between devices, local(): lax.all_to_all(summed.reshape(width, CAP, narrow), 'expert', split_axis=0...  11.9 us
    ppermute x3, starting transfers between devices, gather_dp(): lax.ppermute(piece, 'dp', [(i, (i + shift) % size) for i in range(size)])  9.52 us
    unnamed x33, local copies, waits for them, and re-layouts  8.43 us
    ppermute x3, starting transfers between devices, scatter_sum_dp(): lax.ppermute(outgoing, 'dp', [(i, (i + shift) % size) for i in range(size)])  7.19 us
  transfers between devices with their start and end apart: 9, of which 4 were waited for; matrix products, arithmetic and copies ran while one was open for 15% of the time, Pallas kernels for 0%

profile of v4, /device:TPU:1, one launch (start us, length us, event | category | flops | bytes accessed | tf_op | source)
XLA Modules:
  0.0 211.8 jit_solution(9696166292959542223)
XLA Ops:
  7.2 0.0 all-gather.3.cloned.1.call-start
  7.2 0.7 add_select_fusion
  8.0 0.1 copy.27
  8.1 0.7 fusion.2
  8.7 0.8 copy.28
  9.5 0.4 select_reduce_fusion
  9.9 0.1 convert_element_type.99
  10.1 0.3 convolution_convert_fusion.1
  10.4 0.1 reshape.103
  10.5 1.2 convolution_convert_fusion.2
  11.7 0.1 reshape.102
  11.8 0.1 pad.23.clone
  11.9 0.3 fusion.28
  12.2 31.9 %all_to_all.10 = bf16[16,40,512]{2,1,0:T(8,128)(2,1)S(1)} all-to-all(bf16[16,40,512]{2,1,0:T(8,128)(2,1)S(1)} %fusion.28), channel_id=1, replica_groups=mesh['dp'=4,'expert'=16,'etp'=8] {'expert'}, dimensions={0} | all-to-all | bytes 1310720 | tf_op jit(solution)/shard_map/all_to_all | solution.py:91
  44.0 0.1 fusion.50
  44.2 0.1 stack_reshape.7
  44.3 0.1 stack_reshape.6
  44.4 0.9 pad_maximum_fusion.3
  45.3 0.0 reduce-scatter.2.cloned.1.call-start
  45.4 1.2 fusion.47
  46.6 4.4 %collective-permute-start.2 = (bf16[3,1024,192]{1,2,0:T(8,128)(2,1)}, bf16[3,1024,192]{1,2,0:T(8,128)(2,1)S(1)}, u32[]{:S(2)}, u32[]{:S(2)}) collective-permute-start(bf16[3,1024,192]{1,2,0:T(8,128)(2,1)} %get-tuple-element.28), channel_id=1, source_target_pairs={{0,384},{128,0},{256,128},{384,256},{1,385},{129,1},{257,129},{385... | collective-permute-start | bytes 3538952 | tf_op jit(solution)/shard_map/ppermute | solution.py:46
  51.0 2.4 %collective-permute-start.1 = (bf16[3,1024,192]{1,2,0:T(8,128)(2,1)}, bf16[3,1024,192]{1,2,0:T(8,128)(2,1)}, u32[]{:S(2)}, u32[]{:S(2)}) collective-permute-start(bf16[3,1024,192]{1,2,0:T(8,128)(2,1)} %get-tuple-element.28), channel_id=1, source_target_pairs={{0,256},{128,384},{256,0},{384,128},{1,257},{129,385},{257,1},{385... | collective-permute-start | bytes 3538952 | tf_op jit(solution)/shard_map/ppermute | solution.py:46
  53.5 2.7 %collective-permute-start = (bf16[3,1024,192]{1,2,0:T(8,128)(2,1)}, bf16[3,1024,192]{1,2,0:T(8,128)(2,1)}, u32[]{:S(2)}, u32[]{:S(2)}) collective-permute-start(bf16[3,1024,192]{1,2,0:T(8,128)(2,1)} %get-tuple-element.28), channel_id=1, source_target_pairs={{0,128},{128,256},{256,384},{384,0},{1,129},{129,257},{257,385},{3... | collective-permute-start | bytes 3538952 | tf_op jit(solution)/shard_map/ppermute | solution.py:46
  56.2 45.7 %collective-permute-done.2 = bf16[3,1024,192]{1,2,0:T(8,128)(2,1)S(1)} collective-permute-done((bf16[3,1024,192]{1,2,0:T(8,128)(2,1)}, bf16[3,1024,192]{1,2,0:T(8,128)(2,1)S(1)}, u32[]{:S(2)}, u32[]{:S(2)}) %collective-permute-start.2) | collective-permute-done | bytes 1179680 | tf_op jit(solution)/shard_map/ppermute | solution.py:46
  102.0 6.0 %collective-permute-done = bf16[3,1024,192]{1,2,0:T(8,128)(2,1)} collective-permute-done((bf16[3,1024,192]{1,2,0:T(8,128)(2,1)}, bf16[3,1024,192]{1,2,0:T(8,128)(2,1)}, u32[]{:S(2)}, u32[]{:S(2)}) %collective-permute-start) | collective-permute-done | bytes 1179680 | tf_op jit(solution)/shard_map/ppermute | solution.py:46
  108.0 3.7 %pad_maximum_fusion = bf16[4,3,1024,192]{2,3,1,0:T(8,128)(2,1)} fusion(bf16[1,3,1024,192]{2,3,1,0:T(8,128)(2,1)S(1)} %bitcast.91, bf16[1,3,1024,192]{2,3,1,0:T(8,128)(2,1)} %bitcast.6, bf16[1,3,1024,192]{2,3,1,0:T(8,128)(2,1)} %bitcast.5, bf16[1,3,1024,192]{2,3,1,0:T(8,128)(2,1)S(1)} %get-tuple-element.27), kind=kLoop, calls=%fused_computation.5 | loop fusion | flops 7077888 | bytes 9437184 | tf_op jit(solution)/shard_map/stack | solution.py:48
  111.7 5.4 %gather_fusion = bf16[4,3,1024,192]{2,3,1,0:T(8,128)(2,1)} fusion(bf16[4,3,1024,192]{2,3,1,0:T(8,128)(2,1)} %pad_maximum_fusion, s32[1024]{0:T(1024)S(1)} %pad_clamp_fusion), kind=kCustom, calls=%fused_computation | custom fusion | bytes 9437200 | tf_op jit(solution)/shard_map/jit(_take)/gather | solution.py:48
  117.1 2.9 %broadcast_select_fusion = bf16[4,3,1024,192]{2,3,1,0:T(8,128)(2,1)S(1)} fusion(bf16[4,3,1024,192]{2,3,1,0:T(8,128)(2,1)} %gather_fusion, pred[4]{0:T(512)(128)(4,1)S(1)} %compare_and_fusion), kind=kLoop, calls=%fused_computation.7 | loop fusion | flops 2359296 | bytes 9437188 | tf_op jit(solution)/shard_map/jit(_take)/select_n | solution.py:48
  119.9 0.5 slice_bitcast_fusion.3
  120.4 0.5 pad_maximum_fusion.1
  120.9 0.6 fusion.49
  121.5 1.6 copy-done.2
  123.1 1.9 copy.45
  124.9 1.8 copy.43
  126.7 1.8 copy.44
  128.5 0.1 reshape.170
  128.6 2.9 %fusion.48 = (bf16[1,2432,512]{2,1,0:T(8,128)(2,1)S(1)}, bf16[1,2432,512]{2,1,0:T(8,128)(2,1)S(1)}) fusion(bf16[2,2432,512]{2,1,0:T(8,128)(2,1)} %all-gather.3.cloned.1.call-done), kind=kLoop, calls=%fused_computation.83 | loop fusion | bytes 9961472 | tf_op jit(solution)/shard_map/slice | solution.py:102
  131.6 1.2 fusion.23
  132.8 0.2 copy-done.7
  133.0 1.3 fusion.20
  134.3 0.5 copy-done.5
  134.8 1.2 fusion.17
  136.0 0.9 fusion.4
  136.9 2.3 %fusion = bf16[304,4096]{1,0:T(8,128)(2,1)} fusion(f32[304,4096]{1,0:T(8,128)S(1)} %fusion.4, f32[304,192]{0,1:T(8,128)S(1)} %fusion.17, f32[304,192]{0,1:T(8,128)S(1)} %fusion.23, bf16[3,4096,192]{1,2,0:T(8,128)(2,1)S(1)} %bitcast.79), kind=kOutput, calls=%fused_computation.2 | convolution fusion | flops 480991232 | bytes 9633792 | tf_op jit(solution)/shard_map/dot_general | solution.py:31
  139.3 0.9 fusion.1
  140.2 0.3 copy.42
  140.6 0.6 copy-done.4
  141.2 0.1 copy-done.9
  141.3 1.0 convolution_convert_fusion
  142.3 1.2 reshape.106
  143.5 3.5 %constant_dynamic-slice_fusion.3 = (bf16[192,1,1024]{2,1,0:T(2,128)(2,1)S(1)}, bf16[192,1,1024]{2,1,0:T(2,128)(2,1)S(1)}, bf16[192,1,1024]{2,1,0:T(2,128)(2,1)S(1)}, bf16[192,1,1024]{2,1,0:T(2,128)(2,1)S(1)}) fusion(bf16[192,4,1024]{2,1,0:T(4,128)(2,1)S(1)} %reshape.106, s32[]{:T(128)S(6)} %select_n.90, s32[]{:T(128)S(6)} %select_n.94, s32[]{:T(128)S(6)} %select_n.92, ...), kind=kLoop, calls=%fused_computation.73 | loop fusion | bytes 3145744 | tf_op jit(solution)/shard_map/jit(_take) | solution.py:57
  147.0 0.2 fusion.30
  147.2 1.9 collective-permute-start.5
  149.1 0.2 fusion.31
  149.3 2.4 %collective-permute-start.4 = (bf16[192,1024]{1,0:T(8,128)(2,1)S(1)}, bf16[192,1024]{1,0:T(8,128)(2,1)S(1)}, u32[]{:S(2)}, u32[]{:S(2)}) collective-permute-start(bf16[192,1024]{1,0:T(8,128)(2,1)S(1)} %fusion.31), channel_id=1, source_target_pairs={{0,256},{128,384},{256,0},{384,128},{1,257},{129,385},{257,1},{385... | collective-permute-start | bytes 1179656 | tf_op jit(solution)/shard_map/ppermute | solution.py:60
  151.7 0.9 fusion.32
  152.6 2.8 %collective-permute-start.3 = (bf16[192,1024]{1,0:T(8,128)(2,1)}, bf16[192,1024]{1,0:T(8,128)(2,1)S(1)}, u32[]{:S(2)}, u32[]{:S(2)}) collective-permute-start(bf16[192,1024]{1,0:T(8,128)(2,1)} %fusion.32), channel_id=1, source_target_pairs={{0,128},{128,256},{256,384},{384,0},{1,129},{129,257},{257,385},{3... | collective-permute-start | bytes 1179656 | tf_op jit(solution)/shard_map/ppermute | solution.py:60
  155.4 20.3 %reduce-scatter.2.cloned.1.call-done = bf16[304,512]{1,0:T(8,128)(2,1)} async-done(((bf16[304,4096]{1,0:T(8,128)(2,1)}), bf16[304,512]{1,0:T(8,128)(2,1)}) %reduce-scatter.2.cloned.1.call-update) | async-done | bytes 311312 | tf_op jit(solution)/shard_map/reduce_scatter | solution.py:108
  175.7 1.8 reshape.104
  177.5 11.9 %all-to-all-start.1 = ((bf16[16,19,512]{2,1,0:T(8,128)(2,1)}), bf16[16,19,512]{2,1,0:T(8,128)(2,1)S(1)}, u32[]{:S(2)}, u32[]{:S(2)}) async-start(bf16[16,19,512]{2,1,0:T(8,128)(2,1)} %reshape.104), calls=%async_computation.2 | async-start | bytes 786432 | tf_op jit(solution)/shard_map/all_to_all | solution.py:109
  189.5 1.1 fusion.29
  190.6 13.4 %all-to-all-done.1 = bf16[16,19,512]{2,1,0:T(8,128)(2,1)S(1)} async-done(((bf16[16,19,512]{2,1,0:T(8,128)(2,1)}), bf16[16,19,512]{2,1,0:T(8,128)(2,1)S(1)}, u32[]{:S(2)}, u32[]{:S(2)}) %all-to-all-start.1) | async-done | bytes 311328 | tf_op jit(solution)/shard_map/all_to_all | solution.py:109
  204.0 0.1 reshape.105
  204.1 0.9 convolution_convert_fusion.3
  (37 shorter events, 0.2 us)
Async XLA Ops:
  7.2 2.9 %copy-start = (bf16[152,512]{1,0:T(8,128)(2,1)S(1)}, bf16[152,512]{1,0:T(8,128)(2,1)}, u32[]{:S(2)}) copy-start(bf16[152,512]{1,0:T(8,128)(2,1)} %param.11) | copy-start | bytes 466948
  7.2 121.4 %all-gather.3.cloned.1.call-start = ((), (), s32[]{:S(2)}) async-start(), calls=%async_computation.4 | async-start | bytes 5603328 | tf_op jit(solution)/shard_map/all_gather | solution.py:100
  44.1 1.2 copy-start.10
  44.2 1.2 copy-start.11
  44.2 1.2 copy-start.12
  45.3 130.4 %reduce-scatter.2.cloned.1.call-start = ((), (), s32[]{:S(2)}) async-start(), calls=%async_computation.3 | async-start | bytes 2801664 | tf_op jit(solution)/shard_map/reduce_scatter | solution.py:108
  46.6 55.3 %collective-permute-start.2 = (bf16[3,1024,192]{1,2,0:T(8,128)(2,1)}, bf16[3,1024,192]{1,2,0:T(8,128)(2,1)S(1)}, u32[]{:S(2)}, u32[]{:S(2)}) collective-permute-start(bf16[3,1024,192]{1,2,0:T(8,128)(2,1)} %get-tuple-element.28), channel_id=1, source_target_pairs={{0,384},{128,0},{256,128},{384,256},{1,385},{129,1},{257,129},{385... | collective-permute-start | bytes 3538952 | tf_op jit(solution)/shard_map/ppermute | solution.py:46
  51.0 51.0 %collective-permute-start.1 = (bf16[3,1024,192]{1,2,0:T(8,128)(2,1)}, bf16[3,1024,192]{1,2,0:T(8,128)(2,1)}, u32[]{:S(2)}, u32[]{:S(2)}) collective-permute-start(bf16[3,1024,192]{1,2,0:T(8,128)(2,1)} %get-tuple-element.28), channel_id=1, source_target_pairs={{0,256},{128,384},{256,0},{384,128},{1,257},{129,385},{257,1},{385... | collective-permute-start | bytes 3538952 | tf_op jit(solution)/shard_map/ppermute | solution.py:46
  53.5 54.5 %collective-permute-start = (bf16[3,1024,192]{1,2,0:T(8,128)(2,1)}, bf16[3,1024,192]{1,2,0:T(8,128)(2,1)}, u32[]{:S(2)}, u32[]{:S(2)}) collective-permute-start(bf16[3,1024,192]{1,2,0:T(8,128)(2,1)} %get-tuple-element.28), channel_id=1, source_target_pairs={{0,128},{128,256},{256,384},{384,0},{1,129},{129,257},{257,385},{3... | collective-permute-start | bytes 3538952 | tf_op jit(solution)/shard_map/ppermute | solution.py:46
  120.9 2.2 %copy-start.2 = (bf16[3,4096,192]{1,2,0:T(8,128)(2,1)}, bf16[3,4096,192]{1,2,0:T(8,128)(2,1)S(1)}, u32[]{:S(2)}) copy-start(bf16[3,4096,192]{1,2,0:T(8,128)(2,1)S(1)} %pad_maximum_fusion.1) | copy-start | bytes 14155780
  128.6 2.9 %copy-start.6 = (bf16[24,8,8,512]{3,2,1,0:T(8,128)(2,1)S(1)}, bf16[24,8,8,512]{3,2,1,0:T(8,128)(2,1)}, u32[]{:S(2)}) copy-start(bf16[24,8,8,512]{3,2,1,0:T(8,128)(2,1)} %copy.45) | copy-start | bytes 4718596
  131.5 1.4 copy-start.7
  131.6 4.4 %slice-start = ((s8[4718592]{0:T(1024)(128)(4,1)}), s8[4194304]{0:T(1024)(128)(4,1)S(1)}, s32[]{:S(2)}) async-start(s8[4718592]{0:T(1024)(128)(4,1)} %bitcast.78), calls=%async_computation.5 | async-start | bytes 8388608
  132.8 4.1 %copy-start.3 = (f32[304,192]{0,1:T(8,128)}, f32[304,192]{0,1:T(8,128)S(1)}, u32[]{:S(2)}) copy-start(f32[304,192]{0,1:T(8,128)S(1)} %fusion.23) | copy-start | bytes 700420
  133.0 1.8 copy-start.5
  133.0 3.0 %slice-start.1 = ((s8[4718592]{0:T(1024)(128)(4,1)}), s8[524288]{0:T(1024)(128)(4,1)S(1)}, s32[]{:S(2)}) async-start(s8[4718592]{0:T(1024)(128)(4,1)} %bitcast.78), calls=%async_computation.6 | async-start | bytes 1048576
  134.3 1.7 copy-start.8
  140.2 1.0 copy-start.4
  140.2 1.0 copy-start.9
  147.2 42.3 %collective-permute-start.5 = (bf16[192,1024]{1,0:T(8,128)(2,1)S(1)}, bf16[192,1024]{1,0:T(8,128)(2,1)S(1)}, u32[]{:S(2)}, u32[]{:S(2)}) collective-permute-start(bf16[192,1024]{1,0:T(8,128)(2,1)S(1)} %fusion.30), channel_id=1, source_target_pairs={{0,384},{128,0},{256,128},{384,256},{1,385},{129,1},{257,129},{385... | collective-permute-start | bytes 1179656 | tf_op jit(solution)/shard_map/ppermute | solution.py:60
  149.3 40.2 %collective-permute-start.4 = (bf16[192,1024]{1,0:T(8,128)(2,1)S(1)}, bf16[192,1024]{1,0:T(8,128)(2,1)S(1)}, u32[]{:S(2)}, u32[]{:S(2)}) collective-permute-start(bf16[192,1024]{1,0:T(8,128)(2,1)S(1)} %fusion.31), channel_id=1, source_target_pairs={{0,256},{128,384},{256,0},{384,128},{1,257},{129,385},{257,1},{385... | collective-permute-start | bytes 1179656 | tf_op jit(solution)/shard_map/ppermute | solution.py:60
  152.6 36.9 %collective-permute-start.3 = (bf16[192,1024]{1,0:T(8,128)(2,1)}, bf16[192,1024]{1,0:T(8,128)(2,1)S(1)}, u32[]{:S(2)}, u32[]{:S(2)}) collective-permute-start(bf16[192,1024]{1,0:T(8,128)(2,1)} %fusion.32), channel_id=1, source_target_pairs={{0,128},{128,256},{256,384},{384,0},{1,129},{129,257},{257,385},{3... | collective-permute-start | bytes 1179656 | tf_op jit(solution)/shard_map/ppermute | solution.py:60
  177.5 26.4 %all-to-all-start.1 = ((bf16[16,19,512]{2,1,0:T(8,128)(2,1)}), bf16[16,19,512]{2,1,0:T(8,128)(2,1)S(1)}, u32[]{:S(2)}, u32[]{:S(2)}) async-start(bf16[16,19,512]{2,1,0:T(8,128)(2,1)} %reshape.104), calls=%async_computation.2 | async-start | bytes 786432 | tf_op jit(solution)/shard_map/all_to_all | solution.py:109
  189.4 15.6 %copy-start.1 = (bf16[152,512]{1,0:T(8,128)(2,1)S(1)}, bf16[152,512]{1,0:T(8,128)(2,1)}, u32[]{:S(2)}) copy-start(bf16[152,512]{1,0:T(8,128)(2,1)} %param.11) | copy-start | bytes 466948
Sparse Core Ops, SparseCore 0:
  45.5 60.9 all-gather.2
  139.4 36.2 reduce-scatter.1

commit v5 on v4

--- a/solution.py
+++ b/solution.py
@@ -6,47 +6,55 @@
 CAP = 19
 
 
-def expert_grads(feats, grads, gate_col, w_gate, w_up, w_down_t):
-    split, _, narrow = feats.shape
+def expert_grads(feats, grads, gate_col, pieces):
+    split, slots, narrow = feats.shape
+    size = len(pieces)
+    me = lax.axis_index("dp")
+    per = split // size
+    quarter = per * narrow
     by_block = (((0, 2), (0, 1)), ((), ()))
-    gate_pre = lax.dot_general(
-        feats, w_gate.reshape(split, narrow, -1), by_block, preferred_element_type=jnp.float32
-    )
-    up_pre = lax.dot_general(
-        feats, w_up.reshape(split, narrow, -1), by_block, preferred_element_type=jnp.float32
-    )
+    gate_pre = 0.0
+    up_pre = 0.0
+    back = 0.0
+    for k, piece in enumerate(pieces):
+        start = ((me - k) % size) * per
+        f_k = lax.dynamic_slice_in_dim(feats, start, per, axis=0)
+        g_k = lax.dynamic_slice_in_dim(grads, start, per, axis=0)
+        w_k = piece.reshape(3, per, narrow, -1)
+        gate_pre = gate_pre + lax.dot_general(f_k, w_k[0], by_block, preferred_element_type=jnp.float32)
+        up_pre = up_pre + lax.dot_general(f_k, w_k[1], by_block, preferred_element_type=jnp.float32)
+        back = back + lax.dot_general(g_k, w_k[2], by_block, preferred_element_type=jnp.float32)
     sig = jax.nn.sigmoid(gate_pre)
     act = gate_pre * sig
     hidden_b = (act * up_pre).astype(jnp.bfloat16)
-    back = lax.dot_general(
-        grads, w_down_t.reshape(split, narrow, -1), by_block, preferred_element_type=jnp.float32
-    )
     gate_f = gate_col.astype(jnp.float32)[:, None]
     d_hidden = gate_f * back
     d_gate_b = (d_hidden * up_pre * sig * (1.0 + gate_pre * (1.0 - sig))).astype(jnp.bfloat16)
     d_up_b = (d_hidden * act).astype(jnp.bfloat16)
-    d_part = lax.dot_general(
-        d_gate_b, w_gate, (((1,), (1,)), ((), ())), preferred_element_type=jnp.float32
-    )
-    d_part = d_part + lax.dot_general(
-        d_up_b, w_up, (((1,), (1,)), ((), ())), preferred_element_type=jnp.float32
-    )
+    d_part = jnp.zeros((slots, size * quarter), jnp.bfloat16)
+    for k, piece in enumerate(pieces):
+        part = lax.dot_general(
+            d_gate_b, piece[0], (((1,), (1,)), ((), ())), preferred_element_type=jnp.float32
+        )
+        part = part + lax.dot_general(
+            d_up_b, piece[1], (((1,), (1,)), ((), ())), preferred_element_type=jnp.float32
+        )
+        d_part = lax.dynamic_update_slice_in_dim(
+            d_part, part.astype(jnp.bfloat16), ((me - k) % size) * quarter, axis=1
+        )
     scaled = (gate_f[None] * grads).astype(jnp.bfloat16)
     term = lax.dot_general(
         hidden_b, scaled, (((0,), (1,)), ((), ())), preferred_element_type=jnp.float32
     )
-    return (d_part.astype(jnp.bfloat16), term.reshape(term.shape[0], split * narrow))
+    return (d_part, term.reshape(term.shape[0], split * narrow))
 
 
-def gather_dp(piece, axis):
+def pieces_dp(piece):
     size = lax.axis_size("dp")
-    me = lax.axis_index("dp")
     got = [piece]
     for shift in range(1, size):
         got.append(lax.ppermute(piece, "dp", [(i, (i + shift) % size) for i in range(size)]))
-    order = (me - jnp.arange(size, dtype=jnp.int32)) % size
-    ranked = jnp.take(jnp.stack(got, axis=0), order, axis=0)
-    return jnp.concatenate([ranked[i] for i in range(size)], axis=axis)
+    return got
 
 
 def scatter_sum_dp(term_b):
@@ -101,9 +109,7 @@
     feats = full[0]
     grads = full[1]
     stack = jnp.stack([gate_w[0], up_w[0], down_w[0].T], axis=0)
-    w_all = gather_dp(stack, 1)
-    w_gate, w_up, w_down_t = w_all[0], w_all[1], w_all[2]
-    d_part_b, term = expert_grads(feats, grads, recv_gate, w_gate, w_up, w_down_t)
+    d_part_b, term = expert_grads(feats, grads, recv_gate, pieces_dp(stack))
     down_grad = scatter_sum_dp(term.astype(jnp.bfloat16))[None]
     summed = lax.psum_scatter(d_part_b, "etp", scatter_dimension=1, tiled=True)
     returned = lax.all_to_all(

time: 212 us -> 217 us (1.024)
  waiting for transfers between devices: 85.4 us -> 76.8 us
  local copies, waits for them, and re-layouts: 26.5 us -> 34.6 us
  matrix products: 10.3 us -> 17.2 us
  other arithmetic: 14.5 us -> 8.67 us
  starting transfers between devices: 28.7 us -> 31.8 us
    squeeze x1 -> x11, local copies, waits for them, and re-layouts: 0.51 us -> 15.5 us  [the longest x4 7.28 us: expert_grads(): w_k[1]]
    ppermute x3, waiting for transfers between devices: 51.7 us -> 43.7 us  [pieces_dp(): lax.ppermute(piece, 'dp', [(i, (i + shift) % size) for i in range(size)])]
    dot_general x5 -> x20, matrix products: 6.9 us -> 13.7 us  [the longest x4 4.99 us: expert_grads(): lax.dot_general(d_gate_b, piece[0], (((1,), (1,)), ((), ())), preferred_e...]
    unnamed x33 -> x63, local copies, waits for them, and re-layouts: 8.43 us -> 2.51 us
    gather x1 -> x0, local copies, waits for them, and re-layouts: 5.41 us -> none  [gather_dp(): ranked = jnp.take(jnp.stack(got, axis=0), order, axis=0)]
    slice x1 -> x3, local copies, waits for them, and re-layouts: 0.56 us -> 4.52 us  [expert_grads(): w_k[1]]
    another operation x2 -> x1, other arithmetic: 4.94 us -> 1.14 us  [local(): stack = jnp.stack([gate_w[0], up_w[0], down_w[0].T], axis=0)]
    ppermute x3, starting transfers between devices: 7.19 us -> 10.5 us  [scatter_sum_dp(): lax.ppermute(outgoing, 'dp', [(i, (i + shift) % size) for i in range(size)])]
  transfers between devices with their start and end apart: 9 -> 9, of which waited for: 4 -> 3; matrix products, arithmetic and copies ran while one was open for 15% -> 16% of each run, Pallas kernels for 0% -> 0%
where the time goes in v5:
time: 217 us; the launch traced here: 216 us
  waiting for transfers between devices  76.8 us (35%)
  local copies, waits for them, and re-layouts  34.6 us (16%)
  blocking collectives  31.9 us (15%)
  starting transfers between devices  31.8 us (15%)
  matrix products  17.2 us (8%)
  between operations  14.8 us (7%)
  other arithmetic  8.67 us (4%)
    ppermute x3, waiting for transfers between devices, pieces_dp(): lax.ppermute(piece, 'dp', [(i, (i + shift) % size) for i in range(size)])  43.7 us
    all_to_all x1, blocking collectives, local(): lax.all_to_all(block, 'expert', split_axis=0, concat_axis=0, tiled=True)  31.9 us
    reduce_scatter x1, waiting for transfers between devices, local(): summed = lax.psum_scatter(d_part_b, 'etp', scatter_dimension=1, tiled=True)  19.6 us
    all_to_all x1, waiting for transfers between devices, local(): lax.all_to_all(summed.reshape(width, CAP, narrow), 'expert', split_axis=0...  13.4 us
    all_to_all x1, starting transfers between devices, local(): lax.all_to_all(summed.reshape(width, CAP, narrow), 'expert', split_axis=0...  11.8 us
    ppermute x3, starting transfers between devices, scatter_sum_dp(): lax.ppermute(outgoing, 'dp', [(i, (i + shift) % size) for i in range(size)])  10.5 us
    ppermute x3, starting transfers between devices, pieces_dp(): lax.ppermute(piece, 'dp', [(i, (i + shift) % size) for i in range(size)])  9.51 us
    squeeze x4, local copies, waits for them, and re-layouts, expert_grads(): w_k[1]  7.28 us
  transfers between devices with their start and end apart: 9, of which 3 were waited for; matrix products, arithmetic and copies ran while one was open for 16% of the time, Pallas kernels for 0%

profile of v5, /device:TPU:1, one launch (start us, length us, event | category | flops | bytes accessed | tf_op | source)
XLA Modules:
  0.0 215.7 jit_solution(15863325775446063341)
XLA Ops:
  7.2 0.7 add_select_fusion
  8.1 0.7 fusion.1
  9.2 1.2 convolution_convert_fusion.1
  10.6 0.4 select_reduce_fusion
  11.5 31.9 %all_to_all.10 = bf16[16,40,512]{2,1,0:T(8,128)(2,1)S(1)} all-to-all(bf16[16,40,512]{2,1,0:T(8,128)(2,1)S(1)} %fusion.24), channel_id=1, replica_groups=mesh['dp'=4,'expert'=16,'etp'=8] {'expert'}, dimensions={0} | all-to-all | bytes 1310720 | tf_op jit(solution)/shard_map/all_to_all | solution.py:99
  43.4 0.9 copy-done.7
  44.6 0.9 pad_maximum_fusion.1
  45.6 1.1 pad_maximum_fusion
  46.8 4.4 %collective-permute-start.2 = (bf16[3,1024,192]{1,2,0:T(8,128)(2,1)}, bf16[3,1024,192]{1,2,0:T(8,128)(2,1)S(1)}, u32[]{:S(2)}, u32[]{:S(2)}) collective-permute-start(bf16[3,1024,192]{1,2,0:T(8,128)(2,1)} %pad_maximum_fusion), channel_id=1, source_target_pairs={{0,384},{128,0},{256,128},{384,256},{1,385},{129,1},{257,129},{385... | collective-permute-start | bytes 3538952 | tf_op jit(solution)/shard_map/ppermute | solution.py:56
  51.2 2.4 %collective-permute-start.1 = (bf16[3,1024,192]{1,2,0:T(8,128)(2,1)}, bf16[3,1024,192]{1,2,0:T(8,128)(2,1)S(1)}, u32[]{:S(2)}, u32[]{:S(2)}) collective-permute-start(bf16[3,1024,192]{1,2,0:T(8,128)(2,1)} %pad_maximum_fusion), channel_id=1, source_target_pairs={{0,256},{128,384},{256,0},{384,128},{1,257},{129,385},{257,1},{385... | collective-permute-start | bytes 3538952 | tf_op jit(solution)/shard_map/ppermute | solution.py:56
  53.6 2.7 %collective-permute-start = (bf16[3,1024,192]{1,2,0:T(8,128)(2,1)}, bf16[3,1024,192]{1,2,0:T(8,128)(2,1)}, u32[]{:S(2)}, u32[]{:S(2)}) collective-permute-start(bf16[3,1024,192]{1,2,0:T(8,128)(2,1)} %pad_maximum_fusion), channel_id=1, source_target_pairs={{0,128},{128,256},{256,384},{384,0},{1,129},{129,257},{257,385},{3... | collective-permute-start | bytes 3538952 | tf_op jit(solution)/shard_map/ppermute | solution.py:56
  56.4 1.0 squeeze.64
  57.4 1.0 squeeze.68
  58.4 43.7 %collective-permute-done.2 = bf16[3,1024,192]{1,2,0:T(8,128)(2,1)S(1)} collective-permute-done((bf16[3,1024,192]{1,2,0:T(8,128)(2,1)}, bf16[3,1024,192]{1,2,0:T(8,128)(2,1)S(1)}, u32[]{:S(2)}, u32[]{:S(2)}) %collective-permute-start.2) | collective-permute-done | bytes 1179680 | tf_op jit(solution)/shard_map/ppermute | solution.py:56
  102.1 1.1 fusion.104
  103.2 2.0 squeeze.67
  105.3 1.1 fusion.103
  106.4 2.1 squeeze.66
  108.4 2.3 %fusion.102 = (bf16[1,1024,192]{1,2,0:T(8,128)(2,1)}, bf16[1,1024,192]{1,2,0:T(8,128)(2,1)}, bf16[1,1024,192]{1,2,0:T(8,128)(2,1)}) fusion(bf16[3,1024,192]{1,2,0:T(8,128)(2,1)} %collective-permute-done), kind=kLoop, calls=%fused_computation.143 | loop fusion | bytes 2359296 | tf_op jit(solution)/shard_map/slice | solution.py:25
  110.8 2.2 %squeeze.65 = bf16[2,512,192]{1,0,2:T(2,128)(2,1)} reshape(bf16[1,1024,192]{1,2,0:T(8,128)(2,1)} %get-tuple-element.20) | data formatting | bytes 786432 | tf_op jit(solution)/shard_map/squeeze | solution.py:25
  112.9 2.1 squeeze.70
  115.0 1.0 squeeze.71
  116.0 1.0 squeeze.69
  117.1 1.1 squeeze.63
  118.1 1.0 squeeze.62
  119.2 1.0 squeeze.61
  120.2 0.8 fusion.81
  121.1 2.8 %fusion.101 = (bf16[1,2432,512]{2,1,0:T(8,128)(2,1)S(1)}, bf16[1,2432,512]{2,1,0:T(8,128)(2,1)S(1)}) fusion(bf16[2,2432,512]{2,1,0:T(8,128)(2,1)} %all-gather.3.cloned.1.call-done), kind=kLoop, calls=%fused_computation.142 | loop fusion | bytes 9961472 | tf_op jit(solution)/shard_map/slice | solution.py:110
  124.0 0.4 convolution_bitcast_fusion.5
  124.5 0.4 convolution_bitcast_fusion.1
  125.0 0.4 convolution_bitcast_fusion.4
  125.4 0.4 convolution_bitcast_fusion
  125.9 0.4 convolution_bitcast_fusion.7
  126.3 0.4 convolution_bitcast_fusion.3
  126.8 0.4 convolution_bitcast_fusion.8
  127.3 0.4 convolution_bitcast_fusion.9
  127.7 0.4 convolution_bitcast_fusion.11
  128.2 0.4 fusion.18
  128.7 0.5 fusion.21
  129.2 0.6 multiply_convert_fusion.1
  129.8 0.3 fusion.66
  130.2 1.8 broadcast_in_dim.39
  131.9 1.2 fusion.3
  133.1 1.4 fusion.62
  134.6 0.3 fusion.59
  135.0 0.3 fusion.56
  135.3 2.2 %fusion.5 = bf16[304,4096]{1,0:T(8,128)(2,1)} fusion(bf16[304,4096]{1,0:T(8,128)(2,1)} %fusion.3, s32[]{:T(128)S(6)} %select_n.92, f32[304,1024]{1,0:T(8,128)S(1)} %fusion.62, bf16[304,192]{0,1:T(8,128)(2,1)S(1)} %get-tuple-element.32, bf16[3,1024,192]{1,2,0:T(8,128)(2,1)} %collective-permute-done), kind=kOutput, calls=%fused_computation.15 | convolution fusion | flops 120160256 | bytes 2377732 | tf_op jit(solution)/shard_map/dot_general | solution.py:36
  137.5 1.2 fusion.7
  138.7 1.2 fusion.9
  140.0 1.4 fusion
  141.5 1.3 copy.64
  142.8 1.0 convolution_convert_fusion
  143.8 1.2 reshape.91
  145.0 3.3 %constant_dynamic-slice_fusion.2 = (bf16[192,1,1024]{2,1,0:T(2,128)(2,1)S(1)}, bf16[192,1,1024]{2,1,0:T(2,128)(2,1)S(1)}, bf16[192,1,1024]{2,1,0:T(2,128)(2,1)S(1)}, bf16[192,1,1024]{2,1,0:T(2,128)(2,1)S(1)}) fusion(bf16[192,4,1024]{2,1,0:T(4,128)(2,1)S(1)} %reshape.91, s32[]{:T(128)S(6)} %select_n.112, s32[]{:T(128)S(6)} %select_n.116, s32[]{:T(128)S(6)} %select_n.114, ...), kind=kLoop, calls=%fused_computation.125 | loop fusion | bytes 3145744 | tf_op jit(solution)/shard_map/jit(_take) | solution.py:65
  148.5 1.9 collective-permute-start.3
  150.6 6.6 %collective-permute-start.4 = (bf16[192,1024]{1,0:T(8,128)(2,1)S(1)}, bf16[192,1024]{1,0:T(8,128)(2,1)S(1)}, u32[]{:S(2)}, u32[]{:S(2)}) collective-permute-start(bf16[192,1024]{1,0:T(8,128)(2,1)S(1)} %fusion.53), channel_id=1, source_target_pairs={{0,256},{128,384},{256,0},{384,128},{1,257},{129,385},{257,1},{385... | collective-permute-start | bytes 1179656 | tf_op jit(solution)/shard_map/ppermute | solution.py:68
  157.2 0.9 fusion.52
  158.2 1.9 collective-permute-start.5
  160.1 19.6 %reduce-scatter.2.cloned.1.call-done = bf16[304,512]{1,0:T(8,128)(2,1)} async-done(((bf16[304,4096]{1,0:T(8,128)(2,1)}), bf16[304,512]{1,0:T(8,128)(2,1)}) %reduce-scatter.2.cloned.1.call-update) | async-done | bytes 311312 | tf_op jit(solution)/shard_map/reduce_scatter | solution.py:114
  179.7 1.8 reshape.89
  181.5 11.8 %all-to-all-start.1 = ((bf16[16,19,512]{2,1,0:T(8,128)(2,1)}), bf16[16,19,512]{2,1,0:T(8,128)(2,1)S(1)}, u32[]{:S(2)}, u32[]{:S(2)}) async-start(bf16[16,19,512]{2,1,0:T(8,128)(2,1)} %reshape.89), calls=%async_computation.2 | async-start | bytes 786432 | tf_op jit(solution)/shard_map/all_to_all | solution.py:115
  193.3 1.1 fusion.49
  194.5 13.4 %all-to-all-done.1 = bf16[16,19,512]{2,1,0:T(8,128)(2,1)S(1)} async-done(((bf16[16,19,512]{2,1,0:T(8,128)(2,1)}), bf16[16,19,512]{2,1,0:T(8,128)(2,1)S(1)}, u32[]{:S(2)}, u32[]{:S(2)}) %all-to-all-start.1) | async-done | bytes 311328 | tf_op jit(solution)/shard_map/all_to_all | solution.py:115
  208.0 0.9 convolution_convert_fusion.3
  (86 shorter events, 2.5 us)
Async XLA Ops:
  7.2 1.6 copy-start
  7.2 3.3 %copy-start.30 = (bf16[152,8]{0,1:T(8,128)(2,1)S(1)}, bf16[152,8]{0,1:T(8,128)(2,1)}, u32[]{:S(2)}) copy-start(bf16[152,8]{0,1:T(8,128)(2,1)} %param.12) | copy-start | bytes 7300
  7.2 113.9 %all-gather.3.cloned.1.call-start = ((), (), s32[]{:S(2)}) async-start(), calls=%async_computation.4 | async-start | bytes 5603328 | tf_op jit(solution)/shard_map/all_gather | solution.py:108
  43.4 0.9 copy-start.7
  44.4 1.3 copy-start.1
  44.4 1.3 copy-start.2
  44.4 1.3 copy-start.8
  45.6 134.1 %reduce-scatter.2.cloned.1.call-start = ((), (), s32[]{:S(2)}) async-start(), calls=%async_computation.3 | async-start | bytes 2801664 | tf_op jit(solution)/shard_map/reduce_scatter | solution.py:114
  46.8 55.3 %collective-permute-start.2 = (bf16[3,1024,192]{1,2,0:T(8,128)(2,1)}, bf16[3,1024,192]{1,2,0:T(8,128)(2,1)S(1)}, u32[]{:S(2)}, u32[]{:S(2)}) collective-permute-start(bf16[3,1024,192]{1,2,0:T(8,128)(2,1)} %pad_maximum_fusion), channel_id=1, source_target_pairs={{0,384},{128,0},{256,128},{384,256},{1,385},{129,1},{257,129},{385... | collective-permute-start | bytes 3538952 | tf_op jit(solution)/shard_map/ppermute | solution.py:56
  51.2 54.1 %collective-permute-start.1 = (bf16[3,1024,192]{1,2,0:T(8,128)(2,1)}, bf16[3,1024,192]{1,2,0:T(8,128)(2,1)S(1)}, u32[]{:S(2)}, u32[]{:S(2)}) collective-permute-start(bf16[3,1024,192]{1,2,0:T(8,128)(2,1)} %pad_maximum_fusion), channel_id=1, source_target_pairs={{0,256},{128,384},{256,0},{384,128},{1,257},{129,385},{257,1},{385... | collective-permute-start | bytes 3538952 | tf_op jit(solution)/shard_map/ppermute | solution.py:56
  53.6 54.8 %collective-permute-start = (bf16[3,1024,192]{1,2,0:T(8,128)(2,1)}, bf16[3,1024,192]{1,2,0:T(8,128)(2,1)}, u32[]{:S(2)}, u32[]{:S(2)}) collective-permute-start(bf16[3,1024,192]{1,2,0:T(8,128)(2,1)} %pad_maximum_fusion), channel_id=1, source_target_pairs={{0,128},{128,256},{256,384},{384,0},{1,129},{129,257},{257,385},{3... | collective-permute-start | bytes 3538952 | tf_op jit(solution)/shard_map/ppermute | solution.py:56
  102.1 4.3 %copy-start.3 = (bf16[3,1024,192]{1,2,0:T(8,128)(2,1)}, bf16[3,1024,192]{1,2,0:T(8,128)(2,1)S(1)}, u32[]{:S(2)}) copy-start(bf16[3,1024,192]{1,2,0:T(8,128)(2,1)S(1)} %collective-permute-done.2) | copy-start | bytes 3538948
  105.3 5.5 %copy-start.5 = (bf16[3,1024,192]{1,2,0:T(8,128)(2,1)}, bf16[3,1024,192]{1,2,0:T(8,128)(2,1)S(1)}, u32[]{:S(2)}) copy-start(bf16[3,1024,192]{1,2,0:T(8,128)(2,1)S(1)} %collective-permute-done.1) | copy-start | bytes 3538948
  108.4 6.6 %copy-start.13 = (bf16[1,1024,192]{1,2,0:T(8,128)(2,1)S(1)}, bf16[1,1024,192]{1,2,0:T(8,128)(2,1)}, u32[]{:S(2)}) copy-start(bf16[1,1024,192]{1,2,0:T(8,128)(2,1)} %get-tuple-element.27) | copy-start | bytes 1179652
  110.8 6.3 %copy-start.12 = (bf16[1,1024,192]{1,2,0:T(8,128)(2,1)S(1)}, bf16[1,1024,192]{1,2,0:T(8,128)(2,1)}, u32[]{:S(2)}) copy-start(bf16[1,1024,192]{1,2,0:T(8,128)(2,1)} %get-tuple-element.28) | copy-start | bytes 1179652
  110.8 5.3 %copy-start.16 = (bf16[1,1024,192]{1,2,0:T(8,128)(2,1)S(1)}, bf16[1,1024,192]{1,2,0:T(8,128)(2,1)}, u32[]{:S(2)}) copy-start(bf16[1,1024,192]{1,2,0:T(8,128)(2,1)} %get-tuple-element.21) | copy-start | bytes 1179652
  110.8 7.4 %copy-start.14 = (bf16[1,1024,192]{1,2,0:T(8,128)(2,1)S(1)}, bf16[1,1024,192]{1,2,0:T(8,128)(2,1)}, u32[]{:S(2)}) copy-start(bf16[1,1024,192]{1,2,0:T(8,128)(2,1)} %get-tuple-element.25) | copy-start | bytes 1179652
  112.9 6.2 %copy-start.15 = (bf16[1,1024,192]{1,2,0:T(8,128)(2,1)S(1)}, bf16[1,1024,192]{1,2,0:T(8,128)(2,1)}, u32[]{:S(2)}) copy-start(bf16[1,1024,192]{1,2,0:T(8,128)(2,1)} %get-tuple-element.22) | copy-start | bytes 1179652
  121.1 2.9 %copy-start.20 = (bf16[2,512,192]{1,0,2:T(2,128)(2,1)S(1)}, bf16[2,512,192]{1,0,2:T(2,128)(2,1)}, u32[]{:S(2)}) copy-start(bf16[2,512,192]{1,0,2:T(2,128)(2,1)} %squeeze.66) | copy-start | bytes 1179652
  121.1 3.3 %copy-start.24 = (bf16[2,512,192]{1,0,2:T(2,128)(2,1)S(1)}, bf16[2,512,192]{1,0,2:T(2,128)(2,1)}, u32[]{:S(2)}) copy-start(bf16[2,512,192]{1,0,2:T(2,128)(2,1)} %squeeze.70) | copy-start | bytes 1179652
  124.0 1.0 copy-start.19
  124.0 1.4 copy-start.23
  124.4 1.4 copy-start.17
  125.0 1.4 copy-start.18
  125.4 1.4 copy-start.21
  125.9 1.4 copy-start.22
  126.3 1.4 copy-start.9
  126.8 1.4 copy-start.10
  127.7 1.0 copy-start.11
  128.2 1.0 copy-start.29
  128.7 1.0 copy-start.25
  129.2 0.9 copy-start.27
  131.9 2.7 %copy-start.6 = (bf16[3,1024,192]{1,2,0:T(8,128)(2,1)S(1)}, bf16[3,1024,192]{1,2,0:T(8,128)(2,1)}, u32[]{:S(2)}) copy-start(bf16[3,1024,192]{1,2,0:T(8,128)(2,1)} %copy-done.5) | copy-start | bytes 3538948
  133.1 1.8 copy-start.4
  141.4 1.4 copy-start.26
  141.5 1.4 copy-start.28
  148.5 44.8 %collective-permute-start.3 = (bf16[192,1024]{1,0:T(8,128)(2,1)S(1)}, bf16[192,1024]{1,0:T(8,128)(2,1)S(1)}, u32[]{:S(2)}, u32[]{:S(2)}) collective-permute-start(bf16[192,1024]{1,0:T(8,128)(2,1)S(1)} %fusion.54), channel_id=1, source_target_pairs={{0,128},{128,256},{256,384},{384,0},{1,129},{129,257},{257,385},{3... | collective-permute-start | bytes 1179656 | tf_op jit(solution)/shard_map/ppermute | solution.py:68
  150.6 42.7 %collective-permute-start.4 = (bf16[192,1024]{1,0:T(8,128)(2,1)S(1)}, bf16[192,1024]{1,0:T(8,128)(2,1)S(1)}, u32[]{:S(2)}, u32[]{:S(2)}) collective-permute-start(bf16[192,1024]{1,0:T(8,128)(2,1)S(1)} %fusion.53), channel_id=1, source_target_pairs={{0,256},{128,384},{256,0},{384,128},{1,257},{129,385},{257,1},{385... | collective-permute-start | bytes 1179656 | tf_op jit(solution)/shard_map/ppermute | solution.py:68
  158.2 35.2 %collective-permute-start.5 = (bf16[192,1024]{1,0:T(8,128)(2,1)}, bf16[192,1024]{1,0:T(8,128)(2,1)S(1)}, u32[]{:S(2)}, u32[]{:S(2)}) collective-permute-start(bf16[192,1024]{1,0:T(8,128)(2,1)} %fusion.52), channel_id=1, source_target_pairs={{0,384},{128,0},{256,128},{384,256},{1,385},{129,1},{257,129},{385... | collective-permute-start | bytes 1179656 | tf_op jit(solution)/shard_map/ppermute | solution.py:68
  181.5 26.3 %all-to-all-start.1 = ((bf16[16,19,512]{2,1,0:T(8,128)(2,1)}), bf16[16,19,512]{2,1,0:T(8,128)(2,1)S(1)}, u32[]{:S(2)}, u32[]{:S(2)}) async-start(bf16[16,19,512]{2,1,0:T(8,128)(2,1)} %reshape.89), calls=%async_computation.2 | async-start | bytes 786432 | tf_op jit(solution)/shard_map/all_to_all | solution.py:115
Sparse Core Ops, SparseCore 0:
  45.7 60.9 all-gather.2
  140.1 39.5 reduce-scatter.1

commit v6 on v5

--- a/solution.py
+++ b/solution.py
@@ -7,23 +7,20 @@
 
 
 def expert_grads(feats, grads, gate_col, pieces):
-    split, slots, narrow = feats.shape
+    slots = feats.shape[0]
     size = len(pieces)
+    quarter = pieces[0].shape[1]
     me = lax.axis_index("dp")
-    per = split // size
-    quarter = per * narrow
-    by_block = (((0, 2), (0, 1)), ((), ()))
     gate_pre = 0.0
     up_pre = 0.0
     back = 0.0
     for k, piece in enumerate(pieces):
-        start = ((me - k) % size) * per
-        f_k = lax.dynamic_slice_in_dim(feats, start, per, axis=0)
-        g_k = lax.dynamic_slice_in_dim(grads, start, per, axis=0)
-        w_k = piece.reshape(3, per, narrow, -1)
-        gate_pre = gate_pre + lax.dot_general(f_k, w_k[0], by_block, preferred_element_type=jnp.float32)
-        up_pre = up_pre + lax.dot_general(f_k, w_k[1], by_block, preferred_element_type=jnp.float32)
-        back = back + lax.dot_general(g_k, w_k[2], by_block, preferred_element_type=jnp.float32)
+        start = ((me - k) % size) * quarter
+        f_k = lax.dynamic_slice_in_dim(feats, start, quarter, axis=1)
+        g_k = lax.dynamic_slice_in_dim(grads, start, quarter, axis=1)
+        gate_pre = gate_pre + jnp.dot(f_k, piece[0], preferred_element_type=jnp.float32)
+        up_pre = up_pre + jnp.dot(f_k, piece[1], preferred_element_type=jnp.float32)
+        back = back + jnp.dot(g_k, piece[2], preferred_element_type=jnp.float32)
     sig = jax.nn.sigmoid(gate_pre)
     act = gate_pre * sig
     hidden_b = (act * up_pre).astype(jnp.bfloat16)
@@ -42,11 +39,11 @@
         d_part = lax.dynamic_update_slice_in_dim(
             d_part, part.astype(jnp.bfloat16), ((me - k) % size) * quarter, axis=1
         )
-    scaled = (gate_f[None] * grads).astype(jnp.bfloat16)
+    scaled = (gate_f * grads).astype(jnp.bfloat16)
     term = lax.dot_general(
-        hidden_b, scaled, (((0,), (1,)), ((), ())), preferred_element_type=jnp.float32
+        hidden_b, scaled, (((0,), (0,)), ((), ())), preferred_element_type=jnp.float32
     )
-    return (d_part, term.reshape(term.shape[0], split * narrow))
+    return (d_part, term)
 
 
 def pieces_dp(piece):
@@ -105,7 +102,7 @@
         ],
         axis=0,
     )
-    full = lax.all_gather(pair, "etp", axis=1, tiled=False)
+    full = lax.all_gather(pair, "etp", axis=2, tiled=True)
     feats = full[0]
     grads = full[1]
     stack = jnp.stack([gate_w[0], up_w[0], down_w[0].T], axis=0)

time: 217 us -> 207 us (0.954)
  local copies, waits for them, and re-layouts: 34.6 us -> 12.5 us
  waiting for transfers between devices: 76.8 us -> 84.5 us
  matrix products: 17.2 us -> 22.8 us
    all_gather x1, waiting for transfers between devices: 0.02 us -> 49.2 us  [local(): full = lax.all_gather(pair, 'etp', axis=2, tiled=True)]
    ppermute x3, waiting for transfers between devices: 43.7 us -> 0.01 us  [pieces_dp(): lax.ppermute(piece, 'dp', [(i, (i + shift) % size) for i in range(size)])]
    squeeze x11 -> x0, local copies, waits for them, and re-layouts: 15.5 us -> none  [the longest x4 7.28 us: expert_grads(): w_k[1]]
    dot_general x13, matrix products: 6.4 us -> 14.4 us  [the longest x4 3.96 us: expert_grads(): back = back + jnp.dot(g_k, piece[2], preferred_element_type=jnp.float32)]
    slice x3 -> x0, local copies, waits for them, and re-layouts: 4.52 us -> none  [expert_grads(): w_k[1]]
    reduce_scatter x1, waiting for transfers between devices: 19.6 us -> 21.8 us  [local(): summed = lax.psum_scatter(d_part_b, 'etp', scatter_dimension=1, tiled=True)]
  transfers between devices with their start and end apart: 9 -> 9, of which waited for: 3 -> 3; matrix products, arithmetic and copies ran while one was open for 16% -> 11% of each run, Pallas kernels for 0% -> 0%
where the time goes in v6:
time: 207 us; the launch traced here: 206 us
  waiting for transfers between devices  84.5 us (41%)
  starting transfers between devices  32.8 us (16%)
  blocking collectives  31.9 us (15%)
  matrix products  22.8 us (11%)
  between operations  14.7 us (7%)
  local copies, waits for them, and re-layouts  12.5 us (6%)
  other arithmetic  6.72 us (3%)
    all_gather x1, waiting for transfers between devices, local(): full = lax.all_gather(pair, 'etp', axis=2, tiled=True)  49.2 us
    all_to_all x1, blocking collectives, local(): lax.all_to_all(block, 'expert', split_axis=0, concat_axis=0, tiled=True)  31.9 us
    reduce_scatter x1, waiting for transfers between devices, local(): summed = lax.psum_scatter(d_part_b, 'etp', scatter_dimension=1, tiled=True)  21.8 us
    all_to_all x1, waiting for transfers between devices, local(): lax.all_to_all(summed.reshape(width, CAP, narrow), 'expert', split_axis=0...  13.4 us
    all_to_all x1, starting transfers between devices, local(): lax.all_to_all(summed.reshape(width, CAP, narrow), 'expert', split_axis=0...  12.1 us
    ppermute x3, starting transfers between devices, scatter_sum_dp(): lax.ppermute(outgoing, 'dp', [(i, (i + shift) % size) for i in range(size)])  10.5 us
    ppermute x3, starting transfers between devices, pieces_dp(): lax.ppermute(piece, 'dp', [(i, (i + shift) % size) for i in range(size)])  10.1 us
  transfers between devices with their start and end apart: 9, of which 3 were waited for; matrix products, arithmetic and copies ran while one was open for 11% of the time, Pallas kernels for 0%

profile of v6, /device:TPU:1, one launch (start us, length us, event | category | flops | bytes accessed | tf_op | source)
XLA Modules:
  0.0 205.8 jit_solution(12363988781526055902)
XLA Ops:
  7.2 0.8 add_select_fusion
  8.0 0.1 copy.23
  8.2 0.6 fusion.4
  8.8 0.3 convolution_convert_fusion.2
  9.1 0.1 reshape.51
  9.3 0.3 convolution_convert_fusion.1
  9.5 0.1 reshape.52
  9.7 0.1 copy.24
  9.8 0.4 select_reduce_fusion
  10.2 0.1 convert_element_type.112
  10.3 0.1 pad.15.clone
  10.4 0.3 fusion.21
  10.7 31.9 %all_to_all.10 = bf16[16,40,512]{2,1,0:T(8,128)(2,1)S(1)} all-to-all(bf16[16,40,512]{2,1,0:T(8,128)(2,1)S(1)} %fusion.21), channel_id=1, replica_groups=mesh['dp'=4,'expert'=16,'etp'=8] {'expert'}, dimensions={0} | all-to-all | bytes 1310720 | tf_op jit(solution)/shard_map/all_to_all | solution.py:96
  42.5 0.1 fusion.84
  42.6 0.1 stack_reshape.6
  42.8 0.1 stack_reshape.7
  42.9 1.0 pad_maximum_fusion.1
  44.0 0.2 copy-done.6
  44.2 1.2 pad_maximum_fusion
  45.4 3.1 %collective-permute-start = (bf16[3,1024,192]{1,2,0:T(8,128)(2,1)}, bf16[3,1024,192]{1,2,0:T(8,128)(2,1)}, u32[]{:S(2)}, u32[]{:S(2)}) collective-permute-start(bf16[3,1024,192]{1,2,0:T(8,128)(2,1)} %pad_maximum_fusion), channel_id=1, source_target_pairs={{0,128},{128,256},{256,384},{384,0},{1,129},{129,257},{257,385},{3... | collective-permute-start | bytes 3538952 | tf_op jit(solution)/shard_map/ppermute | solution.py:53
  48.6 3.4 %collective-permute-start.2 = (bf16[3,1024,192]{1,2,0:T(8,128)(2,1)}, bf16[3,1024,192]{1,2,0:T(8,128)(2,1)S(1)}, u32[]{:S(2)}, u32[]{:S(2)}) collective-permute-start(bf16[3,1024,192]{1,2,0:T(8,128)(2,1)} %pad_maximum_fusion), channel_id=1, source_target_pairs={{0,384},{128,0},{256,128},{384,256},{1,385},{129,1},{257,129},{385... | collective-permute-start | bytes 3538952 | tf_op jit(solution)/shard_map/ppermute | solution.py:53
  52.0 3.6 %collective-permute-start.1 = (bf16[3,1024,192]{1,2,0:T(8,128)(2,1)}, bf16[3,1024,192]{1,2,0:T(8,128)(2,1)}, u32[]{:S(2)}, u32[]{:S(2)}) collective-permute-start(bf16[3,1024,192]{1,2,0:T(8,128)(2,1)} %pad_maximum_fusion), channel_id=1, source_target_pairs={{0,256},{128,384},{256,0},{384,128},{1,257},{129,385},{257,1},{385... | collective-permute-start | bytes 3538952 | tf_op jit(solution)/shard_map/ppermute | solution.py:53
  55.7 0.1 reshape.119
  55.8 49.2 %all-gather.2.cloned.1.call-done = bf16[2,304,4096]{2,1,0:T(8,128)(2,1)} async-done(((bf16[2,304,512]{2,1,0:T(8,128)(2,1)}), bf16[2,304,4096]{2,1,0:T(8,128)(2,1)}) %all-gather.2.cloned.1.call-update) | async-done | bytes 4980752 | tf_op jit(solution)/shard_map/all_gather | solution.py:105
  105.0 2.8 %fusion.83 = (bf16[1,304,4096]{2,1,0:T(8,128)(2,1)S(1)}, bf16[1,304,4096]{2,1,0:T(8,128)(2,1)S(1)}) fusion(bf16[2,304,4096]{2,1,0:T(8,128)(2,1)} %all-gather.2.cloned.1.call-done), kind=kLoop, calls=%fused_computation.126 | loop fusion | bytes 9961472 | tf_op jit(solution)/shard_map/slice | solution.py:107
  107.8 0.4 fusion.32
  108.3 0.4 fusion.30
  108.7 0.4 fusion.38
  109.2 0.4 fusion.24
  109.6 0.4 fusion.22
  110.1 0.2 copy-done.4
  110.3 0.4 fusion.34
  110.7 1.4 convolution_add_fusion.7
  112.2 1.4 convolution_add_fusion.5
  113.6 1.4 convolution_add_fusion.9
  115.1 1.4 fusion.17
  116.5 1.4 fusion.18
  118.0 1.6 multiply_convert_fusion.1
  119.6 0.3 fusion.57
  120.0 0.3 broadcast_in_dim.39
  120.3 0.4 fusion.6
  120.7 1.3 fusion.63
  122.0 1.4 fusion.64
  123.5 0.3 fusion.65
  123.8 1.4 fusion.8
  125.2 1.4 fusion.10
  126.5 0.4 fusion.12
  126.9 1.5 copy-done.1
  128.5 2.9 %convolution_convert_fusion = bf16[192,4096]{1,0:T(8,128)(2,1)S(1)} fusion(f32[304]{0:T(512)S(1)} %reshape.119, f32[304,192]{0,1:T(8,128)S(1)} %fusion.17, f32[304,192]{0,1:T(8,128)} %copy-done.7, bf16[2,304,4096]{2,1,0:T(8,128)(2,1)} %all-gather.2.cloned.1.call-done), kind=kOutput, calls=%fused_computation | convolution fusion | flops 483022848 | bytes 4592832 | tf_op jit(solution)/shard_map/dot_general | solution.py:43
  131.4 1.2 reshape.55
  132.6 3.3 %constant_dynamic-slice_fusion.2 = (bf16[192,1,1024]{2,1,0:T(2,128)(2,1)S(1)}, bf16[192,1,1024]{2,1,0:T(2,128)(2,1)S(1)}, bf16[192,1,1024]{2,1,0:T(2,128)(2,1)S(1)}, bf16[192,1,1024]{2,1,0:T(2,128)(2,1)S(1)}) fusion(bf16[192,4,1024]{2,1,0:T(4,128)(2,1)S(1)} %reshape.55, s32[]{:T(128)S(6)} %select_n.100, s32[]{:T(128)S(6)} %select_n.104, s32[]{:T(128)S(6)} %select_n.102, ...), kind=kLoop, calls=%fused_computation.114 | loop fusion | bytes 3145744 | tf_op jit(solution)/shard_map/jit(_take) | solution.py:62
  135.9 0.2 fusion.55
  136.0 3.1 %collective-permute-start.3 = (bf16[192,1024]{1,0:T(8,128)(2,1)S(1)}, bf16[192,1024]{1,0:T(8,128)(2,1)S(1)}, u32[]{:S(2)}, u32[]{:S(2)}) collective-permute-start(bf16[192,1024]{1,0:T(8,128)(2,1)S(1)} %fusion.55), channel_id=1, source_target_pairs={{0,128},{128,256},{256,384},{384,0},{1,129},{129,257},{257,385},{3... | collective-permute-start | bytes 1179656 | tf_op jit(solution)/shard_map/ppermute | solution.py:65
  139.1 0.2 fusion.54
  139.3 4.3 %collective-permute-start.4 = (bf16[192,1024]{1,0:T(8,128)(2,1)S(1)}, bf16[192,1024]{1,0:T(8,128)(2,1)S(1)}, u32[]{:S(2)}, u32[]{:S(2)}) collective-permute-start(bf16[192,1024]{1,0:T(8,128)(2,1)S(1)} %fusion.54), channel_id=1, source_target_pairs={{0,256},{128,384},{256,0},{384,128},{1,257},{129,385},{257,1},{385... | collective-permute-start | bytes 1179656 | tf_op jit(solution)/shard_map/ppermute | solution.py:65
  143.6 0.9 fusion.53
  144.5 3.1 %collective-permute-start.5 = (bf16[192,1024]{1,0:T(8,128)(2,1)}, bf16[192,1024]{1,0:T(8,128)(2,1)S(1)}, u32[]{:S(2)}, u32[]{:S(2)}) collective-permute-start(bf16[192,1024]{1,0:T(8,128)(2,1)} %fusion.53), channel_id=1, source_target_pairs={{0,384},{128,0},{256,128},{384,256},{1,385},{129,1},{257,129},{385... | collective-permute-start | bytes 1179656 | tf_op jit(solution)/shard_map/ppermute | solution.py:65
  147.6 21.8 %reduce-scatter.2.cloned.1.call-done = bf16[304,512]{1,0:T(8,128)(2,1)} async-done(((bf16[304,4096]{1,0:T(8,128)(2,1)}), bf16[304,512]{1,0:T(8,128)(2,1)}) %reduce-scatter.2.cloned.1.call-update) | async-done | bytes 311312 | tf_op jit(solution)/shard_map/reduce_scatter | solution.py:111
  169.4 1.8 reshape.53
  171.2 12.1 %all-to-all-start.1 = ((bf16[16,19,512]{2,1,0:T(8,128)(2,1)}), bf16[16,19,512]{2,1,0:T(8,128)(2,1)S(1)}, u32[]{:S(2)}, u32[]{:S(2)}) async-start(bf16[16,19,512]{2,1,0:T(8,128)(2,1)} %reshape.53), calls=%async_computation.2 | async-start | bytes 786432 | tf_op jit(solution)/shard_map/all_to_all | solution.py:112
  183.4 1.1 fusion.52
  184.5 13.4 %all-to-all-done.1 = bf16[16,19,512]{2,1,0:T(8,128)(2,1)S(1)} async-done(((bf16[16,19,512]{2,1,0:T(8,128)(2,1)}), bf16[16,19,512]{2,1,0:T(8,128)(2,1)S(1)}, u32[]{:S(2)}, u32[]{:S(2)}) %all-to-all-start.1) | async-done | bytes 311328 | tf_op jit(solution)/shard_map/all_to_all | solution.py:112
  197.9 0.1 reshape.54
  198.0 0.9 convolution_convert_fusion.3
  (28 shorter events, 0.2 us)
Async XLA Ops:
  7.2 1.6 copy-start
  7.2 2.1 %copy-start.8 = (bf16[152,512]{1,0:T(8,128)(2,1)S(1)}, bf16[152,512]{1,0:T(8,128)(2,1)}, u32[]{:S(2)}) copy-start(bf16[152,512]{1,0:T(8,128)(2,1)} %param.11) | copy-start | bytes 466948
  7.2 97.9 %all-gather.2.cloned.1.call-start = ((), (), s32[]{:S(2)}) async-start(), calls=%async_computation.3 | async-start | bytes 5603328 | tf_op jit(solution)/shard_map/all_gather | solution.py:105
  8.1 1.5 copy-start.9
  42.8 1.2 copy-start.2
  42.8 1.2 copy-start.3
  42.8 1.4 copy-start.6
  43.9 125.5 %reduce-scatter.2.cloned.1.call-start = ((), (), s32[]{:S(2)}) async-start(), calls=%async_computation.4 | async-start | bytes 2801664 | tf_op jit(solution)/shard_map/reduce_scatter | solution.py:111
  45.4 65.3 %collective-permute-start = (bf16[3,1024,192]{1,2,0:T(8,128)(2,1)}, bf16[3,1024,192]{1,2,0:T(8,128)(2,1)}, u32[]{:S(2)}, u32[]{:S(2)}) collective-permute-start(bf16[3,1024,192]{1,2,0:T(8,128)(2,1)} %pad_maximum_fusion), channel_id=1, source_target_pairs={{0,128},{128,256},{256,384},{384,0},{1,129},{129,257},{257,385},{3... | collective-permute-start | bytes 3538952 | tf_op jit(solution)/shard_map/ppermute | solution.py:53
  48.6 60.6 %collective-permute-start.2 = (bf16[3,1024,192]{1,2,0:T(8,128)(2,1)}, bf16[3,1024,192]{1,2,0:T(8,128)(2,1)S(1)}, u32[]{:S(2)}, u32[]{:S(2)}) collective-permute-start(bf16[3,1024,192]{1,2,0:T(8,128)(2,1)} %pad_maximum_fusion), channel_id=1, source_target_pairs={{0,384},{128,0},{256,128},{384,256},{1,385},{129,1},{257,129},{385... | collective-permute-start | bytes 3538952 | tf_op jit(solution)/shard_map/ppermute | solution.py:53
  52.0 63.1 %collective-permute-start.1 = (bf16[3,1024,192]{1,2,0:T(8,128)(2,1)}, bf16[3,1024,192]{1,2,0:T(8,128)(2,1)}, u32[]{:S(2)}, u32[]{:S(2)}) collective-permute-start(bf16[3,1024,192]{1,2,0:T(8,128)(2,1)} %pad_maximum_fusion), channel_id=1, source_target_pairs={{0,256},{128,384},{256,0},{384,128},{1,257},{129,385},{257,1},{385... | collective-permute-start | bytes 3538952 | tf_op jit(solution)/shard_map/ppermute | solution.py:53
  109.2 1.1 copy-start.4
  118.0 2.0 copy-start.7
  122.0 1.5 copy-start.5
  126.9 1.5 copy-start.1
  136.0 47.3 %collective-permute-start.3 = (bf16[192,1024]{1,0:T(8,128)(2,1)S(1)}, bf16[192,1024]{1,0:T(8,128)(2,1)S(1)}, u32[]{:S(2)}, u32[]{:S(2)}) collective-permute-start(bf16[192,1024]{1,0:T(8,128)(2,1)S(1)} %fusion.55), channel_id=1, source_target_pairs={{0,128},{128,256},{256,384},{384,0},{1,129},{129,257},{257,385},{3... | collective-permute-start | bytes 1179656 | tf_op jit(solution)/shard_map/ppermute | solution.py:65
  139.3 44.0 %collective-permute-start.4 = (bf16[192,1024]{1,0:T(8,128)(2,1)S(1)}, bf16[192,1024]{1,0:T(8,128)(2,1)S(1)}, u32[]{:S(2)}, u32[]{:S(2)}) collective-permute-start(bf16[192,1024]{1,0:T(8,128)(2,1)S(1)} %fusion.54), channel_id=1, source_target_pairs={{0,256},{128,384},{256,0},{384,128},{1,257},{129,385},{257,1},{385... | collective-permute-start | bytes 1179656 | tf_op jit(solution)/shard_map/ppermute | solution.py:65
  144.5 38.8 %collective-permute-start.5 = (bf16[192,1024]{1,0:T(8,128)(2,1)}, bf16[192,1024]{1,0:T(8,128)(2,1)S(1)}, u32[]{:S(2)}, u32[]{:S(2)}) collective-permute-start(bf16[192,1024]{1,0:T(8,128)(2,1)} %fusion.53), channel_id=1, source_target_pairs={{0,384},{128,0},{256,128},{384,256},{1,385},{129,1},{257,129},{385... | collective-permute-start | bytes 1179656 | tf_op jit(solution)/shard_map/ppermute | solution.py:65
  171.2 26.7 %all-to-all-start.1 = ((bf16[16,19,512]{2,1,0:T(8,128)(2,1)}), bf16[16,19,512]{2,1,0:T(8,128)(2,1)S(1)}, u32[]{:S(2)}, u32[]{:S(2)}) async-start(bf16[16,19,512]{2,1,0:T(8,128)(2,1)} %reshape.53), calls=%async_computation.2 | async-start | bytes 786432 | tf_op jit(solution)/shard_map/all_to_all | solution.py:112
Sparse Core Ops, SparseCore 0:
  44.0 60.9 all-gather.1
  128.5 40.8 reduce-scatter.1

commit v7 on v6

--- a/solution.py
+++ b/solution.py
@@ -1,49 +1,62 @@
 import jax
 import jax.numpy as jnp
 from jax import lax
+from jax.experimental import pallas as pl
+from jax.experimental.pallas import tpu as pltpu
 from jax.sharding import PartitionSpec as P
 
 CAP = 19
 
 
-def expert_grads(feats, grads, gate_col, pieces):
-    slots = feats.shape[0]
-    size = len(pieces)
-    quarter = pieces[0].shape[1]
-    me = lax.axis_index("dp")
-    gate_pre = 0.0
-    up_pre = 0.0
-    back = 0.0
-    for k, piece in enumerate(pieces):
-        start = ((me - k) % size) * quarter
-        f_k = lax.dynamic_slice_in_dim(feats, start, quarter, axis=1)
-        g_k = lax.dynamic_slice_in_dim(grads, start, quarter, axis=1)
-        gate_pre = gate_pre + jnp.dot(f_k, piece[0], preferred_element_type=jnp.float32)
-        up_pre = up_pre + jnp.dot(f_k, piece[1], preferred_element_type=jnp.float32)
-        back = back + jnp.dot(g_k, piece[2], preferred_element_type=jnp.float32)
+def _expert_kernel(me_ref, rows_ref, gate_ref, w0_ref, w1_ref, w2_ref, w3_ref, q_ref, term_ref):
+    size = 4
+    quarter = w0_ref.shape[1]
+    me = me_ref[0]
+    pieces = (w0_ref, w1_ref, w2_ref, w3_ref)
+    gate_pre = None
+    for k, w_ref in enumerate(pieces):
+        start = pl.multiple_of(((me + size - k) % size) * quarter, quarter)
+        f_k = rows_ref[0, :, pl.ds(start, quarter)]
+        g_k = rows_ref[1, :, pl.ds(start, quarter)]
+        a = jnp.dot(f_k, w_ref[0], preferred_element_type=jnp.float32)
+        b = jnp.dot(f_k, w_ref[1], preferred_element_type=jnp.float32)
+        c = jnp.dot(g_k, w_ref[2], preferred_element_type=jnp.float32)
+        if gate_pre is None:
+            gate_pre, up_pre, back = a, b, c
+        else:
+            gate_pre, up_pre, back = gate_pre + a, up_pre + b, back + c
     sig = jax.nn.sigmoid(gate_pre)
     act = gate_pre * sig
-    hidden_b = (act * up_pre).astype(jnp.bfloat16)
-    gate_f = gate_col.astype(jnp.float32)[:, None]
+    hidden = act * up_pre
+    gate_f = gate_ref[...].astype(jnp.float32)
     d_hidden = gate_f * back
     d_gate_b = (d_hidden * up_pre * sig * (1.0 + gate_pre * (1.0 - sig))).astype(jnp.bfloat16)
     d_up_b = (d_hidden * act).astype(jnp.bfloat16)
-    d_part = jnp.zeros((slots, size * quarter), jnp.bfloat16)
-    for k, piece in enumerate(pieces):
-        part = lax.dot_general(
-            d_gate_b, piece[0], (((1,), (1,)), ((), ())), preferred_element_type=jnp.float32
-        )
-        part = part + lax.dot_general(
-            d_up_b, piece[1], (((1,), (1,)), ((), ())), preferred_element_type=jnp.float32
-        )
-        d_part = lax.dynamic_update_slice_in_dim(
-            d_part, part.astype(jnp.bfloat16), ((me - k) % size) * quarter, axis=1
-        )
-    scaled = (gate_f * grads).astype(jnp.bfloat16)
-    term = lax.dot_general(
-        hidden_b, scaled, (((0,), (0,)), ((), ())), preferred_element_type=jnp.float32
-    )
-    return (d_part, term)
+    nt = (((1,), (1,)), ((), ()))
+    for k, w_ref in enumerate(pieces):
+        start = pl.multiple_of(((me + size - k) % size) * quarter, quarter)
+        part = lax.dot_general(d_gate_b, w_ref[0], nt, preferred_element_type=jnp.float32)
+        part = part + lax.dot_general(d_up_b, w_ref[1], nt, preferred_element_type=jnp.float32)
+        q_ref[:, pl.ds(start, quarter)] = part.astype(jnp.bfloat16)
+    hidden_t = hidden.T.astype(jnp.bfloat16)
+    scaled = (gate_f * rows_ref[1].astype(jnp.float32)).astype(jnp.bfloat16)
+    term_ref[...] = jnp.dot(hidden_t, scaled, preferred_element_type=jnp.float32).astype(jnp.bfloat16)
+
+
+def expert_kernel(me, rows, gate_col, pieces):
+    _, slots, width = rows.shape
+    ffb = pieces[0].shape[2]
+    vmem = pltpu.VMEM
+    return pl.pallas_call(
+        _expert_kernel,
+        out_shape=(
+            jax.ShapeDtypeStruct((slots, width), jnp.bfloat16),
+            jax.ShapeDtypeStruct((ffb, width), jnp.bfloat16),
+        ),
+        in_specs=[pl.BlockSpec(memory_space=pltpu.SMEM)] + [pl.BlockSpec(memory_space=vmem)] * 6,
+        out_specs=(pl.BlockSpec(memory_space=vmem), pl.BlockSpec(memory_space=vmem)),
+        compiler_params=pltpu.CompilerParams(vmem_limit_bytes=48 * 1024 * 1024),
+    )(me.reshape(1), rows, gate_col.reshape(slots, 1), *pieces)
 
 
 def pieces_dp(piece):
@@ -103,11 +116,9 @@
         axis=0,
     )
     full = lax.all_gather(pair, "etp", axis=2, tiled=True)
-    feats = full[0]
-    grads = full[1]
     stack = jnp.stack([gate_w[0], up_w[0], down_w[0].T], axis=0)
-    d_part_b, term = expert_grads(feats, grads, recv_gate, pieces_dp(stack))
-    down_grad = scatter_sum_dp(term.astype(jnp.bfloat16))[None]
+    d_part_b, term_b = expert_kernel(lax.axis_index("dp"), full, recv_gate, pieces_dp(stack))
+    down_grad = scatter_sum_dp(term_b)[None]
     summed = lax.psum_scatter(d_part_b, "etp", scatter_dimension=1, tiled=True)
     returned = lax.all_to_all(
         summed.reshape(width, CAP, narrow), "expert", split_axis=0, concat_axis=0, tiled=True

time: 207 us -> 197 us (0.952)
  matrix products: 22.8 us -> 1.5 us
  Pallas kernels: 0 us -> 9.61 us
  local copies, waits for them, and re-layouts: 12.5 us -> 21.2 us
  waiting for transfers between devices: 84.5 us -> 80.2 us
    all_gather x1, waiting for transfers between devices: 49.2 us -> 0.02 us  [local(): full = lax.all_gather(pair, 'etp', axis=2, tiled=True)]
    ppermute x3, waiting for transfers between devices: 0.01 us -> 45 us  [pieces_dp(): lax.ppermute(piece, 'dp', [(i, (i + shift) % size) for i in range(size)])]
    dot_general x21 -> x0, matrix products: 21.3 us -> none  [the longest x4 3.96 us: expert_grads(): back = back + jnp.dot(g_k, piece[2], preferred_element_type=jnp.float32)]
    pallas_call x0 -> x1, Pallas kernels: none -> 9.61 us  [expert_kernel(): pl.pallas_call(_expert_kernel, out_shape=(jax.ShapeDtypeStruct((slots, wi...]
    ppermute x0 -> x3, local copies, waits for them, and re-layouts: none -> 6.73 us  [pieces_dp(): lax.ppermute(piece, 'dp', [(i, (i + shift) % size) for i in range(size)])]
  transfers between devices with their start and end apart: 9 -> 9, of which waited for: 3 -> 4; matrix products, arithmetic and copies ran while one was open for 11% -> 10% of each run, Pallas kernels for 0% -> 0%
where the time goes in v7:
time: 197 us; the launch traced here: 196 us
  waiting for transfers between devices  80.2 us (41%)
  blocking collectives  31.9 us (16%)
  starting transfers between devices  31.6 us (16%)
  local copies, waits for them, and re-layouts  21.2 us (11%)
  between operations  14.4 us (7%)
  Pallas kernels  9.61 us (5%)
  other arithmetic  5.73 us (3%)
    ppermute x3, waiting for transfers between devices, pieces_dp(): lax.ppermute(piece, 'dp', [(i, (i + shift) % size) for i in range(size)])  45 us
    all_to_all x1, blocking collectives, local(): lax.all_to_all(block, 'expert', split_axis=0, concat_axis=0, tiled=True)  31.9 us
    reduce_scatter x1, waiting for transfers between devices, local(): summed = lax.psum_scatter(d_part_b, 'etp', scatter_dimension=1, tiled=True)  21.8 us
    all_to_all x1, waiting for transfers between devices, local(): lax.all_to_all(summed.reshape(width, CAP, narrow), 'expert', split_axis=0...  13.4 us
    all_to_all x1, starting transfers between devices, local(): lax.all_to_all(summed.reshape(width, CAP, narrow), 'expert', split_axis=0...  12 us
    ppermute x3, starting transfers between devices, pieces_dp(): lax.ppermute(piece, 'dp', [(i, (i + shift) % size) for i in range(size)])  10.7 us
    pallas_call x1, Pallas kernels, expert_kernel(): pl.pallas_call(_expert_kernel, out_shape=(jax.ShapeDtypeStruct((slots, wi...  9.61 us
    ppermute x3, starting transfers between devices, scatter_sum_dp(): lax.ppermute(outgoing, 'dp', [(i, (i + shift) % size) for i in range(size)])  8.79 us
  transfers between devices with their start and end apart: 9, of which 4 were waited for; matrix products, arithmetic and copies ran while one was open for 10% of the time, Pallas kernels for 0%

profile of v7, /device:TPU:1, one launch (start us, length us, event | category | flops | bytes accessed | tf_op | source)
XLA Modules:
  0.0 196.2 jit_solution(11294993011499444306)
XLA Ops:
  7.2 0.0 copy-start
  7.2 0.0 all-gather.2.cloned.1.call-start
  7.2 0.8 add_select_fusion
  8.0 0.1 copy.61
  8.1 0.7 fusion
  8.8 0.8 copy.62
  9.6 0.4 select_reduce_fusion
  10.0 0.1 convert_element_type.54
  10.1 0.3 convolution_convert_fusion
  10.4 0.1 reshape.39
  10.5 0.3 convolution_convert_fusion.1
  10.8 0.1 reshape.38
  11.0 0.1 pad.15.clone
  11.0 0.3 fusion.5
  11.3 31.9 %all_to_all.10 = bf16[16,40,512]{2,1,0:T(8,128)(2,1)S(1)} all-to-all(bf16[16,40,512]{2,1,0:T(8,128)(2,1)S(1)} %fusion.5), channel_id=1, replica_groups=mesh['dp'=4,'expert'=16,'etp'=8] {'expert'}, dimensions={0} | all-to-all | bytes 1310720 | tf_op jit(solution)/shard_map/all_to_all | solution.py:109
  43.2 0.9 copy-done.3
  44.0 0.1 fusion.11
  44.2 0.0 copy-start.4
  44.2 0.1 stack_reshape.7
  44.3 0.0 copy-start.5
  44.3 0.1 stack_reshape.6
  44.4 0.0 copy-start.6
  44.4 0.9 pad_maximum_fusion.1
  45.3 0.0 all-gather.2.cloned.1.call-update
  45.3 0.0 reduce-scatter.2.cloned.1.call-start
  45.4 0.2 copy.64
  45.6 0.2 copy.66
  45.8 0.2 copy.65
  46.0 0.4 pad_maximum_fusion.w0_ref
  46.4 1.6 copy.67
  48.0 3.1 %collective-permute-start = (bf16[3,1024,192]{1,2,0:T(8,128)(2,1)}, bf16[3,1024,192]{1,2,0:T(8,128)(2,1)}, u32[]{:S(2)}, u32[]{:S(2)}) collective-permute-start(bf16[3,1024,192]{1,2,0:T(8,128)(2,1)} %copy.67), channel_id=1, source_target_pairs={{0,128},{128,256},{256,384},{384,0},{1,129},{129,257},{257,385},{3... | collective-permute-start | bytes 3538952 | tf_op jit(solution)/shard_map/ppermute | solution.py:66
  51.1 4.4 %collective-permute-start.1 = (bf16[3,1024,192]{1,2,0:T(8,128)(2,1)}, bf16[3,1024,192]{1,2,0:T(8,128)(2,1)}, u32[]{:S(2)}, u32[]{:S(2)}) collective-permute-start(bf16[3,1024,192]{1,2,0:T(8,128)(2,1)} %copy.67), channel_id=1, source_target_pairs={{0,256},{128,384},{256,0},{384,128},{1,257},{129,385},{257,1},{385... | collective-permute-start | bytes 3538952 | tf_op jit(solution)/shard_map/ppermute | solution.py:66
  55.5 3.2 %collective-permute-start.2 = (bf16[3,1024,192]{1,2,0:T(8,128)(2,1)}, bf16[3,1024,192]{1,2,0:T(8,128)(2,1)}, u32[]{:S(2)}, u32[]{:S(2)}) collective-permute-start(bf16[3,1024,192]{1,2,0:T(8,128)(2,1)} %copy.67), channel_id=1, source_target_pairs={{0,384},{128,0},{256,128},{384,256},{1,385},{129,1},{257,129},{385... | collective-permute-start | bytes 3538952 | tf_op jit(solution)/shard_map/ppermute | solution.py:66
  58.7 20.4 %collective-permute-done = bf16[3,1024,192]{1,2,0:T(8,128)(2,1)} collective-permute-done((bf16[3,1024,192]{1,2,0:T(8,128)(2,1)}, bf16[3,1024,192]{1,2,0:T(8,128)(2,1)}, u32[]{:S(2)}, u32[]{:S(2)}) %collective-permute-start) | collective-permute-done | bytes 1179680 | tf_op jit(solution)/shard_map/ppermute | solution.py:66
  79.1 1.6 copy.71.w1_ref
  80.7 24.6 %collective-permute-done.1 = bf16[3,1024,192]{1,2,0:T(8,128)(2,1)} collective-permute-done((bf16[3,1024,192]{1,2,0:T(8,128)(2,1)}, bf16[3,1024,192]{1,2,0:T(8,128)(2,1)}, u32[]{:S(2)}, u32[]{:S(2)}) %collective-permute-start.1) | collective-permute-done | bytes 1179680 | tf_op jit(solution)/shard_map/ppermute | solution.py:66
  105.4 2.6 %copy.72.w2_ref = bf16[3,1024,192]{2,1,0:T(8,128)(2,1)} copy(bf16[3,1024,192]{1,2,0:T(8,128)(2,1)} %collective-permute-done.1) | data formatting | bytes 2359296 | tf_op jit(solution)/shard_map/ppermute | solution.py:66
  107.9 0.0 collective-permute-done.2
  108.0 2.5 %copy.73.w3_ref = bf16[3,1024,192]{2,1,0:T(8,128)(2,1)} copy(bf16[3,1024,192]{1,2,0:T(8,128)(2,1)} %collective-permute-done.2) | data formatting | bytes 2359296 | tf_op jit(solution)/shard_map/ppermute | solution.py:66
  110.5 0.8 slice_reduce_fusion
  111.3 0.1 reshape_reshape_squeeze.4.gate_ref
  111.4 0.0 all-gather.2.cloned.1.call-done.rows_ref
  111.4 9.6 %shard_map.95 = (bf16[304,4096]{1,0:T(8,128)(2,1)}, bf16[192,4096]{1,0:T(8,128)(2,1)S(1)}) custom-call(s32[1]{0:T(128)} %bitcast.me_ref, bf16[2,304,4096]{2,1,0:T(8,128)(2,1)} %all-gather.2.cloned.1.call-done.rows_ref, bf16[304,1]{1,0:T(8,128)(2,1)S(1)} %reshape_reshape_squeeze.4.gate_ref, bf16[3,1024,192]{2,1,0:T(8,128)(2,1)S(1)} %pad_maximum_fusion.w0_ref, ...), custom_call_target="tpu_custom_call" | custom-call | tf_op jit(solution)/shard_map/pallas_call | solution.py:50
  121.0 1.2 copy-done.1
  122.2 0.0 reduce-scatter.2.cloned.1.call-update
  122.3 1.3 copy-done.2
  123.6 1.2 reshape.42
  124.8 3.3 %constant_dynamic-slice_fusion.3 = (bf16[192,1,1024]{2,1,0:T(2,128)(2,1)S(1)}, bf16[192,1,1024]{2,1,0:T(2,128)(2,1)S(1)}, bf16[192,1,1024]{2,1,0:T(2,128)(2,1)S(1)}, bf16[192,1,1024]{2,1,0:T(2,128)(2,1)S(1)}) fusion(bf16[192,4,1024]{2,1,0:T(4,128)(2,1)S(1)} %reshape.42, s32[]{:T(128)S(6)} %select_n.48, s32[]{:T(128)S(6)} %select_n.52, s32[]{:T(128)S(6)} %select_n.50, ...), kind=kLoop, calls=%fused_computation.30 | loop fusion | bytes 3145744 | tf_op jit(solution)/shard_map/jit(_take) | solution.py:75
  128.1 0.2 fusion.7
  128.3 3.4 %collective-permute-start.5 = (bf16[192,1024]{1,0:T(8,128)(2,1)S(1)}, bf16[192,1024]{1,0:T(8,128)(2,1)S(1)}, u32[]{:S(2)}, u32[]{:S(2)}) collective-permute-start(bf16[192,1024]{1,0:T(8,128)(2,1)S(1)} %fusion.7), channel_id=1, source_target_pairs={{0,384},{128,0},{256,128},{384,256},{1,385},{129,1},{257,129},{385... | collective-permute-start | bytes 1179656 | tf_op jit(solution)/shard_map/ppermute | solution.py:78
  131.7 0.2 fusion.8
  131.9 3.4 %collective-permute-start.4 = (bf16[192,1024]{1,0:T(8,128)(2,1)S(1)}, bf16[192,1024]{1,0:T(8,128)(2,1)S(1)}, u32[]{:S(2)}, u32[]{:S(2)}) collective-permute-start(bf16[192,1024]{1,0:T(8,128)(2,1)S(1)} %fusion.8), channel_id=1, source_target_pairs={{0,256},{128,384},{256,0},{384,128},{1,257},{129,385},{257,1},{385... | collective-permute-start | bytes 1179656 | tf_op jit(solution)/shard_map/ppermute | solution.py:78
  135.3 0.9 fusion.9
  136.2 1.9 collective-permute-start.3
  138.1 21.8 %reduce-scatter.2.cloned.1.call-done = bf16[304,512]{1,0:T(8,128)(2,1)} async-done(((bf16[304,4096]{1,0:T(8,128)(2,1)}), bf16[304,512]{1,0:T(8,128)(2,1)}) %reduce-scatter.2.cloned.1.call-update) | async-done | bytes 311312 | tf_op jit(solution)/shard_map/reduce_scatter | solution.py:122
  159.9 1.8 reshape.40
  161.7 12.0 %all-to-all-start.1 = ((bf16[16,19,512]{2,1,0:T(8,128)(2,1)}), bf16[16,19,512]{2,1,0:T(8,128)(2,1)S(1)}, u32[]{:S(2)}, u32[]{:S(2)}) async-start(bf16[16,19,512]{2,1,0:T(8,128)(2,1)} %reshape.40), calls=%async_computation.2 | async-start | bytes 786432 | tf_op jit(solution)/shard_map/all_to_all | solution.py:123
  173.8 0.0 collective-permute-done.5
  173.8 0.0 collective-permute-done.4
  173.8 0.0 collective-permute-done.3
  173.8 1.1 fusion.6
  174.9 13.4 %all-to-all-done.1 = bf16[16,19,512]{2,1,0:T(8,128)(2,1)S(1)} async-done(((bf16[16,19,512]{2,1,0:T(8,128)(2,1)}), bf16[16,19,512]{2,1,0:T(8,128)(2,1)S(1)}, u32[]{:S(2)}, u32[]{:S(2)}) %all-to-all-start.1) | async-done | bytes 311328 | tf_op jit(solution)/shard_map/all_to_all | solution.py:123
  188.3 0.1 reshape.41
  188.5 0.9 convolution_convert_fusion.2
  (9 shorter events, 0.0 us)
Async XLA Ops:
  7.2 2.9 %copy-start = (bf16[152,512]{1,0:T(8,128)(2,1)S(1)}, bf16[152,512]{1,0:T(8,128)(2,1)}, u32[]{:S(2)}) copy-start(bf16[152,512]{1,0:T(8,128)(2,1)} %param.11) | copy-start | bytes 466948
  7.2 3.4 %copy-start.7 = (bf16[152,512]{1,0:T(8,128)(2,1)S(1)}, bf16[152,512]{1,0:T(8,128)(2,1)}, u32[]{:S(2)}) copy-start(bf16[152,512]{1,0:T(8,128)(2,1)} %param.10) | copy-start | bytes 466948
  7.2 104.2 %all-gather.2.cloned.1.call-start = ((), (), s32[]{:S(2)}) async-start(), calls=%async_computation.3 | async-start | bytes 5603328 | tf_op jit(solution)/shard_map/all_gather | solution.py:118
  43.2 0.9 copy-start.3
  44.2 1.2 copy-start.4
  44.3 1.3 copy-start.5
  44.4 1.4 copy-start.6
  45.3 114.6 %reduce-scatter.2.cloned.1.call-start = ((), (), s32[]{:S(2)}) async-start(), calls=%async_computation.4 | async-start | bytes 2801664 | tf_op jit(solution)/shard_map/reduce_scatter | solution.py:122
  48.0 31.1 %collective-permute-start = (bf16[3,1024,192]{1,2,0:T(8,128)(2,1)}, bf16[3,1024,192]{1,2,0:T(8,128)(2,1)}, u32[]{:S(2)}, u32[]{:S(2)}) collective-permute-start(bf16[3,1024,192]{1,2,0:T(8,128)(2,1)} %copy.67), channel_id=1, source_target_pairs={{0,128},{128,256},{256,384},{384,0},{1,129},{129,257},{257,385},{3... | collective-permute-start | bytes 3538952 | tf_op jit(solution)/shard_map/ppermute | solution.py:66
  51.1 54.3 %collective-permute-start.1 = (bf16[3,1024,192]{1,2,0:T(8,128)(2,1)}, bf16[3,1024,192]{1,2,0:T(8,128)(2,1)}, u32[]{:S(2)}, u32[]{:S(2)}) collective-permute-start(bf16[3,1024,192]{1,2,0:T(8,128)(2,1)} %copy.67), channel_id=1, source_target_pairs={{0,256},{128,384},{256,0},{384,128},{1,257},{129,385},{257,1},{385... | collective-permute-start | bytes 3538952 | tf_op jit(solution)/shard_map/ppermute | solution.py:66
  55.5 52.5 %collective-permute-start.2 = (bf16[3,1024,192]{1,2,0:T(8,128)(2,1)}, bf16[3,1024,192]{1,2,0:T(8,128)(2,1)}, u32[]{:S(2)}, u32[]{:S(2)}) collective-permute-start(bf16[3,1024,192]{1,2,0:T(8,128)(2,1)} %copy.67), channel_id=1, source_target_pairs={{0,384},{128,0},{256,128},{384,256},{1,385},{129,1},{257,129},{385... | collective-permute-start | bytes 3538952 | tf_op jit(solution)/shard_map/ppermute | solution.py:66
  121.0 1.2 copy-start.1
  122.2 1.4 copy-start.2
  128.3 45.5 %collective-permute-start.5 = (bf16[192,1024]{1,0:T(8,128)(2,1)S(1)}, bf16[192,1024]{1,0:T(8,128)(2,1)S(1)}, u32[]{:S(2)}, u32[]{:S(2)}) collective-permute-start(bf16[192,1024]{1,0:T(8,128)(2,1)S(1)} %fusion.7), channel_id=1, source_target_pairs={{0,384},{128,0},{256,128},{384,256},{1,385},{129,1},{257,129},{385... | collective-permute-start | bytes 1179656 | tf_op jit(solution)/shard_map/ppermute | solution.py:78
  131.9 41.9 %collective-permute-start.4 = (bf16[192,1024]{1,0:T(8,128)(2,1)S(1)}, bf16[192,1024]{1,0:T(8,128)(2,1)S(1)}, u32[]{:S(2)}, u32[]{:S(2)}) collective-permute-start(bf16[192,1024]{1,0:T(8,128)(2,1)S(1)} %fusion.8), channel_id=1, source_target_pairs={{0,256},{128,384},{256,0},{384,128},{1,257},{129,385},{257,1},{385... | collective-permute-start | bytes 1179656 | tf_op jit(solution)/shard_map/ppermute | solution.py:78
  136.2 37.6 %collective-permute-start.3 = (bf16[192,1024]{1,0:T(8,128)(2,1)}, bf16[192,1024]{1,0:T(8,128)(2,1)S(1)}, u32[]{:S(2)}, u32[]{:S(2)}) collective-permute-start(bf16[192,1024]{1,0:T(8,128)(2,1)} %fusion.9), channel_id=1, source_target_pairs={{0,128},{128,256},{256,384},{384,0},{1,129},{129,257},{257,385},{3... | collective-permute-start | bytes 1179656 | tf_op jit(solution)/shard_map/ppermute | solution.py:78
  161.7 26.6 %all-to-all-start.1 = ((bf16[16,19,512]{2,1,0:T(8,128)(2,1)}), bf16[16,19,512]{2,1,0:T(8,128)(2,1)S(1)}, u32[]{:S(2)}, u32[]{:S(2)}) async-start(bf16[16,19,512]{2,1,0:T(8,128)(2,1)} %reshape.40), calls=%async_computation.2 | async-start | bytes 786432 | tf_op jit(solution)/shard_map/all_to_all | solution.py:123
Sparse Core Ops, SparseCore 0:
  45.5 60.9 all-gather.1
  122.3 37.5 reduce-scatter.1

commit v8 on v7

--- a/solution.py
+++ b/solution.py
@@ -8,19 +8,21 @@
 CAP = 19
 
 
-def _expert_kernel(me_ref, rows_ref, gate_ref, w0_ref, w1_ref, w2_ref, w3_ref, q_ref, term_ref):
-    size = 4
-    quarter = w0_ref.shape[1]
+def _expert_kernel(me_ref, rows_ref, gate_ref, *refs):
+    size = len(refs) - 2
+    w_refs = refs[:size]
+    q_ref, term_ref = refs[size:]
+    quarter = w_refs[0].shape[2]
     me = me_ref[0]
-    pieces = (w0_ref, w1_ref, w2_ref, w3_ref)
+    nt = (((1,), (1,)), ((), ()))
     gate_pre = None
-    for k, w_ref in enumerate(pieces):
+    for k in range(size):
         start = pl.multiple_of(((me + size - k) % size) * quarter, quarter)
         f_k = rows_ref[0, :, pl.ds(start, quarter)]
         g_k = rows_ref[1, :, pl.ds(start, quarter)]
-        a = jnp.dot(f_k, w_ref[0], preferred_element_type=jnp.float32)
-        b = jnp.dot(f_k, w_ref[1], preferred_element_type=jnp.float32)
-        c = jnp.dot(g_k, w_ref[2], preferred_element_type=jnp.float32)
+        a = lax.dot_general(f_k, w_refs[k][0], nt, preferred_element_type=jnp.float32)
+        b = lax.dot_general(f_k, w_refs[k][1], nt, preferred_element_type=jnp.float32)
+        c = lax.dot_general(g_k, w_refs[k][2], nt, preferred_element_type=jnp.float32)
         if gate_pre is None:
             gate_pre, up_pre, back = a, b, c
         else:
@@ -32,20 +34,21 @@
     d_hidden = gate_f * back
     d_gate_b = (d_hidden * up_pre * sig * (1.0 + gate_pre * (1.0 - sig))).astype(jnp.bfloat16)
     d_up_b = (d_hidden * act).astype(jnp.bfloat16)
-    nt = (((1,), (1,)), ((), ()))
-    for k, w_ref in enumerate(pieces):
+    for k in range(size):
         start = pl.multiple_of(((me + size - k) % size) * quarter, quarter)
-        part = lax.dot_general(d_gate_b, w_ref[0], nt, preferred_element_type=jnp.float32)
-        part = part + lax.dot_general(d_up_b, w_ref[1], nt, preferred_element_type=jnp.float32)
+        part = jnp.dot(d_gate_b, w_refs[k][0], preferred_element_type=jnp.float32)
+        part = part + jnp.dot(d_up_b, w_refs[k][1], preferred_element_type=jnp.float32)
         q_ref[:, pl.ds(start, quarter)] = part.astype(jnp.bfloat16)
     hidden_t = hidden.T.astype(jnp.bfloat16)
     scaled = (gate_f * rows_ref[1].astype(jnp.float32)).astype(jnp.bfloat16)
-    term_ref[...] = jnp.dot(hidden_t, scaled, preferred_element_type=jnp.float32).astype(jnp.bfloat16)
+    term_ref[...] = jnp.dot(hidden_t, scaled, preferred_element_type=jnp.float32).astype(
+        jnp.bfloat16
+    )
 
 
 def expert_kernel(me, rows, gate_col, pieces):
     _, slots, width = rows.shape
-    ffb = pieces[0].shape[2]
+    ffb = pieces[0].shape[1]
     vmem = pltpu.VMEM
     return pl.pallas_call(
         _expert_kernel,
@@ -53,7 +56,8 @@
             jax.ShapeDtypeStruct((slots, width), jnp.bfloat16),
             jax.ShapeDtypeStruct((ffb, width), jnp.bfloat16),
         ),
-        in_specs=[pl.BlockSpec(memory_space=pltpu.SMEM)] + [pl.BlockSpec(memory_space=vmem)] * 6,
+        in_specs=[pl.BlockSpec(memory_space=pltpu.SMEM)]
+        + [pl.BlockSpec(memory_space=vmem)] * (2 + len(pieces)),
         out_specs=(pl.BlockSpec(memory_space=vmem), pl.BlockSpec(memory_space=vmem)),
         compiler_params=pltpu.CompilerParams(vmem_limit_bytes=48 * 1024 * 1024),
     )(me.reshape(1), rows, gate_col.reshape(slots, 1), *pieces)
@@ -116,7 +120,7 @@
         axis=0,
     )
     full = lax.all_gather(pair, "etp", axis=2, tiled=True)
-    stack = jnp.stack([gate_w[0], up_w[0], down_w[0].T], axis=0)
+    stack = jnp.stack([gate_w[0].T, up_w[0].T, down_w[0]], axis=0)
     d_part_b, term_b = expert_kernel(lax.axis_index("dp"), full, recv_gate, pieces_dp(stack))
     down_grad = scatter_sum_dp(term_b)[None]
     summed = lax.psum_scatter(d_part_b, "etp", scatter_dimension=1, tiled=True)

time: 197 us -> 193 us (0.980)
  local copies, waits for them, and re-layouts: 21.2 us -> 9.85 us
  waiting for transfers between devices: 80.2 us -> 88 us
    ppermute x3 -> x0, local copies, waits for them, and re-layouts: 6.73 us -> none  [pieces_dp(): lax.ppermute(piece, 'dp', [(i, (i + shift) % size) for i in range(size)])]
    reduce_scatter x1, waiting for transfers between devices: 21.8 us -> 24.7 us  [local(): summed = lax.psum_scatter(d_part_b, 'etp', scatter_dimension=1, tiled=True)]
    ppermute x3, waiting for transfers between devices: 45 us -> 47.8 us  [pieces_dp(): lax.ppermute(piece, 'dp', [(i, (i + shift) % size) for i in range(size)])]
    unnamed x19 -> x12, local copies, waits for them, and re-layouts: 3.99 us -> 1.67 us
    all_gather x1, waiting for transfers between devices: 0.02 us -> 2.04 us  [local(): full = lax.all_gather(pair, 'etp', axis=2, tiled=True)]
  transfers between devices with their start and end apart: 9 -> 9, of which waited for: 4 -> 6; matrix products, arithmetic and copies ran while one was open for 10% -> 5% of each run, Pallas kernels for 0% -> 0%
where the time goes in v8:
time: 193 us
  waiting for transfers between devices  88 us (46%)
  starting transfers between devices  31.9 us (17%)
  blocking collectives  31.9 us (17%)
  between operations  14.4 us (7%)
  Pallas kernels  9.91 us (5%)
  local copies, waits for them, and re-layouts  9.85 us (5%)
  other arithmetic  5.52 us (3%)
    ppermute x3, waiting for transfers between devices, pieces_dp(): lax.ppermute(piece, 'dp', [(i, (i + shift) % size) for i in range(size)])  47.8 us
    all_to_all x1, blocking collectives, local(): lax.all_to_all(block, 'expert', split_axis=0, concat_axis=0, tiled=True)  31.9 us
    reduce_scatter x1, waiting for transfers between devices, local(): summed = lax.psum_scatter(d_part_b, 'etp', scatter_dimension=1, tiled=True)  24.7 us
    all_to_all x1, waiting for transfers between devices, local(): lax.all_to_all(summed.reshape(width, CAP, narrow), 'expert', split_axis=0...  13.4 us
    all_to_all x1, starting transfers between devices, local(): lax.all_to_all(summed.reshape(width, CAP, narrow), 'expert', split_axis=0...  12 us
    ppermute x3, starting transfers between devices, pieces_dp(): lax.ppermute(piece, 'dp', [(i, (i + shift) % size) for i in range(size)])  10.6 us
    pallas_call x1, Pallas kernels, expert_kernel(): pl.pallas_call(_expert_kernel, out_shape=(jax.ShapeDtypeStruct((slots, wi...  9.91 us
    ppermute x3, starting transfers between devices, scatter_sum_dp(): lax.ppermute(outgoing, 'dp', [(i, (i + shift) % size) for i in range(size)])  9.27 us
  transfers between devices with their start and end apart: 9, of which 6 were waited for; matrix products, arithmetic and copies ran while one was open for 5% of the time, Pallas kernels for 0%

profile of v8, /device:TPU:1, one launch (start us, length us, event | category | flops | bytes accessed | tf_op | source)
XLA Modules:
  0.0 193.0 jit_solution(10984629027569846093)
XLA Ops:
  7.2 0.0 copy-start
  7.2 0.0 copy-start.5
  7.2 0.0 all-gather.2.cloned.1.call-start
  7.2 0.8 add_select_fusion
  8.0 0.1 copy.35
  8.1 0.7 fusion
  8.8 0.8 copy.36
  9.6 0.4 select_reduce_fusion
  10.0 0.1 convert_element_type.54
  10.1 0.0 copy-done
  10.1 0.3 convolution_convert_fusion
  10.4 0.1 reshape.39
  10.5 0.0 copy-done.5
  10.5 0.3 convolution_convert_fusion.1
  10.8 0.1 reshape.38
  11.0 0.1 pad.15.clone
  11.0 0.3 fusion.5
  11.3 31.9 %all_to_all.10 = bf16[16,40,512]{2,1,0:T(8,128)(2,1)S(1)} all-to-all(bf16[16,40,512]{2,1,0:T(8,128)(2,1)S(1)} %fusion.5), channel_id=1, replica_groups=mesh['dp'=4,'expert'=16,'etp'=8] {'expert'}, dimensions={0} | all-to-all | bytes 1310720 | tf_op jit(solution)/shard_map/all_to_all | solution.py:113
  43.2 0.1 fusion.11
  43.3 0.1 stack_reshape.7
  43.4 0.0 copy-start.2
  43.4 0.0 copy-start.3
  43.5 0.0 copy-start.4
  43.5 0.1 stack_reshape.6
  43.6 0.9 pad_maximum_fusion.1
  44.5 0.0 all-gather.2.cloned.1.call-update
  44.5 0.0 reduce-scatter.2.cloned.1.call-start
  44.6 0.0 copy-done.2
  44.6 0.0 copy-done.3
  44.6 0.3 copy-done.4
  44.9 0.1 pad_maximum_fusion.refs_0_
  45.0 3.1 %collective-permute-start = (bf16[3,192,1024]{2,1,0:T(8,128)(2,1)S(1)}, bf16[3,192,1024]{2,1,0:T(8,128)(2,1)S(1)}, u32[]{:S(2)}, u32[]{:S(2)}) collective-permute-start(bf16[3,192,1024]{2,1,0:T(8,128)(2,1)S(1)} %pad_maximum_fusion.refs_0_), channel_id=1, source_target_pairs={{0,128},{128,256},{256,384},{384,0},{1,129},{129,257},{257,385},{3... | collective-permute-start | bytes 3538952 | tf_op jit(solution)/shard_map/ppermute | solution.py:70
  48.2 4.4 %collective-permute-start.1 = (bf16[3,192,1024]{2,1,0:T(8,128)(2,1)S(1)}, bf16[3,192,1024]{2,1,0:T(8,128)(2,1)}, u32[]{:S(2)}, u32[]{:S(2)}) collective-permute-start(bf16[3,192,1024]{2,1,0:T(8,128)(2,1)S(1)} %pad_maximum_fusion.refs_0_), channel_id=1, source_target_pairs={{0,256},{128,384},{256,0},{384,128},{1,257},{129,385},{257,1},{385... | collective-permute-start | bytes 3538952 | tf_op jit(solution)/shard_map/ppermute | solution.py:70
  52.5 3.1 %collective-permute-start.2 = (bf16[3,192,1024]{2,1,0:T(8,128)(2,1)S(1)}, bf16[3,192,1024]{2,1,0:T(8,128)(2,1)}, u32[]{:S(2)}, u32[]{:S(2)}) collective-permute-start(bf16[3,192,1024]{2,1,0:T(8,128)(2,1)S(1)} %pad_maximum_fusion.refs_0_), channel_id=1, source_target_pairs={{0,384},{128,0},{256,128},{384,256},{1,385},{129,1},{257,129},{385... | collective-permute-start | bytes 3538952 | tf_op jit(solution)/shard_map/ppermute | solution.py:70
  55.7 0.1 reshape_reshape_squeeze.4.gate_ref
  55.8 20.2 %collective-permute-done.refs_1_ = bf16[3,192,1024]{2,1,0:T(8,128)(2,1)S(1)} collective-permute-done((bf16[3,192,1024]{2,1,0:T(8,128)(2,1)S(1)}, bf16[3,192,1024]{2,1,0:T(8,128)(2,1)S(1)}, u32[]{:S(2)}, u32[]{:S(2)}) %collective-permute-start) | collective-permute-done | bytes 1179680 | tf_op jit(solution)/shard_map/ppermute | solution.py:70
  76.0 26.3 %collective-permute-done.1.refs_2_ = bf16[3,192,1024]{2,1,0:T(8,128)(2,1)} collective-permute-done((bf16[3,192,1024]{2,1,0:T(8,128)(2,1)S(1)}, bf16[3,192,1024]{2,1,0:T(8,128)(2,1)}, u32[]{:S(2)}, u32[]{:S(2)}) %collective-permute-start.1) | collective-permute-done | bytes 1179680 | tf_op jit(solution)/shard_map/ppermute | solution.py:70
  102.2 1.4 collective-permute-done.2.refs_3_
  103.6 2.0 %all-gather.2.cloned.1.call-done.rows_ref = bf16[2,304,4096]{2,1,0:T(8,128)(2,1)} async-done(((bf16[2,304,512]{2,1,0:T(8,128)(2,1)}), bf16[2,304,4096]{2,1,0:T(8,128)(2,1)}) %all-gather.2.cloned.1.call-update) | async-done | bytes 4980752 | tf_op jit(solution)/shard_map/all_gather | solution.py:122
  105.6 9.9 %shard_map.95 = (bf16[304,4096]{1,0:T(8,128)(2,1)}, bf16[192,4096]{1,0:T(8,128)(2,1)}) custom-call(s32[1]{0:T(128)} %bitcast.me_ref, bf16[2,304,4096]{2,1,0:T(8,128)(2,1)} %all-gather.2.cloned.1.call-done.rows_ref, bf16[304,1]{1,0:T(8,128)(2,1)S(1)} %reshape_reshape_squeeze.4.gate_ref, bf16[3,192,1024]{2,1,0:T(8,128)(2,1)S(1)} %pad_maximum_fusion.refs_0_, ...), custom_call_target="tpu_custom_call" | custom-call | tf_op jit(solution)/shard_map/pallas_call | solution.py:53
  115.5 0.0 copy-start.1
  115.5 0.0 reduce-scatter.2.cloned.1.call-update
  115.6 1.3 copy-done.1
  117.0 1.2 reshape.42
  118.1 3.3 %constant_dynamic-slice_fusion.3 = (bf16[192,1,1024]{2,1,0:T(2,128)(2,1)S(1)}, bf16[192,1,1024]{2,1,0:T(2,128)(2,1)S(1)}, bf16[192,1,1024]{2,1,0:T(2,128)(2,1)S(1)}, bf16[192,1,1024]{2,1,0:T(2,128)(2,1)S(1)}) fusion(bf16[192,4,1024]{2,1,0:T(4,128)(2,1)S(1)} %reshape.42, s32[]{:T(128)S(6)} %select_n.48, s32[]{:T(128)S(6)} %select_n.52, s32[]{:T(128)S(6)} %select_n.50, ...), kind=kLoop, calls=%fused_computation.30 | loop fusion | bytes 3145744 | tf_op jit(solution)/shard_map/jit(_take) | solution.py:79
  121.4 0.2 fusion.7
  121.6 4.3 %collective-permute-start.5 = (bf16[192,1024]{1,0:T(8,128)(2,1)S(1)}, bf16[192,1024]{1,0:T(8,128)(2,1)S(1)}, u32[]{:S(2)}, u32[]{:S(2)}) collective-permute-start(bf16[192,1024]{1,0:T(8,128)(2,1)S(1)} %fusion.7), channel_id=1, source_target_pairs={{0,384},{128,0},{256,128},{384,256},{1,385},{129,1},{257,129},{385... | collective-permute-start | bytes 1179656 | tf_op jit(solution)/shard_map/ppermute | solution.py:82
  125.9 0.2 fusion.8
  126.1 2.5 %collective-permute-start.4 = (bf16[192,1024]{1,0:T(8,128)(2,1)S(1)}, bf16[192,1024]{1,0:T(8,128)(2,1)S(1)}, u32[]{:S(2)}, u32[]{:S(2)}) collective-permute-start(bf16[192,1024]{1,0:T(8,128)(2,1)S(1)} %fusion.8), channel_id=1, source_target_pairs={{0,256},{128,384},{256,0},{384,128},{1,257},{129,385},{257,1},{385... | collective-permute-start | bytes 1179656 | tf_op jit(solution)/shard_map/ppermute | solution.py:82
  128.6 0.9 fusion.9
  129.5 2.5 %collective-permute-start.3 = (bf16[192,1024]{1,0:T(8,128)(2,1)}, bf16[192,1024]{1,0:T(8,128)(2,1)S(1)}, u32[]{:S(2)}, u32[]{:S(2)}) collective-permute-start(bf16[192,1024]{1,0:T(8,128)(2,1)} %fusion.9), channel_id=1, source_target_pairs={{0,128},{128,256},{256,384},{384,0},{1,129},{129,257},{257,385},{3... | collective-permute-start | bytes 1179656 | tf_op jit(solution)/shard_map/ppermute | solution.py:82
  132.0 24.7 %reduce-scatter.2.cloned.1.call-done = bf16[304,512]{1,0:T(8,128)(2,1)} async-done(((bf16[304,4096]{1,0:T(8,128)(2,1)}), bf16[304,512]{1,0:T(8,128)(2,1)}) %reduce-scatter.2.cloned.1.call-update) | async-done | bytes 311312 | tf_op jit(solution)/shard_map/reduce_scatter | solution.py:126
  156.7 1.8 reshape.40
  158.5 12.0 %all-to-all-start.1 = ((bf16[16,19,512]{2,1,0:T(8,128)(2,1)}), bf16[16,19,512]{2,1,0:T(8,128)(2,1)S(1)}, u32[]{:S(2)}, u32[]{:S(2)}) async-start(bf16[16,19,512]{2,1,0:T(8,128)(2,1)} %reshape.40), calls=%async_computation.2 | async-start | bytes 786432 | tf_op jit(solution)/shard_map/all_to_all | solution.py:127
  170.5 0.0 collective-permute-done.5
  170.5 0.0 collective-permute-done.4
  170.5 0.0 collective-permute-done.3
  170.6 1.1 fusion.6
  171.7 13.4 %all-to-all-done.1 = bf16[16,19,512]{2,1,0:T(8,128)(2,1)S(1)} async-done(((bf16[16,19,512]{2,1,0:T(8,128)(2,1)}), bf16[16,19,512]{2,1,0:T(8,128)(2,1)S(1)}, u32[]{:S(2)}, u32[]{:S(2)}) %all-to-all-start.1) | async-done | bytes 311328 | tf_op jit(solution)/shard_map/all_to_all | solution.py:127
  185.1 0.1 reshape.41
  185.2 0.9 convolution_convert_fusion.2
  (1 shorter events, 0.0 us)
Async XLA Ops:
  7.2 2.9 %copy-start = (bf16[152,512]{1,0:T(8,128)(2,1)S(1)}, bf16[152,512]{1,0:T(8,128)(2,1)}, u32[]{:S(2)}) copy-start(bf16[152,512]{1,0:T(8,128)(2,1)} %param.11) | copy-start | bytes 466948
  7.2 3.4 %copy-start.5 = (bf16[152,512]{1,0:T(8,128)(2,1)S(1)}, bf16[152,512]{1,0:T(8,128)(2,1)}, u32[]{:S(2)}) copy-start(bf16[152,512]{1,0:T(8,128)(2,1)} %param.10) | copy-start | bytes 466948
  7.2 98.4 %all-gather.2.cloned.1.call-start = ((), (), s32[]{:S(2)}) async-start(), calls=%async_computation.3 | async-start | bytes 5603328 | tf_op jit(solution)/shard_map/all_gather | solution.py:122
  43.4 1.1 copy-start.2
  43.4 1.1 copy-start.3
  43.5 1.4 copy-start.4
  44.5 112.2 %reduce-scatter.2.cloned.1.call-start = ((), (), s32[]{:S(2)}) async-start(), calls=%async_computation.4 | async-start | bytes 2801664 | tf_op jit(solution)/shard_map/reduce_scatter | solution.py:126
  45.0 30.9 %collective-permute-start = (bf16[3,192,1024]{2,1,0:T(8,128)(2,1)S(1)}, bf16[3,192,1024]{2,1,0:T(8,128)(2,1)S(1)}, u32[]{:S(2)}, u32[]{:S(2)}) collective-permute-start(bf16[3,192,1024]{2,1,0:T(8,128)(2,1)S(1)} %pad_maximum_fusion.refs_0_), channel_id=1, source_target_pairs={{0,128},{128,256},{256,384},{384,0},{1,129},{129,257},{257,385},{3... | collective-permute-start | bytes 3538952 | tf_op jit(solution)/shard_map/ppermute | solution.py:70
  48.2 54.1 %collective-permute-start.1 = (bf16[3,192,1024]{2,1,0:T(8,128)(2,1)S(1)}, bf16[3,192,1024]{2,1,0:T(8,128)(2,1)}, u32[]{:S(2)}, u32[]{:S(2)}) collective-permute-start(bf16[3,192,1024]{2,1,0:T(8,128)(2,1)S(1)} %pad_maximum_fusion.refs_0_), channel_id=1, source_target_pairs={{0,256},{128,384},{256,0},{384,128},{1,257},{129,385},{257,1},{385... | collective-permute-start | bytes 3538952 | tf_op jit(solution)/shard_map/ppermute | solution.py:70
  52.5 51.1 %collective-permute-start.2 = (bf16[3,192,1024]{2,1,0:T(8,128)(2,1)S(1)}, bf16[3,192,1024]{2,1,0:T(8,128)(2,1)}, u32[]{:S(2)}, u32[]{:S(2)}) collective-permute-start(bf16[3,192,1024]{2,1,0:T(8,128)(2,1)S(1)} %pad_maximum_fusion.refs_0_), channel_id=1, source_target_pairs={{0,384},{128,0},{256,128},{384,256},{1,385},{129,1},{257,129},{385... | collective-permute-start | bytes 3538952 | tf_op jit(solution)/shard_map/ppermute | solution.py:70
  115.5 1.4 copy-start.1
  121.6 48.9 %collective-permute-start.5 = (bf16[192,1024]{1,0:T(8,128)(2,1)S(1)}, bf16[192,1024]{1,0:T(8,128)(2,1)S(1)}, u32[]{:S(2)}, u32[]{:S(2)}) collective-permute-start(bf16[192,1024]{1,0:T(8,128)(2,1)S(1)} %fusion.7), channel_id=1, source_target_pairs={{0,384},{128,0},{256,128},{384,256},{1,385},{129,1},{257,129},{385... | collective-permute-start | bytes 1179656 | tf_op jit(solution)/shard_map/ppermute | solution.py:82
  126.1 44.4 %collective-permute-start.4 = (bf16[192,1024]{1,0:T(8,128)(2,1)S(1)}, bf16[192,1024]{1,0:T(8,128)(2,1)S(1)}, u32[]{:S(2)}, u32[]{:S(2)}) collective-permute-start(bf16[192,1024]{1,0:T(8,128)(2,1)S(1)} %fusion.8), channel_id=1, source_target_pairs={{0,256},{128,384},{256,0},{384,128},{1,257},{129,385},{257,1},{385... | collective-permute-start | bytes 1179656 | tf_op jit(solution)/shard_map/ppermute | solution.py:82
  129.5 41.1 %collective-permute-start.3 = (bf16[192,1024]{1,0:T(8,128)(2,1)}, bf16[192,1024]{1,0:T(8,128)(2,1)S(1)}, u32[]{:S(2)}, u32[]{:S(2)}) collective-permute-start(bf16[192,1024]{1,0:T(8,128)(2,1)} %fusion.9), channel_id=1, source_target_pairs={{0,128},{128,256},{256,384},{384,0},{1,129},{129,257},{257,385},{3... | collective-permute-start | bytes 1179656 | tf_op jit(solution)/shard_map/ppermute | solution.py:82
  158.5 26.6 %all-to-all-start.1 = ((bf16[16,19,512]{2,1,0:T(8,128)(2,1)}), bf16[16,19,512]{2,1,0:T(8,128)(2,1)S(1)}, u32[]{:S(2)}, u32[]{:S(2)}) async-start(bf16[16,19,512]{2,1,0:T(8,128)(2,1)} %reshape.40), calls=%async_computation.2 | async-start | bytes 786432 | tf_op jit(solution)/shard_map/all_to_all | solution.py:127
Sparse Core Ops, SparseCore 0:
  44.6 60.9 all-gather.1
  115.7 40.9 reduce-scatter.1

commit v9 on v8

--- a/solution.py
+++ b/solution.py
@@ -1,3 +1,5 @@
+import functools
+
 import jax
 import jax.numpy as jnp
 from jax import lax
@@ -8,10 +10,10 @@
 CAP = 19
 
 
-def _expert_kernel(me_ref, rows_ref, gate_ref, *refs):
-    size = len(refs) - 2
+def _expert_kernel(me_ref, rows_ref, gate_ref, *refs, size, carry):
     w_refs = refs[:size]
-    q_ref, term_ref = refs[size:]
+    acc_ref = refs[size] if carry else None
+    q_ref, term_ref = refs[-2:]
     quarter = w_refs[0].shape[2]
     me = me_ref[0]
     nt = (((1,), (1,)), ((), ()))
@@ -41,26 +43,28 @@
         q_ref[:, pl.ds(start, quarter)] = part.astype(jnp.bfloat16)
     hidden_t = hidden.T.astype(jnp.bfloat16)
     scaled = (gate_f * rows_ref[1].astype(jnp.float32)).astype(jnp.bfloat16)
-    term_ref[...] = jnp.dot(hidden_t, scaled, preferred_element_type=jnp.float32).astype(
-        jnp.bfloat16
-    )
+    term = jnp.dot(hidden_t, scaled, preferred_element_type=jnp.float32)
+    if carry:
+        term = term + acc_ref[...]
+    term_ref[...] = term.astype(term_ref.dtype)
 
 
-def expert_kernel(me, rows, gate_col, pieces):
+def expert_kernel(me, rows, gate_col, pieces, acc=None):
     _, slots, width = rows.shape
     ffb = pieces[0].shape[1]
     vmem = pltpu.VMEM
+    extra = [] if acc is None else [acc]
     return pl.pallas_call(
-        _expert_kernel,
+        functools.partial(_expert_kernel, size=len(pieces), carry=acc is not None),
         out_shape=(
             jax.ShapeDtypeStruct((slots, width), jnp.bfloat16),
-            jax.ShapeDtypeStruct((ffb, width), jnp.bfloat16),
+            jax.ShapeDtypeStruct((ffb, width), jnp.float32 if acc is None else jnp.bfloat16),
         ),
         in_specs=[pl.BlockSpec(memory_space=pltpu.SMEM)]
-        + [pl.BlockSpec(memory_space=vmem)] * (2 + len(pieces)),
+        + [pl.BlockSpec(memory_space=vmem)] * (2 + len(pieces) + len(extra)),
         out_specs=(pl.BlockSpec(memory_space=vmem), pl.BlockSpec(memory_space=vmem)),
         compiler_params=pltpu.CompilerParams(vmem_limit_bytes=48 * 1024 * 1024),
-    )(me.reshape(1), rows, gate_col.reshape(slots, 1), *pieces)
+    )(me.reshape(1), rows, gate_col.reshape(slots, 1), *pieces, *extra)
 
 
 def pieces_dp(piece):
@@ -100,35 +104,46 @@
     ).astype(jnp.bfloat16)
     packed_x = jnp.dot(onehot, tokens, preferred_element_type=jnp.float32).astype(jnp.bfloat16)
     packed_dy = jnp.dot(onehot, cotangent, preferred_element_type=jnp.float32).astype(jnp.bfloat16)
+    packed_x = packed_x.reshape(width, CAP, narrow)
+    packed_dy = packed_dy.reshape(width, CAP, narrow)
     gate_row = jnp.pad(slot_gate.reshape(width, 1, CAP), ((0, 0), (0, 0), (0, narrow - CAP)))
-    block = jnp.concatenate(
-        [
-            packed_x.reshape(width, CAP, narrow),
-            gate_row,
-            packed_dy.reshape(width, CAP, narrow),
-            jnp.zeros_like(gate_row),
-        ],
-        axis=1,
-    )
-    recv = lax.all_to_all(block, "expert", split_axis=0, concat_axis=0, tiled=True)
-    recv_gate = recv[:, CAP, :CAP].reshape(slots)
-    pair = jnp.stack(
-        [
-            recv[:, :CAP, :].reshape(slots, narrow),
-            recv[:, CAP + 1 : 2 * CAP + 1, :].reshape(slots, narrow),
-        ],
-        axis=0,
-    )
-    full = lax.all_gather(pair, "etp", axis=2, tiled=True)
+    cut = (CAP + 1) // 2
+    spans = ((0, cut), (cut, CAP))
     stack = jnp.stack([gate_w[0].T, up_w[0].T, down_w[0]], axis=0)
-    d_part_b, term_b = expert_kernel(lax.axis_index("dp"), full, recv_gate, pieces_dp(stack))
-    down_grad = scatter_sum_dp(term_b)[None]
-    summed = lax.psum_scatter(d_part_b, "etp", scatter_dimension=1, tiled=True)
-    returned = lax.all_to_all(
-        summed.reshape(width, CAP, narrow), "expert", split_axis=0, concat_axis=0, tiled=True
-    ).reshape(slots, narrow)
+    pieces = pieces_dp(stack)
+    me = lax.axis_index("dp")
+    acc = None
+    returned = []
+    recv_gate = None
+    for idx, (lo, hi) in enumerate(spans):
+        n = hi - lo
+        parts = [packed_x[:, lo:hi], packed_dy[:, lo:hi]]
+        if idx == 0:
+            parts.append(gate_row)
+        block = jnp.concatenate(parts, axis=1)
+        recv = lax.all_to_all(block, "expert", split_axis=0, concat_axis=0, tiled=True)
+        if idx == 0:
+            recv_gate = recv[:, 2 * n, :CAP]
+        pair = jnp.stack(
+            [
+                recv[:, :n, :].reshape(width * n, narrow),
+                recv[:, n : 2 * n, :].reshape(width * n, narrow),
+            ],
+            axis=0,
+        )
+        full = lax.all_gather(pair, "etp", axis=2, tiled=True)
+        gate_col = recv_gate[:, lo:hi].reshape(width * n)
+        d_part_b, acc = expert_kernel(me, full, gate_col, pieces, acc)
+        summed = lax.psum_scatter(d_part_b, "etp", scatter_dimension=1, tiled=True)
+        returned.append(
+            lax.all_to_all(
+                summed.reshape(width, n, narrow), "expert", split_axis=0, concat_axis=0, tiled=True
+            )
+        )
+    down_grad = scatter_sum_dp(acc)[None]
+    table = jnp.concatenate(returned, axis=1).reshape(slots, narrow)
     total = lax.dot_general(
-        onehot, returned, (((0,), (0,)), ((), ())), preferred_element_type=jnp.float32
+        onehot, table, (((0,), (0,)), ((), ())), preferred_element_type=jnp.float32
     )
     input_grad = total.astype(jnp.bfloat16)
     return (input_grad, down_grad)

time: 193 us -> 247 us (1.28)
  waiting for transfers between devices: 88 us -> 108 us
  starting transfers between devices: 31.9 us -> 44.5 us
  blocking collectives: 31.9 us -> 43.4 us
  Pallas kernels: 9.91 us -> 15.4 us
  local copies, waits for them, and re-layouts: 9.85 us -> 12.5 us
    reduce_scatter x1 -> x2, waiting for transfers between devices: 24.7 us -> 49 us  [local(): summed = lax.psum_scatter(d_part_b, 'etp', scatter_dimension=1, tiled=True)]
    all_to_all x1 -> x2, starting transfers between devices: 12 us -> 24.1 us  [local(): lax.all_to_all(summed.reshape(width, n, narrow), 'expert', split_axis=0,...]
    all_to_all x1 -> x2, blocking collectives: 31.9 us -> 43.4 us  [local(): lax.all_to_all(block, 'expert', split_axis=0, concat_axis=0, tiled=True)]
    pallas_call x1 -> x2, Pallas kernels: 9.91 us -> 15.4 us  [expert_kernel(): pl.pallas_call(functools.partial(_expert_kernel, size=len(pieces), carry=...]
    all_to_all x1 -> x2, waiting for transfers between devices: 13.4 us -> 10.6 us  [local(): lax.all_to_all(summed.reshape(width, n, narrow), 'expert', split_axis=0,...]
  transfers between devices with their start and end apart: 9 -> 12, of which waited for: 6 -> 6; matrix products, arithmetic and copies ran while one was open for 5% -> 5% of each run, Pallas kernels for 0% -> 3%
where the time goes in v9:
time: 247 us; the launch traced here: 246 us
  waiting for transfers between devices  108 us (44%)
  starting transfers between devices  44.5 us (18%)
  blocking collectives  43.4 us (18%)
  Pallas kernels  15.4 us (6%)
  between operations  14.2 us (6%)
  local copies, waits for them, and re-layouts  12.5 us (5%)
  other arithmetic  6.92 us (3%)
    reduce_scatter x2, waiting for transfers between devices, local(): summed = lax.psum_scatter(d_part_b, 'etp', scatter_dimension=1, tiled=True)  49 us
    ppermute x3, waiting for transfers between devices, pieces_dp(): lax.ppermute(piece, 'dp', [(i, (i + shift) % size) for i in range(size)])  48.1 us
    all_to_all x2, blocking collectives, local(): lax.all_to_all(block, 'expert', split_axis=0, concat_axis=0, tiled=True)  43.4 us
    all_to_all x2, starting transfers between devices, local(): lax.all_to_all(summed.reshape(width, n, narrow), 'expert', split_axis=0,...  24.1 us
    pallas_call x2, Pallas kernels, expert_kernel(): pl.pallas_call(functools.partial(_expert_kernel, size=len(pieces), carry=...  15.4 us
    all_to_all x2, waiting for transfers between devices, local(): lax.all_to_all(summed.reshape(width, n, narrow), 'expert', split_axis=0,...  10.6 us
    ppermute x3, starting transfers between devices, pieces_dp(): lax.ppermute(piece, 'dp', [(i, (i + shift) % size) for i in range(size)])  10.5 us
    ppermute x3, starting transfers between devices, scatter_sum_dp(): lax.ppermute(outgoing, 'dp', [(i, (i + shift) % size) for i in range(size)])  9.59 us
  transfers between devices with their start and end apart: 12, of which 6 were waited for; matrix products, arithmetic and copies ran while one was open for 5% of the time, Pallas kernels for 3%

profile of v9, /device:TPU:1, one launch (start us, length us, event | category | flops | bytes accessed | tf_op | source)
XLA Modules:
  0.0 246.5 jit_solution(8350375867590941409)
XLA Ops:
  7.2 0.8 add_select_fusion
  8.1 0.1 copy.37
  8.2 0.7 fusion
  8.8 0.3 convolution_convert_fusion
  9.1 0.1 reshape.43
  9.3 0.3 convolution_convert_fusion.1
  9.6 0.1 reshape.42
  9.7 0.1 copy.38
  9.8 0.4 select_reduce_fusion
  10.2 0.1 convert_element_type.54
  10.4 0.1 fusion.2
  10.5 26.2 %all_to_all.20 = bf16[16,21,512]{2,1,0:T(8,128)(2,1)S(1)} all-to-all(bf16[16,21,512]{2,1,0:T(8,128)(2,1)S(1)} %fusion.2), channel_id=1, replica_groups=mesh['dp'=4,'expert'=16,'etp'=8] {'expert'}, dimensions={0} | all-to-all | bytes 688128 | tf_op jit(solution)/shard_map/all_to_all | solution.py:124
  36.7 0.1 fusion.8
  36.7 0.1 stack_reshape.13
  36.8 0.1 stack_reshape.12
  36.9 0.8 pad_maximum_fusion.3
  37.7 0.0 all-gather.5.cloned.1.call-start
  37.7 0.1 slice.60
  37.8 0.1 slice.59
  37.9 0.1 pad_maximum_fusion.1
  38.0 17.2 %all_to_all.21 = bf16[16,18,512]{2,1,0:T(8,128)(2,1)S(1)} all-to-all(bf16[16,18,512]{2,1,0:T(8,128)(2,1)S(1)} %pad_maximum_fusion.1), channel_id=1, replica_groups=mesh['dp'=4,'expert'=16,'etp'=8] {'expert'}, dimensions={0} | all-to-all | bytes 589824 | tf_op jit(solution)/shard_map/all_to_all | solution.py:124
  55.2 0.1 fusion.9
  55.3 0.1 stack_reshape.15
  55.3 0.1 stack_reshape.14
  55.4 0.7 pad_maximum_fusion.4
  56.2 0.0 reduce-scatter.5.cloned.1.call-start
  56.3 0.0 copy-done.5
  56.3 0.2 copy-done.6
  56.5 0.1 pad_maximum_fusion.refs_0_
  56.7 3.1 %collective-permute-start = (bf16[3,192,1024]{2,1,0:T(8,128)(2,1)S(1)}, bf16[3,192,1024]{2,1,0:T(8,128)(2,1)S(1)}, u32[]{:S(2)}, u32[]{:S(2)}) collective-permute-start(bf16[3,192,1024]{2,1,0:T(8,128)(2,1)S(1)} %pad_maximum_fusion.refs_0_), channel_id=1, source_target_pairs={{0,128},{128,256},{256,384},{384,0},{1,129},{129,257},{257,385},{3... | collective-permute-start | bytes 3538952 | tf_op jit(solution)/shard_map/ppermute | solution.py:74
  59.8 4.4 %collective-permute-start.1 = (bf16[3,192,1024]{2,1,0:T(8,128)(2,1)S(1)}, bf16[3,192,1024]{2,1,0:T(8,128)(2,1)}, u32[]{:S(2)}, u32[]{:S(2)}) collective-permute-start(bf16[3,192,1024]{2,1,0:T(8,128)(2,1)S(1)} %pad_maximum_fusion.refs_0_), channel_id=1, source_target_pairs={{0,256},{128,384},{256,0},{384,128},{1,257},{129,385},{257,1},{385... | collective-permute-start | bytes 3538952 | tf_op jit(solution)/shard_map/ppermute | solution.py:74
  64.2 3.1 %collective-permute-start.2 = (bf16[3,192,1024]{2,1,0:T(8,128)(2,1)S(1)}, bf16[3,192,1024]{2,1,0:T(8,128)(2,1)}, u32[]{:S(2)}, u32[]{:S(2)}) collective-permute-start(bf16[3,192,1024]{2,1,0:T(8,128)(2,1)S(1)} %pad_maximum_fusion.refs_0_), channel_id=1, source_target_pairs={{0,384},{128,0},{256,128},{384,256},{1,385},{129,1},{257,129},{385... | collective-permute-start | bytes 3538952 | tf_op jit(solution)/shard_map/ppermute | solution.py:74
  67.3 0.1 slice.63
  67.3 0.1 reshape_reshape.9.gate_ref
  67.5 0.1 reshape_reshape.8.gate_ref
  67.6 19.6 %collective-permute-done.refs_1_ = bf16[3,192,1024]{2,1,0:T(8,128)(2,1)S(1)} collective-permute-done((bf16[3,192,1024]{2,1,0:T(8,128)(2,1)S(1)}, bf16[3,192,1024]{2,1,0:T(8,128)(2,1)S(1)}, u32[]{:S(2)}, u32[]{:S(2)}) %collective-permute-start) | collective-permute-done | bytes 1179680 | tf_op jit(solution)/shard_map/ppermute | solution.py:74
  87.2 26.4 %collective-permute-done.1.refs_2_ = bf16[3,192,1024]{2,1,0:T(8,128)(2,1)} collective-permute-done((bf16[3,192,1024]{2,1,0:T(8,128)(2,1)S(1)}, bf16[3,192,1024]{2,1,0:T(8,128)(2,1)}, u32[]{:S(2)}, u32[]{:S(2)}) %collective-permute-start.1) | collective-permute-done | bytes 1179680 | tf_op jit(solution)/shard_map/ppermute | solution.py:74
  113.5 2.1 collective-permute-done.2.refs_3_
  115.7 7.5 %shard_map.95 = (bf16[160,4096]{1,0:T(8,128)(2,1)S(1)}, f32[192,4096]{1,0:T(8,128)}) custom-call(s32[1]{0:T(128)} %bitcast.me_ref, bf16[2,160,4096]{2,1,0:T(8,128)(2,1)} %all-gather.3.cloned.1.call-done.rows_ref, bf16[160,1]{1,0:T(8,128)(2,1)S(1)} %reshape_reshape.8.gate_ref, bf16[3,192,1024]{2,1,0:T(8,128)(2,1)S(1)} %pad_maximum_fusion.refs_0_, ...), custom_call_target="tpu_custom_call" | custom-call | tf_op jit(solution)/shard_map/pallas_call | solution.py:57
  123.2 1.1 copy-done.1
  124.3 7.9 %shard_map.96 = (bf16[144,4096]{1,0:T(8,128)(2,1)S(1)}, bf16[192,4096]{1,0:T(8,128)(2,1)}) custom-call(s32[1]{0:T(128)} %bitcast.me_ref, bf16[2,144,4096]{2,1,0:T(8,128)(2,1)} %all-gather.5.cloned.1.call-done.rows_ref, bf16[144,1]{1,0:T(8,128)(2,1)S(1)} %reshape_reshape.9.gate_ref, bf16[3,192,1024]{2,1,0:T(8,128)(2,1)S(1)} %pad_maximum_fusion.refs_0_, ...), custom_call_target="tpu_custom_call" | custom-call | tf_op jit(solution)/shard_map/pallas_call | solution.py:57
  132.2 1.0 copy-done.2
  133.2 0.2 reduce-scatter.3.cloned.1.call-start
  133.5 0.3 reduce-scatter.3.cloned.1.call-update
  133.9 0.7 copy-done.3
  134.6 1.2 reshape.47
  135.8 3.3 %constant_dynamic-slice_fusion.3 = (bf16[192,1,1024]{2,1,0:T(2,128)(2,1)S(1)}, bf16[192,1,1024]{2,1,0:T(2,128)(2,1)S(1)}, bf16[192,1,1024]{2,1,0:T(2,128)(2,1)S(1)}, bf16[192,1,1024]{2,1,0:T(2,128)(2,1)S(1)}) fusion(bf16[192,4,1024]{2,1,0:T(4,128)(2,1)S(1)} %reshape.47, s32[]{:T(128)S(6)} %select_n.48, s32[]{:T(128)S(6)} %select_n.52, s32[]{:T(128)S(6)} %select_n.50, ...), kind=kLoop, calls=%fused_computation.29 | loop fusion | bytes 3145744 | tf_op jit(solution)/shard_map/jit(_take) | solution.py:83
  139.1 0.2 fusion.4
  139.3 4.2 %collective-permute-start.5 = (bf16[192,1024]{1,0:T(8,128)(2,1)S(1)}, bf16[192,1024]{1,0:T(8,128)(2,1)S(1)}, u32[]{:S(2)}, u32[]{:S(2)}) collective-permute-start(bf16[192,1024]{1,0:T(8,128)(2,1)S(1)} %fusion.4), channel_id=1, source_target_pairs={{0,384},{128,0},{256,128},{384,256},{1,385},{129,1},{257,129},{385... | collective-permute-start | bytes 1179656 | tf_op jit(solution)/shard_map/ppermute | solution.py:86
  143.5 0.9 fusion.5
  144.4 3.4 %collective-permute-start.4 = (bf16[192,1024]{1,0:T(8,128)(2,1)}, bf16[192,1024]{1,0:T(8,128)(2,1)S(1)}, u32[]{:S(2)}, u32[]{:S(2)}) collective-permute-start(bf16[192,1024]{1,0:T(8,128)(2,1)} %fusion.5), channel_id=1, source_target_pairs={{0,256},{128,384},{256,0},{384,128},{1,257},{129,385},{257,1},{385... | collective-permute-start | bytes 1179656 | tf_op jit(solution)/shard_map/ppermute | solution.py:86
  147.9 0.9 fusion.6
  148.8 1.9 collective-permute-start.3
  150.7 19.2 %reduce-scatter.5.cloned.1.call-done = bf16[144,512]{1,0:T(8,128)(2,1)} async-done(((bf16[144,4096]{1,0:T(8,128)(2,1)}), bf16[144,512]{1,0:T(8,128)(2,1)}) %reduce-scatter.5.cloned.1.call-update) | async-done | bytes 147472 | tf_op jit(solution)/shard_map/reduce_scatter | solution.py:137
  169.9 1.7 reshape.45
  171.6 12.0 %all-to-all-start.3 = ((bf16[16,9,512]{2,1,0:T(8,128)(2,1)}), bf16[16,9,512]{2,1,0:T(8,128)(2,1)S(1)}, u32[]{:S(2)}, u32[]{:S(2)}) async-start(bf16[16,9,512]{2,1,0:T(8,128)(2,1)} %reshape.45), calls=%async_computation.5 | async-start | bytes 524288 | tf_op jit(solution)/shard_map/all_to_all | solution.py:139
  183.5 29.8 %reduce-scatter.3.cloned.1.call-done = bf16[160,512]{1,0:T(8,128)(2,1)} async-done(((bf16[160,4096]{1,0:T(8,128)(2,1)}), bf16[160,512]{1,0:T(8,128)(2,1)}) %reduce-scatter.3.cloned.1.call-update) | async-done | bytes 163856 | tf_op jit(solution)/shard_map/reduce_scatter | solution.py:137
  213.3 1.7 reshape.44
  215.0 12.1 %all-to-all-start.1 = ((bf16[16,10,512]{2,1,0:T(8,128)(2,1)}), bf16[16,10,512]{2,1,0:T(8,128)(2,1)S(1)}, u32[]{:S(2)}, u32[]{:S(2)}) async-start(bf16[16,10,512]{2,1,0:T(8,128)(2,1)} %reshape.44), calls=%async_computation.2 | async-start | bytes 524288 | tf_op jit(solution)/shard_map/all_to_all | solution.py:139
  227.1 1.1 fusion.3
  228.2 10.6 %all-to-all-done.1 = bf16[16,10,512]{2,1,0:T(8,128)(2,1)S(1)} async-done(((bf16[16,10,512]{2,1,0:T(8,128)(2,1)}), bf16[16,10,512]{2,1,0:T(8,128)(2,1)S(1)}, u32[]{:S(2)}, u32[]{:S(2)}) %all-to-all-start.1) | async-done | bytes 163872 | tf_op jit(solution)/shard_map/all_to_all | solution.py:139
  238.8 0.1 pad_maximum_fusion.2
  238.9 0.1 reshape.46
  239.0 0.9 convolution_convert_fusion.2
  (27 shorter events, 0.2 us)
Async XLA Ops:
  7.2 1.7 copy-start
  7.2 2.1 copy-start.7
  7.2 2.5 %copy-start.8 = (bf16[152,8]{0,1:T(8,128)(2,1)S(1)}, bf16[152,8]{0,1:T(8,128)(2,1)}, u32[]{:S(2)}) copy-start(bf16[152,8]{0,1:T(8,128)(2,1)} %param.12) | copy-start | bytes 7300
  7.2 108.5 %all-gather.3.cloned.1.call-start = ((), (), s32[]{:S(2)}) async-start(), calls=%async_computation.6 | async-start | bytes 2949120 | tf_op jit(solution)/shard_map/all_gather | solution.py:134
  37.7 86.6 %all-gather.5.cloned.1.call-start = ((), (), s32[]{:S(2)}) async-start(), calls=%async_computation.8 | async-start | bytes 2654208 | tf_op jit(solution)/shard_map/all_gather | solution.py:134
  55.2 1.1 copy-start.4
  55.2 1.1 copy-start.5
  55.2 1.3 copy-start.6
  56.2 113.7 %reduce-scatter.5.cloned.1.call-start = ((), (), s32[]{:S(2)}) async-start(), calls=%async_computation.9 | async-start | bytes 1327104 | tf_op jit(solution)/shard_map/reduce_scatter | solution.py:137
  56.7 30.5 %collective-permute-start = (bf16[3,192,1024]{2,1,0:T(8,128)(2,1)S(1)}, bf16[3,192,1024]{2,1,0:T(8,128)(2,1)S(1)}, u32[]{:S(2)}, u32[]{:S(2)}) collective-permute-start(bf16[3,192,1024]{2,1,0:T(8,128)(2,1)S(1)} %pad_maximum_fusion.refs_0_), channel_id=1, source_target_pairs={{0,128},{128,256},{256,384},{384,0},{1,129},{129,257},{257,385},{3... | collective-permute-start | bytes 3538952 | tf_op jit(solution)/shard_map/ppermute | solution.py:74
  59.8 53.8 %collective-permute-start.1 = (bf16[3,192,1024]{2,1,0:T(8,128)(2,1)S(1)}, bf16[3,192,1024]{2,1,0:T(8,128)(2,1)}, u32[]{:S(2)}, u32[]{:S(2)}) collective-permute-start(bf16[3,192,1024]{2,1,0:T(8,128)(2,1)S(1)} %pad_maximum_fusion.refs_0_), channel_id=1, source_target_pairs={{0,256},{128,384},{256,0},{384,128},{1,257},{129,385},{257,1},{385... | collective-permute-start | bytes 3538952 | tf_op jit(solution)/shard_map/ppermute | solution.py:74
  64.2 51.5 %collective-permute-start.2 = (bf16[3,192,1024]{2,1,0:T(8,128)(2,1)S(1)}, bf16[3,192,1024]{2,1,0:T(8,128)(2,1)}, u32[]{:S(2)}, u32[]{:S(2)}) collective-permute-start(bf16[3,192,1024]{2,1,0:T(8,128)(2,1)S(1)} %pad_maximum_fusion.refs_0_), channel_id=1, source_target_pairs={{0,384},{128,0},{256,128},{384,256},{1,385},{129,1},{257,129},{385... | collective-permute-start | bytes 3538952 | tf_op jit(solution)/shard_map/ppermute | solution.py:74
  123.2 1.1 copy-start.1
  132.2 1.0 copy-start.2
  133.2 1.4 copy-start.3
  133.2 80.1 %reduce-scatter.3.cloned.1.call-start = ((), (), s32[]{:S(2)}) async-start(), calls=%async_computation.7 | async-start | bytes 1474560 | tf_op jit(solution)/shard_map/reduce_scatter | solution.py:137
  139.3 87.8 %collective-permute-start.5 = (bf16[192,1024]{1,0:T(8,128)(2,1)S(1)}, bf16[192,1024]{1,0:T(8,128)(2,1)S(1)}, u32[]{:S(2)}, u32[]{:S(2)}) collective-permute-start(bf16[192,1024]{1,0:T(8,128)(2,1)S(1)} %fusion.4), channel_id=1, source_target_pairs={{0,384},{128,0},{256,128},{384,256},{1,385},{129,1},{257,129},{385... | collective-permute-start | bytes 1179656 | tf_op jit(solution)/shard_map/ppermute | solution.py:86
  144.4 82.7 %collective-permute-start.4 = (bf16[192,1024]{1,0:T(8,128)(2,1)}, bf16[192,1024]{1,0:T(8,128)(2,1)S(1)}, u32[]{:S(2)}, u32[]{:S(2)}) collective-permute-start(bf16[192,1024]{1,0:T(8,128)(2,1)} %fusion.5), channel_id=1, source_target_pairs={{0,256},{128,384},{256,0},{384,128},{1,257},{129,385},{257,1},{385... | collective-permute-start | bytes 1179656 | tf_op jit(solution)/shard_map/ppermute | solution.py:86
  148.8 78.3 %collective-permute-start.3 = (bf16[192,1024]{1,0:T(8,128)(2,1)}, bf16[192,1024]{1,0:T(8,128)(2,1)S(1)}, u32[]{:S(2)}, u32[]{:S(2)}) collective-permute-start(bf16[192,1024]{1,0:T(8,128)(2,1)} %fusion.6), channel_id=1, source_target_pairs={{0,128},{128,256},{256,384},{384,0},{1,129},{129,257},{257,385},{3... | collective-permute-start | bytes 1179656 | tf_op jit(solution)/shard_map/ppermute | solution.py:86
  171.6 43.4 %all-to-all-start.3 = ((bf16[16,9,512]{2,1,0:T(8,128)(2,1)}), bf16[16,9,512]{2,1,0:T(8,128)(2,1)S(1)}, u32[]{:S(2)}, u32[]{:S(2)}) async-start(bf16[16,9,512]{2,1,0:T(8,128)(2,1)} %reshape.45), calls=%async_computation.5 | async-start | bytes 524288 | tf_op jit(solution)/shard_map/all_to_all | solution.py:139
  215.0 23.8 %all-to-all-start.1 = ((bf16[16,10,512]{2,1,0:T(8,128)(2,1)}), bf16[16,10,512]{2,1,0:T(8,128)(2,1)S(1)}, u32[]{:S(2)}, u32[]{:S(2)}) async-start(bf16[16,10,512]{2,1,0:T(8,128)(2,1)} %reshape.44), calls=%async_computation.2 | async-start | bytes 524288 | tf_op jit(solution)/shard_map/all_to_all | solution.py:139
Sparse Core Ops, SparseCore 0:
  37.8 38.3 all-gather.2
  78.3 43.0 all-gather.4
  133.4 36.4 reduce-scatter.4
  172.5 40.7 reduce-scatter.2

commit v10 on v8

--- a/solution.py
+++ b/solution.py
@@ -13,6 +13,7 @@
     w_refs = refs[:size]
     q_ref, term_ref = refs[size:]
     quarter = w_refs[0].shape[2]
+    narrow = q_ref.shape[2]
     me = me_ref[0]
     nt = (((1,), (1,)), ((), ()))
     gate_pre = None
@@ -38,7 +39,11 @@
         start = pl.multiple_of(((me + size - k) % size) * quarter, quarter)
         part = jnp.dot(d_gate_b, w_refs[k][0], preferred_element_type=jnp.float32)
         part = part + jnp.dot(d_up_b, w_refs[k][1], preferred_element_type=jnp.float32)
-        q_ref[:, pl.ds(start, quarter)] = part.astype(jnp.bfloat16)
+        part = part.astype(jnp.bfloat16)
+        per = quarter // narrow
+        block = ((me + size - k) % size) * per
+        for h in range(per):
+            q_ref[block + h] = part[:, h * narrow : (h + 1) * narrow]
     hidden_t = hidden.T.astype(jnp.bfloat16)
     scaled = (gate_f * rows_ref[1].astype(jnp.float32)).astype(jnp.bfloat16)
     term_ref[...] = jnp.dot(hidden_t, scaled, preferred_element_type=jnp.float32).astype(
@@ -46,14 +51,14 @@
     )
 
 
-def expert_kernel(me, rows, gate_col, pieces):
+def expert_kernel(me, rows, gate_col, pieces, split):
     _, slots, width = rows.shape
     ffb = pieces[0].shape[1]
     vmem = pltpu.VMEM
     return pl.pallas_call(
         _expert_kernel,
         out_shape=(
-            jax.ShapeDtypeStruct((slots, width), jnp.bfloat16),
+            jax.ShapeDtypeStruct((split, slots, width // split), jnp.bfloat16),
             jax.ShapeDtypeStruct((ffb, width), jnp.bfloat16),
         ),
         in_specs=[pl.BlockSpec(memory_space=pltpu.SMEM)]
@@ -121,9 +126,11 @@
     )
     full = lax.all_gather(pair, "etp", axis=2, tiled=True)
     stack = jnp.stack([gate_w[0].T, up_w[0].T, down_w[0]], axis=0)
-    d_part_b, term_b = expert_kernel(lax.axis_index("dp"), full, recv_gate, pieces_dp(stack))
+    d_part_b, term_b = expert_kernel(
+        lax.axis_index("dp"), full, recv_gate, pieces_dp(stack), lax.axis_size("etp")
+    )
     down_grad = scatter_sum_dp(term_b)[None]
-    summed = lax.psum_scatter(d_part_b, "etp", scatter_dimension=1, tiled=True)
+    summed = lax.psum_scatter(d_part_b, "etp", scatter_dimension=0, tiled=True)[0]
     returned = lax.all_to_all(
         summed.reshape(width, CAP, narrow), "expert", split_axis=0, concat_axis=0, tiled=True
     ).reshape(slots, narrow)

time: 193 us -> 193 us (level)
  no operation moved by 1% of the time
where the time goes in v10:
time: 193 us
  waiting for transfers between devices  88.1 us (46%)
  blocking collectives  31.9 us (17%)
  starting transfers between devices  31.8 us (16%)
  between operations  14.4 us (7%)
  Pallas kernels  9.91 us (5%)
  local copies, waits for them, and re-layouts  9.85 us (5%)
  other arithmetic  5.52 us (3%)
    ppermute x3, waiting for transfers between devices, pieces_dp(): lax.ppermute(piece, 'dp', [(i, (i + shift) % size) for i in range(size)])  47.8 us
    all_to_all x1, blocking collectives, local(): lax.all_to_all(block, 'expert', split_axis=0, concat_axis=0, tiled=True)  31.9 us
    reduce_scatter x1, waiting for transfers between devices, local(): lax.psum_scatter(d_part_b, 'etp', scatter_dimension=0, tiled=True)[0]  24.8 us
    all_to_all x1, waiting for transfers between devices, local(): lax.all_to_all(summed.reshape(width, CAP, narrow), 'expert', split_axis=0...  13.4 us
    all_to_all x1, starting transfers between devices, local(): lax.all_to_all(summed.reshape(width, CAP, narrow), 'expert', split_axis=0...  11.9 us
    ppermute x3, starting transfers between devices, pieces_dp(): lax.ppermute(piece, 'dp', [(i, (i + shift) % size) for i in range(size)])  10.6 us
    pallas_call x1, Pallas kernels, expert_kernel(): pl.pallas_call(_expert_kernel, out_shape=(jax.ShapeDtypeStruct((split, sl...  9.91 us
    ppermute x3, starting transfers between devices, scatter_sum_dp(): lax.ppermute(outgoing, 'dp', [(i, (i + shift) % size) for i in range(size)])  9.27 us
  transfers between devices with their start and end apart: 9, of which 6 were waited for; matrix products, arithmetic and copies ran while one was open for 5% of the time, Pallas kernels for 0%

profile of v10, /device:TPU:1, one launch (start us, length us, event | category | flops | bytes accessed | tf_op | source)
XLA Modules:
  0.0 192.9 jit_solution(4306322376758340422)
XLA Ops:
  7.2 0.0 copy-start
  7.2 0.0 copy-start.5
  7.2 0.0 all-gather.2.cloned.1.call-start
  7.2 0.8 add_select_fusion
  8.0 0.1 copy.35
  8.1 0.7 fusion
  8.8 0.8 copy.36
  9.6 0.4 select_reduce_fusion
  10.0 0.1 convert_element_type.54
  10.1 0.0 copy-done
  10.1 0.3 convolution_convert_fusion
  10.4 0.1 reshape.36
  10.5 0.0 copy-done.5
  10.5 0.3 convolution_convert_fusion.1
  10.8 0.1 reshape.35
  11.0 0.1 pad.15.clone
  11.0 0.3 fusion.5
  11.3 31.9 %all_to_all.10 = bf16[16,40,512]{2,1,0:T(8,128)(2,1)S(1)} all-to-all(bf16[16,40,512]{2,1,0:T(8,128)(2,1)S(1)} %fusion.5), channel_id=1, replica_groups=mesh['dp'=4,'expert'=16,'etp'=8] {'expert'}, dimensions={0} | all-to-all | bytes 1310720 | tf_op jit(solution)/shard_map/all_to_all | solution.py:118
  43.2 0.1 fusion.11
  43.3 0.1 stack_reshape.7
  43.4 0.0 copy-start.2
  43.4 0.0 copy-start.3
  43.5 0.0 copy-start.4
  43.5 0.1 stack_reshape.6
  43.6 0.9 pad_maximum_fusion.1
  44.5 0.0 all-gather.2.cloned.1.call-update
  44.5 0.0 reduce-scatter.2.cloned.1.call-start
  44.6 0.0 copy-done.2
  44.6 0.0 copy-done.3
  44.6 0.3 copy-done.4
  44.9 0.1 pad_maximum_fusion.refs_0_
  45.0 3.1 %collective-permute-start = (bf16[3,192,1024]{2,1,0:T(8,128)(2,1)S(1)}, bf16[3,192,1024]{2,1,0:T(8,128)(2,1)S(1)}, u32[]{:S(2)}, u32[]{:S(2)}) collective-permute-start(bf16[3,192,1024]{2,1,0:T(8,128)(2,1)S(1)} %pad_maximum_fusion.refs_0_), channel_id=1, source_target_pairs={{0,128},{128,256},{256,384},{384,0},{1,129},{129,257},{257,385},{3... | collective-permute-start | bytes 3538952 | tf_op jit(solution)/shard_map/ppermute | solution.py:75
  48.2 4.4 %collective-permute-start.1 = (bf16[3,192,1024]{2,1,0:T(8,128)(2,1)S(1)}, bf16[3,192,1024]{2,1,0:T(8,128)(2,1)}, u32[]{:S(2)}, u32[]{:S(2)}) collective-permute-start(bf16[3,192,1024]{2,1,0:T(8,128)(2,1)S(1)} %pad_maximum_fusion.refs_0_), channel_id=1, source_target_pairs={{0,256},{128,384},{256,0},{384,128},{1,257},{129,385},{257,1},{385... | collective-permute-start | bytes 3538952 | tf_op jit(solution)/shard_map/ppermute | solution.py:75
  52.5 3.1 %collective-permute-start.2 = (bf16[3,192,1024]{2,1,0:T(8,128)(2,1)S(1)}, bf16[3,192,1024]{2,1,0:T(8,128)(2,1)}, u32[]{:S(2)}, u32[]{:S(2)}) collective-permute-start(bf16[3,192,1024]{2,1,0:T(8,128)(2,1)S(1)} %pad_maximum_fusion.refs_0_), channel_id=1, source_target_pairs={{0,384},{128,0},{256,128},{384,256},{1,385},{129,1},{257,129},{385... | collective-permute-start | bytes 3538952 | tf_op jit(solution)/shard_map/ppermute | solution.py:75
  55.7 0.1 reshape_reshape_squeeze.4.gate_ref
  55.8 20.2 %collective-permute-done.refs_1_ = bf16[3,192,1024]{2,1,0:T(8,128)(2,1)S(1)} collective-permute-done((bf16[3,192,1024]{2,1,0:T(8,128)(2,1)S(1)}, bf16[3,192,1024]{2,1,0:T(8,128)(2,1)S(1)}, u32[]{:S(2)}, u32[]{:S(2)}) %collective-permute-start) | collective-permute-done | bytes 1179680 | tf_op jit(solution)/shard_map/ppermute | solution.py:75
  76.0 26.3 %collective-permute-done.1.refs_2_ = bf16[3,192,1024]{2,1,0:T(8,128)(2,1)} collective-permute-done((bf16[3,192,1024]{2,1,0:T(8,128)(2,1)S(1)}, bf16[3,192,1024]{2,1,0:T(8,128)(2,1)}, u32[]{:S(2)}, u32[]{:S(2)}) %collective-permute-start.1) | collective-permute-done | bytes 1179680 | tf_op jit(solution)/shard_map/ppermute | solution.py:75
  102.2 1.4 collective-permute-done.2.refs_3_
  103.6 2.0 %all-gather.2.cloned.1.call-done.rows_ref = bf16[2,304,4096]{2,1,0:T(8,128)(2,1)} async-done(((bf16[2,304,512]{2,1,0:T(8,128)(2,1)}), bf16[2,304,4096]{2,1,0:T(8,128)(2,1)}) %all-gather.2.cloned.1.call-update) | async-done | bytes 4980752 | tf_op jit(solution)/shard_map/all_gather | solution.py:127
  105.6 9.9 %shard_map.95 = (bf16[8,304,512]{2,1,0:T(8,128)(2,1)}, bf16[192,4096]{1,0:T(8,128)(2,1)}) custom-call(s32[1]{0:T(128)} %bitcast.me_ref, bf16[2,304,4096]{2,1,0:T(8,128)(2,1)} %all-gather.2.cloned.1.call-done.rows_ref, bf16[304,1]{1,0:T(8,128)(2,1)S(1)} %reshape_reshape_squeeze.4.gate_ref, bf16[3,192,1024]{2,1,0:T(8,128)(2,1)S(1)} %pad_maximum_fusion.refs_0_, ...), custom_call_target="tpu_custom_call" | custom-call | tf_op jit(solution)/shard_map/pallas_call | solution.py:58
  115.5 0.0 copy-start.1
  115.5 0.0 reduce-scatter.2.cloned.1.call-update
  115.6 1.3 copy-done.1
  117.0 1.2 reshape.38
  118.1 3.3 %constant_dynamic-slice_fusion.3 = (bf16[192,1,1024]{2,1,0:T(2,128)(2,1)S(1)}, bf16[192,1,1024]{2,1,0:T(2,128)(2,1)S(1)}, bf16[192,1,1024]{2,1,0:T(2,128)(2,1)S(1)}, bf16[192,1,1024]{2,1,0:T(2,128)(2,1)S(1)}) fusion(bf16[192,4,1024]{2,1,0:T(4,128)(2,1)S(1)} %reshape.38, s32[]{:T(128)S(6)} %select_n.48, s32[]{:T(128)S(6)} %select_n.52, s32[]{:T(128)S(6)} %select_n.50, ...), kind=kLoop, calls=%fused_computation.30 | loop fusion | bytes 3145744 | tf_op jit(solution)/shard_map/jit(_take) | solution.py:84
  121.4 0.2 fusion.7
  121.6 4.3 %collective-permute-start.5 = (bf16[192,1024]{1,0:T(8,128)(2,1)S(1)}, bf16[192,1024]{1,0:T(8,128)(2,1)S(1)}, u32[]{:S(2)}, u32[]{:S(2)}) collective-permute-start(bf16[192,1024]{1,0:T(8,128)(2,1)S(1)} %fusion.7), channel_id=1, source_target_pairs={{0,384},{128,0},{256,128},{384,256},{1,385},{129,1},{257,129},{385... | collective-permute-start | bytes 1179656 | tf_op jit(solution)/shard_map/ppermute | solution.py:87
  125.9 0.2 fusion.8
  126.1 2.5 %collective-permute-start.4 = (bf16[192,1024]{1,0:T(8,128)(2,1)S(1)}, bf16[192,1024]{1,0:T(8,128)(2,1)S(1)}, u32[]{:S(2)}, u32[]{:S(2)}) collective-permute-start(bf16[192,1024]{1,0:T(8,128)(2,1)S(1)} %fusion.8), channel_id=1, source_target_pairs={{0,256},{128,384},{256,0},{384,128},{1,257},{129,385},{257,1},{385... | collective-permute-start | bytes 1179656 | tf_op jit(solution)/shard_map/ppermute | solution.py:87
  128.6 0.9 fusion.9
  129.5 2.5 %collective-permute-start.3 = (bf16[192,1024]{1,0:T(8,128)(2,1)}, bf16[192,1024]{1,0:T(8,128)(2,1)S(1)}, u32[]{:S(2)}, u32[]{:S(2)}) collective-permute-start(bf16[192,1024]{1,0:T(8,128)(2,1)} %fusion.9), channel_id=1, source_target_pairs={{0,128},{128,256},{256,384},{384,0},{1,129},{129,257},{257,385},{3... | collective-permute-start | bytes 1179656 | tf_op jit(solution)/shard_map/ppermute | solution.py:87
  132.0 24.8 %reduce-scatter.2.cloned.1.call-done = bf16[1,304,512]{2,1,0:T(8,128)(2,1)} async-done(((bf16[8,304,512]{2,1,0:T(8,128)(2,1)}), bf16[1,304,512]{2,1,0:T(8,128)(2,1)}) %reduce-scatter.2.cloned.1.call-update) | async-done | bytes 311312 | tf_op jit(solution)/shard_map/reduce_scatter | solution.py:133
  156.8 1.8 reshape_squeeze.3
  158.6 11.9 %all-to-all-start.1 = ((bf16[16,19,512]{2,1,0:T(8,128)(2,1)}), bf16[16,19,512]{2,1,0:T(8,128)(2,1)S(1)}, u32[]{:S(2)}, u32[]{:S(2)}) async-start(bf16[16,19,512]{2,1,0:T(8,128)(2,1)} %reshape_squeeze.3), calls=%async_computation.2 | async-start | bytes 786432 | tf_op jit(solution)/shard_map/all_to_all | solution.py:134
  170.5 0.0 collective-permute-done.5
  170.5 0.0 collective-permute-done.4
  170.5 0.0 collective-permute-done.3
  170.5 1.1 fusion.6
  171.7 13.4 %all-to-all-done.1 = bf16[16,19,512]{2,1,0:T(8,128)(2,1)S(1)} async-done(((bf16[16,19,512]{2,1,0:T(8,128)(2,1)}), bf16[16,19,512]{2,1,0:T(8,128)(2,1)S(1)}, u32[]{:S(2)}, u32[]{:S(2)}) %all-to-all-start.1) | async-done | bytes 311328 | tf_op jit(solution)/shard_map/all_to_all | solution.py:134
  185.1 0.1 reshape.37
  185.2 0.9 convolution_convert_fusion.2
  (1 shorter events, 0.0 us)
Async XLA Ops:
  7.2 2.9 %copy-start = (bf16[152,512]{1,0:T(8,128)(2,1)S(1)}, bf16[152,512]{1,0:T(8,128)(2,1)}, u32[]{:S(2)}) copy-start(bf16[152,512]{1,0:T(8,128)(2,1)} %param.11) | copy-start | bytes 466948
  7.2 3.4 %copy-start.5 = (bf16[152,512]{1,0:T(8,128)(2,1)S(1)}, bf16[152,512]{1,0:T(8,128)(2,1)}, u32[]{:S(2)}) copy-start(bf16[152,512]{1,0:T(8,128)(2,1)} %param.10) | copy-start | bytes 466948
  7.2 98.4 %all-gather.2.cloned.1.call-start = ((), (), s32[]{:S(2)}) async-start(), calls=%async_computation.3 | async-start | bytes 5603328 | tf_op jit(solution)/shard_map/all_gather | solution.py:127
  43.4 1.1 copy-start.2
  43.4 1.1 copy-start.3
  43.5 1.4 copy-start.4
  44.5 112.2 %reduce-scatter.2.cloned.1.call-start = ((), (), s32[]{:S(2)}) async-start(), calls=%async_computation.4 | async-start | bytes 2801664 | tf_op jit(solution)/shard_map/reduce_scatter | solution.py:133
  45.0 30.9 %collective-permute-start = (bf16[3,192,1024]{2,1,0:T(8,128)(2,1)S(1)}, bf16[3,192,1024]{2,1,0:T(8,128)(2,1)S(1)}, u32[]{:S(2)}, u32[]{:S(2)}) collective-permute-start(bf16[3,192,1024]{2,1,0:T(8,128)(2,1)S(1)} %pad_maximum_fusion.refs_0_), channel_id=1, source_target_pairs={{0,128},{128,256},{256,384},{384,0},{1,129},{129,257},{257,385},{3... | collective-permute-start | bytes 3538952 | tf_op jit(solution)/shard_map/ppermute | solution.py:75
  48.2 54.1 %collective-permute-start.1 = (bf16[3,192,1024]{2,1,0:T(8,128)(2,1)S(1)}, bf16[3,192,1024]{2,1,0:T(8,128)(2,1)}, u32[]{:S(2)}, u32[]{:S(2)}) collective-permute-start(bf16[3,192,1024]{2,1,0:T(8,128)(2,1)S(1)} %pad_maximum_fusion.refs_0_), channel_id=1, source_target_pairs={{0,256},{128,384},{256,0},{384,128},{1,257},{129,385},{257,1},{385... | collective-permute-start | bytes 3538952 | tf_op jit(solution)/shard_map/ppermute | solution.py:75
  52.5 51.1 %collective-permute-start.2 = (bf16[3,192,1024]{2,1,0:T(8,128)(2,1)S(1)}, bf16[3,192,1024]{2,1,0:T(8,128)(2,1)}, u32[]{:S(2)}, u32[]{:S(2)}) collective-permute-start(bf16[3,192,1024]{2,1,0:T(8,128)(2,1)S(1)} %pad_maximum_fusion.refs_0_), channel_id=1, source_target_pairs={{0,384},{128,0},{256,128},{384,256},{1,385},{129,1},{257,129},{385... | collective-permute-start | bytes 3538952 | tf_op jit(solution)/shard_map/ppermute | solution.py:75
  115.5 1.4 copy-start.1
  121.6 48.9 %collective-permute-start.5 = (bf16[192,1024]{1,0:T(8,128)(2,1)S(1)}, bf16[192,1024]{1,0:T(8,128)(2,1)S(1)}, u32[]{:S(2)}, u32[]{:S(2)}) collective-permute-start(bf16[192,1024]{1,0:T(8,128)(2,1)S(1)} %fusion.7), channel_id=1, source_target_pairs={{0,384},{128,0},{256,128},{384,256},{1,385},{129,1},{257,129},{385... | collective-permute-start | bytes 1179656 | tf_op jit(solution)/shard_map/ppermute | solution.py:87
  126.1 44.4 %collective-permute-start.4 = (bf16[192,1024]{1,0:T(8,128)(2,1)S(1)}, bf16[192,1024]{1,0:T(8,128)(2,1)S(1)}, u32[]{:S(2)}, u32[]{:S(2)}) collective-permute-start(bf16[192,1024]{1,0:T(8,128)(2,1)S(1)} %fusion.8), channel_id=1, source_target_pairs={{0,256},{128,384},{256,0},{384,128},{1,257},{129,385},{257,1},{385... | collective-permute-start | bytes 1179656 | tf_op jit(solution)/shard_map/ppermute | solution.py:87
  129.5 41.0 %collective-permute-start.3 = (bf16[192,1024]{1,0:T(8,128)(2,1)}, bf16[192,1024]{1,0:T(8,128)(2,1)S(1)}, u32[]{:S(2)}, u32[]{:S(2)}) collective-permute-start(bf16[192,1024]{1,0:T(8,128)(2,1)} %fusion.9), channel_id=1, source_target_pairs={{0,128},{128,256},{256,384},{384,0},{1,129},{129,257},{257,385},{3... | collective-permute-start | bytes 1179656 | tf_op jit(solution)/shard_map/ppermute | solution.py:87
  158.6 26.5 %all-to-all-start.1 = ((bf16[16,19,512]{2,1,0:T(8,128)(2,1)}), bf16[16,19,512]{2,1,0:T(8,128)(2,1)S(1)}, u32[]{:S(2)}, u32[]{:S(2)}) async-start(bf16[16,19,512]{2,1,0:T(8,128)(2,1)} %reshape_squeeze.3), calls=%async_computation.2 | async-start | bytes 786432 | tf_op jit(solution)/shard_map/all_to_all | solution.py:134
Sparse Core Ops, SparseCore 0:
  44.6 60.9 all-gather.1
  115.7 41.0 reduce-scatter.1

commit v11 on v8

--- a/solution.py
+++ b/solution.py
@@ -11,7 +11,7 @@
 def _expert_kernel(me_ref, rows_ref, gate_ref, *refs):
     size = len(refs) - 2
     w_refs = refs[:size]
-    q_ref, term_ref = refs[size:]
+    q_ref, hidden_ref = refs[size:]
     quarter = w_refs[0].shape[2]
     me = me_ref[0]
     nt = (((1,), (1,)), ((), ()))
@@ -39,11 +39,7 @@
         part = jnp.dot(d_gate_b, w_refs[k][0], preferred_element_type=jnp.float32)
         part = part + jnp.dot(d_up_b, w_refs[k][1], preferred_element_type=jnp.float32)
         q_ref[:, pl.ds(start, quarter)] = part.astype(jnp.bfloat16)
-    hidden_t = hidden.T.astype(jnp.bfloat16)
-    scaled = (gate_f * rows_ref[1].astype(jnp.float32)).astype(jnp.bfloat16)
-    term_ref[...] = jnp.dot(hidden_t, scaled, preferred_element_type=jnp.float32).astype(
-        jnp.bfloat16
-    )
+    hidden_ref[...] = hidden.astype(jnp.bfloat16)
 
 
 def expert_kernel(me, rows, gate_col, pieces):
@@ -54,7 +50,7 @@
         _expert_kernel,
         out_shape=(
             jax.ShapeDtypeStruct((slots, width), jnp.bfloat16),
-            jax.ShapeDtypeStruct((ffb, width), jnp.bfloat16),
+            jax.ShapeDtypeStruct((slots, ffb), jnp.bfloat16),
         ),
         in_specs=[pl.BlockSpec(memory_space=pltpu.SMEM)]
         + [pl.BlockSpec(memory_space=vmem)] * (2 + len(pieces)),
@@ -121,9 +117,15 @@
     )
     full = lax.all_gather(pair, "etp", axis=2, tiled=True)
     stack = jnp.stack([gate_w[0].T, up_w[0].T, down_w[0]], axis=0)
-    d_part_b, term_b = expert_kernel(lax.axis_index("dp"), full, recv_gate, pieces_dp(stack))
-    down_grad = scatter_sum_dp(term_b)[None]
+    d_part_b, hidden_b = expert_kernel(lax.axis_index("dp"), full, recv_gate, pieces_dp(stack))
     summed = lax.psum_scatter(d_part_b, "etp", scatter_dimension=1, tiled=True)
+    scaled = (recv_gate.astype(jnp.float32)[:, None] * full[1].astype(jnp.float32)).astype(
+        jnp.bfloat16
+    )
+    term = lax.dot_general(
+        hidden_b, scaled, (((0,), (0,)), ((), ())), preferred_element_type=jnp.float32
+    )
+    down_grad = scatter_sum_dp(term.astype(jnp.bfloat16))[None]
     returned = lax.all_to_all(
         summed.reshape(width, CAP, narrow), "expert", split_axis=0, concat_axis=0, tiled=True
     ).reshape(slots, narrow)

time: 193 us -> 193 us (level)
  matrix products: 1.5 us -> 4.29 us
    ppermute x3, waiting for transfers between devices: 47.8 us -> 51.6 us  [pieces_dp(): lax.ppermute(piece, 'dp', [(i, (i + shift) % size) for i in range(size)])]
    dot_general x0 -> x1, matrix products: none -> 2.79 us  [local(): lax.dot_general(hidden_b, scaled, (((0,), (0,)), ((), ())), preferred_ele...]
    reduce_scatter x1, waiting for transfers between devices: 24.7 us -> 22.1 us  [local(): summed = lax.psum_scatter(d_part_b, 'etp', scatter_dimension=1, tiled=True)]
    all_gather x1, waiting for transfers between devices: 2.04 us -> 0.01 us  [local(): full = lax.all_gather(pair, 'etp', axis=2, tiled=True)]
  transfers between devices with their start and end apart: 9 -> 9, of which waited for: 6 -> 4; matrix products, arithmetic and copies ran while one was open for 5% -> 6% of each run, Pallas kernels for 0% -> 0%
where the time goes in v11:
time: 193 us; the launch traced here: 192 us
  waiting for transfers between devices  87.1 us (45%)
  blocking collectives  31.9 us (17%)
  starting transfers between devices  31.6 us (16%)
  between operations  14.4 us (7%)
  Pallas kernels  9.36 us (5%)
  local copies, waits for them, and re-layouts  8.33 us (4%)
  other arithmetic  5.55 us (3%)
  matrix products  4.29 us (2%)
    ppermute x3, waiting for transfers between devices, pieces_dp(): lax.ppermute(piece, 'dp', [(i, (i + shift) % size) for i in range(size)])  51.6 us
    all_to_all x1, blocking collectives, local(): lax.all_to_all(block, 'expert', split_axis=0, concat_axis=0, tiled=True)  31.9 us
    reduce_scatter x1, waiting for transfers between devices, local(): summed = lax.psum_scatter(d_part_b, 'etp', scatter_dimension=1, tiled=True)  22.1 us
    all_to_all x1, waiting for transfers between devices, local(): lax.all_to_all(summed.reshape(width, CAP, narrow), 'expert', split_axis=0...  13.4 us
    all_to_all x1, starting transfers between devices, local(): lax.all_to_all(summed.reshape(width, CAP, narrow), 'expert', split_axis=0...  12.5 us
    ppermute x3, starting transfers between devices, scatter_sum_dp(): lax.ppermute(outgoing, 'dp', [(i, (i + shift) % size) for i in range(size)])  9.67 us
    pallas_call x1, Pallas kernels, expert_kernel(): pl.pallas_call(_expert_kernel, out_shape=(jax.ShapeDtypeStruct((slots, wi...  9.36 us
    ppermute x3, starting transfers between devices, pieces_dp(): lax.ppermute(piece, 'dp', [(i, (i + shift) % size) for i in range(size)])  9.35 us
  transfers between devices with their start and end apart: 9, of which 4 were waited for; matrix products, arithmetic and copies ran while one was open for 6% of the time, Pallas kernels for 0%

profile of v11, /device:TPU:1, one launch (start us, length us, event | category | flops | bytes accessed | tf_op | source)
XLA Modules:
  0.0 192.4 jit_solution(17729945969189654179)
XLA Ops:
  7.2 0.0 copy-start
  7.2 0.0 copy-start.4
  7.2 0.0 all-gather.2.cloned.1.call-start
  7.2 0.8 add_select_fusion
  8.0 0.1 copy.35
  8.1 0.7 fusion.3
  8.8 0.8 copy.36
  9.6 0.4 select_reduce_fusion
  10.0 0.1 convert_element_type.84
  10.1 0.0 copy-done
  10.1 0.3 convolution_convert_fusion.1
  10.4 0.1 reshape.48
  10.5 0.0 copy-done.4
  10.5 0.3 convolution_convert_fusion.2
  10.8 0.1 reshape.47
  11.0 0.1 pad.15.clone
  11.0 0.3 fusion.8
  11.3 31.9 %all_to_all.10 = bf16[16,40,512]{2,1,0:T(8,128)(2,1)S(1)} all-to-all(bf16[16,40,512]{2,1,0:T(8,128)(2,1)S(1)} %fusion.8), channel_id=1, replica_groups=mesh['dp'=4,'expert'=16,'etp'=8] {'expert'}, dimensions={0} | all-to-all | bytes 1310720 | tf_op jit(solution)/shard_map/all_to_all | solution.py:109
  43.2 0.1 fusion.14
  43.3 0.0 copy-start.1
  43.3 0.0 copy-start.2
  43.3 0.0 copy-start.3
  43.3 0.1 stack_reshape.6
  43.5 0.1 stack_reshape.7
  43.6 0.9 pad_maximum_fusion.1
  44.5 0.0 all-gather.2.cloned.1.call-update
  44.5 0.0 reduce-scatter.2.cloned.1.call-start
  44.6 0.0 copy-done.1
  44.6 0.0 copy-done.2
  44.6 0.0 copy-done.3
  44.6 0.1 pad_maximum_fusion.refs_0_
  44.7 4.4 %collective-permute-start.2 = (bf16[3,192,1024]{2,1,0:T(8,128)(2,1)S(1)}, bf16[3,192,1024]{2,1,0:T(8,128)(2,1)S(1)}, u32[]{:S(2)}, u32[]{:S(2)}) collective-permute-start(bf16[3,192,1024]{2,1,0:T(8,128)(2,1)S(1)} %pad_maximum_fusion.refs_0_), channel_id=1, source_target_pairs={{0,384},{128,0},{256,128},{384,256},{1,385},{129,1},{257,129},{385... | collective-permute-start | bytes 3538952 | tf_op jit(solution)/shard_map/ppermute | solution.py:66
  49.1 2.4 %collective-permute-start.1 = (bf16[3,192,1024]{2,1,0:T(8,128)(2,1)S(1)}, bf16[3,192,1024]{2,1,0:T(8,128)(2,1)}, u32[]{:S(2)}, u32[]{:S(2)}) collective-permute-start(bf16[3,192,1024]{2,1,0:T(8,128)(2,1)S(1)} %pad_maximum_fusion.refs_0_), channel_id=1, source_target_pairs={{0,256},{128,384},{256,0},{384,128},{1,257},{129,385},{257,1},{385... | collective-permute-start | bytes 3538952 | tf_op jit(solution)/shard_map/ppermute | solution.py:66
  51.6 2.5 %collective-permute-start = (bf16[3,192,1024]{2,1,0:T(8,128)(2,1)S(1)}, bf16[3,192,1024]{2,1,0:T(8,128)(2,1)}, u32[]{:S(2)}, u32[]{:S(2)}) collective-permute-start(bf16[3,192,1024]{2,1,0:T(8,128)(2,1)S(1)} %pad_maximum_fusion.refs_0_), channel_id=1, source_target_pairs={{0,128},{128,256},{256,384},{384,0},{1,129},{129,257},{257,385},{3... | collective-permute-start | bytes 3538952 | tf_op jit(solution)/shard_map/ppermute | solution.py:66
  54.1 0.1 reshape_reshape_squeeze.4.gate_ref
  54.3 45.5 %collective-permute-done.2.refs_3_ = bf16[3,192,1024]{2,1,0:T(8,128)(2,1)S(1)} collective-permute-done((bf16[3,192,1024]{2,1,0:T(8,128)(2,1)S(1)}, bf16[3,192,1024]{2,1,0:T(8,128)(2,1)S(1)}, u32[]{:S(2)}, u32[]{:S(2)}) %collective-permute-start.2) | collective-permute-done | bytes 1179680 | tf_op jit(solution)/shard_map/ppermute | solution.py:66
  99.8 0.0 collective-permute-done.1.refs_2_
  99.8 6.1 %collective-permute-done.refs_1_ = bf16[3,192,1024]{2,1,0:T(8,128)(2,1)} collective-permute-done((bf16[3,192,1024]{2,1,0:T(8,128)(2,1)S(1)}, bf16[3,192,1024]{2,1,0:T(8,128)(2,1)}, u32[]{:S(2)}, u32[]{:S(2)}) %collective-permute-start) | collective-permute-done | bytes 1179680 | tf_op jit(solution)/shard_map/ppermute | solution.py:66
  105.8 0.0 all-gather.2.cloned.1.call-done.rows_ref
  105.8 9.4 %shard_map.95 = (bf16[304,4096]{1,0:T(8,128)(2,1)}, bf16[304,192]{1,0:T(8,128)(2,1)S(1)}) custom-call(s32[1]{0:T(128)} %bitcast.me_ref, bf16[2,304,4096]{2,1,0:T(8,128)(2,1)} %all-gather.2.cloned.1.call-done.rows_ref, bf16[304,1]{1,0:T(8,128)(2,1)S(1)} %reshape_reshape_squeeze.4.gate_ref, bf16[3,192,1024]{2,1,0:T(8,128)(2,1)S(1)} %pad_maximum_fusion.refs_0_, ...), custom_call_target="tpu_custom_call" | custom-call | tf_op jit(solution)/shard_map/pallas_call | solution.py:49
  115.2 0.0 reduce-scatter.2.cloned.1.call-update
  115.3 0.1 reshape.115
  115.4 2.8 %convolution_convert_fusion = bf16[192,4096]{1,0:T(8,128)(2,1)S(1)} fusion(bf16[304,192]{1,0:T(8,128)(2,1)S(1)} %get-tuple-element.6, bf16[2,304,4096]{2,1,0:T(8,128)(2,1)} %all-gather.2.cloned.1.call-done.rows_ref, f32[304]{0:T(512)S(1)} %reshape.115), kind=kOutput, calls=%fused_computation | convolution fusion | flops 482672640 | bytes 4181184 | tf_op jit(solution)/shard_map/dot_general | solution.py:125
  118.2 1.2 reshape.51
  119.4 3.3 %constant_dynamic-slice_fusion.3 = (bf16[192,1,1024]{2,1,0:T(2,128)(2,1)S(1)}, bf16[192,1,1024]{2,1,0:T(2,128)(2,1)S(1)}, bf16[192,1,1024]{2,1,0:T(2,128)(2,1)S(1)}, bf16[192,1,1024]{2,1,0:T(2,128)(2,1)S(1)}) fusion(bf16[192,4,1024]{2,1,0:T(4,128)(2,1)S(1)} %reshape.51, s32[]{:T(128)S(6)} %select_n.48, s32[]{:T(128)S(6)} %select_n.52, s32[]{:T(128)S(6)} %select_n.50, ...), kind=kLoop, calls=%fused_computation.36 | loop fusion | bytes 3145744 | tf_op jit(solution)/shard_map/jit(_take) | solution.py:75
  122.7 0.2 fusion.10
  122.9 4.1 %collective-permute-start.5 = (bf16[192,1024]{1,0:T(8,128)(2,1)S(1)}, bf16[192,1024]{1,0:T(8,128)(2,1)S(1)}, u32[]{:S(2)}, u32[]{:S(2)}) collective-permute-start(bf16[192,1024]{1,0:T(8,128)(2,1)S(1)} %fusion.10), channel_id=1, source_target_pairs={{0,384},{128,0},{256,128},{384,256},{1,385},{129,1},{257,129},{385... | collective-permute-start | bytes 1179656 | tf_op jit(solution)/shard_map/ppermute | solution.py:78
  127.0 0.2 fusion.12
  127.1 1.9 collective-permute-start.3
  129.1 0.9 fusion.11
  130.0 3.6 %collective-permute-start.4 = (bf16[192,1024]{1,0:T(8,128)(2,1)}, bf16[192,1024]{1,0:T(8,128)(2,1)S(1)}, u32[]{:S(2)}, u32[]{:S(2)}) collective-permute-start(bf16[192,1024]{1,0:T(8,128)(2,1)} %fusion.11), channel_id=1, source_target_pairs={{0,256},{128,384},{256,0},{384,128},{1,257},{129,385},{257,1},{385... | collective-permute-start | bytes 1179656 | tf_op jit(solution)/shard_map/ppermute | solution.py:78
  133.6 22.1 %reduce-scatter.2.cloned.1.call-done = bf16[304,512]{1,0:T(8,128)(2,1)} async-done(((bf16[304,4096]{1,0:T(8,128)(2,1)}), bf16[304,512]{1,0:T(8,128)(2,1)}) %reduce-scatter.2.cloned.1.call-update) | async-done | bytes 311312 | tf_op jit(solution)/shard_map/reduce_scatter | solution.py:121
  155.7 1.8 reshape.49
  157.5 12.5 %all-to-all-start.1 = ((bf16[16,19,512]{2,1,0:T(8,128)(2,1)}), bf16[16,19,512]{2,1,0:T(8,128)(2,1)S(1)}, u32[]{:S(2)}, u32[]{:S(2)}) async-start(bf16[16,19,512]{2,1,0:T(8,128)(2,1)} %reshape.49), calls=%async_computation.2 | async-start | bytes 786432 | tf_op jit(solution)/shard_map/all_to_all | solution.py:129
  170.0 0.0 collective-permute-done.5
  170.0 0.0 collective-permute-done.3
  170.0 0.0 collective-permute-done.4
  170.0 1.1 fusion.9
  171.2 13.4 %all-to-all-done.1 = bf16[16,19,512]{2,1,0:T(8,128)(2,1)S(1)} async-done(((bf16[16,19,512]{2,1,0:T(8,128)(2,1)}), bf16[16,19,512]{2,1,0:T(8,128)(2,1)S(1)}, u32[]{:S(2)}, u32[]{:S(2)}) %all-to-all-start.1) | async-done | bytes 311328 | tf_op jit(solution)/shard_map/all_to_all | solution.py:129
  184.6 0.1 reshape.50
  184.7 0.9 convolution_convert_fusion.3
  (2 shorter events, 0.1 us)
Async XLA Ops:
  7.2 2.9 %copy-start = (bf16[152,512]{1,0:T(8,128)(2,1)S(1)}, bf16[152,512]{1,0:T(8,128)(2,1)}, u32[]{:S(2)}) copy-start(bf16[152,512]{1,0:T(8,128)(2,1)} %param.11) | copy-start | bytes 466948
  7.2 3.4 %copy-start.4 = (bf16[152,512]{1,0:T(8,128)(2,1)S(1)}, bf16[152,512]{1,0:T(8,128)(2,1)}, u32[]{:S(2)}) copy-start(bf16[152,512]{1,0:T(8,128)(2,1)} %param.10) | copy-start | bytes 466948
  7.2 98.6 %all-gather.2.cloned.1.call-start = ((), (), s32[]{:S(2)}) async-start(), calls=%async_computation.3 | async-start | bytes 5603328 | tf_op jit(solution)/shard_map/all_gather | solution.py:118
  43.3 1.3 copy-start.1
  43.3 1.3 copy-start.2
  43.3 1.3 copy-start.3
  44.5 111.2 %reduce-scatter.2.cloned.1.call-start = ((), (), s32[]{:S(2)}) async-start(), calls=%async_computation.4 | async-start | bytes 2801664 | tf_op jit(solution)/shard_map/reduce_scatter | solution.py:121
  44.7 55.0 %collective-permute-start.2 = (bf16[3,192,1024]{2,1,0:T(8,128)(2,1)S(1)}, bf16[3,192,1024]{2,1,0:T(8,128)(2,1)S(1)}, u32[]{:S(2)}, u32[]{:S(2)}) collective-permute-start(bf16[3,192,1024]{2,1,0:T(8,128)(2,1)S(1)} %pad_maximum_fusion.refs_0_), channel_id=1, source_target_pairs={{0,384},{128,0},{256,128},{384,256},{1,385},{129,1},{257,129},{385... | collective-permute-start | bytes 3538952 | tf_op jit(solution)/shard_map/ppermute | solution.py:66
  49.1 50.6 %collective-permute-start.1 = (bf16[3,192,1024]{2,1,0:T(8,128)(2,1)S(1)}, bf16[3,192,1024]{2,1,0:T(8,128)(2,1)}, u32[]{:S(2)}, u32[]{:S(2)}) collective-permute-start(bf16[3,192,1024]{2,1,0:T(8,128)(2,1)S(1)} %pad_maximum_fusion.refs_0_), channel_id=1, source_target_pairs={{0,256},{128,384},{256,0},{384,128},{1,257},{129,385},{257,1},{385... | collective-permute-start | bytes 3538952 | tf_op jit(solution)/shard_map/ppermute | solution.py:66
  51.6 54.3 %collective-permute-start = (bf16[3,192,1024]{2,1,0:T(8,128)(2,1)S(1)}, bf16[3,192,1024]{2,1,0:T(8,128)(2,1)}, u32[]{:S(2)}, u32[]{:S(2)}) collective-permute-start(bf16[3,192,1024]{2,1,0:T(8,128)(2,1)S(1)} %pad_maximum_fusion.refs_0_), channel_id=1, source_target_pairs={{0,128},{128,256},{256,384},{384,0},{1,129},{129,257},{257,385},{3... | collective-permute-start | bytes 3538952 | tf_op jit(solution)/shard_map/ppermute | solution.py:66
  122.9 47.1 %collective-permute-start.5 = (bf16[192,1024]{1,0:T(8,128)(2,1)S(1)}, bf16[192,1024]{1,0:T(8,128)(2,1)S(1)}, u32[]{:S(2)}, u32[]{:S(2)}) collective-permute-start(bf16[192,1024]{1,0:T(8,128)(2,1)S(1)} %fusion.10), channel_id=1, source_target_pairs={{0,384},{128,0},{256,128},{384,256},{1,385},{129,1},{257,129},{385... | collective-permute-start | bytes 1179656 | tf_op jit(solution)/shard_map/ppermute | solution.py:78
  127.1 42.9 %collective-permute-start.3 = (bf16[192,1024]{1,0:T(8,128)(2,1)S(1)}, bf16[192,1024]{1,0:T(8,128)(2,1)S(1)}, u32[]{:S(2)}, u32[]{:S(2)}) collective-permute-start(bf16[192,1024]{1,0:T(8,128)(2,1)S(1)} %fusion.12), channel_id=1, source_target_pairs={{0,128},{128,256},{256,384},{384,0},{1,129},{129,257},{257,385},{3... | collective-permute-start | bytes 1179656 | tf_op jit(solution)/shard_map/ppermute | solution.py:78
  130.0 40.0 %collective-permute-start.4 = (bf16[192,1024]{1,0:T(8,128)(2,1)}, bf16[192,1024]{1,0:T(8,128)(2,1)S(1)}, u32[]{:S(2)}, u32[]{:S(2)}) collective-permute-start(bf16[192,1024]{1,0:T(8,128)(2,1)} %fusion.11), channel_id=1, source_target_pairs={{0,256},{128,384},{256,0},{384,128},{1,257},{129,385},{257,1},{385... | collective-permute-start | bytes 1179656 | tf_op jit(solution)/shard_map/ppermute | solution.py:78
  157.5 27.0 %all-to-all-start.1 = ((bf16[16,19,512]{2,1,0:T(8,128)(2,1)}), bf16[16,19,512]{2,1,0:T(8,128)(2,1)S(1)}, u32[]{:S(2)}, u32[]{:S(2)}) async-start(bf16[16,19,512]{2,1,0:T(8,128)(2,1)} %reshape.49), calls=%async_computation.2 | async-start | bytes 786432 | tf_op jit(solution)/shard_map/all_to_all | solution.py:129
Sparse Core Ops, SparseCore 0:
  44.6 60.9 all-gather.1
  115.3 40.3 reduce-scatter.1

commit v12 on v11

--- a/solution.py
+++ b/solution.py
@@ -8,7 +8,7 @@
 CAP = 19
 
 
-def _expert_kernel(me_ref, rows_ref, gate_ref, *refs):
+def _expert_kernel(me_ref, x_ref, dy_ref, gate_ref, *refs):
     size = len(refs) - 2
     w_refs = refs[:size]
     q_ref, hidden_ref = refs[size:]
@@ -18,8 +18,8 @@
     gate_pre = None
     for k in range(size):
         start = pl.multiple_of(((me + size - k) % size) * quarter, quarter)
-        f_k = rows_ref[0, :, pl.ds(start, quarter)]
-        g_k = rows_ref[1, :, pl.ds(start, quarter)]
+        f_k = x_ref[:, pl.ds(start, quarter)]
+        g_k = dy_ref[:, pl.ds(start, quarter)]
         a = lax.dot_general(f_k, w_refs[k][0], nt, preferred_element_type=jnp.float32)
         b = lax.dot_general(f_k, w_refs[k][1], nt, preferred_element_type=jnp.float32)
         c = lax.dot_general(g_k, w_refs[k][2], nt, preferred_element_type=jnp.float32)
@@ -42,8 +42,8 @@
     hidden_ref[...] = hidden.astype(jnp.bfloat16)
 
 
-def expert_kernel(me, rows, gate_col, pieces):
-    _, slots, width = rows.shape
+def expert_kernel(me, feats, grads, gate_col, pieces):
+    slots, width = feats.shape
     ffb = pieces[0].shape[1]
     vmem = pltpu.VMEM
     return pl.pallas_call(
@@ -53,18 +53,43 @@
             jax.ShapeDtypeStruct((slots, ffb), jnp.bfloat16),
         ),
         in_specs=[pl.BlockSpec(memory_space=pltpu.SMEM)]
-        + [pl.BlockSpec(memory_space=vmem)] * (2 + len(pieces)),
+        + [pl.BlockSpec(memory_space=vmem)] * (3 + len(pieces)),
         out_specs=(pl.BlockSpec(memory_space=vmem), pl.BlockSpec(memory_space=vmem)),
         compiler_params=pltpu.CompilerParams(vmem_limit_bytes=48 * 1024 * 1024),
-    )(me.reshape(1), rows, gate_col.reshape(slots, 1), *pieces)
+    )(me.reshape(1), feats, grads, gate_col.reshape(slots, 1), *pieces)
+
+
+def shift(value, axis, step):
+    size = lax.axis_size(axis)
+    return lax.ppermute(value, axis, [(i, (i + step) % size) for i in range(size)])
 
 
 def pieces_dp(piece):
-    size = lax.axis_size("dp")
-    got = [piece]
-    for shift in range(1, size):
-        got.append(lax.ppermute(piece, "dp", [(i, (i + shift) % size) for i in range(size)]))
-    return got
+    assert lax.axis_size("dp") == 4
+    half = piece.shape[-1] // 2
+    from_left = shift(piece, "dp", 1)
+    from_right = shift(piece, "dp", -1)
+    far = jnp.concatenate(
+        [shift(from_left[..., :half], "dp", 1), shift(from_right[..., half:], "dp", -1)], axis=-1
+    )
+    return [piece, from_left, far, from_right]
+
+
+def ring_gather_etp(block):
+    size = lax.axis_size("etp")
+    me = lax.axis_index("etp")
+    narrow = block.shape[-1]
+    out = jnp.zeros(block.shape[:-1] + (size * narrow,), block.dtype)
+    out = lax.dynamic_update_slice_in_dim(out, block, me * narrow, axis=1)
+    right = block
+    left = block
+    for step in range(1, size // 2 + 1):
+        right = shift(right, "etp", 1)
+        out = lax.dynamic_update_slice_in_dim(out, right, ((me - step) % size) * narrow, axis=1)
+        if step < size - size // 2:
+            left = shift(left, "etp", -1)
+            out = lax.dynamic_update_slice_in_dim(out, left, ((me + step) % size) * narrow, axis=1)
+    return out
 
 
 def scatter_sum_dp(term_b):
@@ -108,18 +133,14 @@
     )
     recv = lax.all_to_all(block, "expert", split_axis=0, concat_axis=0, tiled=True)
     recv_gate = recv[:, CAP, :CAP].reshape(slots)
-    pair = jnp.stack(
-        [
-            recv[:, :CAP, :].reshape(slots, narrow),
-            recv[:, CAP + 1 : 2 * CAP + 1, :].reshape(slots, narrow),
-        ],
-        axis=0,
+    feats = lax.all_gather(recv[:, :CAP, :].reshape(slots, narrow), "etp", axis=1, tiled=True)
+    grads = ring_gather_etp(recv[:, CAP + 1 : 2 * CAP + 1, :].reshape(slots, narrow))
+    stack = jnp.stack([gate_w[0].T, up_w[0].T, down_w[0]], axis=0)
+    d_part_b, hidden_b = expert_kernel(
+        lax.axis_index("dp"), feats, grads, recv_gate, pieces_dp(stack)
     )
-    full = lax.all_gather(pair, "etp", axis=2, tiled=True)
-    stack = jnp.stack([gate_w[0].T, up_w[0].T, down_w[0]], axis=0)
-    d_part_b, hidden_b = expert_kernel(lax.axis_index("dp"), full, recv_gate, pieces_dp(stack))
     summed = lax.psum_scatter(d_part_b, "etp", scatter_dimension=1, tiled=True)
-    scaled = (recv_gate.astype(jnp.float32)[:, None] * full[1].astype(jnp.float32)).astype(
+    scaled = (recv_gate.astype(jnp.float32)[:, None] * grads.astype(jnp.float32)).astype(
         jnp.bfloat16
     )
     term = lax.dot_general(

time: 193 us -> 213 us (1.10)
  waiting for transfers between devices: 87.1 us -> 55.7 us
  starting transfers between devices: 31.6 us -> 58.7 us
  local copies, waits for them, and re-layouts: 8.33 us -> 28.6 us
    ppermute x3 -> x11, starting transfers between devices: 9.35 us -> 37.8 us  [shift(): lax.ppermute(value, axis, [(i, (i + step) % size) for i in range(size)])]
    ppermute x3 -> x11, waiting for transfers between devices: 51.6 us -> 23.9 us  [shift(): lax.ppermute(value, axis, [(i, (i + step) % size) for i in range(size)])]
    dynamic_update_slice x0 -> x8, local copies, waits for them, and re-layouts: none -> 10.1 us  [the longest x4 5.01 us: ring_gather_etp(): lax.dynamic_update_slice_in_dim(out, right, (me - step) % size * narrow,...]
    slice x1 -> x3, local copies, waits for them, and re-layouts: 0.11 us -> 3.81 us  [the longest x1 1.95 us: pieces_dp(): from_left[..., :half]]
    reduce_scatter x1, waiting for transfers between devices: 22.1 us -> 18.4 us  [local(): summed = lax.psum_scatter(d_part_b, 'etp', scatter_dimension=1, tiled=True)]
    reshape x0 -> x2, local copies, waits for them, and re-layouts: none -> 2.67 us  [the longest x1 1.83 us: local(): recv[:, CAP + 1:2 * CAP + 1, :].reshape(slots, narrow)]
  transfers between devices with their start and end apart: 9 -> 17, of which waited for: 4 -> 5; matrix products, arithmetic and copies ran while one was open for 6% -> 16% of each run, Pallas kernels for 0% -> 0%
where the time goes in v12:
time: 213 us; the launch traced here: 212 us
  starting transfers between devices  58.7 us (28%)
  waiting for transfers between devices  55.7 us (26%)
  blocking collectives  31.9 us (15%)
  local copies, waits for them, and re-layouts  28.6 us (13%)
  between operations  14.6 us (7%)
  Pallas kernels  9.07 us (4%)
  other arithmetic  6.97 us (3%)
  matrix products  6.39 us (3%)
    ppermute x11, starting transfers between devices, shift(): lax.ppermute(value, axis, [(i, (i + step) % size) for i in range(size)])  37.8 us
    all_to_all x1, blocking collectives, local(): lax.all_to_all(block, 'expert', split_axis=0, concat_axis=0, tiled=True)  31.9 us
    ppermute x11, waiting for transfers between devices, shift(): lax.ppermute(value, axis, [(i, (i + step) % size) for i in range(size)])  23.9 us
    reduce_scatter x1, waiting for transfers between devices, local(): summed = lax.psum_scatter(d_part_b, 'etp', scatter_dimension=1, tiled=True)  18.4 us
    all_to_all x1, waiting for transfers between devices, local(): lax.all_to_all(summed.reshape(width, CAP, narrow), 'expert', split_axis=0...  13.4 us
    all_to_all x1, starting transfers between devices, local(): lax.all_to_all(summed.reshape(width, CAP, narrow), 'expert', split_axis=0...  11.9 us
    pallas_call x1, Pallas kernels, expert_kernel(): pl.pallas_call(_expert_kernel, out_shape=(jax.ShapeDtypeStruct((slots, wi...  9.07 us
    ppermute x3, starting transfers between devices, scatter_sum_dp(): lax.ppermute(outgoing, 'dp', [(i, (i + shift) % size) for i in range(size)])  8.95 us
  transfers between devices with their start and end apart: 17, of which 5 were waited for; matrix products, arithmetic and copies ran while one was open for 16% of the time, Pallas kernels for 0%

profile of v12, /device:TPU:1, one launch (start us, length us, event | category | flops | bytes accessed | tf_op | source)
XLA Modules:
  0.0 211.8 jit_solution(16883582775575886713)
XLA Ops:
  7.2 0.7 add_select_fusion
  8.0 0.1 copy.35
  8.1 0.7 fusion.1
  8.8 0.3 convolution_convert_fusion.2
  9.1 0.1 reshape.51
  9.2 1.2 convolution_convert_fusion.1
  10.4 0.1 reshape.52
  10.5 0.1 copy.36
  10.6 0.4 select_reduce_fusion
  11.0 0.1 convert_element_type.79
  11.1 0.1 pad.15.clone
  11.2 0.3 fusion.6
  11.5 31.9 %all_to_all.10 = bf16[16,40,512]{2,1,0:T(8,128)(2,1)S(1)} all-to-all(bf16[16,40,512]{2,1,0:T(8,128)(2,1)S(1)} %fusion.6), channel_id=1, replica_groups=mesh['dp'=4,'expert'=16,'etp'=8] {'expert'}, dimensions={0} | all-to-all | bytes 1310720 | tf_op jit(solution)/shard_map/all_to_all | solution.py:134
  43.4 0.9 fusion.12
  44.2 0.8 reshape.53
  45.1 0.0 reduce-scatter.2.cloned.1.call-start
  45.1 1.1 pad_maximum_fusion.refs_0_
  46.3 4.4 %collective-permute-start.9 = (bf16[3,192,1024]{2,1,0:T(8,128)(2,1)S(1)}, bf16[3,192,1024]{2,1,0:T(8,128)(2,1)S(1)}, u32[]{:S(2)}, u32[]{:S(2)}) collective-permute-start(bf16[3,192,1024]{2,1,0:T(8,128)(2,1)S(1)} %pad_maximum_fusion.refs_0_), channel_id=1, source_target_pairs={{0,384},{128,0},{256,128},{384,256},{1,385},{129,1},{257,129},{385... | collective-permute-start | bytes 3538952 | tf_op jit(solution)/shard_map/ppermute | solution.py:64
  50.7 1.9 collective-permute-start.7
  52.6 1.8 reshape.54
  54.4 3.2 %collective-permute-start = (bf16[304,512]{1,0:T(8,128)(2,1)}, bf16[304,512]{1,0:T(8,128)(2,1)}, u32[]{:S(2)}, u32[]{:S(2)}) collective-permute-start(bf16[304,512]{1,0:T(8,128)(2,1)} %reshape.54), channel_id=1, source_target_pairs={{0,1},{1,2},{2,3},{3,4},{4,5},{5,6},{6,7},{7,0},{8,9},{9,10},{10,1... | collective-permute-start | bytes 933896 | tf_op jit(solution)/shard_map/ppermute | solution.py:64
  57.7 18.5 %collective-permute-done.9.refs_3_ = bf16[3,192,1024]{2,1,0:T(8,128)(2,1)S(1)} collective-permute-done((bf16[3,192,1024]{2,1,0:T(8,128)(2,1)S(1)}, bf16[3,192,1024]{2,1,0:T(8,128)(2,1)S(1)}, u32[]{:S(2)}, u32[]{:S(2)}) %collective-permute-start.9) | collective-permute-done | bytes 1179680 | tf_op jit(solution)/shard_map/ppermute | solution.py:64
  76.2 1.0 slice.33
  77.2 5.4 %collective-permute-start.10 = (bf16[3,192,512]{2,1,0:T(8,128)(2,1)}, bf16[3,192,512]{2,1,0:T(8,128)(2,1)}, u32[]{:S(2)}, u32[]{:S(2)}) collective-permute-start(bf16[3,192,512]{2,1,0:T(8,128)(2,1)} %slice.33), channel_id=1, source_target_pairs={{0,384},{128,0},{256,128},{384,256},{1,385},{129,1},{257,129},{385... | collective-permute-start | bytes 1769480 | tf_op jit(solution)/shard_map/ppermute | solution.py:64
  82.6 2.0 slice.32
  84.6 1.9 collective-permute-start.8
  86.5 5.1 %collective-permute-start.1 = (bf16[304,512]{1,0:T(8,128)(2,1)}, bf16[304,512]{1,0:T(8,128)(2,1)}, u32[]{:S(2)}, u32[]{:S(2)}) collective-permute-start(bf16[304,512]{1,0:T(8,128)(2,1)} %reshape.54), channel_id=1, source_target_pairs={{0,7},{1,0},{2,1},{3,2},{4,3},{5,4},{6,5},{7,6},{8,15},{9,8},{10,9... | collective-permute-start | bytes 933896 | tf_op jit(solution)/shard_map/ppermute | solution.py:64
  91.7 1.9 collective-permute-start.2
  93.7 0.1 reshape_reshape_squeeze.4.gate_ref
  93.8 1.7 broadcast_in_dim.42
  95.6 1.8 constant_dynamic-update-slice_fusion.7
  97.3 0.4 collective-permute-done.1
  97.7 5.3 %collective-permute-start.3 = (bf16[304,512]{1,0:T(8,128)(2,1)}, bf16[304,512]{1,0:T(8,128)(2,1)S(1)}, u32[]{:S(2)}, u32[]{:S(2)}) collective-permute-start(bf16[304,512]{1,0:T(8,128)(2,1)} %collective-permute-done.1), channel_id=1, source_target_pairs={{0,7},{1,0},{2,1},{3,2},{4,3},{5,4},{6,5},{7,6},{8,15},{9,8},{10,9... | collective-permute-start | bytes 933896 | tf_op jit(solution)/shard_map/ppermute | solution.py:64
  103.0 1.8 constant_dynamic-update-slice_fusion.6
  104.8 1.9 collective-permute-start.4
  106.7 1.7 constant_dynamic-update-slice_fusion.5
  108.5 1.4 pad_maximum_fusion.1.refs_2_
  109.8 4.6 %collective-permute-start.5 = (bf16[304,512]{1,0:T(8,128)(2,1)S(1)}, bf16[304,512]{1,0:T(8,128)(2,1)S(1)}, u32[]{:S(2)}, u32[]{:S(2)}) collective-permute-start(bf16[304,512]{1,0:T(8,128)(2,1)S(1)} %collective-permute-done.3), channel_id=1, source_target_pairs={{0,7},{1,0},{2,1},{3,2},{4,3},{5,4},{6,5},{7,6},{8,15},{9,8},{10,9... | collective-permute-start | bytes 933896 | tf_op jit(solution)/shard_map/ppermute | solution.py:64
  114.5 1.7 constant_dynamic-update-slice_fusion.4
  116.2 2.1 collective-permute-start.6
  118.3 0.8 constant_dynamic-update-slice_fusion.3
  119.1 0.8 constant_dynamic-update-slice_fusion.2
  119.8 0.8 constant_dynamic-update-slice_fusion.1
  120.6 4.9 %collective-permute-done.6 = bf16[304,512]{1,0:T(8,128)(2,1)S(1)} collective-permute-done((bf16[304,512]{1,0:T(8,128)(2,1)S(1)}, bf16[304,512]{1,0:T(8,128)(2,1)S(1)}, u32[]{:S(2)}, u32[]{:S(2)}) %collective-permute-start.6) | collective-permute-done | bytes 311328 | tf_op jit(solution)/shard_map/ppermute | solution.py:64
  125.6 0.8 constant_dynamic-update-slice_fusion.dy_ref
  126.3 1.3 copy-done.2
  127.6 9.1 %shard_map.95 = (bf16[304,4096]{1,0:T(8,128)(2,1)}, bf16[304,192]{1,0:T(8,128)(2,1)S(1)}) custom-call(s32[1]{0:T(128)} %bitcast.me_ref, bf16[304,4096]{1,0:T(8,128)(2,1)} %all-gather.2.cloned.1.call-done.x_ref, bf16[304,4096]{1,0:T(8,128)(2,1)} %constant_dynamic-update-slice_fusion.dy_ref, bf16[304,1]{1,0:T(8,128)(2,1)S(1)} %reshape_reshape_squeeze.4.gate_ref, ...), custom_call_target="tpu_custom_call" | custom-call | tf_op jit(solution)/shard_map/pallas_call | solution.py:49
  136.8 0.1 reshape.121
  136.9 4.0 %convolution_convert_fusion = bf16[192,4096]{1,0:T(8,128)(2,1)} fusion(bf16[304,192]{1,0:T(8,128)(2,1)S(1)} %get-tuple-element.6, bf16[304,4096]{1,0:T(8,128)(2,1)} %constant_dynamic-update-slice_fusion.dy_ref, f32[304]{0:T(512)S(1)} %reshape.121), kind=kOutput, calls=%fused_computation | convolution fusion | flops 482672640 | bytes 4181184 | tf_op jit(solution)/shard_map/dot_general | solution.py:146
  140.8 2.9 %reshape.57 = bf16[192,4,1024]{2,1,0:T(4,128)(2,1)S(1)} reshape(bf16[192,4096]{1,0:T(8,128)(2,1)} %convolution_convert_fusion) | data formatting | bytes 3145728 | tf_op jit(solution)/shard_map/reshape | solution.py:99
  143.7 3.3 %constant_dynamic-slice_fusion.3 = (bf16[192,1,1024]{2,1,0:T(2,128)(2,1)S(1)}, bf16[192,1,1024]{2,1,0:T(2,128)(2,1)S(1)}, bf16[192,1,1024]{2,1,0:T(2,128)(2,1)S(1)}, bf16[192,1,1024]{2,1,0:T(2,128)(2,1)S(1)}) fusion(bf16[192,4,1024]{2,1,0:T(4,128)(2,1)S(1)} %reshape.57, s32[]{:T(128)S(6)} %select_n.115, s32[]{:T(128)S(6)} %select_n.119, s32[]{:T(128)S(6)} %select_n.117, ...), kind=kLoop, calls=%fused_computation.34 | loop fusion | bytes 3145744 | tf_op jit(solution)/shard_map/jit(_take) | solution.py:100
  147.0 0.2 fusion.10
  147.2 1.9 collective-permute-start.11
  149.1 0.2 fusion.9
  149.3 4.9 %collective-permute-start.12 = (bf16[192,1024]{1,0:T(8,128)(2,1)S(1)}, bf16[192,1024]{1,0:T(8,128)(2,1)S(1)}, u32[]{:S(2)}, u32[]{:S(2)}) collective-permute-start(bf16[192,1024]{1,0:T(8,128)(2,1)S(1)} %fusion.9), channel_id=1, source_target_pairs={{0,256},{128,384},{256,0},{384,128},{1,257},{129,385},{257,1},{385... | collective-permute-start | bytes 1179656 | tf_op jit(solution)/shard_map/ppermute | solution.py:103
  154.2 0.9 fusion.8
  155.1 2.1 %collective-permute-start.13 = (bf16[192,1024]{1,0:T(8,128)(2,1)}, bf16[192,1024]{1,0:T(8,128)(2,1)S(1)}, u32[]{:S(2)}, u32[]{:S(2)}) collective-permute-start(bf16[192,1024]{1,0:T(8,128)(2,1)} %fusion.8), channel_id=1, source_target_pairs={{0,384},{128,0},{256,128},{384,256},{1,385},{129,1},{257,129},{385... | collective-permute-start | bytes 1179656 | tf_op jit(solution)/shard_map/ppermute | solution.py:103
  157.3 18.4 %reduce-scatter.2.cloned.1.call-done = bf16[304,512]{1,0:T(8,128)(2,1)} async-done(((bf16[304,4096]{1,0:T(8,128)(2,1)}), bf16[304,512]{1,0:T(8,128)(2,1)}) %reduce-scatter.2.cloned.1.call-update) | async-done | bytes 311312 | tf_op jit(solution)/shard_map/reduce_scatter | solution.py:142
  175.6 1.8 reshape.55
  177.5 11.9 %all-to-all-start.1 = ((bf16[16,19,512]{2,1,0:T(8,128)(2,1)}), bf16[16,19,512]{2,1,0:T(8,128)(2,1)S(1)}, u32[]{:S(2)}, u32[]{:S(2)}) async-start(bf16[16,19,512]{2,1,0:T(8,128)(2,1)} %reshape.55), calls=%async_computation.2 | async-start | bytes 786432 | tf_op jit(solution)/shard_map/all_to_all | solution.py:150
  189.4 1.1 fusion.7
  190.5 13.4 %all-to-all-done.1 = bf16[16,19,512]{2,1,0:T(8,128)(2,1)S(1)} async-done(((bf16[16,19,512]{2,1,0:T(8,128)(2,1)}), bf16[16,19,512]{2,1,0:T(8,128)(2,1)S(1)}, u32[]{:S(2)}, u32[]{:S(2)}) %all-to-all-start.1) | async-done | bytes 311328 | tf_op jit(solution)/shard_map/all_to_all | solution.py:150
  203.9 0.1 reshape.56
  204.0 0.9 convolution_convert_fusion.3
  (28 shorter events, 0.2 us)
Async XLA Ops:
  7.2 1.6 copy-start
  7.2 3.3 %copy-start.5 = (bf16[152,8]{0,1:T(8,128)(2,1)S(1)}, bf16[152,8]{0,1:T(8,128)(2,1)}, u32[]{:S(2)}) copy-start(bf16[152,8]{0,1:T(8,128)(2,1)} %param.12) | copy-start | bytes 7300
  7.2 119.1 %all-gather.2.cloned.1.call-start = ((), (), s32[]{:S(2)}) async-start(), calls=%async_computation.3 | async-start | bytes 2801664 | tf_op jit(solution)/shard_map/all_gather | solution.py:136
  11.2 33.9 %copy-start.3 = (bf16[1,192,1024]{2,1,0:T(8,128)(2,1)S(1)}, bf16[1,192,1024]{2,1,0:T(8,128)(2,1)}, u32[]{:S(2)}) copy-start(bf16[1,192,1024]{2,1,0:T(8,128)(2,1)} %param.17) | copy-start | bytes 1179652
  11.2 33.9 %copy-start.4 = (bf16[1,1024,192]{1,2,0:T(8,128)(2,1)S(1)}, bf16[1,1024,192]{1,2,0:T(8,128)(2,1)}, u32[]{:S(2)}) copy-start(bf16[1,1024,192]{1,2,0:T(8,128)(2,1)} %param.16) | copy-start | bytes 1179652
  45.1 130.6 %reduce-scatter.2.cloned.1.call-start = ((), (), s32[]{:S(2)}) async-start(), calls=%async_computation.4 | async-start | bytes 2801664 | tf_op jit(solution)/shard_map/reduce_scatter | solution.py:142
  46.3 29.9 %collective-permute-start.9 = (bf16[3,192,1024]{2,1,0:T(8,128)(2,1)S(1)}, bf16[3,192,1024]{2,1,0:T(8,128)(2,1)S(1)}, u32[]{:S(2)}, u32[]{:S(2)}) collective-permute-start(bf16[3,192,1024]{2,1,0:T(8,128)(2,1)S(1)} %pad_maximum_fusion.refs_0_), channel_id=1, source_target_pairs={{0,384},{128,0},{256,128},{384,256},{1,385},{129,1},{257,129},{385... | collective-permute-start | bytes 3538952 | tf_op jit(solution)/shard_map/ppermute | solution.py:64
  50.7 31.9 %collective-permute-start.7 = (bf16[3,192,1024]{2,1,0:T(8,128)(2,1)S(1)}, bf16[3,192,1024]{2,1,0:T(8,128)(2,1)}, u32[]{:S(2)}, u32[]{:S(2)}) collective-permute-start(bf16[3,192,1024]{2,1,0:T(8,128)(2,1)S(1)} %pad_maximum_fusion.refs_0_), channel_id=1, source_target_pairs={{0,128},{128,256},{256,384},{384,0},{1,129},{129,257},{257,385},{3... | collective-permute-start | bytes 3538952 | tf_op jit(solution)/shard_map/ppermute | solution.py:64
  54.4 37.3 %collective-permute-start = (bf16[304,512]{1,0:T(8,128)(2,1)}, bf16[304,512]{1,0:T(8,128)(2,1)}, u32[]{:S(2)}, u32[]{:S(2)}) collective-permute-start(bf16[304,512]{1,0:T(8,128)(2,1)} %reshape.54), channel_id=1, source_target_pairs={{0,1},{1,2},{2,3},{3,4},{4,5},{5,6},{6,7},{7,0},{8,9},{9,10},{10,1... | collective-permute-start | bytes 933896 | tf_op jit(solution)/shard_map/ppermute | solution.py:64
  76.2 19.4 %copy-start.1 = (bf16[3,192,1024]{2,1,0:T(8,128)(2,1)}, bf16[3,192,1024]{2,1,0:T(8,128)(2,1)S(1)}, u32[]{:S(2)}) copy-start(bf16[3,192,1024]{2,1,0:T(8,128)(2,1)S(1)} %collective-permute-done.9.refs_3_) | copy-start | bytes 3538948
  77.2 31.3 %collective-permute-start.10 = (bf16[3,192,512]{2,1,0:T(8,128)(2,1)}, bf16[3,192,512]{2,1,0:T(8,128)(2,1)}, u32[]{:S(2)}, u32[]{:S(2)}) collective-permute-start(bf16[3,192,512]{2,1,0:T(8,128)(2,1)} %slice.33), channel_id=1, source_target_pairs={{0,384},{128,0},{256,128},{384,256},{1,385},{129,1},{257,129},{385... | collective-permute-start | bytes 1769480 | tf_op jit(solution)/shard_map/ppermute | solution.py:64
  84.6 23.9 %collective-permute-start.8 = (bf16[3,192,512]{2,1,0:T(8,128)(2,1)}, bf16[3,192,512]{2,1,0:T(8,128)(2,1)}, u32[]{:S(2)}, u32[]{:S(2)}) collective-permute-start(bf16[3,192,512]{2,1,0:T(8,128)(2,1)} %slice.32), channel_id=1, source_target_pairs={{0,128},{128,256},{256,384},{384,0},{1,129},{129,257},{257,385},{3... | collective-permute-start | bytes 1769480 | tf_op jit(solution)/shard_map/ppermute | solution.py:64
  86.5 11.2 %collective-permute-start.1 = (bf16[304,512]{1,0:T(8,128)(2,1)}, bf16[304,512]{1,0:T(8,128)(2,1)}, u32[]{:S(2)}, u32[]{:S(2)}) collective-permute-start(bf16[304,512]{1,0:T(8,128)(2,1)} %reshape.54), channel_id=1, source_target_pairs={{0,7},{1,0},{2,1},{3,2},{4,3},{5,4},{6,5},{7,6},{8,15},{9,8},{10,9... | collective-permute-start | bytes 933896 | tf_op jit(solution)/shard_map/ppermute | solution.py:64
  91.7 13.1 %collective-permute-start.2 = (bf16[304,512]{1,0:T(8,128)(2,1)}, bf16[304,512]{1,0:T(8,128)(2,1)}, u32[]{:S(2)}, u32[]{:S(2)}) collective-permute-start(bf16[304,512]{1,0:T(8,128)(2,1)} %collective-permute-done), channel_id=1, source_target_pairs={{0,1},{1,2},{2,3},{3,4},{4,5},{5,6},{6,7},{7,0},{8,9},{9,10},{10,1... | collective-permute-start | bytes 933896 | tf_op jit(solution)/shard_map/ppermute | solution.py:64
  97.7 12.1 %collective-permute-start.3 = (bf16[304,512]{1,0:T(8,128)(2,1)}, bf16[304,512]{1,0:T(8,128)(2,1)S(1)}, u32[]{:S(2)}, u32[]{:S(2)}) collective-permute-start(bf16[304,512]{1,0:T(8,128)(2,1)} %collective-permute-done.1), channel_id=1, source_target_pairs={{0,7},{1,0},{2,1},{3,2},{4,3},{5,4},{6,5},{7,6},{8,15},{9,8},{10,9... | collective-permute-start | bytes 933896 | tf_op jit(solution)/shard_map/ppermute | solution.py:64
  104.8 11.4 %collective-permute-start.4 = (bf16[304,512]{1,0:T(8,128)(2,1)}, bf16[304,512]{1,0:T(8,128)(2,1)S(1)}, u32[]{:S(2)}, u32[]{:S(2)}) collective-permute-start(bf16[304,512]{1,0:T(8,128)(2,1)} %collective-permute-done.2), channel_id=1, source_target_pairs={{0,1},{1,2},{2,3},{3,4},{4,5},{5,6},{6,7},{7,0},{8,9},{9,10},{10,1... | collective-permute-start | bytes 933896 | tf_op jit(solution)/shard_map/ppermute | solution.py:64
  109.8 10.0 %collective-permute-start.5 = (bf16[304,512]{1,0:T(8,128)(2,1)S(1)}, bf16[304,512]{1,0:T(8,128)(2,1)S(1)}, u32[]{:S(2)}, u32[]{:S(2)}) collective-permute-start(bf16[304,512]{1,0:T(8,128)(2,1)S(1)} %collective-permute-done.3), channel_id=1, source_target_pairs={{0,7},{1,0},{2,1},{3,2},{4,3},{5,4},{6,5},{7,6},{8,15},{9,8},{10,9... | collective-permute-start | bytes 933896 | tf_op jit(solution)/shard_map/ppermute | solution.py:64
  116.2 9.4 %collective-permute-start.6 = (bf16[304,512]{1,0:T(8,128)(2,1)S(1)}, bf16[304,512]{1,0:T(8,128)(2,1)S(1)}, u32[]{:S(2)}, u32[]{:S(2)}) collective-permute-start(bf16[304,512]{1,0:T(8,128)(2,1)S(1)} %collective-permute-done.4), channel_id=1, source_target_pairs={{0,1},{1,2},{2,3},{3,4},{4,5},{5,6},{6,7},{7,0},{8,9},{9,10},{10,1... | collective-permute-start | bytes 933896 | tf_op jit(solution)/shard_map/ppermute | solution.py:64
  126.3 1.3 copy-start.2
  147.2 42.1 %collective-permute-start.11 = (bf16[192,1024]{1,0:T(8,128)(2,1)S(1)}, bf16[192,1024]{1,0:T(8,128)(2,1)S(1)}, u32[]{:S(2)}, u32[]{:S(2)}) collective-permute-start(bf16[192,1024]{1,0:T(8,128)(2,1)S(1)} %fusion.10), channel_id=1, source_target_pairs={{0,128},{128,256},{256,384},{384,0},{1,129},{129,257},{257,385},{3... | collective-permute-start | bytes 1179656 | tf_op jit(solution)/shard_map/ppermute | solution.py:103
  149.3 40.0 %collective-permute-start.12 = (bf16[192,1024]{1,0:T(8,128)(2,1)S(1)}, bf16[192,1024]{1,0:T(8,128)(2,1)S(1)}, u32[]{:S(2)}, u32[]{:S(2)}) collective-permute-start(bf16[192,1024]{1,0:T(8,128)(2,1)S(1)} %fusion.9), channel_id=1, source_target_pairs={{0,256},{128,384},{256,0},{384,128},{1,257},{129,385},{257,1},{385... | collective-permute-start | bytes 1179656 | tf_op jit(solution)/shard_map/ppermute | solution.py:103
  155.1 34.2 %collective-permute-start.13 = (bf16[192,1024]{1,0:T(8,128)(2,1)}, bf16[192,1024]{1,0:T(8,128)(2,1)S(1)}, u32[]{:S(2)}, u32[]{:S(2)}) collective-permute-start(bf16[192,1024]{1,0:T(8,128)(2,1)} %fusion.8), channel_id=1, source_target_pairs={{0,384},{128,0},{256,128},{384,256},{1,385},{129,1},{257,129},{385... | collective-permute-start | bytes 1179656 | tf_op jit(solution)/shard_map/ppermute | solution.py:103
  177.5 26.4 %all-to-all-start.1 = ((bf16[16,19,512]{2,1,0:T(8,128)(2,1)}), bf16[16,19,512]{2,1,0:T(8,128)(2,1)S(1)}, u32[]{:S(2)}, u32[]{:S(2)}) async-start(bf16[16,19,512]{2,1,0:T(8,128)(2,1)} %reshape.55), calls=%async_computation.2 | async-start | bytes 786432 | tf_op jit(solution)/shard_map/all_to_all | solution.py:150
Sparse Core Ops, SparseCore 0:
  45.2 44.2 all-gather.1
  136.8 38.7 reduce-scatter.1

commit v13 on v11

--- a/solution.py
+++ b/solution.py
@@ -89,11 +89,16 @@
     valid = experts_hit >= 0
     flat = jnp.where(valid, experts_hit * CAP + positions, slots)
     slot_ids = jnp.arange(slots, dtype=jnp.int32)
-    hit = flat[None, :, :] == slot_ids[:, None, None]
-    onehot = jnp.any(hit, axis=2).astype(jnp.bfloat16)
-    slot_gate = jnp.sum(
-        jnp.where(hit, gates.astype(jnp.float32)[None, :, :], 0.0), axis=(1, 2)
-    ).astype(jnp.bfloat16)
+    flat_t = flat.T
+    gates_t = gates.astype(jnp.float32).T
+    filled = jnp.zeros((slots, rows_dev), jnp.bool_)
+    gate_sum = jnp.zeros((slots, rows_dev), jnp.float32)
+    for route in range(routes):
+        hit = flat_t[route][None, :] == slot_ids[:, None]
+        filled = filled | hit
+        gate_sum = gate_sum + jnp.where(hit, gates_t[route][None, :], 0.0)
+    onehot = filled.astype(jnp.bfloat16)
+    slot_gate = jnp.sum(gate_sum, axis=1).astype(jnp.bfloat16)
     packed_x = jnp.dot(onehot, tokens, preferred_element_type=jnp.float32).astype(jnp.bfloat16)
     packed_dy = jnp.dot(onehot, cotangent, preferred_element_type=jnp.float32).astype(jnp.bfloat16)
     gate_row = jnp.pad(slot_gate.reshape(width, 1, CAP), ((0, 0), (0, 0), (0, narrow - CAP)))

time: 193 us -> 193 us (level)
  no operation moved by 1% of the time
where the time goes in v13:
time: 193 us; the launch traced here: 192 us
  waiting for transfers between devices  87.4 us (45%)
  blocking collectives  31.9 us (17%)
  starting transfers between devices  30.9 us (16%)
  between operations  14.4 us (7%)
  Pallas kernels  9.32 us (5%)
  local copies, waits for them, and re-layouts  7.76 us (4%)
  other arithmetic  5.6 us (3%)
  matrix products  5.05 us (3%)
    ppermute x3, waiting for transfers between devices, pieces_dp(): lax.ppermute(piece, 'dp', [(i, (i + shift) % size) for i in range(size)])  51.6 us
    all_to_all x1, blocking collectives, local(): lax.all_to_all(block, 'expert', split_axis=0, concat_axis=0, tiled=True)  31.9 us
    reduce_scatter x1, waiting for transfers between devices, local(): summed = lax.psum_scatter(d_part_b, 'etp', scatter_dimension=1, tiled=True)  22.4 us
    all_to_all x1, waiting for transfers between devices, local(): lax.all_to_all(summed.reshape(width, CAP, narrow), 'expert', split_axis=0...  13.4 us
    all_to_all x1, starting transfers between devices, local(): lax.all_to_all(summed.reshape(width, CAP, narrow), 'expert', split_axis=0...  12.1 us
    ppermute x3, starting transfers between devices, scatter_sum_dp(): lax.ppermute(outgoing, 'dp', [(i, (i + shift) % size) for i in range(size)])  9.4 us
    ppermute x3, starting transfers between devices, pieces_dp(): lax.ppermute(piece, 'dp', [(i, (i + shift) % size) for i in range(size)])  9.34 us
    pallas_call x1, Pallas kernels, expert_kernel(): pl.pallas_call(_expert_kernel, out_shape=(jax.ShapeDtypeStruct((slots, wi...  9.32 us
  transfers between devices with their start and end apart: 9, of which 4 were waited for; matrix products, arithmetic and copies ran while one was open for 6% of the time, Pallas kernels for 0%

profile of v13, /device:TPU:1, one launch (start us, length us, event | category | flops | bytes accessed | tf_op | source)
XLA Modules:
  0.0 192.3 jit_solution(1584757848838926060)
XLA Ops:
  7.2 0.0 copy-start
  7.2 0.0 copy-start.4
  7.2 0.0 all-gather.2.cloned.1.call-start
  7.2 0.8 convert_bitcast_fusion
  8.0 0.7 select_bitcast_fusion
  8.7 0.4 add_reduce_fusion
  9.2 0.1 convert_element_type.81
  9.3 0.0 copy-done
  9.3 0.6 convolution_convert_fusion.1
  9.8 0.1 reshape.46
  10.0 0.0 copy-done.4
  10.0 0.6 convolution_convert_fusion.2
  10.5 0.1 reshape.45
  10.7 0.1 pad.15.clone
  10.7 0.3 fusion.7
  11.0 31.9 %all_to_all.10 = bf16[16,40,512]{2,1,0:T(8,128)(2,1)S(1)} all-to-all(bf16[16,40,512]{2,1,0:T(8,128)(2,1)S(1)} %fusion.7), channel_id=1, replica_groups=mesh['dp'=4,'expert'=16,'etp'=8] {'expert'}, dimensions={0} | all-to-all | bytes 1310720 | tf_op jit(solution)/shard_map/all_to_all | solution.py:114
  42.9 0.1 fusion.23
  43.0 0.1 stack_reshape.6
  43.1 0.0 copy-start.1
  43.1 0.0 copy-start.2
  43.1 0.0 copy-start.3
  43.1 0.1 stack_reshape.7
  43.3 0.9 pad_maximum_fusion.1
  44.2 0.0 all-gather.2.cloned.1.call-update
  44.2 0.0 reduce-scatter.2.cloned.1.call-start
  44.3 0.0 copy-done.1
  44.3 0.0 copy-done.2
  44.3 0.3 copy-done.3
  44.6 0.1 pad_maximum_fusion.refs_0_
  44.7 4.4 %collective-permute-start.2 = (bf16[3,192,1024]{2,1,0:T(8,128)(2,1)S(1)}, bf16[3,192,1024]{2,1,0:T(8,128)(2,1)S(1)}, u32[]{:S(2)}, u32[]{:S(2)}) collective-permute-start(bf16[3,192,1024]{2,1,0:T(8,128)(2,1)S(1)} %pad_maximum_fusion.refs_0_), channel_id=1, source_target_pairs={{0,384},{128,0},{256,128},{384,256},{1,385},{129,1},{257,129},{385... | collective-permute-start | bytes 3538952 | tf_op jit(solution)/shard_map/ppermute | solution.py:66
  49.1 2.4 %collective-permute-start.1 = (bf16[3,192,1024]{2,1,0:T(8,128)(2,1)S(1)}, bf16[3,192,1024]{2,1,0:T(8,128)(2,1)}, u32[]{:S(2)}, u32[]{:S(2)}) collective-permute-start(bf16[3,192,1024]{2,1,0:T(8,128)(2,1)S(1)} %pad_maximum_fusion.refs_0_), channel_id=1, source_target_pairs={{0,256},{128,384},{256,0},{384,128},{1,257},{129,385},{257,1},{385... | collective-permute-start | bytes 3538952 | tf_op jit(solution)/shard_map/ppermute | solution.py:66
  51.6 2.5 %collective-permute-start = (bf16[3,192,1024]{2,1,0:T(8,128)(2,1)S(1)}, bf16[3,192,1024]{2,1,0:T(8,128)(2,1)}, u32[]{:S(2)}, u32[]{:S(2)}) collective-permute-start(bf16[3,192,1024]{2,1,0:T(8,128)(2,1)S(1)} %pad_maximum_fusion.refs_0_), channel_id=1, source_target_pairs={{0,128},{128,256},{256,384},{384,0},{1,129},{129,257},{257,385},{3... | collective-permute-start | bytes 3538952 | tf_op jit(solution)/shard_map/ppermute | solution.py:66
  54.1 0.1 reshape_reshape_squeeze.4.gate_ref
  54.2 45.5 %collective-permute-done.2.refs_3_ = bf16[3,192,1024]{2,1,0:T(8,128)(2,1)S(1)} collective-permute-done((bf16[3,192,1024]{2,1,0:T(8,128)(2,1)S(1)}, bf16[3,192,1024]{2,1,0:T(8,128)(2,1)S(1)}, u32[]{:S(2)}, u32[]{:S(2)}) %collective-permute-start.2) | collective-permute-done | bytes 1179680 | tf_op jit(solution)/shard_map/ppermute | solution.py:66
  99.7 0.0 collective-permute-done.1.refs_2_
  99.7 6.1 %collective-permute-done.refs_1_ = bf16[3,192,1024]{2,1,0:T(8,128)(2,1)} collective-permute-done((bf16[3,192,1024]{2,1,0:T(8,128)(2,1)S(1)}, bf16[3,192,1024]{2,1,0:T(8,128)(2,1)}, u32[]{:S(2)}, u32[]{:S(2)}) %collective-permute-start) | collective-permute-done | bytes 1179680 | tf_op jit(solution)/shard_map/ppermute | solution.py:66
  105.8 0.0 all-gather.2.cloned.1.call-done.rows_ref
  105.8 9.3 %shard_map.95 = (bf16[304,4096]{1,0:T(8,128)(2,1)}, bf16[304,192]{1,0:T(8,128)(2,1)S(1)}) custom-call(s32[1]{0:T(128)} %bitcast.9.me_ref, bf16[2,304,4096]{2,1,0:T(8,128)(2,1)} %all-gather.2.cloned.1.call-done.rows_ref, bf16[304,1]{1,0:T(8,128)(2,1)S(1)} %reshape_reshape_squeeze.4.gate_ref, bf16[3,192,1024]{2,1,0:T(8,128)(2,1)S(1)} %pad_maximum_fusion.refs_0_, ...), custom_call_target="tpu_custom_call" | custom-call | tf_op jit(solution)/shard_map/pallas_call | solution.py:49
  115.1 0.0 reduce-scatter.2.cloned.1.call-update
  115.3 0.1 reshape.113
  115.4 2.8 %convolution_convert_fusion = bf16[192,4096]{1,0:T(8,128)(2,1)S(1)} fusion(bf16[304,192]{1,0:T(8,128)(2,1)S(1)} %get-tuple-element.6, bf16[2,304,4096]{2,1,0:T(8,128)(2,1)} %all-gather.2.cloned.1.call-done.rows_ref, f32[304]{0:T(512)S(1)} %reshape.113), kind=kOutput, calls=%fused_computation | convolution fusion | flops 482672640 | bytes 4181184 | tf_op jit(solution)/shard_map/dot_general | solution.py:130
  118.1 1.2 reshape.49
  119.3 3.3 %constant_dynamic-slice_fusion.3 = (bf16[192,1,1024]{2,1,0:T(2,128)(2,1)S(1)}, bf16[192,1,1024]{2,1,0:T(2,128)(2,1)S(1)}, bf16[192,1,1024]{2,1,0:T(2,128)(2,1)S(1)}, bf16[192,1,1024]{2,1,0:T(2,128)(2,1)S(1)}) fusion(bf16[192,4,1024]{2,1,0:T(4,128)(2,1)S(1)} %reshape.49, s32[]{:T(128)S(6)} %select_n.76, s32[]{:T(128)S(6)} %select_n.80, s32[]{:T(128)S(6)} %select_n.78, ...), kind=kLoop, calls=%fused_computation.50 | loop fusion | bytes 3145744 | tf_op jit(solution)/shard_map/jit(_take) | solution.py:75
  122.7 0.2 fusion.9
  122.8 3.9 %collective-permute-start.5 = (bf16[192,1024]{1,0:T(8,128)(2,1)S(1)}, bf16[192,1024]{1,0:T(8,128)(2,1)S(1)}, u32[]{:S(2)}, u32[]{:S(2)}) collective-permute-start(bf16[192,1024]{1,0:T(8,128)(2,1)S(1)} %fusion.9), channel_id=1, source_target_pairs={{0,384},{128,0},{256,128},{384,256},{1,385},{129,1},{257,129},{385... | collective-permute-start | bytes 1179656 | tf_op jit(solution)/shard_map/ppermute | solution.py:78
  126.7 0.2 fusion.11
  126.9 1.9 collective-permute-start.3
  128.8 0.9 fusion.10
  129.7 3.6 %collective-permute-start.4 = (bf16[192,1024]{1,0:T(8,128)(2,1)}, bf16[192,1024]{1,0:T(8,128)(2,1)S(1)}, u32[]{:S(2)}, u32[]{:S(2)}) collective-permute-start(bf16[192,1024]{1,0:T(8,128)(2,1)} %fusion.10), channel_id=1, source_target_pairs={{0,256},{128,384},{256,0},{384,128},{1,257},{129,385},{257,1},{385... | collective-permute-start | bytes 1179656 | tf_op jit(solution)/shard_map/ppermute | solution.py:78
  133.3 22.4 %reduce-scatter.2.cloned.1.call-done = bf16[304,512]{1,0:T(8,128)(2,1)} async-done(((bf16[304,4096]{1,0:T(8,128)(2,1)}), bf16[304,512]{1,0:T(8,128)(2,1)}) %reduce-scatter.2.cloned.1.call-update) | async-done | bytes 311312 | tf_op jit(solution)/shard_map/reduce_scatter | solution.py:126
  155.7 1.8 reshape.47
  157.6 12.1 %all-to-all-start.1 = ((bf16[16,19,512]{2,1,0:T(8,128)(2,1)}), bf16[16,19,512]{2,1,0:T(8,128)(2,1)S(1)}, u32[]{:S(2)}, u32[]{:S(2)}) async-start(bf16[16,19,512]{2,1,0:T(8,128)(2,1)} %reshape.47), calls=%async_computation.2 | async-start | bytes 786432 | tf_op jit(solution)/shard_map/all_to_all | solution.py:134
  169.6 0.0 collective-permute-done.5
  169.6 0.0 collective-permute-done.3
  169.7 0.0 collective-permute-done.4
  169.7 1.1 fusion.8
  170.8 13.4 %all-to-all-done.1 = bf16[16,19,512]{2,1,0:T(8,128)(2,1)S(1)} async-done(((bf16[16,19,512]{2,1,0:T(8,128)(2,1)}), bf16[16,19,512]{2,1,0:T(8,128)(2,1)S(1)}, u32[]{:S(2)}, u32[]{:S(2)}) %all-to-all-start.1) | async-done | bytes 311328 | tf_op jit(solution)/shard_map/all_to_all | solution.py:134
  184.2 0.1 reshape.48
  184.3 1.1 convolution_convert_fusion.3
  (4 shorter events, 0.1 us)
Async XLA Ops:
  7.2 2.1 %copy-start = (bf16[152,512]{1,0:T(8,128)(2,1)S(1)}, bf16[152,512]{1,0:T(8,128)(2,1)}, u32[]{:S(2)}) copy-start(bf16[152,512]{1,0:T(8,128)(2,1)} %param.11) | copy-start | bytes 466948
  7.2 2.8 %copy-start.4 = (bf16[152,512]{1,0:T(8,128)(2,1)S(1)}, bf16[152,512]{1,0:T(8,128)(2,1)}, u32[]{:S(2)}) copy-start(bf16[152,512]{1,0:T(8,128)(2,1)} %param.10) | copy-start | bytes 466948
  7.2 98.6 %all-gather.2.cloned.1.call-start = ((), (), s32[]{:S(2)}) async-start(), calls=%async_computation.3 | async-start | bytes 5603328 | tf_op jit(solution)/shard_map/all_gather | solution.py:123
  43.1 1.1 copy-start.1
  43.1 1.1 copy-start.2
  43.1 1.4 copy-start.3
  44.2 111.5 %reduce-scatter.2.cloned.1.call-start = ((), (), s32[]{:S(2)}) async-start(), calls=%async_computation.4 | async-start | bytes 2801664 | tf_op jit(solution)/shard_map/reduce_scatter | solution.py:126
  44.7 55.0 %collective-permute-start.2 = (bf16[3,192,1024]{2,1,0:T(8,128)(2,1)S(1)}, bf16[3,192,1024]{2,1,0:T(8,128)(2,1)S(1)}, u32[]{:S(2)}, u32[]{:S(2)}) collective-permute-start(bf16[3,192,1024]{2,1,0:T(8,128)(2,1)S(1)} %pad_maximum_fusion.refs_0_), channel_id=1, source_target_pairs={{0,384},{128,0},{256,128},{384,256},{1,385},{129,1},{257,129},{385... | collective-permute-start | bytes 3538952 | tf_op jit(solution)/shard_map/ppermute | solution.py:66
  49.1 50.6 %collective-permute-start.1 = (bf16[3,192,1024]{2,1,0:T(8,128)(2,1)S(1)}, bf16[3,192,1024]{2,1,0:T(8,128)(2,1)}, u32[]{:S(2)}, u32[]{:S(2)}) collective-permute-start(bf16[3,192,1024]{2,1,0:T(8,128)(2,1)S(1)} %pad_maximum_fusion.refs_0_), channel_id=1, source_target_pairs={{0,256},{128,384},{256,0},{384,128},{1,257},{129,385},{257,1},{385... | collective-permute-start | bytes 3538952 | tf_op jit(solution)/shard_map/ppermute | solution.py:66
  51.6 54.3 %collective-permute-start = (bf16[3,192,1024]{2,1,0:T(8,128)(2,1)S(1)}, bf16[3,192,1024]{2,1,0:T(8,128)(2,1)}, u32[]{:S(2)}, u32[]{:S(2)}) collective-permute-start(bf16[3,192,1024]{2,1,0:T(8,128)(2,1)S(1)} %pad_maximum_fusion.refs_0_), channel_id=1, source_target_pairs={{0,128},{128,256},{256,384},{384,0},{1,129},{129,257},{257,385},{3... | collective-permute-start | bytes 3538952 | tf_op jit(solution)/shard_map/ppermute | solution.py:66
  122.8 46.8 %collective-permute-start.5 = (bf16[192,1024]{1,0:T(8,128)(2,1)S(1)}, bf16[192,1024]{1,0:T(8,128)(2,1)S(1)}, u32[]{:S(2)}, u32[]{:S(2)}) collective-permute-start(bf16[192,1024]{1,0:T(8,128)(2,1)S(1)} %fusion.9), channel_id=1, source_target_pairs={{0,384},{128,0},{256,128},{384,256},{1,385},{129,1},{257,129},{385... | collective-permute-start | bytes 1179656 | tf_op jit(solution)/shard_map/ppermute | solution.py:78
  126.9 42.8 %collective-permute-start.3 = (bf16[192,1024]{1,0:T(8,128)(2,1)S(1)}, bf16[192,1024]{1,0:T(8,128)(2,1)S(1)}, u32[]{:S(2)}, u32[]{:S(2)}) collective-permute-start(bf16[192,1024]{1,0:T(8,128)(2,1)S(1)} %fusion.11), channel_id=1, source_target_pairs={{0,128},{128,256},{256,384},{384,0},{1,129},{129,257},{257,385},{3... | collective-permute-start | bytes 1179656 | tf_op jit(solution)/shard_map/ppermute | solution.py:78
  129.7 40.0 %collective-permute-start.4 = (bf16[192,1024]{1,0:T(8,128)(2,1)}, bf16[192,1024]{1,0:T(8,128)(2,1)S(1)}, u32[]{:S(2)}, u32[]{:S(2)}) collective-permute-start(bf16[192,1024]{1,0:T(8,128)(2,1)} %fusion.10), channel_id=1, source_target_pairs={{0,256},{128,384},{256,0},{384,128},{1,257},{129,385},{257,1},{385... | collective-permute-start | bytes 1179656 | tf_op jit(solution)/shard_map/ppermute | solution.py:78
  157.6 26.6 %all-to-all-start.1 = ((bf16[16,19,512]{2,1,0:T(8,128)(2,1)}), bf16[16,19,512]{2,1,0:T(8,128)(2,1)S(1)}, u32[]{:S(2)}, u32[]{:S(2)}) async-start(bf16[16,19,512]{2,1,0:T(8,128)(2,1)} %reshape.47), calls=%async_computation.2 | async-start | bytes 786432 | tf_op jit(solution)/shard_map/all_to_all | solution.py:134
Sparse Core Ops, SparseCore 0:
  44.3 60.9 all-gather.1
  115.3 40.4 reduce-scatter.1

commit v14 on v11

--- a/solution.py
+++ b/solution.py
@@ -59,12 +59,20 @@
     )(me.reshape(1), rows, gate_col.reshape(slots, 1), *pieces)
 
 
+def shift(value, axis, step):
+    size = lax.axis_size(axis)
+    return lax.ppermute(value, axis, [(i, (i + step) % size) for i in range(size)])
+
+
 def pieces_dp(piece):
-    size = lax.axis_size("dp")
-    got = [piece]
-    for shift in range(1, size):
-        got.append(lax.ppermute(piece, "dp", [(i, (i + shift) % size) for i in range(size)]))
-    return got
+    assert lax.axis_size("dp") == 4
+    half = piece.shape[-1] // 2
+    from_left = shift(piece, "dp", 1)
+    from_right = shift(piece, "dp", -1)
+    far = jnp.concatenate(
+        [shift(from_left[..., :half], "dp", 1), shift(from_right[..., half:], "dp", -1)], axis=-1
+    )
+    return [piece, from_left, far, from_right]
 
 
 def scatter_sum_dp(term_b):

time: 193 us -> 195 us (1.010)
  waiting for transfers between devices: 87.1 us -> 80.4 us
  starting transfers between devices: 31.6 us -> 35.8 us
  local copies, waits for them, and re-layouts: 8.33 us -> 11.9 us
    ppermute x3 -> x4, waiting for transfers between devices: 51.6 us -> 38.7 us  [shift(): lax.ppermute(value, axis, [(i, (i + step) % size) for i in range(size)])]
    all_gather x1, waiting for transfers between devices: 0.01 us -> 5.91 us  [local(): full = lax.all_gather(pair, 'etp', axis=2, tiled=True)]
    ppermute x3 -> x4, starting transfers between devices: 9.35 us -> 13.6 us  [shift(): lax.ppermute(value, axis, [(i, (i + step) % size) for i in range(size)])]
    unnamed x10 -> x18, local copies, waits for them, and re-layouts: 0.03 us -> 3.54 us
  transfers between devices with their start and end apart: 9 -> 10, of which waited for: 4 -> 6; matrix products, arithmetic and copies ran while one was open for 6% -> 7% of each run, Pallas kernels for 0% -> 0%
where the time goes in v14:
time: 195 us; the launch traced here: 194 us
  waiting for transfers between devices  80.4 us (41%)
  starting transfers between devices  35.8 us (18%)
  blocking collectives  31.9 us (16%)
  between operations  14.5 us (7%)
  local copies, waits for them, and re-layouts  11.9 us (6%)
  Pallas kernels  8.69 us (4%)
  other arithmetic  6.91 us (4%)
  matrix products  4.29 us (2%)
    ppermute x4, waiting for transfers between devices, shift(): lax.ppermute(value, axis, [(i, (i + step) % size) for i in range(size)])  38.7 us
    all_to_all x1, blocking collectives, local(): lax.all_to_all(block, 'expert', split_axis=0, concat_axis=0, tiled=True)  31.9 us
    reduce_scatter x1, waiting for transfers between devices, local(): summed = lax.psum_scatter(d_part_b, 'etp', scatter_dimension=1, tiled=True)  22.3 us
    ppermute x4, starting transfers between devices, shift(): lax.ppermute(value, axis, [(i, (i + step) % size) for i in range(size)])  13.6 us
    all_to_all x1, waiting for transfers between devices, local(): lax.all_to_all(summed.reshape(width, CAP, narrow), 'expert', split_axis=0...  13.4 us
    all_to_all x1, starting transfers between devices, local(): lax.all_to_all(summed.reshape(width, CAP, narrow), 'expert', split_axis=0...  12.2 us
    ppermute x3, starting transfers between devices, scatter_sum_dp(): lax.ppermute(outgoing, 'dp', [(i, (i + shift) % size) for i in range(size)])  9.88 us
    pallas_call x1, Pallas kernels, expert_kernel(): pl.pallas_call(_expert_kernel, out_shape=(jax.ShapeDtypeStruct((slots, wi...  8.69 us
  transfers between devices with their start and end apart: 10, of which 6 were waited for; matrix products, arithmetic and copies ran while one was open for 7% of the time, Pallas kernels for 0%

profile of v14, /device:TPU:1, one launch (start us, length us, event | category | flops | bytes accessed | tf_op | source)
XLA Modules:
  0.0 194.3 jit_solution(6751653004898126492)
XLA Ops:
  7.2 0.0 copy-start
  7.2 0.0 all-gather.2.cloned.1.call-start
  7.2 0.8 add_select_fusion
  8.0 0.1 copy.35
  8.1 0.7 fusion.3
  8.8 0.8 copy.36
  9.6 0.4 select_reduce_fusion
  10.0 0.1 convert_element_type.84
  10.1 0.3 convolution_convert_fusion.1
  10.4 0.1 reshape.48
  10.5 0.3 convolution_convert_fusion.2
  10.8 0.1 reshape.47
  11.0 0.1 pad.17.clone
  11.0 0.3 fusion.8
  11.3 31.9 %all_to_all.10 = bf16[16,40,512]{2,1,0:T(8,128)(2,1)S(1)} all-to-all(bf16[16,40,512]{2,1,0:T(8,128)(2,1)S(1)} %fusion.8), channel_id=1, replica_groups=mesh['dp'=4,'expert'=16,'etp'=8] {'expert'}, dimensions={0} | all-to-all | bytes 1310720 | tf_op jit(solution)/shard_map/all_to_all | solution.py:117
  43.2 0.1 fusion.14
  43.3 0.0 copy-start.5
  43.3 0.0 copy-start.6
  43.3 0.0 copy-start.7
  43.3 0.1 stack_reshape.6
  43.5 0.1 stack_reshape.7
  43.6 0.9 pad_maximum_fusion.2
  44.5 0.0 all-gather.2.cloned.1.call-update
  44.5 0.0 reduce-scatter.2.cloned.1.call-start
  44.6 0.0 copy-done.5
  44.6 0.0 copy-done.6
  44.6 0.0 copy-done.7
  44.6 0.1 pad_maximum_fusion.refs_0_
  44.7 4.4 %collective-permute-start.2 = (bf16[3,192,1024]{2,1,0:T(8,128)(2,1)S(1)}, bf16[3,192,1024]{2,1,0:T(8,128)(2,1)S(1)}, u32[]{:S(2)}, u32[]{:S(2)}) collective-permute-start(bf16[3,192,1024]{2,1,0:T(8,128)(2,1)S(1)} %pad_maximum_fusion.refs_0_), channel_id=1, source_target_pairs={{0,384},{128,0},{256,128},{384,256},{1,385},{129,1},{257,129},{385... | collective-permute-start | bytes 3538952 | tf_op jit(solution)/shard_map/ppermute | solution.py:64
  49.1 1.9 collective-permute-start
  51.0 23.6 %collective-permute-done.2.refs_3_ = bf16[3,192,1024]{2,1,0:T(8,128)(2,1)S(1)} collective-permute-done((bf16[3,192,1024]{2,1,0:T(8,128)(2,1)S(1)}, bf16[3,192,1024]{2,1,0:T(8,128)(2,1)S(1)}, u32[]{:S(2)}, u32[]{:S(2)}) %collective-permute-start.2) | collective-permute-done | bytes 1179680 | tf_op jit(solution)/shard_map/ppermute | solution.py:64
  74.7 5.4 %collective-permute-start.3 = (bf16[3,192,512]{2,1,0:T(8,128)(2,1)S(1)}, bf16[3,192,512]{2,1,0:T(8,128)(2,1)}, u32[]{:S(2)}, u32[]{:S(2)}) collective-permute-start(bf16[3,192,512]{2,1,0:T(8,128)(2,1)S(1)} %slice.37), channel_id=1, source_target_pairs={{0,384},{128,0},{256,128},{384,256},{1,385},{129,1},{257,129},{385... | collective-permute-start | bytes 1769480 | tf_op jit(solution)/shard_map/ppermute | solution.py:64
  80.1 0.0 collective-permute-done.refs_1_
  80.2 1.0 copy-done.3
  81.1 1.9 collective-permute-start.1
  83.1 0.1 reshape_reshape_squeeze.4.gate_ref
  83.2 9.0 %collective-permute-done.3 = bf16[3,192,512]{2,1,0:T(8,128)(2,1)} collective-permute-done((bf16[3,192,512]{2,1,0:T(8,128)(2,1)S(1)}, bf16[3,192,512]{2,1,0:T(8,128)(2,1)}, u32[]{:S(2)}, u32[]{:S(2)}) %collective-permute-start.3) | collective-permute-done | bytes 589856 | tf_op jit(solution)/shard_map/ppermute | solution.py:64
  92.2 6.2 %collective-permute-done.1 = bf16[3,192,512]{2,1,0:T(8,128)(2,1)} collective-permute-done((bf16[3,192,512]{2,1,0:T(8,128)(2,1)S(1)}, bf16[3,192,512]{2,1,0:T(8,128)(2,1)}, u32[]{:S(2)}, u32[]{:S(2)}) %collective-permute-start.1) | collective-permute-done | bytes 589856 | tf_op jit(solution)/shard_map/ppermute | solution.py:64
  98.4 1.4 pad_maximum_fusion.1.refs_2_
  99.7 5.9 %all-gather.2.cloned.1.call-done.rows_ref = bf16[2,304,4096]{2,1,0:T(8,128)(2,1)} async-done(((bf16[2,304,512]{2,1,0:T(8,128)(2,1)}), bf16[2,304,4096]{2,1,0:T(8,128)(2,1)}) %all-gather.2.cloned.1.call-update) | async-done | bytes 4980752 | tf_op jit(solution)/shard_map/all_gather | solution.py:126
  105.6 1.3 copy-done.2
  106.9 1.3 copy-done.4
  108.2 8.7 %shard_map.95 = (bf16[304,4096]{1,0:T(8,128)(2,1)}, bf16[304,192]{1,0:T(8,128)(2,1)S(1)}) custom-call(s32[1]{0:T(128)} %bitcast.me_ref, bf16[2,304,4096]{2,1,0:T(8,128)(2,1)} %all-gather.2.cloned.1.call-done.rows_ref, bf16[304,1]{1,0:T(8,128)(2,1)S(1)} %reshape_reshape_squeeze.4.gate_ref, bf16[3,192,1024]{2,1,0:T(8,128)(2,1)S(1)} %pad_maximum_fusion.refs_0_, ...), custom_call_target="tpu_custom_call" | custom-call | tf_op jit(solution)/shard_map/pallas_call | solution.py:49
  116.9 0.0 reduce-scatter.2.cloned.1.call-update
  117.0 0.1 reshape.115
  117.1 2.8 %convolution_convert_fusion = bf16[192,4096]{1,0:T(8,128)(2,1)S(1)} fusion(bf16[304,192]{1,0:T(8,128)(2,1)S(1)} %get-tuple-element.6, bf16[2,304,4096]{2,1,0:T(8,128)(2,1)} %all-gather.2.cloned.1.call-done.rows_ref, f32[304]{0:T(512)S(1)} %reshape.115), kind=kOutput, calls=%fused_computation | convolution fusion | flops 482672640 | bytes 4181184 | tf_op jit(solution)/shard_map/dot_general | solution.py:133
  119.9 1.2 reshape.51
  121.1 3.3 %constant_dynamic-slice_fusion.3 = (bf16[192,1,1024]{2,1,0:T(2,128)(2,1)S(1)}, bf16[192,1,1024]{2,1,0:T(2,128)(2,1)S(1)}, bf16[192,1,1024]{2,1,0:T(2,128)(2,1)S(1)}, bf16[192,1,1024]{2,1,0:T(2,128)(2,1)S(1)}) fusion(bf16[192,4,1024]{2,1,0:T(4,128)(2,1)S(1)} %reshape.51, s32[]{:T(128)S(6)} %select_n.48, s32[]{:T(128)S(6)} %select_n.52, s32[]{:T(128)S(6)} %select_n.50, ...), kind=kLoop, calls=%fused_computation.37 | loop fusion | bytes 3145744 | tf_op jit(solution)/shard_map/jit(_take) | solution.py:83
  124.4 0.2 fusion.10
  124.5 4.3 %collective-permute-start.6 = (bf16[192,1024]{1,0:T(8,128)(2,1)S(1)}, bf16[192,1024]{1,0:T(8,128)(2,1)S(1)}, u32[]{:S(2)}, u32[]{:S(2)}) collective-permute-start(bf16[192,1024]{1,0:T(8,128)(2,1)S(1)} %fusion.10), channel_id=1, source_target_pairs={{0,384},{128,0},{256,128},{384,256},{1,385},{129,1},{257,129},{385... | collective-permute-start | bytes 1179656 | tf_op jit(solution)/shard_map/ppermute | solution.py:86
  128.9 0.2 fusion.12
  129.0 1.9 collective-permute-start.4
  131.0 0.9 fusion.11
  131.9 3.6 %collective-permute-start.5 = (bf16[192,1024]{1,0:T(8,128)(2,1)}, bf16[192,1024]{1,0:T(8,128)(2,1)S(1)}, u32[]{:S(2)}, u32[]{:S(2)}) collective-permute-start(bf16[192,1024]{1,0:T(8,128)(2,1)} %fusion.11), channel_id=1, source_target_pairs={{0,256},{128,384},{256,0},{384,128},{1,257},{129,385},{257,1},{385... | collective-permute-start | bytes 1179656 | tf_op jit(solution)/shard_map/ppermute | solution.py:86
  135.5 22.3 %reduce-scatter.2.cloned.1.call-done = bf16[304,512]{1,0:T(8,128)(2,1)} async-done(((bf16[304,4096]{1,0:T(8,128)(2,1)}), bf16[304,512]{1,0:T(8,128)(2,1)}) %reduce-scatter.2.cloned.1.call-update) | async-done | bytes 311312 | tf_op jit(solution)/shard_map/reduce_scatter | solution.py:129
  157.8 1.8 reshape.49
  159.7 12.2 %all-to-all-start.1 = ((bf16[16,19,512]{2,1,0:T(8,128)(2,1)}), bf16[16,19,512]{2,1,0:T(8,128)(2,1)S(1)}, u32[]{:S(2)}, u32[]{:S(2)}) async-start(bf16[16,19,512]{2,1,0:T(8,128)(2,1)} %reshape.49), calls=%async_computation.2 | async-start | bytes 786432 | tf_op jit(solution)/shard_map/all_to_all | solution.py:137
  171.8 0.0 collective-permute-done.6
  171.9 0.0 collective-permute-done.4
  171.9 0.0 collective-permute-done.5
  171.9 1.1 fusion.9
  173.0 13.4 %all-to-all-done.1 = bf16[16,19,512]{2,1,0:T(8,128)(2,1)S(1)} async-done(((bf16[16,19,512]{2,1,0:T(8,128)(2,1)}), bf16[16,19,512]{2,1,0:T(8,128)(2,1)S(1)}, u32[]{:S(2)}, u32[]{:S(2)}) %all-to-all-start.1) | async-done | bytes 311328 | tf_op jit(solution)/shard_map/all_to_all | solution.py:137
  186.4 0.1 reshape.50
  186.5 0.9 convolution_convert_fusion.3
  (12 shorter events, 0.2 us)
Async XLA Ops:
  7.2 2.9 %copy-start = (bf16[152,512]{1,0:T(8,128)(2,1)S(1)}, bf16[152,512]{1,0:T(8,128)(2,1)}, u32[]{:S(2)}) copy-start(bf16[152,512]{1,0:T(8,128)(2,1)} %param.11) | copy-start | bytes 466948
  7.2 3.4 %copy-start.8 = (bf16[152,512]{1,0:T(8,128)(2,1)S(1)}, bf16[152,512]{1,0:T(8,128)(2,1)}, u32[]{:S(2)}) copy-start(bf16[152,512]{1,0:T(8,128)(2,1)} %param.10) | copy-start | bytes 466948
  7.2 98.4 %all-gather.2.cloned.1.call-start = ((), (), s32[]{:S(2)}) async-start(), calls=%async_computation.3 | async-start | bytes 5603328 | tf_op jit(solution)/shard_map/all_gather | solution.py:126
  43.3 1.3 copy-start.5
  43.3 1.3 copy-start.6
  43.3 1.3 copy-start.7
  44.5 113.3 %reduce-scatter.2.cloned.1.call-start = ((), (), s32[]{:S(2)}) async-start(), calls=%async_computation.4 | async-start | bytes 2801664 | tf_op jit(solution)/shard_map/reduce_scatter | solution.py:129
  44.7 29.9 %collective-permute-start.2 = (bf16[3,192,1024]{2,1,0:T(8,128)(2,1)S(1)}, bf16[3,192,1024]{2,1,0:T(8,128)(2,1)S(1)}, u32[]{:S(2)}, u32[]{:S(2)}) collective-permute-start(bf16[3,192,1024]{2,1,0:T(8,128)(2,1)S(1)} %pad_maximum_fusion.refs_0_), channel_id=1, source_target_pairs={{0,384},{128,0},{256,128},{384,256},{1,385},{129,1},{257,129},{385... | collective-permute-start | bytes 3538952 | tf_op jit(solution)/shard_map/ppermute | solution.py:64
  49.1 31.0 %collective-permute-start = (bf16[3,192,1024]{2,1,0:T(8,128)(2,1)S(1)}, bf16[3,192,1024]{2,1,0:T(8,128)(2,1)S(1)}, u32[]{:S(2)}, u32[]{:S(2)}) collective-permute-start(bf16[3,192,1024]{2,1,0:T(8,128)(2,1)S(1)} %pad_maximum_fusion.refs_0_), channel_id=1, source_target_pairs={{0,128},{128,256},{256,384},{384,0},{1,129},{129,257},{257,385},{3... | collective-permute-start | bytes 3538952 | tf_op jit(solution)/shard_map/ppermute | solution.py:64
  74.6 5.5 %copy-start.1 = (bf16[3,192,1024]{2,1,0:T(8,128)(2,1)}, bf16[3,192,1024]{2,1,0:T(8,128)(2,1)S(1)}, u32[]{:S(2)}) copy-start(bf16[3,192,1024]{2,1,0:T(8,128)(2,1)S(1)} %collective-permute-done.2.refs_3_) | copy-start | bytes 3538948
  74.7 17.5 %collective-permute-start.3 = (bf16[3,192,512]{2,1,0:T(8,128)(2,1)S(1)}, bf16[3,192,512]{2,1,0:T(8,128)(2,1)}, u32[]{:S(2)}, u32[]{:S(2)}) collective-permute-start(bf16[3,192,512]{2,1,0:T(8,128)(2,1)S(1)} %slice.37), channel_id=1, source_target_pairs={{0,384},{128,0},{256,128},{384,256},{1,385},{129,1},{257,129},{385... | collective-permute-start | bytes 1769480 | tf_op jit(solution)/shard_map/ppermute | solution.py:64
  80.1 1.0 copy-start.3
  81.1 17.2 %collective-permute-start.1 = (bf16[3,192,512]{2,1,0:T(8,128)(2,1)S(1)}, bf16[3,192,512]{2,1,0:T(8,128)(2,1)}, u32[]{:S(2)}, u32[]{:S(2)}) collective-permute-start(bf16[3,192,512]{2,1,0:T(8,128)(2,1)S(1)} %slice.36), channel_id=1, source_target_pairs={{0,128},{128,256},{256,384},{384,0},{1,129},{129,257},{257,385},{3... | collective-permute-start | bytes 1769480 | tf_op jit(solution)/shard_map/ppermute | solution.py:64
  105.6 1.3 copy-start.2
  106.9 1.3 copy-start.4
  124.5 47.3 %collective-permute-start.6 = (bf16[192,1024]{1,0:T(8,128)(2,1)S(1)}, bf16[192,1024]{1,0:T(8,128)(2,1)S(1)}, u32[]{:S(2)}, u32[]{:S(2)}) collective-permute-start(bf16[192,1024]{1,0:T(8,128)(2,1)S(1)} %fusion.10), channel_id=1, source_target_pairs={{0,384},{128,0},{256,128},{384,256},{1,385},{129,1},{257,129},{385... | collective-permute-start | bytes 1179656 | tf_op jit(solution)/shard_map/ppermute | solution.py:86
  129.0 42.8 %collective-permute-start.4 = (bf16[192,1024]{1,0:T(8,128)(2,1)S(1)}, bf16[192,1024]{1,0:T(8,128)(2,1)S(1)}, u32[]{:S(2)}, u32[]{:S(2)}) collective-permute-start(bf16[192,1024]{1,0:T(8,128)(2,1)S(1)} %fusion.12), channel_id=1, source_target_pairs={{0,128},{128,256},{256,384},{384,0},{1,129},{129,257},{257,385},{3... | collective-permute-start | bytes 1179656 | tf_op jit(solution)/shard_map/ppermute | solution.py:86
  131.9 40.0 %collective-permute-start.5 = (bf16[192,1024]{1,0:T(8,128)(2,1)}, bf16[192,1024]{1,0:T(8,128)(2,1)S(1)}, u32[]{:S(2)}, u32[]{:S(2)}) collective-permute-start(bf16[192,1024]{1,0:T(8,128)(2,1)} %fusion.11), channel_id=1, source_target_pairs={{0,256},{128,384},{256,0},{384,128},{1,257},{129,385},{257,1},{385... | collective-permute-start | bytes 1179656 | tf_op jit(solution)/shard_map/ppermute | solution.py:86
  159.7 26.7 %all-to-all-start.1 = ((bf16[16,19,512]{2,1,0:T(8,128)(2,1)}), bf16[16,19,512]{2,1,0:T(8,128)(2,1)S(1)}, u32[]{:S(2)}, u32[]{:S(2)}) async-start(bf16[16,19,512]{2,1,0:T(8,128)(2,1)} %reshape.49), calls=%async_computation.2 | async-start | bytes 786432 | tf_op jit(solution)/shard_map/all_to_all | solution.py:137
Sparse Core Ops, SparseCore 0:
  44.6 60.9 all-gather.1
  117.0 40.7 reduce-scatter.1

commit v15 on v11

--- a/solution.py
+++ b/solution.py
@@ -8,18 +8,25 @@
 CAP = 19
 
 
-def _expert_kernel(me_ref, rows_ref, gate_ref, *refs):
-    size = len(refs) - 2
+def _expert_kernel(me_ref, rows_hbm, gate_ref, *refs):
+    size = len(refs) - 5
     w_refs = refs[:size]
-    q_ref, hidden_ref = refs[size:]
+    q_hbm, hidden_ref, rows_buf, q_buf, sems = refs[size:]
     quarter = w_refs[0].shape[2]
     me = me_ref[0]
     nt = (((1,), (1,)), ((), ()))
+    starts = [pl.multiple_of(((me + size - k) % size) * quarter, quarter) for k in range(size)]
+    loads = []
+    for k in range(size):
+        cols = pl.ds(starts[k], quarter)
+        copy = pltpu.make_async_copy(rows_hbm.at[:, :, cols], rows_buf.at[k], sems.at[0, k])
+        copy.start()
+        loads.append(copy)
     gate_pre = None
     for k in range(size):
-        start = pl.multiple_of(((me + size - k) % size) * quarter, quarter)
-        f_k = rows_ref[0, :, pl.ds(start, quarter)]
-        g_k = rows_ref[1, :, pl.ds(start, quarter)]
+        loads[k].wait()
+        f_k = rows_buf[k, 0]
+        g_k = rows_buf[k, 1]
         a = lax.dot_general(f_k, w_refs[k][0], nt, preferred_element_type=jnp.float32)
         b = lax.dot_general(f_k, w_refs[k][1], nt, preferred_element_type=jnp.float32)
         c = lax.dot_general(g_k, w_refs[k][2], nt, preferred_element_type=jnp.float32)
@@ -34,17 +41,26 @@
     d_hidden = gate_f * back
     d_gate_b = (d_hidden * up_pre * sig * (1.0 + gate_pre * (1.0 - sig))).astype(jnp.bfloat16)
     d_up_b = (d_hidden * act).astype(jnp.bfloat16)
+    stores = []
     for k in range(size):
-        start = pl.multiple_of(((me + size - k) % size) * quarter, quarter)
         part = jnp.dot(d_gate_b, w_refs[k][0], preferred_element_type=jnp.float32)
         part = part + jnp.dot(d_up_b, w_refs[k][1], preferred_element_type=jnp.float32)
-        q_ref[:, pl.ds(start, quarter)] = part.astype(jnp.bfloat16)
+        q_buf[k] = part.astype(jnp.bfloat16)
+        copy = pltpu.make_async_copy(
+            q_buf.at[k], q_hbm.at[:, pl.ds(starts[k], quarter)], sems.at[1, k]
+        )
+        copy.start()
+        stores.append(copy)
     hidden_ref[...] = hidden.astype(jnp.bfloat16)
+    for copy in stores:
+        copy.wait()
 
 
 def expert_kernel(me, rows, gate_col, pieces):
     _, slots, width = rows.shape
     ffb = pieces[0].shape[1]
+    size = len(pieces)
+    quarter = width // size
     vmem = pltpu.VMEM
     return pl.pallas_call(
         _expert_kernel,
@@ -52,9 +68,14 @@
             jax.ShapeDtypeStruct((slots, width), jnp.bfloat16),
             jax.ShapeDtypeStruct((slots, ffb), jnp.bfloat16),
         ),
-        in_specs=[pl.BlockSpec(memory_space=pltpu.SMEM)]
-        + [pl.BlockSpec(memory_space=vmem)] * (2 + len(pieces)),
-        out_specs=(pl.BlockSpec(memory_space=vmem), pl.BlockSpec(memory_space=vmem)),
+        in_specs=[pl.BlockSpec(memory_space=pltpu.SMEM), pl.BlockSpec(memory_space=pl.ANY)]
+        + [pl.BlockSpec(memory_space=vmem)] * (1 + size),
+        out_specs=(pl.BlockSpec(memory_space=pl.ANY), pl.BlockSpec(memory_space=vmem)),
+        scratch_shapes=[
+            pltpu.VMEM((size, 2, slots, quarter), jnp.bfloat16),
+            pltpu.VMEM((size, slots, quarter), jnp.bfloat16),
+            pltpu.SemaphoreType.DMA((2, size)),
+        ],
         compiler_params=pltpu.CompilerParams(vmem_limit_bytes=48 * 1024 * 1024),
     )(me.reshape(1), rows, gate_col.reshape(slots, 1), *pieces)
 

time: 193 us -> 193 us (level)
  no operation moved by 1% of the time
where the time goes in v15:
time: 193 us; the launch traced here: 192 us
  waiting for transfers between devices  87.5 us (45%)
  blocking collectives  31.9 us (17%)
  starting transfers between devices  31 us (16%)
  between operations  14.4 us (7%)
  Pallas kernels  9.16 us (5%)
  local copies, waits for them, and re-layouts  8.33 us (4%)
  other arithmetic  5.55 us (3%)
  matrix products  4.3 us (2%)
    ppermute x3, waiting for transfers between devices, pieces_dp(): lax.ppermute(piece, 'dp', [(i, (i + shift) % size) for i in range(size)])  51.6 us
    all_to_all x1, blocking collectives, local(): lax.all_to_all(block, 'expert', split_axis=0, concat_axis=0, tiled=True)  31.9 us
    reduce_scatter x1, waiting for transfers between devices, local(): summed = lax.psum_scatter(d_part_b, 'etp', scatter_dimension=1, tiled=True)  22.5 us
    all_to_all x1, waiting for transfers between devices, local(): lax.all_to_all(summed.reshape(width, CAP, narrow), 'expert', split_axis=0...  13.4 us
    all_to_all x1, starting transfers between devices, local(): lax.all_to_all(summed.reshape(width, CAP, narrow), 'expert', split_axis=0...  11.9 us
    ppermute x3, starting transfers between devices, scatter_sum_dp(): lax.ppermute(outgoing, 'dp', [(i, (i + shift) % size) for i in range(size)])  9.64 us
    ppermute x3, starting transfers between devices, pieces_dp(): lax.ppermute(piece, 'dp', [(i, (i + shift) % size) for i in range(size)])  9.35 us
    pallas_call x1, Pallas kernels, expert_kernel(): pl.pallas_call(_expert_kernel, out_shape=(jax.ShapeDtypeStruct((slots, wi...  9.16 us
  transfers between devices with their start and end apart: 9, of which 4 were waited for; matrix products, arithmetic and copies ran while one was open for 6% of the time, Pallas kernels for 0%

profile of v15, /device:TPU:1, one launch (start us, length us, event | category | flops | bytes accessed | tf_op | source)
XLA Modules:
  0.0 192.0 jit_solution(7614525680275706271)
XLA Ops:
  7.2 0.0 copy-start
  7.2 0.0 copy-start.4
  7.2 0.0 all-gather.2.cloned.1.call-start
  7.2 0.8 add_select_fusion
  8.0 0.1 copy.35
  8.1 0.7 fusion.3
  8.8 0.8 copy.36
  9.6 0.4 select_reduce_fusion
  10.0 0.1 convert_element_type.84
  10.1 0.0 copy-done
  10.1 0.3 convolution_convert_fusion.1
  10.4 0.1 reshape.48
  10.5 0.0 copy-done.4
  10.5 0.3 convolution_convert_fusion.2
  10.8 0.1 reshape.47
  11.0 0.1 pad.15.clone
  11.0 0.3 fusion.8
  11.3 31.9 %all_to_all.10 = bf16[16,40,512]{2,1,0:T(8,128)(2,1)S(1)} all-to-all(bf16[16,40,512]{2,1,0:T(8,128)(2,1)S(1)} %fusion.8), channel_id=1, replica_groups=mesh['dp'=4,'expert'=16,'etp'=8] {'expert'}, dimensions={0} | all-to-all | bytes 1310720 | tf_op jit(solution)/shard_map/all_to_all | solution.py:130
  43.2 0.1 fusion.14
  43.3 0.0 copy-start.1
  43.3 0.0 copy-start.2
  43.3 0.0 copy-start.3
  43.3 0.1 stack_reshape.6
  43.5 0.1 stack_reshape.7
  43.6 0.9 pad_maximum_fusion.1
  44.5 0.0 all-gather.2.cloned.1.call-update
  44.5 0.0 reduce-scatter.2.cloned.1.call-start
  44.6 0.0 copy-done.1
  44.6 0.0 copy-done.2
  44.6 0.0 copy-done.3
  44.6 0.1 pad_maximum_fusion.refs_0_
  44.7 4.4 %collective-permute-start.2 = (bf16[3,192,1024]{2,1,0:T(8,128)(2,1)S(1)}, bf16[3,192,1024]{2,1,0:T(8,128)(2,1)S(1)}, u32[]{:S(2)}, u32[]{:S(2)}) collective-permute-start(bf16[3,192,1024]{2,1,0:T(8,128)(2,1)S(1)} %pad_maximum_fusion.refs_0_), channel_id=1, source_target_pairs={{0,384},{128,0},{256,128},{384,256},{1,385},{129,1},{257,129},{385... | collective-permute-start | bytes 3538952 | tf_op jit(solution)/shard_map/ppermute | solution.py:87
  49.1 2.4 %collective-permute-start.1 = (bf16[3,192,1024]{2,1,0:T(8,128)(2,1)S(1)}, bf16[3,192,1024]{2,1,0:T(8,128)(2,1)}, u32[]{:S(2)}, u32[]{:S(2)}) collective-permute-start(bf16[3,192,1024]{2,1,0:T(8,128)(2,1)S(1)} %pad_maximum_fusion.refs_0_), channel_id=1, source_target_pairs={{0,256},{128,384},{256,0},{384,128},{1,257},{129,385},{257,1},{385... | collective-permute-start | bytes 3538952 | tf_op jit(solution)/shard_map/ppermute | solution.py:87
  51.6 2.5 %collective-permute-start = (bf16[3,192,1024]{2,1,0:T(8,128)(2,1)S(1)}, bf16[3,192,1024]{2,1,0:T(8,128)(2,1)}, u32[]{:S(2)}, u32[]{:S(2)}) collective-permute-start(bf16[3,192,1024]{2,1,0:T(8,128)(2,1)S(1)} %pad_maximum_fusion.refs_0_), channel_id=1, source_target_pairs={{0,128},{128,256},{256,384},{384,0},{1,129},{129,257},{257,385},{3... | collective-permute-start | bytes 3538952 | tf_op jit(solution)/shard_map/ppermute | solution.py:87
  54.1 0.1 reshape_reshape_squeeze.4.gate_ref
  54.3 45.5 %collective-permute-done.2.refs_3_ = bf16[3,192,1024]{2,1,0:T(8,128)(2,1)S(1)} collective-permute-done((bf16[3,192,1024]{2,1,0:T(8,128)(2,1)S(1)}, bf16[3,192,1024]{2,1,0:T(8,128)(2,1)S(1)}, u32[]{:S(2)}, u32[]{:S(2)}) %collective-permute-start.2) | collective-permute-done | bytes 1179680 | tf_op jit(solution)/shard_map/ppermute | solution.py:87
  99.8 0.0 collective-permute-done.1.refs_2_
  99.8 6.1 %collective-permute-done.refs_1_ = bf16[3,192,1024]{2,1,0:T(8,128)(2,1)} collective-permute-done((bf16[3,192,1024]{2,1,0:T(8,128)(2,1)S(1)}, bf16[3,192,1024]{2,1,0:T(8,128)(2,1)}, u32[]{:S(2)}, u32[]{:S(2)}) %collective-permute-start) | collective-permute-done | bytes 1179680 | tf_op jit(solution)/shard_map/ppermute | solution.py:87
  105.8 0.0 all-gather.2.cloned.1.call-done.rows_hbm
  105.8 9.2 %shard_map.95 = (bf16[304,4096]{1,0:T(8,128)(2,1)}, bf16[304,192]{1,0:T(8,128)(2,1)S(1)}) custom-call(s32[1]{0:T(128)} %bitcast.me_ref, bf16[2,304,4096]{2,1,0:T(8,128)(2,1)} %all-gather.2.cloned.1.call-done.rows_hbm, bf16[304,1]{1,0:T(8,128)(2,1)S(1)} %reshape_reshape_squeeze.4.gate_ref, bf16[3,192,1024]{2,1,0:T(8,128)(2,1)S(1)} %pad_maximum_fusion.refs_0_, ...), custom_call_target="tpu_custom_call" | custom-call | tf_op jit(solution)/shard_map/pallas_call | solution.py:65
  115.0 0.0 reduce-scatter.2.cloned.1.call-update
  115.1 0.1 reshape.115
  115.2 2.8 %convolution_convert_fusion = bf16[192,4096]{1,0:T(8,128)(2,1)S(1)} fusion(bf16[304,192]{1,0:T(8,128)(2,1)S(1)} %get-tuple-element.6, bf16[2,304,4096]{2,1,0:T(8,128)(2,1)} %all-gather.2.cloned.1.call-done.rows_hbm, f32[304]{0:T(512)S(1)} %reshape.115), kind=kOutput, calls=%fused_computation | convolution fusion | flops 482672640 | bytes 4181184 | tf_op jit(solution)/shard_map/dot_general | solution.py:146
  118.0 1.2 reshape.51
  119.2 3.3 %constant_dynamic-slice_fusion.3 = (bf16[192,1,1024]{2,1,0:T(2,128)(2,1)S(1)}, bf16[192,1,1024]{2,1,0:T(2,128)(2,1)S(1)}, bf16[192,1,1024]{2,1,0:T(2,128)(2,1)S(1)}, bf16[192,1,1024]{2,1,0:T(2,128)(2,1)S(1)}) fusion(bf16[192,4,1024]{2,1,0:T(4,128)(2,1)S(1)} %reshape.51, s32[]{:T(128)S(6)} %select_n.48, s32[]{:T(128)S(6)} %select_n.52, s32[]{:T(128)S(6)} %select_n.50, ...), kind=kLoop, calls=%fused_computation.36 | loop fusion | bytes 3145744 | tf_op jit(solution)/shard_map/jit(_take) | solution.py:96
  122.5 0.2 fusion.10
  122.7 4.1 %collective-permute-start.5 = (bf16[192,1024]{1,0:T(8,128)(2,1)S(1)}, bf16[192,1024]{1,0:T(8,128)(2,1)S(1)}, u32[]{:S(2)}, u32[]{:S(2)}) collective-permute-start(bf16[192,1024]{1,0:T(8,128)(2,1)S(1)} %fusion.10), channel_id=1, source_target_pairs={{0,384},{128,0},{256,128},{384,256},{1,385},{129,1},{257,129},{385... | collective-permute-start | bytes 1179656 | tf_op jit(solution)/shard_map/ppermute | solution.py:99
  126.8 0.2 fusion.12
  126.9 1.9 %collective-permute-start.3 = (bf16[192,1024]{1,0:T(8,128)(2,1)S(1)}, bf16[192,1024]{1,0:T(8,128)(2,1)S(1)}, u32[]{:S(2)}, u32[]{:S(2)}) collective-permute-start(bf16[192,1024]{1,0:T(8,128)(2,1)S(1)} %fusion.12), channel_id=1, source_target_pairs={{0,128},{128,256},{256,384},{384,0},{1,129},{129,257},{257,385},{3... | collective-permute-start | bytes 1179656 | tf_op jit(solution)/shard_map/ppermute | solution.py:99
  128.9 0.9 fusion.11
  129.8 3.6 %collective-permute-start.4 = (bf16[192,1024]{1,0:T(8,128)(2,1)}, bf16[192,1024]{1,0:T(8,128)(2,1)S(1)}, u32[]{:S(2)}, u32[]{:S(2)}) collective-permute-start(bf16[192,1024]{1,0:T(8,128)(2,1)} %fusion.11), channel_id=1, source_target_pairs={{0,256},{128,384},{256,0},{384,128},{1,257},{129,385},{257,1},{385... | collective-permute-start | bytes 1179656 | tf_op jit(solution)/shard_map/ppermute | solution.py:99
  133.4 22.5 %reduce-scatter.2.cloned.1.call-done = bf16[304,512]{1,0:T(8,128)(2,1)} async-done(((bf16[304,4096]{1,0:T(8,128)(2,1)}), bf16[304,512]{1,0:T(8,128)(2,1)}) %reduce-scatter.2.cloned.1.call-update) | async-done | bytes 311312 | tf_op jit(solution)/shard_map/reduce_scatter | solution.py:142
  155.9 1.8 reshape.49
  157.7 11.9 %all-to-all-start.1 = ((bf16[16,19,512]{2,1,0:T(8,128)(2,1)}), bf16[16,19,512]{2,1,0:T(8,128)(2,1)S(1)}, u32[]{:S(2)}, u32[]{:S(2)}) async-start(bf16[16,19,512]{2,1,0:T(8,128)(2,1)} %reshape.49), calls=%async_computation.2 | async-start | bytes 786432 | tf_op jit(solution)/shard_map/all_to_all | solution.py:150
  169.6 0.0 collective-permute-done.5
  169.6 0.0 collective-permute-done.3
  169.6 0.0 collective-permute-done.4
  169.6 1.1 fusion.9
  170.8 13.4 %all-to-all-done.1 = bf16[16,19,512]{2,1,0:T(8,128)(2,1)S(1)} async-done(((bf16[16,19,512]{2,1,0:T(8,128)(2,1)}), bf16[16,19,512]{2,1,0:T(8,128)(2,1)S(1)}, u32[]{:S(2)}, u32[]{:S(2)}) %all-to-all-start.1) | async-done | bytes 311328 | tf_op jit(solution)/shard_map/all_to_all | solution.py:150
  184.2 0.1 reshape.50
  184.3 0.9 convolution_convert_fusion.3
  (2 shorter events, 0.1 us)
Async XLA Ops:
  7.2 2.9 %copy-start = (bf16[152,512]{1,0:T(8,128)(2,1)S(1)}, bf16[152,512]{1,0:T(8,128)(2,1)}, u32[]{:S(2)}) copy-start(bf16[152,512]{1,0:T(8,128)(2,1)} %param.11) | copy-start | bytes 466948
  7.2 3.4 %copy-start.4 = (bf16[152,512]{1,0:T(8,128)(2,1)S(1)}, bf16[152,512]{1,0:T(8,128)(2,1)}, u32[]{:S(2)}) copy-start(bf16[152,512]{1,0:T(8,128)(2,1)} %param.10) | copy-start | bytes 466948
  7.2 98.6 %all-gather.2.cloned.1.call-start = ((), (), s32[]{:S(2)}) async-start(), calls=%async_computation.3 | async-start | bytes 5603328 | tf_op jit(solution)/shard_map/all_gather | solution.py:139
  43.3 1.3 copy-start.1
  43.3 1.3 copy-start.2
  43.3 1.3 copy-start.3
  44.5 111.4 %reduce-scatter.2.cloned.1.call-start = ((), (), s32[]{:S(2)}) async-start(), calls=%async_computation.4 | async-start | bytes 2801664 | tf_op jit(solution)/shard_map/reduce_scatter | solution.py:142
  44.7 55.0 %collective-permute-start.2 = (bf16[3,192,1024]{2,1,0:T(8,128)(2,1)S(1)}, bf16[3,192,1024]{2,1,0:T(8,128)(2,1)S(1)}, u32[]{:S(2)}, u32[]{:S(2)}) collective-permute-start(bf16[3,192,1024]{2,1,0:T(8,128)(2,1)S(1)} %pad_maximum_fusion.refs_0_), channel_id=1, source_target_pairs={{0,384},{128,0},{256,128},{384,256},{1,385},{129,1},{257,129},{385... | collective-permute-start | bytes 3538952 | tf_op jit(solution)/shard_map/ppermute | solution.py:87
  49.1 50.6 %collective-permute-start.1 = (bf16[3,192,1024]{2,1,0:T(8,128)(2,1)S(1)}, bf16[3,192,1024]{2,1,0:T(8,128)(2,1)}, u32[]{:S(2)}, u32[]{:S(2)}) collective-permute-start(bf16[3,192,1024]{2,1,0:T(8,128)(2,1)S(1)} %pad_maximum_fusion.refs_0_), channel_id=1, source_target_pairs={{0,256},{128,384},{256,0},{384,128},{1,257},{129,385},{257,1},{385... | collective-permute-start | bytes 3538952 | tf_op jit(solution)/shard_map/ppermute | solution.py:87
  51.6 54.3 %collective-permute-start = (bf16[3,192,1024]{2,1,0:T(8,128)(2,1)S(1)}, bf16[3,192,1024]{2,1,0:T(8,128)(2,1)}, u32[]{:S(2)}, u32[]{:S(2)}) collective-permute-start(bf16[3,192,1024]{2,1,0:T(8,128)(2,1)S(1)} %pad_maximum_fusion.refs_0_), channel_id=1, source_target_pairs={{0,128},{128,256},{256,384},{384,0},{1,129},{129,257},{257,385},{3... | collective-permute-start | bytes 3538952 | tf_op jit(solution)/shard_map/ppermute | solution.py:87
  122.7 46.9 %collective-permute-start.5 = (bf16[192,1024]{1,0:T(8,128)(2,1)S(1)}, bf16[192,1024]{1,0:T(8,128)(2,1)S(1)}, u32[]{:S(2)}, u32[]{:S(2)}) collective-permute-start(bf16[192,1024]{1,0:T(8,128)(2,1)S(1)} %fusion.10), channel_id=1, source_target_pairs={{0,384},{128,0},{256,128},{384,256},{1,385},{129,1},{257,129},{385... | collective-permute-start | bytes 1179656 | tf_op jit(solution)/shard_map/ppermute | solution.py:99
  126.9 42.7 %collective-permute-start.3 = (bf16[192,1024]{1,0:T(8,128)(2,1)S(1)}, bf16[192,1024]{1,0:T(8,128)(2,1)S(1)}, u32[]{:S(2)}, u32[]{:S(2)}) collective-permute-start(bf16[192,1024]{1,0:T(8,128)(2,1)S(1)} %fusion.12), channel_id=1, source_target_pairs={{0,128},{128,256},{256,384},{384,0},{1,129},{129,257},{257,385},{3... | collective-permute-start | bytes 1179656 | tf_op jit(solution)/shard_map/ppermute | solution.py:99
  129.8 39.9 %collective-permute-start.4 = (bf16[192,1024]{1,0:T(8,128)(2,1)}, bf16[192,1024]{1,0:T(8,128)(2,1)S(1)}, u32[]{:S(2)}, u32[]{:S(2)}) collective-permute-start(bf16[192,1024]{1,0:T(8,128)(2,1)} %fusion.11), channel_id=1, source_target_pairs={{0,256},{128,384},{256,0},{384,128},{1,257},{129,385},{257,1},{385... | collective-permute-start | bytes 1179656 | tf_op jit(solution)/shard_map/ppermute | solution.py:99
  157.7 26.4 %all-to-all-start.1 = ((bf16[16,19,512]{2,1,0:T(8,128)(2,1)}), bf16[16,19,512]{2,1,0:T(8,128)(2,1)S(1)}, u32[]{:S(2)}, u32[]{:S(2)}) async-start(bf16[16,19,512]{2,1,0:T(8,128)(2,1)} %reshape.49), calls=%async_computation.2 | async-start | bytes 786432 | tf_op jit(solution)/shard_map/all_to_all | solution.py:150
Sparse Core Ops, SparseCore 0:
  44.6 60.9 all-gather.1
  115.1 40.7 reduce-scatter.1

commit v16 on v11

--- a/solution.py
+++ b/solution.py
@@ -106,7 +106,10 @@
         ],
         axis=1,
     )
-    recv = lax.all_to_all(block, "expert", split_axis=0, concat_axis=0, tiled=True)
+    rows_blk = block.shape[1]
+    recv = lax.all_to_all(
+        block.reshape(width, rows_blk * narrow), "expert", split_axis=0, concat_axis=0, tiled=True
+    ).reshape(width, rows_blk, narrow)
     recv_gate = recv[:, CAP, :CAP].reshape(slots)
     pair = jnp.stack(
         [
@@ -127,7 +130,7 @@
     )
     down_grad = scatter_sum_dp(term.astype(jnp.bfloat16))[None]
     returned = lax.all_to_all(
-        summed.reshape(width, CAP, narrow), "expert", split_axis=0, concat_axis=0, tiled=True
+        summed.reshape(width, CAP * narrow), "expert", split_axis=0, concat_axis=0, tiled=True
     ).reshape(slots, narrow)
     total = lax.dot_general(
         onehot, returned, (((0,), (0,)), ((), ())), preferred_element_type=jnp.float32

time: 193 us -> 207 us (1.073)
  other arithmetic: 5.55 us -> 20.3 us
  waiting for transfers between devices: 87.1 us -> 83.8 us
  local copies, waits for them, and re-layouts: 8.33 us -> 11.2 us
    all_to_all x0 -> x4, other arithmetic: none -> 13.3 us  [the longest x2 8.86 us: local(): lax.all_to_all(block.reshape(width, rows_blk * narrow), 'expert', split_a...]
    unnamed x10 -> x15, local copies, waits for them, and re-layouts: 0.03 us -> 2.39 us
  transfers between devices with their start and end apart: 9 -> 9, of which waited for: 4 -> 4; matrix products, arithmetic and copies ran while one was open for 6% -> 7% of each run, Pallas kernels for 0% -> 0%
where the time goes in v16:
time: 207 us
  waiting for transfers between devices  83.8 us (40%)
  blocking collectives  31.9 us (15%)
  starting transfers between devices  31.4 us (15%)
  other arithmetic  20.3 us (10%)
  between operations  14.5 us (7%)
  local copies, waits for them, and re-layouts  11.2 us (5%)
  Pallas kernels  9.34 us (5%)
  matrix products  4.29 us (2%)
    ppermute x3, waiting for transfers between devices, pieces_dp(): lax.ppermute(piece, 'dp', [(i, (i + shift) % size) for i in range(size)])  51.3 us
    all_to_all x1, blocking collectives, local(): lax.all_to_all(block.reshape(width, rows_blk * narrow), 'expert', split_a...  31.9 us
    reduce_scatter x1, waiting for transfers between devices, local(): summed = lax.psum_scatter(d_part_b, 'etp', scatter_dimension=1, tiled=True)  20.9 us
    all_to_all x1, starting transfers between devices, local(): lax.all_to_all(summed.reshape(width, CAP * narrow), 'expert', split_axis=...  12.1 us
    all_to_all x1, waiting for transfers between devices, local(): lax.all_to_all(summed.reshape(width, CAP * narrow), 'expert', split_axis=...  11.6 us
    ppermute x3, starting transfers between devices, scatter_sum_dp(): lax.ppermute(outgoing, 'dp', [(i, (i + shift) % size) for i in range(size)])  9.65 us
    ppermute x3, starting transfers between devices, pieces_dp(): lax.ppermute(piece, 'dp', [(i, (i + shift) % size) for i in range(size)])  9.57 us
    pallas_call x1, Pallas kernels, expert_kernel(): pl.pallas_call(_expert_kernel, out_shape=(jax.ShapeDtypeStruct((slots, wi...  9.34 us
  transfers between devices with their start and end apart: 9, of which 4 were waited for; matrix products, arithmetic and copies ran while one was open for 7% of the time, Pallas kernels for 0%

profile of v16, /device:TPU:1, one launch (start us, length us, event | category | flops | bytes accessed | tf_op | source)
XLA Modules:
  0.0 206.7 jit_solution(6302821103389419249)
XLA Ops:
  7.2 0.0 copy-start
  7.2 0.0 all-gather.2.cloned.1.call-start
  7.2 0.8 add_select_fusion
  8.0 0.1 copy.46
  8.1 0.7 fusion.3
  8.8 0.8 copy.47
  9.6 0.4 select_reduce_fusion
  10.0 0.1 convert_element_type.84
  10.1 0.3 convolution_convert_fusion.1
  10.4 0.1 reshape.58
  10.5 0.3 convolution_convert_fusion.2
  10.8 0.1 reshape.57
  11.0 0.1 pad.15.clone
  11.0 0.3 fusion.8
  11.3 0.4 all_to_all.16
  11.7 0.5 broadcast.84
  12.2 4.7 %reduce.8 = bf16[16,20480]{1,0:T(8,128)(2,1)S(1)} reduce(bf16[16,1,20480]{2,1,0:T(2,128)(2,1)S(1)} %all_to_all.16, bf16[]{:T(256)} %broadcast.84), dimensions={1}, to_apply=%all_to_all.16.reduce_sub_computation | reduce | bytes 1310722 | tf_op jit(solution)/shard_map/all_to_all | solution.py:110
  17.0 0.5 reshape.170
  17.4 31.9 %all_to_all.20 = bf16[16,2,10240]{2,1,0:T(2,128)(2,1)S(1)} all-to-all(bf16[16,2,10240]{2,1,0:T(2,128)(2,1)S(1)} %reshape.170), channel_id=1, replica_groups=mesh['dp'=4,'expert'=16,'etp'=8] {'expert'}, dimensions={0} | all-to-all | bytes 1310720 | tf_op jit(solution)/shard_map/all_to_all | solution.py:110
  49.3 0.6 reshape.171
  49.9 4.1 %reduce = bf16[16,20480]{1,0:T(8,128)(2,1)S(1)} reduce(bf16[16,1,20480]{2,1,0:T(2,128)(2,1)S(1)} %reshape.171, bf16[]{:T(256)} %constant.97), dimensions={1}, to_apply=%all_to_all.13.reduce_sub_computation | reduce | bytes 1310722 | tf_op jit(solution)/shard_map/all_to_all | solution.py:110
  54.1 0.2 copy.60
  54.3 0.1 fusion.14
  54.4 0.0 copy-start.1
  54.4 0.0 copy-start.2
  54.4 0.0 copy-start.3
  54.4 0.1 stack_reshape.6
  54.6 0.1 stack_reshape.7
  54.7 0.9 pad_maximum_fusion.1
  55.6 0.0 all-gather.2.cloned.1.call-update
  55.6 0.0 reduce-scatter.2.cloned.1.call-start
  55.7 0.1 pad_maximum_fusion.refs_0_
  55.8 4.4 %collective-permute-start.2 = (bf16[3,192,1024]{2,1,0:T(8,128)(2,1)S(1)}, bf16[3,192,1024]{2,1,0:T(8,128)(2,1)S(1)}, u32[]{:S(2)}, u32[]{:S(2)}) collective-permute-start(bf16[3,192,1024]{2,1,0:T(8,128)(2,1)S(1)} %pad_maximum_fusion.refs_0_), channel_id=1, source_target_pairs={{0,384},{128,0},{256,128},{384,256},{1,385},{129,1},{257,129},{385... | collective-permute-start | bytes 3538952 | tf_op jit(solution)/shard_map/ppermute | solution.py:66
  60.2 2.4 %collective-permute-start.1 = (bf16[3,192,1024]{2,1,0:T(8,128)(2,1)S(1)}, bf16[3,192,1024]{2,1,0:T(8,128)(2,1)}, u32[]{:S(2)}, u32[]{:S(2)}) collective-permute-start(bf16[3,192,1024]{2,1,0:T(8,128)(2,1)S(1)} %pad_maximum_fusion.refs_0_), channel_id=1, source_target_pairs={{0,256},{128,384},{256,0},{384,128},{1,257},{129,385},{257,1},{385... | collective-permute-start | bytes 3538952 | tf_op jit(solution)/shard_map/ppermute | solution.py:66
  62.7 2.7 %collective-permute-start = (bf16[3,192,1024]{2,1,0:T(8,128)(2,1)S(1)}, bf16[3,192,1024]{2,1,0:T(8,128)(2,1)}, u32[]{:S(2)}, u32[]{:S(2)}) collective-permute-start(bf16[3,192,1024]{2,1,0:T(8,128)(2,1)S(1)} %pad_maximum_fusion.refs_0_), channel_id=1, source_target_pairs={{0,128},{128,256},{256,384},{384,0},{1,129},{129,257},{257,385},{3... | collective-permute-start | bytes 3538952 | tf_op jit(solution)/shard_map/ppermute | solution.py:66
  65.5 0.1 reshape_reshape_squeeze.4.gate_ref
  65.6 45.3 %collective-permute-done.2.refs_3_ = bf16[3,192,1024]{2,1,0:T(8,128)(2,1)S(1)} collective-permute-done((bf16[3,192,1024]{2,1,0:T(8,128)(2,1)S(1)}, bf16[3,192,1024]{2,1,0:T(8,128)(2,1)S(1)}, u32[]{:S(2)}, u32[]{:S(2)}) %collective-permute-start.2) | collective-permute-done | bytes 1179680 | tf_op jit(solution)/shard_map/ppermute | solution.py:66
  110.9 6.1 %collective-permute-done.refs_1_ = bf16[3,192,1024]{2,1,0:T(8,128)(2,1)} collective-permute-done((bf16[3,192,1024]{2,1,0:T(8,128)(2,1)S(1)}, bf16[3,192,1024]{2,1,0:T(8,128)(2,1)}, u32[]{:S(2)}, u32[]{:S(2)}) %collective-permute-start) | collective-permute-done | bytes 1179680 | tf_op jit(solution)/shard_map/ppermute | solution.py:66
  116.9 9.3 %shard_map.95 = (bf16[304,4096]{1,0:T(8,128)(2,1)}, bf16[304,192]{1,0:T(8,128)(2,1)S(1)}) custom-call(s32[1]{0:T(128)} %bitcast.me_ref, bf16[2,304,4096]{2,1,0:T(8,128)(2,1)} %all-gather.2.cloned.1.call-done.rows_ref, bf16[304,1]{1,0:T(8,128)(2,1)S(1)} %reshape_reshape_squeeze.4.gate_ref, bf16[3,192,1024]{2,1,0:T(8,128)(2,1)S(1)} %pad_maximum_fusion.refs_0_, ...), custom_call_target="tpu_custom_call" | custom-call | tf_op jit(solution)/shard_map/pallas_call | solution.py:49
  126.3 0.0 reduce-scatter.2.cloned.1.call-update
  126.4 0.1 reshape.125
  126.5 2.8 %convolution_convert_fusion = bf16[192,4096]{1,0:T(8,128)(2,1)S(1)} fusion(bf16[304,192]{1,0:T(8,128)(2,1)S(1)} %get-tuple-element.6, bf16[2,304,4096]{2,1,0:T(8,128)(2,1)} %all-gather.2.cloned.1.call-done.rows_ref, f32[304]{0:T(512)S(1)} %reshape.125), kind=kOutput, calls=%fused_computation | convolution fusion | flops 482672640 | bytes 4181184 | tf_op jit(solution)/shard_map/dot_general | solution.py:128
  129.3 1.2 reshape.61
  130.5 3.3 %constant_dynamic-slice_fusion.3 = (bf16[192,1,1024]{2,1,0:T(2,128)(2,1)S(1)}, bf16[192,1,1024]{2,1,0:T(2,128)(2,1)S(1)}, bf16[192,1,1024]{2,1,0:T(2,128)(2,1)S(1)}, bf16[192,1,1024]{2,1,0:T(2,128)(2,1)S(1)}) fusion(bf16[192,4,1024]{2,1,0:T(4,128)(2,1)S(1)} %reshape.61, s32[]{:T(128)S(6)} %select_n.48, s32[]{:T(128)S(6)} %select_n.52, s32[]{:T(128)S(6)} %select_n.50, ...), kind=kLoop, calls=%fused_computation.36 | loop fusion | bytes 3145744 | tf_op jit(solution)/shard_map/jit(_take) | solution.py:75
  133.8 0.9 fusion.10
  134.7 4.1 %collective-permute-start.5 = (bf16[192,1024]{1,0:T(8,128)(2,1)}, bf16[192,1024]{1,0:T(8,128)(2,1)S(1)}, u32[]{:S(2)}, u32[]{:S(2)}) collective-permute-start(bf16[192,1024]{1,0:T(8,128)(2,1)} %fusion.10), channel_id=1, source_target_pairs={{0,384},{128,0},{256,128},{384,256},{1,385},{129,1},{257,129},{385... | collective-permute-start | bytes 1179656 | tf_op jit(solution)/shard_map/ppermute | solution.py:78
  138.8 0.9 fusion.12
  139.7 1.9 collective-permute-start.3
  141.7 0.9 fusion.11
  142.6 3.6 %collective-permute-start.4 = (bf16[192,1024]{1,0:T(8,128)(2,1)}, bf16[192,1024]{1,0:T(8,128)(2,1)S(1)}, u32[]{:S(2)}, u32[]{:S(2)}) collective-permute-start(bf16[192,1024]{1,0:T(8,128)(2,1)} %fusion.11), channel_id=1, source_target_pairs={{0,256},{128,384},{256,0},{384,128},{1,257},{129,385},{257,1},{385... | collective-permute-start | bytes 1179656 | tf_op jit(solution)/shard_map/ppermute | solution.py:78
  146.2 20.9 %reduce-scatter.2.cloned.1.call-done = bf16[304,512]{1,0:T(8,128)(2,1)} async-done(((bf16[304,4096]{1,0:T(8,128)(2,1)}), bf16[304,512]{1,0:T(8,128)(2,1)}) %reduce-scatter.2.cloned.1.call-update) | async-done | bytes 311312 | tf_op jit(solution)/shard_map/reduce_scatter | solution.py:124
  167.1 1.1 all_to_all.17
  168.2 2.5 %reduce.9 = bf16[16,9728]{1,0:T(8,128)(2,1)S(1)} reduce(bf16[16,1,9728]{2,1,0:T(2,128)(2,1)S(1)} %all_to_all.17, bf16[]{:T(256)} %broadcast.84), dimensions={1}, to_apply=%all_to_all.17.reduce_sub_computation | reduce | bytes 622594 | tf_op jit(solution)/shard_map/all_to_all | solution.py:132
  170.7 0.8 reshape.172
  171.4 12.1 %all-to-all-start.1 = ((bf16[16,2,4864]{2,1,0:T(2,128)(2,1)}), bf16[16,2,4864]{2,1,0:T(2,128)(2,1)S(1)}, u32[]{:S(2)}, u32[]{:S(2)}) async-start(bf16[16,2,4864]{2,1,0:T(2,128)(2,1)} %reshape.172), calls=%async_computation.2 | async-start | bytes 622592 | tf_op jit(solution)/shard_map/all_to_all | solution.py:132
  183.6 0.0 collective-permute-done.5
  183.6 0.0 collective-permute-done.3
  183.6 0.0 collective-permute-done.4
  183.6 1.1 fusion.9
  184.7 11.6 %all-to-all-done.1 = bf16[16,2,4864]{2,1,0:T(2,128)(2,1)S(1)} async-done(((bf16[16,2,4864]{2,1,0:T(2,128)(2,1)}), bf16[16,2,4864]{2,1,0:T(2,128)(2,1)S(1)}, u32[]{:S(2)}, u32[]{:S(2)}) %all-to-all-start.1) | async-done | bytes 311328 | tf_op jit(solution)/shard_map/all_to_all | solution.py:132
  196.3 0.3 reshape.173
  196.5 1.9 reduce.2
  198.5 0.5 reshape.60
  199.0 0.9 convolution_convert_fusion.3
  (10 shorter events, 0.1 us)
Async XLA Ops:
  7.2 2.9 %copy-start = (bf16[152,512]{1,0:T(8,128)(2,1)S(1)}, bf16[152,512]{1,0:T(8,128)(2,1)}, u32[]{:S(2)}) copy-start(bf16[152,512]{1,0:T(8,128)(2,1)} %param.11) | copy-start | bytes 466948
  7.2 3.4 %copy-start.4 = (bf16[152,512]{1,0:T(8,128)(2,1)S(1)}, bf16[152,512]{1,0:T(8,128)(2,1)}, u32[]{:S(2)}) copy-start(bf16[152,512]{1,0:T(8,128)(2,1)} %param.10) | copy-start | bytes 466948
  7.2 109.7 %all-gather.2.cloned.1.call-start = ((), (), s32[]{:S(2)}) async-start(), calls=%async_computation.3 | async-start | bytes 5603328 | tf_op jit(solution)/shard_map/all_gather | solution.py:121
  54.4 1.3 copy-start.1
  54.4 1.2 copy-start.2
  54.4 1.2 copy-start.3
  55.6 111.5 %reduce-scatter.2.cloned.1.call-start = ((), (), s32[]{:S(2)}) async-start(), calls=%async_computation.4 | async-start | bytes 2801664 | tf_op jit(solution)/shard_map/reduce_scatter | solution.py:124
  55.8 55.0 %collective-permute-start.2 = (bf16[3,192,1024]{2,1,0:T(8,128)(2,1)S(1)}, bf16[3,192,1024]{2,1,0:T(8,128)(2,1)S(1)}, u32[]{:S(2)}, u32[]{:S(2)}) collective-permute-start(bf16[3,192,1024]{2,1,0:T(8,128)(2,1)S(1)} %pad_maximum_fusion.refs_0_), channel_id=1, source_target_pairs={{0,384},{128,0},{256,128},{384,256},{1,385},{129,1},{257,129},{385... | collective-permute-start | bytes 3538952 | tf_op jit(solution)/shard_map/ppermute | solution.py:66
  60.2 50.6 %collective-permute-start.1 = (bf16[3,192,1024]{2,1,0:T(8,128)(2,1)S(1)}, bf16[3,192,1024]{2,1,0:T(8,128)(2,1)}, u32[]{:S(2)}, u32[]{:S(2)}) collective-permute-start(bf16[3,192,1024]{2,1,0:T(8,128)(2,1)S(1)} %pad_maximum_fusion.refs_0_), channel_id=1, source_target_pairs={{0,256},{128,384},{256,0},{384,128},{1,257},{129,385},{257,1},{385... | collective-permute-start | bytes 3538952 | tf_op jit(solution)/shard_map/ppermute | solution.py:66
  62.7 54.3 %collective-permute-start = (bf16[3,192,1024]{2,1,0:T(8,128)(2,1)S(1)}, bf16[3,192,1024]{2,1,0:T(8,128)(2,1)}, u32[]{:S(2)}, u32[]{:S(2)}) collective-permute-start(bf16[3,192,1024]{2,1,0:T(8,128)(2,1)S(1)} %pad_maximum_fusion.refs_0_), channel_id=1, source_target_pairs={{0,128},{128,256},{256,384},{384,0},{1,129},{129,257},{257,385},{3... | collective-permute-start | bytes 3538952 | tf_op jit(solution)/shard_map/ppermute | solution.py:66
  134.7 48.9 %collective-permute-start.5 = (bf16[192,1024]{1,0:T(8,128)(2,1)}, bf16[192,1024]{1,0:T(8,128)(2,1)S(1)}, u32[]{:S(2)}, u32[]{:S(2)}) collective-permute-start(bf16[192,1024]{1,0:T(8,128)(2,1)} %fusion.10), channel_id=1, source_target_pairs={{0,384},{128,0},{256,128},{384,256},{1,385},{129,1},{257,129},{385... | collective-permute-start | bytes 1179656 | tf_op jit(solution)/shard_map/ppermute | solution.py:78
  139.7 43.8 %collective-permute-start.3 = (bf16[192,1024]{1,0:T(8,128)(2,1)}, bf16[192,1024]{1,0:T(8,128)(2,1)S(1)}, u32[]{:S(2)}, u32[]{:S(2)}) collective-permute-start(bf16[192,1024]{1,0:T(8,128)(2,1)} %fusion.12), channel_id=1, source_target_pairs={{0,128},{128,256},{256,384},{384,0},{1,129},{129,257},{257,385},{3... | collective-permute-start | bytes 1179656 | tf_op jit(solution)/shard_map/ppermute | solution.py:78
  142.6 41.0 %collective-permute-start.4 = (bf16[192,1024]{1,0:T(8,128)(2,1)}, bf16[192,1024]{1,0:T(8,128)(2,1)S(1)}, u32[]{:S(2)}, u32[]{:S(2)}) collective-permute-start(bf16[192,1024]{1,0:T(8,128)(2,1)} %fusion.11), channel_id=1, source_target_pairs={{0,256},{128,384},{256,0},{384,128},{1,257},{129,385},{257,1},{385... | collective-permute-start | bytes 1179656 | tf_op jit(solution)/shard_map/ppermute | solution.py:78
  171.4 24.8 %all-to-all-start.1 = ((bf16[16,2,4864]{2,1,0:T(2,128)(2,1)}), bf16[16,2,4864]{2,1,0:T(2,128)(2,1)S(1)}, u32[]{:S(2)}, u32[]{:S(2)}) async-start(bf16[16,2,4864]{2,1,0:T(2,128)(2,1)} %reshape.172), calls=%async_computation.2 | async-start | bytes 622592 | tf_op jit(solution)/shard_map/all_to_all | solution.py:132
Sparse Core Ops, SparseCore 0:
  55.7 60.9 all-gather.1
  126.4 40.5 reduce-scatter.1

commit v17 on v11

--- a/solution.py
+++ b/solution.py
@@ -127,7 +127,7 @@
     )
     down_grad = scatter_sum_dp(term.astype(jnp.bfloat16))[None]
     returned = lax.all_to_all(
-        summed.reshape(width, CAP, narrow), "expert", split_axis=0, concat_axis=0, tiled=True
+        summed.reshape(width, 16, CAP * narrow // 16), "expert", split_axis=0, concat_axis=0, tiled=True
     ).reshape(slots, narrow)
     total = lax.dot_general(
         onehot, returned, (((0,), (0,)), ((), ())), preferred_element_type=jnp.float32

time: 193 us -> 192 us (level)
  no operation moved by 1% of the time
where the time goes in v17:
time: 192 us
  waiting for transfers between devices  85.6 us (45%)
  blocking collectives  31.9 us (17%)
  starting transfers between devices  31.6 us (16%)
  between operations  14.4 us (8%)
  Pallas kernels  9.36 us (5%)
  local copies, waits for them, and re-layouts  9.15 us (5%)
  other arithmetic  5.55 us (3%)
  matrix products  4.29 us (2%)
    ppermute x3, waiting for transfers between devices, pieces_dp(): lax.ppermute(piece, 'dp', [(i, (i + shift) % size) for i in range(size)])  51.6 us
    all_to_all x1, blocking collectives, local(): lax.all_to_all(block, 'expert', split_axis=0, concat_axis=0, tiled=True)  31.9 us
    reduce_scatter x1, waiting for transfers between devices, local(): summed = lax.psum_scatter(d_part_b, 'etp', scatter_dimension=1, tiled=True)  22.1 us
    all_to_all x1, starting transfers between devices, local(): lax.all_to_all(summed.reshape(width, 16, CAP * narrow // 16), 'expert', s...  12.5 us
    all_to_all x1, waiting for transfers between devices, local(): lax.all_to_all(summed.reshape(width, 16, CAP * narrow // 16), 'expert', s...  11.9 us
    ppermute x3, starting transfers between devices, scatter_sum_dp(): lax.ppermute(outgoing, 'dp', [(i, (i + shift) % size) for i in range(size)])  9.67 us
    pallas_call x1, Pallas kernels, expert_kernel(): pl.pallas_call(_expert_kernel, out_shape=(jax.ShapeDtypeStruct((slots, wi...  9.36 us
    ppermute x3, starting transfers between devices, pieces_dp(): lax.ppermute(piece, 'dp', [(i, (i + shift) % size) for i in range(size)])  9.35 us
  transfers between devices with their start and end apart: 9, of which 4 were waited for; matrix products, arithmetic and copies ran while one was open for 6% of the time, Pallas kernels for 0%

profile of v17, /device:TPU:1, one launch (start us, length us, event | category | flops | bytes accessed | tf_op | source)
XLA Modules:
  0.0 191.8 jit_solution(2024130818336147569)
XLA Ops:
  7.2 0.0 copy-start
  7.2 0.0 copy-start.4
  7.2 0.0 all-gather.2.cloned.1.call-start
  7.2 0.8 add_select_fusion
  8.0 0.1 copy.35
  8.1 0.7 fusion.3
  8.8 0.8 copy.36
  9.6 0.4 select_reduce_fusion
  10.0 0.1 convert_element_type.84
  10.1 0.0 copy-done
  10.1 0.3 convolution_convert_fusion.1
  10.4 0.1 reshape.48
  10.5 0.0 copy-done.4
  10.5 0.3 convolution_convert_fusion.2
  10.8 0.1 reshape.47
  11.0 0.1 pad.15.clone
  11.0 0.3 fusion.8
  11.3 31.9 %all_to_all.10 = bf16[16,40,512]{2,1,0:T(8,128)(2,1)S(1)} all-to-all(bf16[16,40,512]{2,1,0:T(8,128)(2,1)S(1)} %fusion.8), channel_id=1, replica_groups=mesh['dp'=4,'expert'=16,'etp'=8] {'expert'}, dimensions={0} | all-to-all | bytes 1310720 | tf_op jit(solution)/shard_map/all_to_all | solution.py:109
  43.2 0.1 fusion.14
  43.3 0.0 copy-start.1
  43.3 0.0 copy-start.2
  43.3 0.0 copy-start.3
  43.3 0.1 stack_reshape.6
  43.5 0.1 stack_reshape.7
  43.6 0.9 pad_maximum_fusion.1
  44.5 0.0 all-gather.2.cloned.1.call-update
  44.5 0.0 reduce-scatter.2.cloned.1.call-start
  44.6 0.0 copy-done.1
  44.6 0.0 copy-done.2
  44.6 0.0 copy-done.3
  44.6 0.1 pad_maximum_fusion.refs_0_
  44.7 4.4 %collective-permute-start.2 = (bf16[3,192,1024]{2,1,0:T(8,128)(2,1)S(1)}, bf16[3,192,1024]{2,1,0:T(8,128)(2,1)S(1)}, u32[]{:S(2)}, u32[]{:S(2)}) collective-permute-start(bf16[3,192,1024]{2,1,0:T(8,128)(2,1)S(1)} %pad_maximum_fusion.refs_0_), channel_id=1, source_target_pairs={{0,384},{128,0},{256,128},{384,256},{1,385},{129,1},{257,129},{385... | collective-permute-start | bytes 3538952 | tf_op jit(solution)/shard_map/ppermute | solution.py:66
  49.1 2.4 %collective-permute-start.1 = (bf16[3,192,1024]{2,1,0:T(8,128)(2,1)S(1)}, bf16[3,192,1024]{2,1,0:T(8,128)(2,1)}, u32[]{:S(2)}, u32[]{:S(2)}) collective-permute-start(bf16[3,192,1024]{2,1,0:T(8,128)(2,1)S(1)} %pad_maximum_fusion.refs_0_), channel_id=1, source_target_pairs={{0,256},{128,384},{256,0},{384,128},{1,257},{129,385},{257,1},{385... | collective-permute-start | bytes 3538952 | tf_op jit(solution)/shard_map/ppermute | solution.py:66
  51.6 2.5 %collective-permute-start = (bf16[3,192,1024]{2,1,0:T(8,128)(2,1)S(1)}, bf16[3,192,1024]{2,1,0:T(8,128)(2,1)}, u32[]{:S(2)}, u32[]{:S(2)}) collective-permute-start(bf16[3,192,1024]{2,1,0:T(8,128)(2,1)S(1)} %pad_maximum_fusion.refs_0_), channel_id=1, source_target_pairs={{0,128},{128,256},{256,384},{384,0},{1,129},{129,257},{257,385},{3... | collective-permute-start | bytes 3538952 | tf_op jit(solution)/shard_map/ppermute | solution.py:66
  54.1 0.1 reshape_reshape_squeeze.4.gate_ref
  54.3 45.5 %collective-permute-done.2.refs_3_ = bf16[3,192,1024]{2,1,0:T(8,128)(2,1)S(1)} collective-permute-done((bf16[3,192,1024]{2,1,0:T(8,128)(2,1)S(1)}, bf16[3,192,1024]{2,1,0:T(8,128)(2,1)S(1)}, u32[]{:S(2)}, u32[]{:S(2)}) %collective-permute-start.2) | collective-permute-done | bytes 1179680 | tf_op jit(solution)/shard_map/ppermute | solution.py:66
  99.8 0.0 collective-permute-done.1.refs_2_
  99.8 6.1 %collective-permute-done.refs_1_ = bf16[3,192,1024]{2,1,0:T(8,128)(2,1)} collective-permute-done((bf16[3,192,1024]{2,1,0:T(8,128)(2,1)S(1)}, bf16[3,192,1024]{2,1,0:T(8,128)(2,1)}, u32[]{:S(2)}, u32[]{:S(2)}) %collective-permute-start) | collective-permute-done | bytes 1179680 | tf_op jit(solution)/shard_map/ppermute | solution.py:66
  105.8 0.0 all-gather.2.cloned.1.call-done.rows_ref
  105.8 9.4 %shard_map.95 = (bf16[304,4096]{1,0:T(8,128)(2,1)}, bf16[304,192]{1,0:T(8,128)(2,1)S(1)}) custom-call(s32[1]{0:T(128)} %bitcast.me_ref, bf16[2,304,4096]{2,1,0:T(8,128)(2,1)} %all-gather.2.cloned.1.call-done.rows_ref, bf16[304,1]{1,0:T(8,128)(2,1)S(1)} %reshape_reshape_squeeze.4.gate_ref, bf16[3,192,1024]{2,1,0:T(8,128)(2,1)S(1)} %pad_maximum_fusion.refs_0_, ...), custom_call_target="tpu_custom_call" | custom-call | tf_op jit(solution)/shard_map/pallas_call | solution.py:49
  115.2 0.0 reduce-scatter.2.cloned.1.call-update
  115.3 0.1 reshape.115
  115.4 2.8 %convolution_convert_fusion = bf16[192,4096]{1,0:T(8,128)(2,1)S(1)} fusion(bf16[304,192]{1,0:T(8,128)(2,1)S(1)} %get-tuple-element.6, bf16[2,304,4096]{2,1,0:T(8,128)(2,1)} %all-gather.2.cloned.1.call-done.rows_ref, f32[304]{0:T(512)S(1)} %reshape.115), kind=kOutput, calls=%fused_computation | convolution fusion | flops 482672640 | bytes 4181184 | tf_op jit(solution)/shard_map/dot_general | solution.py:125
  118.2 1.2 reshape.51
  119.4 3.3 %constant_dynamic-slice_fusion.3 = (bf16[192,1,1024]{2,1,0:T(2,128)(2,1)S(1)}, bf16[192,1,1024]{2,1,0:T(2,128)(2,1)S(1)}, bf16[192,1,1024]{2,1,0:T(2,128)(2,1)S(1)}, bf16[192,1,1024]{2,1,0:T(2,128)(2,1)S(1)}) fusion(bf16[192,4,1024]{2,1,0:T(4,128)(2,1)S(1)} %reshape.51, s32[]{:T(128)S(6)} %select_n.48, s32[]{:T(128)S(6)} %select_n.52, s32[]{:T(128)S(6)} %select_n.50, ...), kind=kLoop, calls=%fused_computation.36 | loop fusion | bytes 3145744 | tf_op jit(solution)/shard_map/jit(_take) | solution.py:75
  122.7 0.2 fusion.10
  122.9 4.1 %collective-permute-start.5 = (bf16[192,1024]{1,0:T(8,128)(2,1)S(1)}, bf16[192,1024]{1,0:T(8,128)(2,1)S(1)}, u32[]{:S(2)}, u32[]{:S(2)}) collective-permute-start(bf16[192,1024]{1,0:T(8,128)(2,1)S(1)} %fusion.10), channel_id=1, source_target_pairs={{0,384},{128,0},{256,128},{384,256},{1,385},{129,1},{257,129},{385... | collective-permute-start | bytes 1179656 | tf_op jit(solution)/shard_map/ppermute | solution.py:78
  127.0 0.2 fusion.12
  127.1 1.9 %collective-permute-start.3 = (bf16[192,1024]{1,0:T(8,128)(2,1)S(1)}, bf16[192,1024]{1,0:T(8,128)(2,1)S(1)}, u32[]{:S(2)}, u32[]{:S(2)}) collective-permute-start(bf16[192,1024]{1,0:T(8,128)(2,1)S(1)} %fusion.12), channel_id=1, source_target_pairs={{0,128},{128,256},{256,384},{384,0},{1,129},{129,257},{257,385},{3... | collective-permute-start | bytes 1179656 | tf_op jit(solution)/shard_map/ppermute | solution.py:78
  129.1 0.9 fusion.11
  130.0 3.6 %collective-permute-start.4 = (bf16[192,1024]{1,0:T(8,128)(2,1)}, bf16[192,1024]{1,0:T(8,128)(2,1)S(1)}, u32[]{:S(2)}, u32[]{:S(2)}) collective-permute-start(bf16[192,1024]{1,0:T(8,128)(2,1)} %fusion.11), channel_id=1, source_target_pairs={{0,256},{128,384},{256,0},{384,128},{1,257},{129,385},{257,1},{385... | collective-permute-start | bytes 1179656 | tf_op jit(solution)/shard_map/ppermute | solution.py:78
  133.6 22.1 %reduce-scatter.2.cloned.1.call-done = bf16[304,512]{1,0:T(8,128)(2,1)} async-done(((bf16[304,4096]{1,0:T(8,128)(2,1)}), bf16[304,512]{1,0:T(8,128)(2,1)}) %reduce-scatter.2.cloned.1.call-update) | async-done | bytes 311312 | tf_op jit(solution)/shard_map/reduce_scatter | solution.py:121
  155.7 2.1 %reshape.49 = bf16[16,16,608]{2,1,0:T(8,128)(2,1)} reshape(bf16[304,512]{1,0:T(8,128)(2,1)} %reduce-scatter.2.cloned.1.call-done) | data formatting | bytes 622592 | tf_op jit(solution)/shard_map/reshape | solution.py:130
  157.8 12.5 %all-to-all-start.1 = ((bf16[16,16,608]{2,1,0:T(8,128)(2,1)}), bf16[16,16,608]{2,1,0:T(8,128)(2,1)S(1)}, u32[]{:S(2)}, u32[]{:S(2)}) async-start(bf16[16,16,608]{2,1,0:T(8,128)(2,1)} %reshape.49), calls=%async_computation.2 | async-start | bytes 655360 | tf_op jit(solution)/shard_map/all_to_all | solution.py:129
  170.3 0.0 collective-permute-done.5
  170.3 0.0 collective-permute-done.3
  170.3 0.0 collective-permute-done.4
  170.4 1.1 fusion.9
  171.5 11.9 %all-to-all-done.1 = bf16[16,16,608]{2,1,0:T(8,128)(2,1)S(1)} async-done(((bf16[16,16,608]{2,1,0:T(8,128)(2,1)}), bf16[16,16,608]{2,1,0:T(8,128)(2,1)S(1)}, u32[]{:S(2)}, u32[]{:S(2)}) %all-to-all-start.1) | async-done | bytes 311328 | tf_op jit(solution)/shard_map/all_to_all | solution.py:129
  183.4 0.6 reshape.50
  184.0 0.9 convolution_convert_fusion.3
  (2 shorter events, 0.1 us)
Async XLA Ops:
  7.2 2.9 %copy-start = (bf16[152,512]{1,0:T(8,128)(2,1)S(1)}, bf16[152,512]{1,0:T(8,128)(2,1)}, u32[]{:S(2)}) copy-start(bf16[152,512]{1,0:T(8,128)(2,1)} %param.11) | copy-start | bytes 466948
  7.2 3.4 %copy-start.4 = (bf16[152,512]{1,0:T(8,128)(2,1)S(1)}, bf16[152,512]{1,0:T(8,128)(2,1)}, u32[]{:S(2)}) copy-start(bf16[152,512]{1,0:T(8,128)(2,1)} %param.10) | copy-start | bytes 466948
  7.2 98.6 %all-gather.2.cloned.1.call-start = ((), (), s32[]{:S(2)}) async-start(), calls=%async_computation.3 | async-start | bytes 5603328 | tf_op jit(solution)/shard_map/all_gather | solution.py:118
  43.3 1.3 copy-start.1
  43.3 1.3 copy-start.2
  43.3 1.3 copy-start.3
  44.5 111.2 %reduce-scatter.2.cloned.1.call-start = ((), (), s32[]{:S(2)}) async-start(), calls=%async_computation.4 | async-start | bytes 2801664 | tf_op jit(solution)/shard_map/reduce_scatter | solution.py:121
  44.7 55.0 %collective-permute-start.2 = (bf16[3,192,1024]{2,1,0:T(8,128)(2,1)S(1)}, bf16[3,192,1024]{2,1,0:T(8,128)(2,1)S(1)}, u32[]{:S(2)}, u32[]{:S(2)}) collective-permute-start(bf16[3,192,1024]{2,1,0:T(8,128)(2,1)S(1)} %pad_maximum_fusion.refs_0_), channel_id=1, source_target_pairs={{0,384},{128,0},{256,128},{384,256},{1,385},{129,1},{257,129},{385... | collective-permute-start | bytes 3538952 | tf_op jit(solution)/shard_map/ppermute | solution.py:66
  49.1 50.6 %collective-permute-start.1 = (bf16[3,192,1024]{2,1,0:T(8,128)(2,1)S(1)}, bf16[3,192,1024]{2,1,0:T(8,128)(2,1)}, u32[]{:S(2)}, u32[]{:S(2)}) collective-permute-start(bf16[3,192,1024]{2,1,0:T(8,128)(2,1)S(1)} %pad_maximum_fusion.refs_0_), channel_id=1, source_target_pairs={{0,256},{128,384},{256,0},{384,128},{1,257},{129,385},{257,1},{385... | collective-permute-start | bytes 3538952 | tf_op jit(solution)/shard_map/ppermute | solution.py:66
  51.6 54.3 %collective-permute-start = (bf16[3,192,1024]{2,1,0:T(8,128)(2,1)S(1)}, bf16[3,192,1024]{2,1,0:T(8,128)(2,1)}, u32[]{:S(2)}, u32[]{:S(2)}) collective-permute-start(bf16[3,192,1024]{2,1,0:T(8,128)(2,1)S(1)} %pad_maximum_fusion.refs_0_), channel_id=1, source_target_pairs={{0,128},{128,256},{256,384},{384,0},{1,129},{129,257},{257,385},{3... | collective-permute-start | bytes 3538952 | tf_op jit(solution)/shard_map/ppermute | solution.py:66
  122.9 47.5 %collective-permute-start.5 = (bf16[192,1024]{1,0:T(8,128)(2,1)S(1)}, bf16[192,1024]{1,0:T(8,128)(2,1)S(1)}, u32[]{:S(2)}, u32[]{:S(2)}) collective-permute-start(bf16[192,1024]{1,0:T(8,128)(2,1)S(1)} %fusion.10), channel_id=1, source_target_pairs={{0,384},{128,0},{256,128},{384,256},{1,385},{129,1},{257,129},{385... | collective-permute-start | bytes 1179656 | tf_op jit(solution)/shard_map/ppermute | solution.py:78
  127.1 43.2 %collective-permute-start.3 = (bf16[192,1024]{1,0:T(8,128)(2,1)S(1)}, bf16[192,1024]{1,0:T(8,128)(2,1)S(1)}, u32[]{:S(2)}, u32[]{:S(2)}) collective-permute-start(bf16[192,1024]{1,0:T(8,128)(2,1)S(1)} %fusion.12), channel_id=1, source_target_pairs={{0,128},{128,256},{256,384},{384,0},{1,129},{129,257},{257,385},{3... | collective-permute-start | bytes 1179656 | tf_op jit(solution)/shard_map/ppermute | solution.py:78
  130.0 40.4 %collective-permute-start.4 = (bf16[192,1024]{1,0:T(8,128)(2,1)}, bf16[192,1024]{1,0:T(8,128)(2,1)S(1)}, u32[]{:S(2)}, u32[]{:S(2)}) collective-permute-start(bf16[192,1024]{1,0:T(8,128)(2,1)} %fusion.11), channel_id=1, source_target_pairs={{0,256},{128,384},{256,0},{384,128},{1,257},{129,385},{257,1},{385... | collective-permute-start | bytes 1179656 | tf_op jit(solution)/shard_map/ppermute | solution.py:78
  157.8 25.6 %all-to-all-start.1 = ((bf16[16,16,608]{2,1,0:T(8,128)(2,1)}), bf16[16,16,608]{2,1,0:T(8,128)(2,1)S(1)}, u32[]{:S(2)}, u32[]{:S(2)}) async-start(bf16[16,16,608]{2,1,0:T(8,128)(2,1)} %reshape.49), calls=%async_computation.2 | async-start | bytes 655360 | tf_op jit(solution)/shard_map/all_to_all | solution.py:129
Sparse Core Ops, SparseCore 0:
  44.6 60.9 all-gather.1
  115.3 40.3 reduce-scatter.1

commit v18 on v11

--- a/solution.py
+++ b/solution.py
@@ -106,7 +106,9 @@
         ],
         axis=1,
     )
-    recv = lax.all_to_all(block, "expert", split_axis=0, concat_axis=0, tiled=True)
+    recv = lax.all_to_all(
+        block.reshape(width, 16, -1), "expert", split_axis=0, concat_axis=0, tiled=True
+    ).reshape(block.shape)
     recv_gate = recv[:, CAP, :CAP].reshape(slots)
     pair = jnp.stack(
         [

time: 193 us -> 194 us (level)
  no operation moved by 1% of the time
where the time goes in v18:
time: 194 us; the launch traced here: 193 us
  waiting for transfers between devices  87.6 us (45%)
  blocking collectives  31.9 us (16%)
  starting transfers between devices  31 us (16%)
  between operations  14.4 us (7%)
  local copies, waits for them, and re-layouts  9.38 us (5%)
  Pallas kernels  9.36 us (5%)
  other arithmetic  5.55 us (3%)
  matrix products  4.29 us (2%)
    ppermute x3, waiting for transfers between devices, pieces_dp(): lax.ppermute(piece, 'dp', [(i, (i + shift) % size) for i in range(size)])  51.6 us
    all_to_all x1, blocking collectives, local(): lax.all_to_all(block.reshape(width, 16, -1), 'expert', split_axis=0, conc...  31.9 us
    reduce_scatter x1, waiting for transfers between devices, local(): summed = lax.psum_scatter(d_part_b, 'etp', scatter_dimension=1, tiled=True)  22.6 us
    all_to_all x1, waiting for transfers between devices, local(): lax.all_to_all(summed.reshape(width, CAP, narrow), 'expert', split_axis=0...  13.4 us
    all_to_all x1, starting transfers between devices, local(): lax.all_to_all(summed.reshape(width, CAP, narrow), 'expert', split_axis=0...  11.9 us
    ppermute x3, starting transfers between devices, scatter_sum_dp(): lax.ppermute(outgoing, 'dp', [(i, (i + shift) % size) for i in range(size)])  9.68 us
    pallas_call x1, Pallas kernels, expert_kernel(): pl.pallas_call(_expert_kernel, out_shape=(jax.ShapeDtypeStruct((slots, wi...  9.36 us
    ppermute x3, starting transfers between devices, pieces_dp(): lax.ppermute(piece, 'dp', [(i, (i + shift) % size) for i in range(size)])  9.35 us
  transfers between devices with their start and end apart: 9, of which 4 were waited for; matrix products, arithmetic and copies ran while one was open for 6% of the time, Pallas kernels for 0%

profile of v18, /device:TPU:1, one launch (start us, length us, event | category | flops | bytes accessed | tf_op | source)
XLA Modules:
  0.0 193.4 jit_solution(6025481931826836113)
XLA Ops:
  7.2 0.0 copy-start
  7.2 0.0 copy-start.4
  7.2 0.0 all-gather.2.cloned.1.call-start
  7.2 0.8 add_select_fusion
  8.0 0.1 copy.26
  8.1 0.7 fusion.3
  8.8 0.8 copy.27
  9.6 0.4 select_reduce_fusion
  10.0 0.1 convert_element_type.84
  10.1 0.0 copy-done
  10.1 0.3 convolution_convert_fusion.1
  10.4 0.1 reshape.54
  10.5 0.0 copy-done.4
  10.5 0.3 convolution_convert_fusion.2
  10.8 0.1 reshape.53
  11.0 0.1 pad.15.clone
  11.0 0.3 fusion.8
  11.3 0.5 reshape.55
  11.9 31.9 %all_to_all.10 = bf16[16,16,1280]{2,1,0:T(8,128)(2,1)S(1)} all-to-all(bf16[16,16,1280]{2,1,0:T(8,128)(2,1)S(1)} %reshape.55), channel_id=1, replica_groups=mesh['dp'=4,'expert'=16,'etp'=8] {'expert'}, dimensions={0} | all-to-all | bytes 1310720 | tf_op jit(solution)/shard_map/all_to_all | solution.py:109
  43.7 0.5 reshape.56
  44.2 0.1 fusion.14
  44.4 0.0 copy-start.1
  44.4 0.0 copy-start.2
  44.4 0.0 copy-start.3
  44.4 0.1 stack_reshape.6
  44.5 0.1 stack_reshape.7
  44.7 0.9 pad_maximum_fusion.1
  45.5 0.0 all-gather.2.cloned.1.call-update
  45.6 0.0 reduce-scatter.2.cloned.1.call-start
  45.6 0.0 copy-done.1
  45.6 0.0 copy-done.2
  45.6 0.0 copy-done.3
  45.6 0.1 pad_maximum_fusion.refs_0_
  45.8 4.4 %collective-permute-start.2 = (bf16[3,192,1024]{2,1,0:T(8,128)(2,1)S(1)}, bf16[3,192,1024]{2,1,0:T(8,128)(2,1)S(1)}, u32[]{:S(2)}, u32[]{:S(2)}) collective-permute-start(bf16[3,192,1024]{2,1,0:T(8,128)(2,1)S(1)} %pad_maximum_fusion.refs_0_), channel_id=1, source_target_pairs={{0,384},{128,0},{256,128},{384,256},{1,385},{129,1},{257,129},{385... | collective-permute-start | bytes 3538952 | tf_op jit(solution)/shard_map/ppermute | solution.py:66
  50.2 2.4 %collective-permute-start.1 = (bf16[3,192,1024]{2,1,0:T(8,128)(2,1)S(1)}, bf16[3,192,1024]{2,1,0:T(8,128)(2,1)}, u32[]{:S(2)}, u32[]{:S(2)}) collective-permute-start(bf16[3,192,1024]{2,1,0:T(8,128)(2,1)S(1)} %pad_maximum_fusion.refs_0_), channel_id=1, source_target_pairs={{0,256},{128,384},{256,0},{384,128},{1,257},{129,385},{257,1},{385... | collective-permute-start | bytes 3538952 | tf_op jit(solution)/shard_map/ppermute | solution.py:66
  52.6 2.5 %collective-permute-start = (bf16[3,192,1024]{2,1,0:T(8,128)(2,1)S(1)}, bf16[3,192,1024]{2,1,0:T(8,128)(2,1)}, u32[]{:S(2)}, u32[]{:S(2)}) collective-permute-start(bf16[3,192,1024]{2,1,0:T(8,128)(2,1)S(1)} %pad_maximum_fusion.refs_0_), channel_id=1, source_target_pairs={{0,128},{128,256},{256,384},{384,0},{1,129},{129,257},{257,385},{3... | collective-permute-start | bytes 3538952 | tf_op jit(solution)/shard_map/ppermute | solution.py:66
  55.2 0.1 reshape_reshape_squeeze.4.gate_ref
  55.3 45.5 %collective-permute-done.2.refs_3_ = bf16[3,192,1024]{2,1,0:T(8,128)(2,1)S(1)} collective-permute-done((bf16[3,192,1024]{2,1,0:T(8,128)(2,1)S(1)}, bf16[3,192,1024]{2,1,0:T(8,128)(2,1)S(1)}, u32[]{:S(2)}, u32[]{:S(2)}) %collective-permute-start.2) | collective-permute-done | bytes 1179680 | tf_op jit(solution)/shard_map/ppermute | solution.py:66
  100.8 0.0 collective-permute-done.1.refs_2_
  100.8 6.1 %collective-permute-done.refs_1_ = bf16[3,192,1024]{2,1,0:T(8,128)(2,1)} collective-permute-done((bf16[3,192,1024]{2,1,0:T(8,128)(2,1)S(1)}, bf16[3,192,1024]{2,1,0:T(8,128)(2,1)}, u32[]{:S(2)}, u32[]{:S(2)}) %collective-permute-start) | collective-permute-done | bytes 1179680 | tf_op jit(solution)/shard_map/ppermute | solution.py:66
  106.9 0.0 all-gather.2.cloned.1.call-done.rows_ref
  106.9 9.4 %shard_map.95 = (bf16[304,4096]{1,0:T(8,128)(2,1)}, bf16[304,192]{1,0:T(8,128)(2,1)S(1)}) custom-call(s32[1]{0:T(128)} %bitcast.me_ref, bf16[2,304,4096]{2,1,0:T(8,128)(2,1)} %all-gather.2.cloned.1.call-done.rows_ref, bf16[304,1]{1,0:T(8,128)(2,1)S(1)} %reshape_reshape_squeeze.4.gate_ref, bf16[3,192,1024]{2,1,0:T(8,128)(2,1)S(1)} %pad_maximum_fusion.refs_0_, ...), custom_call_target="tpu_custom_call" | custom-call | tf_op jit(solution)/shard_map/pallas_call | solution.py:49
  116.3 0.0 reduce-scatter.2.cloned.1.call-update
  116.4 0.1 reshape.123
  116.5 2.8 %convolution_convert_fusion = bf16[192,4096]{1,0:T(8,128)(2,1)S(1)} fusion(bf16[304,192]{1,0:T(8,128)(2,1)S(1)} %get-tuple-element.6, bf16[2,304,4096]{2,1,0:T(8,128)(2,1)} %all-gather.2.cloned.1.call-done.rows_ref, f32[304]{0:T(512)S(1)} %reshape.123), kind=kOutput, calls=%fused_computation | convolution fusion | flops 482672640 | bytes 4181184 | tf_op jit(solution)/shard_map/dot_general | solution.py:127
  119.3 1.2 reshape.59
  120.5 3.3 %constant_dynamic-slice_fusion.3 = (bf16[192,1,1024]{2,1,0:T(2,128)(2,1)S(1)}, bf16[192,1,1024]{2,1,0:T(2,128)(2,1)S(1)}, bf16[192,1,1024]{2,1,0:T(2,128)(2,1)S(1)}, bf16[192,1,1024]{2,1,0:T(2,128)(2,1)S(1)}) fusion(bf16[192,4,1024]{2,1,0:T(4,128)(2,1)S(1)} %reshape.59, s32[]{:T(128)S(6)} %select_n.48, s32[]{:T(128)S(6)} %select_n.52, s32[]{:T(128)S(6)} %select_n.50, ...), kind=kLoop, calls=%fused_computation.36 | loop fusion | bytes 3145744 | tf_op jit(solution)/shard_map/jit(_take) | solution.py:75
  123.8 0.2 fusion.10
  123.9 4.1 %collective-permute-start.5 = (bf16[192,1024]{1,0:T(8,128)(2,1)S(1)}, bf16[192,1024]{1,0:T(8,128)(2,1)S(1)}, u32[]{:S(2)}, u32[]{:S(2)}) collective-permute-start(bf16[192,1024]{1,0:T(8,128)(2,1)S(1)} %fusion.10), channel_id=1, source_target_pairs={{0,384},{128,0},{256,128},{384,256},{1,385},{129,1},{257,129},{385... | collective-permute-start | bytes 1179656 | tf_op jit(solution)/shard_map/ppermute | solution.py:78
  128.1 0.2 fusion.12
  128.2 1.9 collective-permute-start.3
  130.1 0.9 fusion.11
  131.1 3.6 %collective-permute-start.4 = (bf16[192,1024]{1,0:T(8,128)(2,1)}, bf16[192,1024]{1,0:T(8,128)(2,1)S(1)}, u32[]{:S(2)}, u32[]{:S(2)}) collective-permute-start(bf16[192,1024]{1,0:T(8,128)(2,1)} %fusion.11), channel_id=1, source_target_pairs={{0,256},{128,384},{256,0},{384,128},{1,257},{129,385},{257,1},{385... | collective-permute-start | bytes 1179656 | tf_op jit(solution)/shard_map/ppermute | solution.py:78
  134.7 22.6 %reduce-scatter.2.cloned.1.call-done = bf16[304,512]{1,0:T(8,128)(2,1)} async-done(((bf16[304,4096]{1,0:T(8,128)(2,1)}), bf16[304,512]{1,0:T(8,128)(2,1)}) %reduce-scatter.2.cloned.1.call-update) | async-done | bytes 311312 | tf_op jit(solution)/shard_map/reduce_scatter | solution.py:123
  157.3 1.8 reshape.57
  159.1 11.9 %all-to-all-start.1 = ((bf16[16,19,512]{2,1,0:T(8,128)(2,1)}), bf16[16,19,512]{2,1,0:T(8,128)(2,1)S(1)}, u32[]{:S(2)}, u32[]{:S(2)}) async-start(bf16[16,19,512]{2,1,0:T(8,128)(2,1)} %reshape.57), calls=%async_computation.2 | async-start | bytes 786432 | tf_op jit(solution)/shard_map/all_to_all | solution.py:131
  171.0 0.0 collective-permute-done.5
  171.0 0.0 collective-permute-done.3
  171.0 0.0 collective-permute-done.4
  171.0 1.1 fusion.9
  172.1 13.4 %all-to-all-done.1 = bf16[16,19,512]{2,1,0:T(8,128)(2,1)S(1)} async-done(((bf16[16,19,512]{2,1,0:T(8,128)(2,1)}), bf16[16,19,512]{2,1,0:T(8,128)(2,1)S(1)}, u32[]{:S(2)}, u32[]{:S(2)}) %all-to-all-start.1) | async-done | bytes 311328 | tf_op jit(solution)/shard_map/all_to_all | solution.py:131
  185.5 0.1 reshape.58
  185.7 0.9 convolution_convert_fusion.3
  (2 shorter events, 0.1 us)
Async XLA Ops:
  7.2 2.9 %copy-start = (bf16[152,512]{1,0:T(8,128)(2,1)S(1)}, bf16[152,512]{1,0:T(8,128)(2,1)}, u32[]{:S(2)}) copy-start(bf16[152,512]{1,0:T(8,128)(2,1)} %param.11) | copy-start | bytes 466948
  7.2 3.4 %copy-start.4 = (bf16[152,512]{1,0:T(8,128)(2,1)S(1)}, bf16[152,512]{1,0:T(8,128)(2,1)}, u32[]{:S(2)}) copy-start(bf16[152,512]{1,0:T(8,128)(2,1)} %param.10) | copy-start | bytes 466948
  7.2 99.7 %all-gather.2.cloned.1.call-start = ((), (), s32[]{:S(2)}) async-start(), calls=%async_computation.3 | async-start | bytes 5603328 | tf_op jit(solution)/shard_map/all_gather | solution.py:120
  44.4 1.3 copy-start.1
  44.4 1.3 copy-start.2
  44.4 1.3 copy-start.3
  45.6 111.7 %reduce-scatter.2.cloned.1.call-start = ((), (), s32[]{:S(2)}) async-start(), calls=%async_computation.4 | async-start | bytes 2801664 | tf_op jit(solution)/shard_map/reduce_scatter | solution.py:123
  45.8 55.0 %collective-permute-start.2 = (bf16[3,192,1024]{2,1,0:T(8,128)(2,1)S(1)}, bf16[3,192,1024]{2,1,0:T(8,128)(2,1)S(1)}, u32[]{:S(2)}, u32[]{:S(2)}) collective-permute-start(bf16[3,192,1024]{2,1,0:T(8,128)(2,1)S(1)} %pad_maximum_fusion.refs_0_), channel_id=1, source_target_pairs={{0,384},{128,0},{256,128},{384,256},{1,385},{129,1},{257,129},{385... | collective-permute-start | bytes 3538952 | tf_op jit(solution)/shard_map/ppermute | solution.py:66
  50.2 50.6 %collective-permute-start.1 = (bf16[3,192,1024]{2,1,0:T(8,128)(2,1)S(1)}, bf16[3,192,1024]{2,1,0:T(8,128)(2,1)}, u32[]{:S(2)}, u32[]{:S(2)}) collective-permute-start(bf16[3,192,1024]{2,1,0:T(8,128)(2,1)S(1)} %pad_maximum_fusion.refs_0_), channel_id=1, source_target_pairs={{0,256},{128,384},{256,0},{384,128},{1,257},{129,385},{257,1},{385... | collective-permute-start | bytes 3538952 | tf_op jit(solution)/shard_map/ppermute | solution.py:66
  52.6 54.3 %collective-permute-start = (bf16[3,192,1024]{2,1,0:T(8,128)(2,1)S(1)}, bf16[3,192,1024]{2,1,0:T(8,128)(2,1)}, u32[]{:S(2)}, u32[]{:S(2)}) collective-permute-start(bf16[3,192,1024]{2,1,0:T(8,128)(2,1)S(1)} %pad_maximum_fusion.refs_0_), channel_id=1, source_target_pairs={{0,128},{128,256},{256,384},{384,0},{1,129},{129,257},{257,385},{3... | collective-permute-start | bytes 3538952 | tf_op jit(solution)/shard_map/ppermute | solution.py:66
  123.9 47.1 %collective-permute-start.5 = (bf16[192,1024]{1,0:T(8,128)(2,1)S(1)}, bf16[192,1024]{1,0:T(8,128)(2,1)S(1)}, u32[]{:S(2)}, u32[]{:S(2)}) collective-permute-start(bf16[192,1024]{1,0:T(8,128)(2,1)S(1)} %fusion.10), channel_id=1, source_target_pairs={{0,384},{128,0},{256,128},{384,256},{1,385},{129,1},{257,129},{385... | collective-permute-start | bytes 1179656 | tf_op jit(solution)/shard_map/ppermute | solution.py:78
  128.2 42.8 %collective-permute-start.3 = (bf16[192,1024]{1,0:T(8,128)(2,1)S(1)}, bf16[192,1024]{1,0:T(8,128)(2,1)S(1)}, u32[]{:S(2)}, u32[]{:S(2)}) collective-permute-start(bf16[192,1024]{1,0:T(8,128)(2,1)S(1)} %fusion.12), channel_id=1, source_target_pairs={{0,128},{128,256},{256,384},{384,0},{1,129},{129,257},{257,385},{3... | collective-permute-start | bytes 1179656 | tf_op jit(solution)/shard_map/ppermute | solution.py:78
  131.1 39.9 %collective-permute-start.4 = (bf16[192,1024]{1,0:T(8,128)(2,1)}, bf16[192,1024]{1,0:T(8,128)(2,1)S(1)}, u32[]{:S(2)}, u32[]{:S(2)}) collective-permute-start(bf16[192,1024]{1,0:T(8,128)(2,1)} %fusion.11), channel_id=1, source_target_pairs={{0,256},{128,384},{256,0},{384,128},{1,257},{129,385},{257,1},{385... | collective-permute-start | bytes 1179656 | tf_op jit(solution)/shard_map/ppermute | solution.py:78
  159.1 26.4 %all-to-all-start.1 = ((bf16[16,19,512]{2,1,0:T(8,128)(2,1)}), bf16[16,19,512]{2,1,0:T(8,128)(2,1)S(1)}, u32[]{:S(2)}, u32[]{:S(2)}) async-start(bf16[16,19,512]{2,1,0:T(8,128)(2,1)} %reshape.57), calls=%async_computation.2 | async-start | bytes 786432 | tf_op jit(solution)/shard_map/all_to_all | solution.py:131
Sparse Core Ops, SparseCore 0:
  45.7 60.9 all-gather.1
  116.4 40.8 reduce-scatter.1
